TPU v7x, 32 devices: a whole 2x2x4 slice. The times are simulated.
32 devices in a mesh: row: 4 (over y, x), col: 8 (over z, core).
Axes of the slice: x: 2, y: 2, z: 4, core: 2. Of those that a mesh axis runs over, the one named last changes fastest.
Arguments:
- p_tiles: float32 [2304, 4608], P('row', 'col'), may hold values from -0.6 to 0.6
- square_kept: int32 [36, 72], P('row', 'col'), may hold values 0 or 1
- result_kept: int32 [36, 72], P('row', 'col'), may hold values 0 or 1
Outputs:
- purified: float32 [2304, 4608], P('row', 'col')
Inputs may be any that keep to these rules, and one draw needn't show every extreme that they name: `square_kept`: one entry for each block of the layout of p_tiles. `result_kept`: one entry for each block of the layout of p_tiles.
All inputs are finite; a program needn't handle non-finite values.
Results may differ from a plain program's by a relative error of at most 0.0003.
Values sent between devices are 32-bit elements; how exact they have to be, the bound alone decides.
No kernel may reach another device: no remote copies, remote signals or barrier semaphores. Data moves between devices by JAX's collectives and lax.ppermute only.
A program may use at most 64 MiB of HBM per device.

v0:
```python
import jax
import jax.numpy as jnp
from jax import lax
from jax.sharding import PartitionSpec as P


def shifted(block, axis, distance):
    devices = range(lax.axis_size(axis))
    route = [((i - distance) % len(devices), i) for i in devices]
    return lax.ppermute(block, axis, route)


def mask_blocks(own_tile, kept_mask):
    block_count = kept_mask.shape[0]
    block_size = own_tile.shape[0] // block_count
    block_grid = own_tile.reshape(block_count, block_size, kept_mask.shape[1], block_size)
    block_grid = block_grid * kept_mask.astype(jnp.float32)[:, None, :, None]
    return block_grid.reshape(own_tile.shape)


def block_product(left_own, left_prev, left_next, right_own, right_prev, right_next):
    group_rows = left_own.shape[0] // 3
    full_side = 3 * group_rows
    lefts = ((0, left_own, 0), (1, left_next, group_rows), (-1, left_prev, 0))
    rights = ((0, right_own, 0), (1, right_next, group_rows), (-1, right_prev, 0))
    summed = jnp.zeros((full_side, full_side), jnp.float32)
    for row_step, left_part, row_start in lefts:
        for col_step, right_part, col_start in rights:
            product_term = jnp.dot(
                left_part[:, (col_step + 1) * group_rows : (col_step + 2) * group_rows],
                right_part[(row_step + 1) * group_rows : (row_step + 2) * group_rows, :],
                precision=lax.Precision.HIGHEST,
                preferred_element_type=jnp.float32,
            )
            row_after = full_side - row_start - product_term.shape[0]
            col_after = full_side - col_start - product_term.shape[1]
            summed = summed + jnp.pad(
                product_term, ((row_start, row_after), (col_start, col_after))
            )
    return summed


def column_sides(own_tile):
    group_rows = own_tile.shape[0] // 3
    before = shifted(own_tile, "col", 1)
    after = shifted(own_tile, "col", -1)
    return (before[group_rows:], after[: 2 * group_rows])


def row_sides(own_tile):
    group_rows = own_tile.shape[1] // 3
    before = shifted(own_tile, "row", 1)
    after = shifted(own_tile, "row", -1)
    return (before[:, group_rows:], after[:, : 2 * group_rows])


def on_device(p_tiles, square_kept, result_kept):
    left_prev, left_next = column_sides(p_tiles)
    right_prev, right_next = row_sides(p_tiles)
    square = block_product(p_tiles, left_prev, left_next, p_tiles, right_prev, right_next)
    square = mask_blocks(square, square_kept)
    square_prev, square_next = column_sides(square)
    cubed = block_product(square, square_prev, square_next, p_tiles, right_prev, right_next)
    return mask_blocks(3.0 * square - 2.0 * cubed, result_kept)


def solution(mesh):
    return jax.shard_map(
        on_device,
        mesh=mesh,
        in_specs=(P("row", "col"), P("row", "col"), P("row", "col")),
        out_specs=P("row", "col"),
        check_vma=False,
    )
```

profile of v0, /device:TPU:0, one launch (start us, length us, event | category | flops | bytes accessed | tf_op | source)
XLA Modules:
  0.0 139.8 jit_solution(15216078272679939620)
XLA Ops:
  0.0 0.5 collective-permute-start.3
  0.5 2.5 %collective-permute-start.1 = (f32[576,576]{1,0:T(8,128)}, f32[576,576]{1,0:T(8,128)S(1)}, u32[]{:S(2)}, u32[]{:S(2)}) collective-permute-start(f32[576,576]{1,0:T(8,128)} %param.3), channel_id=1, source_target_pairs={{24,0},{0,8},{8,16},{16,24},{25,1},{1,9},{9,17},{17,25},{26,2},{2,... | collective-permute-start | bytes 3981320 | tf_op jit(solution)/shard_map/ppermute | solution.py:10
  2.9 1.0 collective-permute-start
  4.0 3.2 %collective-permute-start.2 = (f32[576,576]{1,0:T(8,128)}, f32[576,576]{1,0:T(8,128)}, u32[]{:S(2)}, u32[]{:S(2)}) collective-permute-start(f32[576,576]{1,0:T(8,128)} %param.3), channel_id=1, source_target_pairs={{1,0},{2,1},{3,2},{4,3},{5,4},{6,5},{7,6},{0,7},{9,8},{10,9},{11,1... | collective-permute-start | bytes 3981320 | tf_op jit(solution)/shard_map/ppermute | solution.py:10
  7.2 0.7 convert_element_type.30
  7.9 2.5 %mul.34 = f32[9,64,9,64]{3,2,1,0:T(8,128)} broadcast(f32[9,9]{1,0:T(8,128)S(1)} %convert_element_type.30), dimensions={0,2} | broadcast | bytes 1327428 | tf_op jit(solution)/shard_map/mul | solution.py:17
  10.4 3.5 %mul.35 = f32[576,576]{1,0:T(8,128)S(1)} reshape(f32[9,64,9,64]{3,2,1,0:T(8,128)} %mul.34) | data formatting | bytes 2654208 | tf_op jit(solution)/shard_map/mul | solution.py:17
  13.9 1.6 %copy.18 = f32[576,576]{0,1:T(8,128)} copy(f32[576,576]{1,0:T(8,128)S(1)} %mul.35) | data formatting | bytes 2654208 | tf_op jit(solution)/shard_map/mul | solution.py:17
  15.5 0.0 copy-start
  15.5 17.1 %collective-permute-done.3 = f32[576,576]{1,0:T(8,128)} collective-permute-done((f32[576,576]{1,0:T(8,128)}, f32[576,576]{1,0:T(8,128)}, u32[]{:S(2)}, u32[]{:S(2)}) %collective-permute-start.3) | collective-permute-done | bytes 1327136 | tf_op jit(solution)/shard_map/ppermute | solution.py:10
  32.6 3.4 %collective-permute-done.1 = f32[576,576]{1,0:T(8,128)S(1)} collective-permute-done((f32[576,576]{1,0:T(8,128)}, f32[576,576]{1,0:T(8,128)S(1)}, u32[]{:S(2)}, u32[]{:S(2)}) %collective-permute-start.1) | collective-permute-done | bytes 1327136 | tf_op jit(solution)/shard_map/ppermute | solution.py:10
  36.0 0.0 copy-start.3
  36.0 2.2 %fusion.26 = f32[384,384]{0,1:T(8,128)S(1)} fusion(f32[576,576]{1,0:T(8,128)} %collective-permute-done.3, f32[576,576]{1,0:T(8,128)S(1)} %collective-permute-done.1), kind=kOutput, calls=%fused_computation.24 | convolution fusion | flops 339738624 | bytes 1277952 | tf_op jit(solution)/shard_map/dot_general | solution.py:29
  38.3 30.5 %collective-permute-done = f32[576,576]{1,0:T(8,128)} collective-permute-done((f32[576,576]{1,0:T(8,128)}, f32[576,576]{1,0:T(8,128)}, u32[]{:S(2)}, u32[]{:S(2)}) %collective-permute-start) | collective-permute-done | bytes 1327136 | tf_op jit(solution)/shard_map/ppermute | solution.py:10
  68.8 2.0 %fusion.28 = f32[384,384]{0,1:T(8,128)S(1)} fusion(f32[576,576]{1,0:T(8,128)} %collective-permute-done.3, f32[576,576]{1,0:T(8,128)} %collective-permute-done), kind=kOutput, calls=%fused_computation.26 | convolution fusion | flops 339738624 | bytes 1277952 | tf_op jit(solution)/shard_map/dot_general | solution.py:29
  70.8 0.0 copy-done
  70.8 2.5 %fusion.18 = f32[384,576]{0,1:T(8,128)S(1)} fusion(f32[576,576]{1,0:T(8,128)S(1)} %copy-done, f32[576,576]{1,0:T(8,128)} %collective-permute-done.3), kind=kOutput, calls=%fused_computation.16 | convolution fusion | flops 509607936 | bytes 1769472 | tf_op jit(solution)/shard_map/dot_general | solution.py:29
  73.3 0.0 collective-permute-done.2
  73.3 2.0 %fusion.31 = f32[384,384]{0,1:T(8,128)S(1)} fusion(f32[576,576]{1,0:T(8,128)} %collective-permute-done.2, f32[576,576]{1,0:T(8,128)S(1)} %collective-permute-done.1), kind=kOutput, calls=%fused_computation.29 | convolution fusion | flops 339738624 | bytes 1277952 | tf_op jit(solution)/shard_map/dot_general | solution.py:29
  75.2 2.0 %fusion.33 = f32[384,384]{0,1:T(8,128)S(1)} fusion(f32[576,576]{1,0:T(8,128)} %collective-permute-done.2, f32[576,576]{1,0:T(8,128)} %collective-permute-done), kind=kOutput, calls=%fused_computation.31 | convolution fusion | flops 339738624 | bytes 1277952 | tf_op jit(solution)/shard_map/dot_general | solution.py:29
  77.2 2.5 %fusion.22 = f32[384,576]{0,1:T(8,128)S(1)} fusion(f32[576,576]{1,0:T(8,128)S(1)} %copy-done, f32[576,576]{1,0:T(8,128)} %collective-permute-done.2), kind=kOutput, calls=%fused_computation.20 | convolution fusion | flops 509607936 | bytes 1769472 | tf_op jit(solution)/shard_map/dot_general | solution.py:29
  79.7 0.0 copy-done.3
  79.7 0.0 copy-start.1
  79.7 1.3 fusion
  81.0 2.1 %fusion.2 = f32[576,384]{0,1:T(8,128)S(1)} fusion(f32[576,576]{1,0:T(8,128)S(1)} %copy-done, f32[576,576]{1,0:T(8,128)} %collective-permute-done), kind=kOutput, calls=%fused_computation.4 | convolution fusion | flops 509607936 | bytes 1769472 | tf_op jit(solution)/shard_map/dot_general | solution.py:29
  83.2 0.0 copy-done.1
  83.2 0.0 copy-start.4
  83.2 2.6 %add_multiply_fusion = f32[576,576]{0,1:T(8,128)S(1)} fusion(f32[576,576]{0,1:T(8,128)S(1)} %copy-done.1, f32[384,384]{0,1:T(8,128)S(1)} %fusion.26, f32[384,384]{0,1:T(8,128)S(1)} %fusion.28, f32[384,576]{0,1:T(8,128)S(1)} %fusion.18, f32[384,384]{0,1:T(8,128)S(1)} %fusion.31, f32[384,384]{0,1:T(8,128)S(1)} %fusion.33, f32[384,576]{0,1:T(8,128)S(1)} %fusion.22, ...), kind=kOutput, calls=%fused_computation.1 | convolution fusion | flops 767397888 | bytes 9977856 | tf_op jit(solution)/shard_map/dot_general | solution.py:29
  85.8 0.6 collective-permute-start.5
  86.4 3.0 %collective-permute-start.4 = (f32[576,576]{0,1:T(8,128)S(1)}, f32[576,576]{0,1:T(8,128)}, u32[]{:S(2)}, u32[]{:S(2)}) collective-permute-start(f32[576,576]{0,1:T(8,128)S(1)} %add_multiply_fusion), channel_id=1, source_target_pairs={{1,0},{2,1},{3,2},{4,3},{5,4},{6,5},{7,6},{0,7},{9,8},{10,9},{11,1... | collective-permute-start | bytes 3981320 | tf_op jit(solution)/shard_map/ppermute | solution.py:10
  89.4 0.0 copy-done.4
  89.4 2.5 %mul.41 = f32[9,64,9,64]{3,2,1,0:T(8,128)} broadcast(f32[9,9]{1,0:T(8,128)S(1)} %convert_element_type.31), dimensions={0,2} | broadcast | bytes 1327428 | tf_op jit(solution)/shard_map/mul | solution.py:17
  91.9 4.6 %mul.42 = f32[576,576]{1,0:T(8,128)} reshape(f32[9,64,9,64]{3,2,1,0:T(8,128)} %mul.41) | data formatting | bytes 2654208 | tf_op jit(solution)/shard_map/mul | solution.py:17
  96.5 3.0 %copy.26 = f32[576,576]{0,1:T(8,128)} copy(f32[576,576]{1,0:T(8,128)} %mul.42) | data formatting | bytes 2654208 | tf_op jit(solution)/shard_map/mul | solution.py:17
  99.5 2.3 %fusion.8 = f32[576,384]{0,1:T(8,128)S(1)} fusion(f32[576,576]{0,1:T(8,128)S(1)} %add_multiply_fusion, f32[576,576]{1,0:T(8,128)} %copy-done.3), kind=kOutput, calls=%fused_computation.8 | convolution fusion | flops 509607936 | bytes 1671168 | tf_op jit(solution)/shard_map/dot_general | solution.py:29
  101.8 2.1 %fusion.10 = f32[576,384]{0,1:T(8,128)S(1)} fusion(f32[576,576]{0,1:T(8,128)S(1)} %add_multiply_fusion, f32[576,576]{1,0:T(8,128)} %collective-permute-done), kind=kOutput, calls=%fused_computation.10 | convolution fusion | flops 509607936 | bytes 1671168 | tf_op jit(solution)/shard_map/dot_general | solution.py:29
  104.0 16.1 %collective-permute-done.5 = f32[576,576]{0,1:T(8,128)} collective-permute-done((f32[576,576]{0,1:T(8,128)S(1)}, f32[576,576]{0,1:T(8,128)}, u32[]{:S(2)}, u32[]{:S(2)}) %collective-permute-start.5) | collective-permute-done | bytes 1327136 | tf_op jit(solution)/shard_map/ppermute | solution.py:10
  120.1 2.2 %fusion.36 = f32[384,384]{0,1:T(8,128)S(1)} fusion(f32[576,576]{0,1:T(8,128)} %collective-permute-done.5, f32[576,576]{1,0:T(8,128)} %copy-done.3), kind=kOutput, calls=%fused_computation.34 | convolution fusion | flops 339738624 | bytes 1179648 | tf_op jit(solution)/shard_map/dot_general | solution.py:29
  122.3 2.1 %fusion.38 = f32[384,384]{0,1:T(8,128)S(1)} fusion(f32[576,576]{0,1:T(8,128)} %collective-permute-done.5, f32[576,576]{1,0:T(8,128)} %collective-permute-done), kind=kOutput, calls=%fused_computation.36 | convolution fusion | flops 339738624 | bytes 1179648 | tf_op jit(solution)/shard_map/dot_general | solution.py:29
  124.4 2.3 %fusion.16 = f32[384,576]{0,1:T(8,128)S(1)} fusion(f32[576,576]{1,0:T(8,128)S(1)} %copy-done, f32[576,576]{0,1:T(8,128)} %collective-permute-done.5), kind=kOutput, calls=%fused_computation.14 | convolution fusion | flops 509607936 | bytes 1671168 | tf_op jit(solution)/shard_map/dot_general | solution.py:29
  126.8 0.0 collective-permute-done.4
  126.8 2.1 %fusion.41 = f32[384,384]{0,1:T(8,128)S(1)} fusion(f32[576,576]{0,1:T(8,128)} %collective-permute-done.4, f32[576,576]{1,0:T(8,128)} %copy-done.3), kind=kOutput, calls=%fused_computation.39 | convolution fusion | flops 339738624 | bytes 1179648 | tf_op jit(solution)/shard_map/dot_general | solution.py:29
  128.9 0.0 copy-start.2
  128.9 2.1 %fusion.43 = f32[384,384]{0,1:T(8,128)S(1)} fusion(f32[576,576]{0,1:T(8,128)} %collective-permute-done.4, f32[576,576]{1,0:T(8,128)} %collective-permute-done), kind=kOutput, calls=%fused_computation.41 | convolution fusion | flops 339738624 | bytes 1179648 | tf_op jit(solution)/shard_map/dot_general | solution.py:29
  130.9 2.2 %fusion.20 = f32[384,576]{0,1:T(8,128)S(1)} fusion(f32[576,576]{1,0:T(8,128)S(1)} %copy-done, f32[576,576]{0,1:T(8,128)} %collective-permute-done.4), kind=kOutput, calls=%fused_computation.18 | convolution fusion | flops 509607936 | bytes 1671168 | tf_op jit(solution)/shard_map/dot_general | solution.py:29
  133.2 0.0 copy-done.2
  133.2 3.7 %subtract_multiply_fusion = f32[576,576]{0,1:T(8,128)} fusion(f32[576,576]{0,1:T(8,128)S(1)} %copy-done.2, f32[384,384]{0,1:T(8,128)S(1)} %fusion.36, f32[384,384]{0,1:T(8,128)S(1)} %fusion.38, f32[384,576]{0,1:T(8,128)S(1)} %fusion.16, f32[384,384]{0,1:T(8,128)S(1)} %fusion.41, f32[384,384]{0,1:T(8,128)S(1)} %fusion.43, f32[384,576]{0,1:T(8,128)S(1)} %fusion.20, ...), kind=kOutput, calls=%fused_computation | convolution fusion | flops 768393216 | bytes 11354112 | tf_op jit(solution)/shard_map/dot_general | solution.py:29
  136.9 3.0 %copy.27 = f32[576,576]{1,0:T(8,128)} copy(f32[576,576]{0,1:T(8,128)} %subtract_multiply_fusion) | data formatting | bytes 2654208 | tf_op jit(solution)/shard_map/mul | solution.py:17
  (1 shorter events, 0.0 us)
Async XLA Ops:
  0.0 32.6 %collective-permute-start.3 = (f32[576,576]{1,0:T(8,128)}, f32[576,576]{1,0:T(8,128)}, u32[]{:S(2)}, u32[]{:S(2)}) collective-permute-start(f32[576,576]{1,0:T(8,128)} %param.3), channel_id=1, source_target_pairs={{7,0},{0,1},{1,2},{2,3},{3,4},{4,5},{5,6},{6,7},{15,8},{8,9},{9,10... | collective-permute-start | bytes 3981320 | tf_op jit(solution)/shard_map/ppermute | solution.py:10
  0.5 35.6 %collective-permute-start.1 = (f32[576,576]{1,0:T(8,128)}, f32[576,576]{1,0:T(8,128)S(1)}, u32[]{:S(2)}, u32[]{:S(2)}) collective-permute-start(f32[576,576]{1,0:T(8,128)} %param.3), channel_id=1, source_target_pairs={{24,0},{0,8},{8,16},{16,24},{25,1},{1,9},{9,17},{17,25},{26,2},{2,... | collective-permute-start | bytes 3981320 | tf_op jit(solution)/shard_map/ppermute | solution.py:10
  2.9 65.9 %collective-permute-start = (f32[576,576]{1,0:T(8,128)}, f32[576,576]{1,0:T(8,128)}, u32[]{:S(2)}, u32[]{:S(2)}) collective-permute-start(f32[576,576]{1,0:T(8,128)} %param.3), channel_id=1, source_target_pairs={{8,0},{16,8},{24,16},{0,24},{9,1},{17,9},{25,17},{1,25},{10,2},{18... | collective-permute-start | bytes 3981320 | tf_op jit(solution)/shard_map/ppermute | solution.py:10
  4.0 69.3 %collective-permute-start.2 = (f32[576,576]{1,0:T(8,128)}, f32[576,576]{1,0:T(8,128)}, u32[]{:S(2)}, u32[]{:S(2)}) collective-permute-start(f32[576,576]{1,0:T(8,128)} %param.3), channel_id=1, source_target_pairs={{1,0},{2,1},{3,2},{4,3},{5,4},{6,5},{7,6},{0,7},{9,8},{10,9},{11,1... | collective-permute-start | bytes 3981320 | tf_op jit(solution)/shard_map/ppermute | solution.py:10
  15.5 55.3 %copy-start = (f32[576,576]{1,0:T(8,128)S(1)}, f32[576,576]{1,0:T(8,128)}, u32[]{:S(2)}) copy-start(f32[576,576]{1,0:T(8,128)} %param.3) | copy-start | bytes 3981316
  36.0 43.7 %copy-start.3 = (f32[576,576]{1,0:T(8,128)}, f32[576,576]{1,0:T(8,128)S(1)}, u32[]{:S(2)}) copy-start(f32[576,576]{1,0:T(8,128)S(1)} %collective-permute-done.1) | copy-start | bytes 3981316
  79.7 3.5 %copy-start.1 = (f32[576,576]{0,1:T(8,128)S(1)}, f32[576,576]{0,1:T(8,128)}, u32[]{:S(2)}) copy-start(f32[576,576]{0,1:T(8,128)} %copy.18) | copy-start | bytes 3981316
  83.2 6.2 %copy-start.4 = (s32[9,9]{1,0:T(8,128)S(1)}, s32[9,9]{1,0:T(8,128)}, u32[]{:S(2)}) copy-start(s32[9,9]{1,0:T(8,128)} %param.5) | copy-start | bytes 976
  85.8 34.3 %collective-permute-start.5 = (f32[576,576]{0,1:T(8,128)S(1)}, f32[576,576]{0,1:T(8,128)}, u32[]{:S(2)}, u32[]{:S(2)}) collective-permute-start(f32[576,576]{0,1:T(8,128)S(1)} %add_multiply_fusion), channel_id=1, source_target_pairs={{7,0},{0,1},{1,2},{2,3},{3,4},{4,5},{5,6},{6,7},{15,8},{8,9},{9,10... | collective-permute-start | bytes 3981320 | tf_op jit(solution)/shard_map/ppermute | solution.py:10
  86.4 40.4 %collective-permute-start.4 = (f32[576,576]{0,1:T(8,128)S(1)}, f32[576,576]{0,1:T(8,128)}, u32[]{:S(2)}, u32[]{:S(2)}) collective-permute-start(f32[576,576]{0,1:T(8,128)S(1)} %add_multiply_fusion), channel_id=1, source_target_pairs={{1,0},{2,1},{3,2},{4,3},{5,4},{6,5},{7,6},{0,7},{9,8},{10,9},{11,1... | collective-permute-start | bytes 3981320 | tf_op jit(solution)/shard_map/ppermute | solution.py:10
  128.9 4.3 %copy-start.2 = (f32[576,576]{0,1:T(8,128)S(1)}, f32[576,576]{0,1:T(8,128)}, u32[]{:S(2)}) copy-start(f32[576,576]{0,1:T(8,128)} %copy.26) | copy-start | bytes 3981316
where the time goes:
time: 141 us; the launch traced here: 140 us
  waiting for transfers between devices  67.2 us (48%)
  matrix products  40.2 us (29%)
  local copies, waits for them, and re-layouts  20.7 us (15%)
  starting transfers between devices  10.8 us (8%)
    ppermute x6, waiting for transfers between devices, shifted(): return lax.ppermute(block, axis, route)  67.2 us
    dot_general x18, matrix products, block_product(): jnp.dot(left_part[:, (col_step + 1) * group_rows:(col_step + 2) * group_r...  40.2 us
    mul x7, local copies, waits for them, and re-layouts, mask_blocks(): block_grid = block_grid * kept_mask.astype(jnp.float32)[:, None, :, None]  20.7 us
    ppermute x6, starting transfers between devices, shifted(): return lax.ppermute(block, axis, route)  10.8 us
  transfers between devices with their start and end apart: 6, of which 4 were waited for; matrix products, arithmetic and copies ran while one was open for 26% of the time, Pallas kernels for 0%

commit v1 on v0

v1 whole, which is shorter than its diff:
```python
import functools

import jax
import jax.numpy as jnp
from jax import lax
from jax.experimental import pallas as pl
from jax.experimental.pallas import tpu as pltpu
from jax.sharding import PartitionSpec as P

LANES = 128
WIDE = 256
F32 = jnp.float32
BF16 = jnp.bfloat16


def low_half(rows):
    return lax.broadcasted_iota(jnp.int32, (rows, LANES), 1) < LANES // 2


def fold(first, second):
    half = first.shape[0] // 2
    tail = jnp.where(low_half(half), second[:half], pltpu.roll(second[half:], LANES // 2, 1))
    return first, tail


def unfold(packed):
    rows = packed.shape[0] * 2 // 3
    half = rows // 2
    tail = packed[rows:]
    keep = low_half(half)
    upper = jnp.where(keep, tail, 0.0)
    lower = jnp.where(keep, pltpu.roll(tail, LANES // 2, 1), 0.0)
    return jnp.concatenate([packed[:rows], jnp.concatenate([upper, lower], 0)], 1)


def column_group(tile_ref, group, start, rows):
    keep = low_half(rows)
    at = pl.ds(start, rows)
    if group == 0:
        return tile_ref[at, 0:128], jnp.where(keep, tile_ref[at, 128:256], 0.0)
    if group == 1:
        one = pltpu.roll(tile_ref[at, 128:256], LANES // 2, 1)
        two = pltpu.roll(tile_ref[at, 256:384], LANES // 2, 1)
        return jnp.where(keep, one, two), jnp.where(keep, two, 0.0)
    last = tile_ref[at, 512:576]
    return tile_ref[at, 384:512], jnp.concatenate([last, jnp.zeros_like(last)], 1)


def split(value):
    high = value.astype(BF16)
    return high, (value - high.astype(F32)).astype(BF16)


def store_fold(out_ref, base, first, second):
    rows = first.shape[0]
    one, two = fold(first, second)
    out_ref[pl.ds(base, rows), :] = one
    out_ref[pl.ds(base + rows, rows // 2), :] = two


def pack_body(tile_ref, to_next, to_prev, middle, left, right):
    side = tile_ref.shape[0]
    group = side // 3
    for g in range(3):
        first, second = column_group(tile_ref, g, 0, side)
        store_fold((left, middle, right)[g], 0, first, second)
        store_fold(to_next, g * 3 * group, first[group:], second[group:])
        store_fold(to_prev, g * 3 * group, first[: 2 * group], second[: 2 * group])


def left_factors(value):
    high, low = split(value)
    return high, low


def right_rows(high, low, ky, group):
    at = slice(ky * group, (ky + 1) * group)
    pad = jnp.zeros((WIDE - group, WIDE), BF16)
    return jnp.concatenate([high[at], pad], 0), jnp.concatenate([low[at], pad], 0)


def passes(lefts, rights):
    wide = [high for high, _ in lefts] + [low for _, low in lefts] + [high for high, _ in lefts]
    tall = [high for high, _ in rights] + [high for high, _ in rights] + [low for _, low in rights]
    return jnp.dot(jnp.concatenate(wide, 1), jnp.concatenate(tall, 0), preferred_element_type=F32)


def mask_lanes(kept_ref, row, first_block):
    lane = lax.broadcasted_iota(jnp.int32, (8, WIDE), 1)
    flags = [kept_ref[row, first_block + j] for j in range(3)]
    chosen = jnp.where(lane < 64, flags[0], jnp.where(lane < 128, flags[1], flags[2]))
    return chosen.astype(F32)[:1]


def masked(value, kept_ref, group_index):
    rows = value.shape[0] // 9
    return jnp.concatenate(
        [value[i * rows : (i + 1) * rows] * mask_lanes(kept_ref, i, 3 * group_index) for i in range(9)], 0
    )


def stacked(own, before, after):
    group = own.shape[0] // 3
    return jnp.concatenate(
        [
            own[:group] + before[:group],
            own[group : 2 * group] + before[group:] + after[:group],
            own[2 * group :] + after[group:],
        ],
        0,
    )


def product(lefts, rights, group):
    parts = [
        passes(lefts[ky], [right_rows(high, low, ky, group) for high, low in rights]) for ky in range(3)
    ]
    return stacked(parts[1], parts[0], parts[2])


def load_left(packed_ref, group):
    return [split(unfold(packed_ref[g * 3 * group : (g + 1) * 3 * group, :])) for g in range(3)]


def own_group(tile_ref, g):
    side = tile_ref.shape[0]
    return split(jnp.concatenate(column_group(tile_ref, g, 0, side), 1))


def store_sides(value, g, to_next, to_prev, base):
    group = value.shape[0] // 3
    store_fold(to_next, base, value[group:, :LANES], value[group:, LANES:])
    store_fold(to_prev, base, value[: 2 * group, :LANES], value[: 2 * group, LANES:])


def neighbours(odd_ref, near_ref, far_ref):
    odd = odd_ref[0] == 1
    near, far = near_ref[...], far_ref[...]
    prev = jnp.where(odd, near, far)
    after = jnp.where(odd, far, near)
    return prev, after


def sides_body(odd, kept, tile, from_prev, from_next, near, far, out_first, out_last, to_next, to_prev):
    group = tile.shape[0] // 3
    own = [own_group(tile, g) for g in range(3)]
    lefts = [load_left(from_prev, group), own, load_left(from_next, group)]
    prev, after = neighbours(odd, near, far)
    first = product([l[:2] for l in lefts], [split(unfold(prev)), own[0]], group)
    first = masked(first, kept, 0)
    out_first[...] = first
    store_sides(first, 0, to_next, to_prev, 0)
    last = product([l[1:] for l in lefts], [own[2], split(unfold(after))], group)
    last = masked(last, kept, 2)
    out_last[...] = last
    store_sides(last, 2, to_next, to_prev, 3 * group)


def middle_body(kept, tile, from_prev, from_next, prev_right, next_left, out, to_next, to_prev):
    group = tile.shape[0] // 3
    own = [own_group(tile, g) for g in range(3)]
    lefts = [load_left(from_prev, group), own, load_left(from_next, group)]
    value = product(lefts, [split(unfold(prev_right[...])), own[1], split(unfold(next_left[...]))], group)
    value = masked(value, kept, 1)
    out[...] = value
    store_sides(value, 1, to_next, to_prev, 0)


def cube_own_body(odd, tile, near, far, prev_right, next_left, first, middle, last, out):
    group = tile.shape[0] // 3
    own = [own_group(tile, g) for g in range(3)]
    prev, after = neighbours(odd, near, far)
    squares = [split(ref[...]) for ref in (first, middle, last)]
    columns = (
        (squares[:2], [split(unfold(prev)), own[0]]),
        (squares, [split(unfold(prev_right[...])), own[1], split(unfold(next_left[...]))]),
        (squares[1:], [own[2], split(unfold(after))]),
    )
    for g, (lefts, rights) in enumerate(columns):
        out[g] = passes(lefts, [right_rows(high, low, 1, group) for high, low in rights])


def add_sides(out, g, total, before, after):
    out[g] = total + jnp.concatenate([before, jnp.zeros_like(before[: before.shape[0] // 2])], 0) + jnp.concatenate(
        [jnp.zeros_like(after[: after.shape[0] // 2]), after], 0
    )


def cube_sides_body(odd, near, far, prev_right, next_left, from_prev, from_next, total, out):
    group = from_prev.shape[0] // 6
    prev, after = neighbours(odd, near, far)
    rights = {
        (0, 0): split(unfold(prev)),
        (0, 1): split(unfold(prev_right[...])),
        (2, 1): split(unfold(next_left[...])),
        (2, 2): split(unfold(after)),
    }
    lefts = {
        (source, kx): split(unfold(ref[at * 3 * group : (at + 1) * 3 * group, :]))
        for source, ref in ((0, from_prev), (2, from_next))
        for at, kx in ((0, 0), (1, 2))
    }
    for g, kxs in ((0, (0,)), (1, (0, 2)), (2, (2,))):
        before, later = (
            passes([lefts[source, kx] for kx in kxs], [right_rows(*rights[kx, g], source, group) for kx in kxs])
            for source in (0, 2)
        )
        add_sides(out, g, total[g], before, later)


def finish_body(kept, tile, from_prev, from_next, first, middle, last, total, out):
    group = tile.shape[0] // 3
    lefts = [split(unfold(ref[...])) for ref in (from_prev, from_next)]
    pieces = []
    for g, square in enumerate((first, middle, last)):
        own = own_group(tile, g)
        before = passes([lefts[0]], [right_rows(*own, 0, group)])
        after = passes([lefts[1]], [right_rows(*own, 2, group)])
        cubed = stacked(total[g], before, after)
        pieces.append(masked(3.0 * square[...] - 2.0 * cubed, kept, g))
    for g, (value, start) in enumerate(zip(pieces, (0, group, 2 * group))):
        out[:, start : start + group] = value[:, :group]


VMEM = pl.BlockSpec(memory_space=pltpu.VMEM)
SMEM = pl.BlockSpec(memory_space=pltpu.SMEM)


def call(body, scalars, arrays, outs, name):
    return pl.pallas_call(
        body,
        out_shape=[jax.ShapeDtypeStruct(shape, F32) for shape in outs],
        in_specs=[SMEM] * len(scalars) + [VMEM] * len(arrays),
        out_specs=[VMEM] * len(outs),
        compiler_params=pltpu.CompilerParams(vmem_limit_bytes=40 << 20),
        name=name,
    )(*scalars, *arrays)


def shifted(block, axis, distance):
    size = lax.axis_size(axis)
    return lax.ppermute(block, axis, [((i - distance) % size, i) for i in range(size)])


def on_device(p_tiles, square_kept, result_kept):
    side = p_tiles.shape[0]
    group = side // 3
    rows = lax.axis_size("row")
    odd = (lax.axis_index("row") % 2).astype(jnp.int32).reshape(1)
    strip = (3 * side // 2, LANES)
    slab = (3 * group, LANES)
    wide = (side, WIDE)

    to_next, to_prev, middle, left, right = call(
        pack_body, (), (p_tiles,), [(9 * group, LANES)] * 2 + [strip] * 3, "pack"
    )
    near = lax.ppermute(middle, "row", [(i, i ^ 1) for i in range(rows)])
    from_prev = shifted(to_next, "col", 1)
    from_next = shifted(to_prev, "col", -1)
    prev_right = shifted(right, "row", 1)
    next_left = shifted(left, "row", -1)
    far = lax.ppermute(near, "row", [(i, (i + (2 if i % 2 == 0 else -2)) % rows) for i in range(rows)])

    first, last, out_next, out_prev = call(
        sides_body,
        (odd, square_kept),
        (p_tiles, from_prev, from_next, near, far),
        [wide] * 2 + [(6 * group, LANES)] * 2,
        "square_sides",
    )
    sides_prev = shifted(out_next, "col", 1)
    sides_next = shifted(out_prev, "col", -1)
    centre, out_next, out_prev = call(
        middle_body,
        (square_kept,),
        (p_tiles, from_prev, from_next, prev_right, next_left),
        [wide] + [slab] * 2,
        "square_middle",
    )
    centre_prev = shifted(out_next, "col", 1)
    centre_next = shifted(out_prev, "col", -1)
    (total,) = call(
        cube_own_body,
        (odd,),
        (p_tiles, near, far, prev_right, next_left, first, centre, last),
        [(3,) + wide],
        "cube_own",
    )
    (total,) = call(
        cube_sides_body,
        (odd,),
        (near, far, prev_right, next_left, sides_prev, sides_next, total),
        [(3,) + wide],
        "cube_sides",
    )
    (purified,) = call(
        finish_body,
        (result_kept,),
        (p_tiles, centre_prev, centre_next, first, centre, last, total),
        [(side, side)],
        "cube_finish",
    )
    return purified


def solution(mesh):
    return jax.shard_map(
        on_device,
        mesh=mesh,
        in_specs=(P("row", "col"), P("row", "col"), P("row", "col")),
        out_specs=P("row", "col"),
        check_vma=False,
    )
```

time: 141 us -> 68.4 us (0.49)
  the two profiles are of different devices: /device:TPU:0 before, /device:TPU:1 now
where the time goes in v1:
time: 68.4 us; the launch traced here: 68.2 us
  waiting for transfers between devices  37.1 us (54%)
  Pallas kernels  15.5 us (23%)
  starting transfers between devices  13.5 us (20%)
  local copies, waits for them, and re-layouts  2.07 us (3%)
    ppermute x1, waiting for transfers between devices, on_device(): lax.ppermute(near, 'row', [(i, (i + (2 if i % 2 == 0 else -2)) % rows) fo...  16.5 us
    pallas_call x6, Pallas kernels, call(): pl.pallas_call(body, out_shape=[jax.ShapeDtypeStruct(shape, F32) for shap...  15.5 us
    ppermute x8, waiting for transfers between devices, shifted(): lax.ppermute(block, axis, [((i - distance) % size, i) for i in range(size)])  12.7 us
    ppermute x8, starting transfers between devices, shifted(): lax.ppermute(block, axis, [((i - distance) % size, i) for i in range(size)])  10.3 us
    ppermute x1, waiting for transfers between devices, on_device(): near = lax.ppermute(middle, 'row', [(i, i ^ 1) for i in range(rows)])  7.86 us
    unnamed x8, local copies, waits for them, and re-layouts  2.07 us
    ppermute x1, starting transfers between devices, on_device(): near = lax.ppermute(middle, 'row', [(i, i ^ 1) for i in range(rows)])  2.04 us
  transfers between devices with their start and end apart: 10, of which 5 were waited for; matrix products, arithmetic and copies ran while one was open for 0% of the time, Pallas kernels for 15%

profile of v1, /device:TPU:1, one launch (start us, length us, event | category | flops | bytes accessed | tf_op | source)
XLA Modules:
  0.0 68.2 jit_solution(8781420191539409786)
XLA Ops:
  0.0 0.0 copy-start
  0.0 1.4 %copy-done = f32[576,576]{1,0:T(8,128)S(1)} copy-done((f32[576,576]{1,0:T(8,128)S(1)}, f32[576,576]{1,0:T(8,128)}, u32[]{:S(2)}) %copy-start) | copy-done | bytes 1327128
  1.4 0.0 copy-start.1
  1.4 1.9 %pack.1 = (f32[1728,128]{1,0:T(8,128)}, f32[1728,128]{1,0:T(8,128)}, f32[864,128]{1,0:T(8,128)S(1)}, f32[864,128]{1,0:T(8,128)}, f32[864,128]{1,0:T(8,128)}) custom-call(f32[576,576]{1,0:T(8,128)S(1)} %copy-done), custom_call_target="tpu_custom_call" | custom-call | tf_op jit(solution)/shard_map/pack/pallas_call | solution.py:230
  3.3 2.0 %collective-permute-start.6 = (f32[864,128]{1,0:T(8,128)S(1)}, f32[864,128]{1,0:T(8,128)S(1)}, u32[]{:S(2)}, u32[]{:S(2)}) collective-permute-start(f32[864,128]{1,0:T(8,128)S(1)} %get-tuple-element.23), channel_id=1, source_target_pairs={{0,8},{8,0},{16,24},{24,16},{1,9},{9,1},{17,25},{25,17},{2,10},{10... | collective-permute-start | bytes 1327112 | tf_op jit(solution)/shard_map/ppermute | solution.py:257
  5.4 2.1 %collective-permute-start = (f32[1728,128]{1,0:T(8,128)}, f32[1728,128]{1,0:T(8,128)}, u32[]{:S(2)}, u32[]{:S(2)}) collective-permute-start(f32[1728,128]{1,0:T(8,128)} %get-tuple-element.17), channel_id=1, source_target_pairs={{7,0},{0,1},{1,2},{2,3},{3,4},{4,5},{5,6},{6,7},{15,8},{8,9},{9,10... | collective-permute-start | bytes 2654216 | tf_op jit(solution)/shard_map/ppermute | solution.py:242
  7.5 0.0 collective-permute-start.1
  7.5 7.9 %collective-permute-done.6.near = f32[864,128]{1,0:T(8,128)S(1)} collective-permute-done((f32[864,128]{1,0:T(8,128)S(1)}, f32[864,128]{1,0:T(8,128)S(1)}, u32[]{:S(2)}, u32[]{:S(2)}) %collective-permute-start.6) | collective-permute-done | bytes 442400 | tf_op jit(solution)/shard_map/ppermute | solution.py:257
  15.4 1.2 %collective-permute-start.7 = (f32[864,128]{1,0:T(8,128)S(1)}, f32[864,128]{1,0:T(8,128)S(1)}, u32[]{:S(2)}, u32[]{:S(2)}) collective-permute-start(f32[864,128]{1,0:T(8,128)S(1)} %collective-permute-done.6.near), channel_id=1, source_target_pairs={{0,16},{8,24},{16,0},{24,8},{1,17},{9,25},{17,1},{25,9},{2,18},{10... | collective-permute-start | bytes 1327112 | tf_op jit(solution)/shard_map/ppermute | solution.py:262
  16.5 1.2 %collective-permute-start.2 = (f32[864,128]{1,0:T(8,128)}, f32[864,128]{1,0:T(8,128)S(1)}, u32[]{:S(2)}, u32[]{:S(2)}) collective-permute-start(f32[864,128]{1,0:T(8,128)} %get-tuple-element.19), channel_id=1, source_target_pairs={{24,0},{0,8},{8,16},{16,24},{25,1},{1,9},{9,17},{17,25},{26,2},{2,... | collective-permute-start | bytes 1327112 | tf_op jit(solution)/shard_map/ppermute | solution.py:242
  17.7 1.2 %collective-permute-start.3 = (f32[864,128]{1,0:T(8,128)}, f32[864,128]{1,0:T(8,128)S(1)}, u32[]{:S(2)}, u32[]{:S(2)}) collective-permute-start(f32[864,128]{1,0:T(8,128)} %get-tuple-element.20), channel_id=1, source_target_pairs={{8,0},{16,8},{24,16},{0,24},{9,1},{17,9},{25,17},{1,25},{10,2},{18... | collective-permute-start | bytes 1327112 | tf_op jit(solution)/shard_map/ppermute | solution.py:242
  18.9 16.5 %collective-permute-done.7.far = f32[864,128]{1,0:T(8,128)S(1)} collective-permute-done((f32[864,128]{1,0:T(8,128)S(1)}, f32[864,128]{1,0:T(8,128)S(1)}, u32[]{:S(2)}, u32[]{:S(2)}) %collective-permute-start.7) | collective-permute-done | bytes 442400 | tf_op jit(solution)/shard_map/ppermute | solution.py:262
  35.4 0.0 collective-permute-done.from_prev
  35.4 0.0 collective-permute-done.1.from_next
  35.4 0.0 copy-done.1
  35.4 0.0 copy-start.2
  35.4 0.7 %copy-done.2 = s32[9,9]{1,0:T(8,128)S(1)} copy-done((s32[9,9]{1,0:T(8,128)S(1)}, s32[9,9]{1,0:T(8,128)}, u32[]{:S(2)}) %copy-start.2) | copy-done | bytes 348
  36.1 3.9 %square_sides.1 = (f32[576,256]{1,0:T(8,128)S(1)}, f32[576,256]{1,0:T(8,128)S(1)}, f32[1152,128]{1,0:T(8,128)S(1)}, f32[1152,128]{1,0:T(8,128)S(1)}) custom-call(s32[1]{0:T(128)} %bitcast.odd, s32[9,9]{1,0:T(8,128)S(1)} %copy-done.2, f32[576,576]{1,0:T(8,128)S(1)} %copy-done.1, f32[1728,128]{1,0:T(8,128)} %collective-permute-done.from_prev, ...), custom_call_target="tpu_custom_call" | custom-call | tf_op jit(solution)/shard_map/square_sides/pallas_call | solution.py:230
  40.0 3.2 %collective-permute-start.8 = (f32[1152,128]{1,0:T(8,128)S(1)}, f32[1152,128]{1,0:T(8,128)S(1)}, u32[]{:S(2)}, u32[]{:S(2)}) collective-permute-start(f32[1152,128]{1,0:T(8,128)S(1)} %get-tuple-element.27), channel_id=1, source_target_pairs={{7,0},{0,1},{1,2},{2,3},{3,4},{4,5},{5,6},{6,7},{15,8},{8,9},{9,10... | collective-permute-start | bytes 1769480 | tf_op jit(solution)/shard_map/ppermute | solution.py:242
  43.2 0.0 collective-permute-start.9
  43.2 0.0 collective-permute-done.2.prev_right
  43.2 0.0 collective-permute-done.3.next_left
  43.2 3.3 %square_middle.1 = (f32[576,256]{1,0:T(8,128)S(1)}, f32[576,128]{1,0:T(8,128)S(1)}, f32[576,128]{1,0:T(8,128)S(1)}) custom-call(s32[9,9]{1,0:T(8,128)S(1)} %copy-done.2, f32[576,576]{1,0:T(8,128)S(1)} %copy-done.1, f32[1728,128]{1,0:T(8,128)} %collective-permute-done.from_prev, f32[1728,128]{1,0:T(8,128)} %collective-permute-done.1.from_next, ...), custom_call_target="tpu_custom_call" | custom-call | tf_op jit(solution)/shard_map/square_middle/pallas_call | solution.py:230
  46.5 1.8 %collective-permute-start.4 = (f32[576,128]{1,0:T(8,128)S(1)}, f32[576,128]{1,0:T(8,128)S(1)}, u32[]{:S(2)}, u32[]{:S(2)}) collective-permute-start(f32[576,128]{1,0:T(8,128)S(1)} %get-tuple-element.21), channel_id=1, source_target_pairs={{7,0},{0,1},{1,2},{2,3},{3,4},{4,5},{5,6},{6,7},{15,8},{8,9},{9,10... | collective-permute-start | bytes 884744 | tf_op jit(solution)/shard_map/ppermute | solution.py:242
  48.3 0.8 %collective-permute-start.5 = (f32[576,128]{1,0:T(8,128)S(1)}, f32[576,128]{1,0:T(8,128)S(1)}, u32[]{:S(2)}, u32[]{:S(2)}) collective-permute-start(f32[576,128]{1,0:T(8,128)S(1)} %get-tuple-element.22), channel_id=1, source_target_pairs={{1,0},{2,1},{3,2},{4,3},{5,4},{6,5},{7,6},{0,7},{9,8},{10,9},{11,1... | collective-permute-start | bytes 884744 | tf_op jit(solution)/shard_map/ppermute | solution.py:242
  49.0 1.8 %cube_own.1.total = f32[3,576,256]{2,1,0:T(8,128)S(1)} custom-call(s32[1]{0:T(128)} %bitcast.odd, f32[576,576]{1,0:T(8,128)S(1)} %copy-done.1, f32[864,128]{1,0:T(8,128)S(1)} %collective-permute-done.6.near, f32[864,128]{1,0:T(8,128)S(1)} %collective-permute-done.7.far, f32[864,128]{1,0:T(8,128)S(1)} %collective-permute-done.2.prev_right, ...), custom_call_target="tpu_custom_call" | custom-call | tf_op jit(solution)/shard_map/cube_own/pallas_call | solution.py:230
  50.9 0.0 copy-start.3
  50.9 2.7 %collective-permute-done.8.from_prev = f32[1152,128]{1,0:T(8,128)S(1)} collective-permute-done((f32[1152,128]{1,0:T(8,128)S(1)}, f32[1152,128]{1,0:T(8,128)S(1)}, u32[]{:S(2)}, u32[]{:S(2)}) %collective-permute-start.8) | collective-permute-done | bytes 589856 | tf_op jit(solution)/shard_map/ppermute | solution.py:242
  53.6 7.5 %collective-permute-done.9.from_next = f32[1152,128]{1,0:T(8,128)S(1)} collective-permute-done((f32[1152,128]{1,0:T(8,128)S(1)}, f32[1152,128]{1,0:T(8,128)S(1)}, u32[]{:S(2)}, u32[]{:S(2)}) %collective-permute-start.9) | collective-permute-done | bytes 589856 | tf_op jit(solution)/shard_map/ppermute | solution.py:242
  61.2 1.5 %cube_sides.1.total = f32[3,576,256]{2,1,0:T(8,128)S(1)} custom-call(s32[1]{0:T(128)} %bitcast.odd, f32[864,128]{1,0:T(8,128)S(1)} %collective-permute-done.6.near, f32[864,128]{1,0:T(8,128)S(1)} %collective-permute-done.7.far, f32[864,128]{1,0:T(8,128)S(1)} %collective-permute-done.2.prev_right, f32[864,128]{1,0:T(8,128)S(1)} %collective-permute-done.3.next_left, ...), custom_call_target="tpu_custom_call" | custom-call | tf_op jit(solution)/shard_map/cube_sides/pallas_call | solution.py:230
  62.7 0.0 collective-permute-done.4.from_prev
  62.7 2.4 %collective-permute-done.5.from_next = f32[576,128]{1,0:T(8,128)S(1)} collective-permute-done((f32[576,128]{1,0:T(8,128)S(1)}, f32[576,128]{1,0:T(8,128)S(1)}, u32[]{:S(2)}, u32[]{:S(2)}) %collective-permute-start.5) | collective-permute-done | bytes 294944 | tf_op jit(solution)/shard_map/ppermute | solution.py:242
  65.1 0.0 copy-done.3
  65.1 3.0 %cube_finish.1 = f32[576,576]{1,0:T(8,128)} custom-call(s32[9,9]{1,0:T(8,128)S(1)} %copy-done.3, f32[576,576]{1,0:T(8,128)S(1)} %copy-done.1, f32[576,128]{1,0:T(8,128)S(1)} %collective-permute-done.4.from_prev, f32[576,128]{1,0:T(8,128)S(1)} %collective-permute-done.5.from_next, f32[576,256]{1,0:T(8,128)S(1)} %get-tuple-element.24.first, ...), custom_call_target="tpu_custom_call" | custom-call | tf_op jit(solution)/shard_map/cube_finish/pallas_call | solution.py:230
Async XLA Ops:
  0.0 1.4 %copy-start = (f32[576,576]{1,0:T(8,128)S(1)}, f32[576,576]{1,0:T(8,128)}, u32[]{:S(2)}) copy-start(f32[576,576]{1,0:T(8,128)} %tile.7) | copy-start | bytes 3981316
  1.4 34.0 %copy-start.1 = (f32[576,576]{1,0:T(8,128)S(1)}, f32[576,576]{1,0:T(8,128)}, u32[]{:S(2)}) copy-start(f32[576,576]{1,0:T(8,128)} %tile.7) | copy-start | bytes 3981316
  3.3 12.0 %collective-permute-start.6 = (f32[864,128]{1,0:T(8,128)S(1)}, f32[864,128]{1,0:T(8,128)S(1)}, u32[]{:S(2)}, u32[]{:S(2)}) collective-permute-start(f32[864,128]{1,0:T(8,128)S(1)} %get-tuple-element.23), channel_id=1, source_target_pairs={{0,8},{8,0},{16,24},{24,16},{1,9},{9,1},{17,25},{25,17},{2,10},{10... | collective-permute-start | bytes 1327112 | tf_op jit(solution)/shard_map/ppermute | solution.py:257
  5.4 30.0 %collective-permute-start = (f32[1728,128]{1,0:T(8,128)}, f32[1728,128]{1,0:T(8,128)}, u32[]{:S(2)}, u32[]{:S(2)}) collective-permute-start(f32[1728,128]{1,0:T(8,128)} %get-tuple-element.17), channel_id=1, source_target_pairs={{7,0},{0,1},{1,2},{2,3},{3,4},{4,5},{5,6},{6,7},{15,8},{8,9},{9,10... | collective-permute-start | bytes 2654216 | tf_op jit(solution)/shard_map/ppermute | solution.py:242
  7.5 27.9 %collective-permute-start.1 = (f32[1728,128]{1,0:T(8,128)}, f32[1728,128]{1,0:T(8,128)}, u32[]{:S(2)}, u32[]{:S(2)}) collective-permute-start(f32[1728,128]{1,0:T(8,128)} %get-tuple-element.18), channel_id=1, source_target_pairs={{1,0},{2,1},{3,2},{4,3},{5,4},{6,5},{7,6},{0,7},{9,8},{10,9},{11,1... | collective-permute-start | bytes 2654216 | tf_op jit(solution)/shard_map/ppermute | solution.py:242
  15.4 20.0 %collective-permute-start.7 = (f32[864,128]{1,0:T(8,128)S(1)}, f32[864,128]{1,0:T(8,128)S(1)}, u32[]{:S(2)}, u32[]{:S(2)}) collective-permute-start(f32[864,128]{1,0:T(8,128)S(1)} %collective-permute-done.6.near), channel_id=1, source_target_pairs={{0,16},{8,24},{16,0},{24,8},{1,17},{9,25},{17,1},{25,9},{2,18},{10... | collective-permute-start | bytes 1327112 | tf_op jit(solution)/shard_map/ppermute | solution.py:262
  16.5 26.7 %collective-permute-start.2 = (f32[864,128]{1,0:T(8,128)}, f32[864,128]{1,0:T(8,128)S(1)}, u32[]{:S(2)}, u32[]{:S(2)}) collective-permute-start(f32[864,128]{1,0:T(8,128)} %get-tuple-element.19), channel_id=1, source_target_pairs={{24,0},{0,8},{8,16},{16,24},{25,1},{1,9},{9,17},{17,25},{26,2},{2,... | collective-permute-start | bytes 1327112 | tf_op jit(solution)/shard_map/ppermute | solution.py:242
  17.7 25.4 %collective-permute-start.3 = (f32[864,128]{1,0:T(8,128)}, f32[864,128]{1,0:T(8,128)S(1)}, u32[]{:S(2)}, u32[]{:S(2)}) collective-permute-start(f32[864,128]{1,0:T(8,128)} %get-tuple-element.20), channel_id=1, source_target_pairs={{8,0},{16,8},{24,16},{0,24},{9,1},{17,9},{25,17},{1,25},{10,2},{18... | collective-permute-start | bytes 1327112 | tf_op jit(solution)/shard_map/ppermute | solution.py:242
  35.4 0.7 %copy-start.2 = (s32[9,9]{1,0:T(8,128)S(1)}, s32[9,9]{1,0:T(8,128)}, u32[]{:S(2)}) copy-start(s32[9,9]{1,0:T(8,128)} %kept.4) | copy-start | bytes 976
  40.0 13.7 %collective-permute-start.8 = (f32[1152,128]{1,0:T(8,128)S(1)}, f32[1152,128]{1,0:T(8,128)S(1)}, u32[]{:S(2)}, u32[]{:S(2)}) collective-permute-start(f32[1152,128]{1,0:T(8,128)S(1)} %get-tuple-element.27), channel_id=1, source_target_pairs={{7,0},{0,1},{1,2},{2,3},{3,4},{4,5},{5,6},{6,7},{15,8},{8,9},{9,10... | collective-permute-start | bytes 1769480 | tf_op jit(solution)/shard_map/ppermute | solution.py:242
  43.2 18.0 %collective-permute-start.9 = (f32[1152,128]{1,0:T(8,128)S(1)}, f32[1152,128]{1,0:T(8,128)S(1)}, u32[]{:S(2)}, u32[]{:S(2)}) collective-permute-start(f32[1152,128]{1,0:T(8,128)S(1)} %get-tuple-element.28), channel_id=1, source_target_pairs={{1,0},{2,1},{3,2},{4,3},{5,4},{6,5},{7,6},{0,7},{9,8},{10,9},{11,1... | collective-permute-start | bytes 1769480 | tf_op jit(solution)/shard_map/ppermute | solution.py:242
  46.5 16.2 %collective-permute-start.4 = (f32[576,128]{1,0:T(8,128)S(1)}, f32[576,128]{1,0:T(8,128)S(1)}, u32[]{:S(2)}, u32[]{:S(2)}) collective-permute-start(f32[576,128]{1,0:T(8,128)S(1)} %get-tuple-element.21), channel_id=1, source_target_pairs={{7,0},{0,1},{1,2},{2,3},{3,4},{4,5},{5,6},{6,7},{15,8},{8,9},{9,10... | collective-permute-start | bytes 884744 | tf_op jit(solution)/shard_map/ppermute | solution.py:242
  48.3 16.8 %collective-permute-start.5 = (f32[576,128]{1,0:T(8,128)S(1)}, f32[576,128]{1,0:T(8,128)S(1)}, u32[]{:S(2)}, u32[]{:S(2)}) collective-permute-start(f32[576,128]{1,0:T(8,128)S(1)} %get-tuple-element.22), channel_id=1, source_target_pairs={{1,0},{2,1},{3,2},{4,3},{5,4},{6,5},{7,6},{0,7},{9,8},{10,9},{11,1... | collective-permute-start | bytes 884744 | tf_op jit(solution)/shard_map/ppermute | solution.py:242
  50.9 14.2 %copy-start.3 = (s32[9,9]{1,0:T(8,128)S(1)}, s32[9,9]{1,0:T(8,128)}, u32[]{:S(2)}) copy-start(s32[9,9]{1,0:T(8,128)} %kept.5) | copy-start | bytes 976

commit v2 on v0

v2 whole, which is shorter than its diff:
```python
import jax
import jax.numpy as jnp
from jax import lax
from jax.experimental import pallas as pl
from jax.experimental.pallas import tpu as pltpu
from jax.sharding import PartitionSpec as P

LANES = 128
WIDE = 256
F32 = jnp.float32
BF16 = jnp.bfloat16
NEAR, MID, FAR = range(3)


def low_half(rows):
    return lax.broadcasted_iota(jnp.int32, (rows, LANES), 1) < LANES // 2


def store_fold(out_ref, base, value):
    rows = value.shape[0]
    half = rows // 2
    tail = value[:, LANES:]
    out_ref[pl.ds(base, rows), :] = value[:, :LANES]
    out_ref[pl.ds(base + rows, half), :] = jnp.where(
        low_half(half), tail[:half], pltpu.roll(tail[half:], LANES // 2, 1)
    )


def unfold(packed):
    rows = packed.shape[0] * 2 // 3
    half = rows // 2
    tail = packed[rows:]
    keep = low_half(half)
    upper = jnp.where(keep, tail, 0.0)
    lower = jnp.where(keep, pltpu.roll(tail, LANES // 2, 1), 0.0)
    return jnp.concatenate([packed[:rows], jnp.concatenate([upper, lower], 0)], 1)


def tile_groups(odd_ref, tile_ref):
    rows = tile_ref.shape[0]
    keep = low_half(rows)
    first = jnp.concatenate([tile_ref[:, 0:128], jnp.where(keep, tile_ref[:, 128:256], 0.0)], 1)
    one = pltpu.roll(tile_ref[:, 128:256], LANES // 2, 1)
    two = pltpu.roll(tile_ref[:, 256:384], LANES // 2, 1)
    middle = jnp.concatenate([jnp.where(keep, one, two), jnp.where(keep, two, 0.0)], 1)
    end = tile_ref[:, 512:576]
    last = jnp.concatenate([tile_ref[:, 384:512], jnp.concatenate([end, jnp.zeros_like(end)], 1)], 1)
    odd = odd_ref[0] == 1
    return jnp.where(odd, first, last), middle, jnp.where(odd, last, first)


def split(value):
    high = value.astype(BF16)
    return high, (value - high.astype(F32)).astype(BF16)


def store_left(out_ref, at, value):
    out_ref[(0,) + at], out_ref[(1,) + at] = split(value)


def store_right(out_ref, at, value):
    group = value.shape[0] // 3
    for half, part in enumerate(split(value)):
        for ky in range(3):
            out_ref[(half,) + at + (pl.ds(ky * WIDE, group),)] = part[ky * group : (ky + 1) * group]
            out_ref[(half,) + at + (pl.ds(ky * WIDE + group, WIDE - group),)] = jnp.zeros((WIDE - group, WIDE), BF16)


def left(ref, *at):
    return ref[(0,) + at], ref[(1,) + at]


def right(ref, ky, *at):
    rows = (pl.ds(ky * WIDE, WIDE),)
    return ref[(0,) + at + rows], ref[(1,) + at + rows]


def passes(lefts, rights):
    wide = [high for high, _ in lefts] + [low for _, low in lefts] + [high for high, _ in lefts]
    tall = [high for high, _ in rights] + [high for high, _ in rights] + [low for _, low in rights]
    return jnp.dot(jnp.concatenate(wide, 1), jnp.concatenate(tall, 0), preferred_element_type=F32)


def stacked(before, own, after):
    group = own.shape[0] // 3
    return jnp.concatenate(
        [
            own[:group] + before[:group],
            own[group : 2 * group] + before[group:] + after[:group],
            own[2 * group :] + after[group:],
        ],
        0,
    )


def first_block(odd_ref, part):
    return 3 if part == MID else jnp.where((odd_ref[0] == 1) == (part == NEAR), 0, 6)


def masked(value, kept_ref, start):
    rows = value.shape[0] // 9
    lane = lax.broadcasted_iota(jnp.int32, (8, WIDE), 1)

    def flags(i):
        one, two, three = (kept_ref[i, start + j] for j in range(3))
        return jnp.where(lane < 64, one, jnp.where(lane < 128, two, three)).astype(F32)[:1]

    return jnp.concatenate([value[i * rows : (i + 1) * rows] * flags(i) for i in range(9)], 0)


def store_sides(value, to_next, to_prev):
    group = value.shape[0] // 3
    store_fold(to_next, 0, value[group:])
    store_fold(to_prev, 0, value[: 2 * group])


def pack_body(odd, tile, a_next, a_prev, b_next, b_prev, mid, near, far):
    groups = tile_groups(odd, tile)
    group = tile.shape[0] // 3
    for part, out_next, out_prev, base in (
        (MID, a_next, a_prev, 0),
        (NEAR, a_next, a_prev, 3 * group),
        (FAR, b_next, b_prev, 0),
    ):
        store_fold(out_next, base, groups[part][group:])
        store_fold(out_prev, base, groups[part][: 2 * group])
    for out, part in ((mid, MID), (near, NEAR), (far, FAR)):
        store_fold(out, 0, groups[part])


def prepare_body(odd, tile, own_left, own_right):
    for part, value in enumerate(tile_groups(odd, tile)):
        store_left(own_left, (part,), value)
        store_right(own_right, (part,), value)


def square_near_body(odd, kept, a_prev, a_next, mid, own_left, own_right, out, to_next, to_prev, lefts, rights):
    group = a_prev.shape[0] // 6
    for side, ref in enumerate((a_prev, a_next)):
        for part, base in ((MID, 0), (NEAR, 3 * group)):
            store_left(lefts, (side, part), unfold(ref[base : base + 3 * group, :]))
    store_right(rights, (), unfold(mid[...]))
    sums = []
    for ky in range(3):
        if ky == 1:
            pair = [left(own_left, NEAR), left(own_left, MID)]
        else:
            pair = [left(lefts, ky // 2, NEAR), left(lefts, ky // 2, MID)]
        sums.append(passes(pair, [right(rights, ky), right(own_right, ky, NEAR)]))
    value = masked(stacked(*sums), kept, first_block(odd, NEAR))
    out[...] = value
    store_sides(value, to_next, to_prev)


def square_far_body(odd, kept, b_prev, b_next, mid, own_left, own_right, near_lefts, out, to_next, to_prev, lefts, rights):
    for side, ref in enumerate((b_prev, b_next)):
        store_left(lefts, (side,), unfold(ref[...]))
    store_right(rights, (), unfold(mid[...]))
    sums = []
    for ky in range(3):
        if ky == 1:
            pair = [left(own_left, FAR), left(own_left, MID)]
        else:
            pair = [left(lefts, ky // 2), left(near_lefts, ky // 2, MID)]
        sums.append(passes(pair, [right(rights, ky), right(own_right, ky, FAR)]))
    value = masked(stacked(*sums), kept, first_block(odd, FAR))
    out[...] = value
    store_sides(value, to_next, to_prev)


def square_mid_start_body(near, own_left, own_right, near_lefts, out, rights):
    store_right(rights, (), unfold(near[...]))
    sums = []
    for ky in range(3):
        if ky == 1:
            pair = [left(own_left, NEAR), left(own_left, MID)]
        else:
            pair = [left(near_lefts, ky // 2, NEAR), left(near_lefts, ky // 2, MID)]
        sums.append(passes(pair, [right(rights, ky), right(own_right, ky, MID)]))
    out[...] = stacked(*sums)


def square_mid_body(kept, far, own_left, far_lefts, begun, out, to_next, to_prev, rights):
    store_right(rights, (), unfold(far[...]))
    sums = []
    for ky in range(3):
        one = left(own_left, FAR) if ky == 1 else left(far_lefts, ky // 2)
        sums.append(passes([one], [right(rights, ky)]))
    value = masked(begun[...] + stacked(*sums), kept, 3)
    out[...] = value
    store_sides(value, to_next, to_prev)


def cube_own_body(near, mid, far, own_right, right_near, right_far, right_mid_near, right_mid_far, out):
    squares = [split(ref[...]) for ref in (near, mid, far)]
    out[NEAR] = passes(squares[:2], [right(right_near, 1), right(own_right, 1, NEAR)])
    out[MID] = passes(squares, [right(right_mid_near, 1), right(own_right, 1, MID), right(right_mid_far, 1)])
    out[FAR] = passes(squares[1:], [right(own_right, 1, FAR), right(right_far, 1)])


def cube_side_body(side, from_prev, from_next, right_side, right_mid, total, out):
    lefts = [split(unfold(ref[...])) for ref in (from_prev, from_next)]
    for part, ref in ((side, right_side), (MID, right_mid)):
        before, after = (passes([lefts[k // 2]], [right(ref, k)]) for k in (0, 2))
        out[part] = stacked(before, total[part], after)
    rest = NEAR + FAR - side
    out[rest] = total[rest]


def finish_body(odd, kept, from_prev, from_next, own_right, near, mid, far, total, out):
    group = out.shape[0] // 3
    lefts = [split(unfold(ref[...])) for ref in (from_prev, from_next)]
    values = []
    for part, square in enumerate((near, mid, far)):
        before, after = (passes([lefts[k // 2]], [right(own_right, k, part)]) for k in (0, 2))
        cubed = stacked(before, total[part], after)
        values.append(masked(3.0 * square[...] - 2.0 * cubed, kept, first_block(odd, part)))
    is_odd = odd[0] == 1
    out[:, :group] = jnp.where(is_odd, values[NEAR], values[FAR])[:, :group]
    out[:, group : 2 * group] = values[MID][:, :group]
    out[:, 2 * group :] = jnp.where(is_odd, values[FAR], values[NEAR])[:, :group]


VMEM = pl.BlockSpec(memory_space=pltpu.VMEM)
SMEM = pl.BlockSpec(memory_space=pltpu.SMEM)


def call(body, name, scalars, arrays, outs):
    return pl.pallas_call(
        body,
        out_shape=[jax.ShapeDtypeStruct(shape, kind) for shape, kind in outs],
        in_specs=[SMEM] * len(scalars) + [VMEM] * len(arrays),
        out_specs=[VMEM] * len(outs),
        compiler_params=pltpu.CompilerParams(vmem_limit_bytes=24 << 20),
        name=name,
    )(*scalars, *arrays)


def on_device(p_tiles, square_kept, result_kept):
    side = p_tiles.shape[0]
    group = side // 3
    n_row, n_col = lax.axis_size("row"), lax.axis_size("col")
    odd = (lax.axis_index("row") % 2).astype(jnp.int32).reshape(1)
    strip = ((3 * side // 2, LANES), F32)
    slab = ((3 * group, LANES), F32)
    two_slabs = ((6 * group, LANES), F32)
    wide = ((side, WIDE), F32)
    rights = ((2, 3 * WIDE, WIDE), BF16)

    def from_columns(to_next, to_prev):
        up = [(i, (i + 1) % n_col) for i in range(n_col)]
        down = [(i, (i - 1) % n_col) for i in range(n_col)]
        return lax.ppermute(to_next, "col", up), lax.ppermute(to_prev, "col", down)

    def on_rows(value, even_step):
        return lax.ppermute(
            value, "row", [(i, (i + (even_step if i % 2 == 0 else -even_step)) % n_row) for i in range(n_row)]
        )

    a_next, a_prev, b_next, b_prev, mid, near, far = call(
        pack_body, "pack", (odd,), (p_tiles,), [two_slabs] * 2 + [slab] * 2 + [strip] * 3
    )
    partner_mid = on_rows(mid, 1)
    a_prev, a_next = from_columns(a_next, a_prev)
    b_prev, b_next = from_columns(b_next, b_prev)
    other_mid = on_rows(partner_mid, 2)
    partner_near = on_rows(near, 1)
    other_far = on_rows(far, -1)

    own_left, own_right = call(
        prepare_body, "prepare", (odd,), (p_tiles,), [((2, 3, side, WIDE), BF16), ((2, 3, 3 * WIDE, WIDE), BF16)]
    )
    s_near, out_next, out_prev, near_lefts, right_near = call(
        square_near_body,
        "square_near",
        (odd, square_kept),
        (a_prev, a_next, partner_mid, own_left, own_right),
        [wide, slab, slab, ((2, 2, 2, 2 * group, WIDE), BF16), rights],
    )
    near_prev, near_next = from_columns(out_next, out_prev)
    s_far, out_next, out_prev, far_lefts, right_far = call(
        square_far_body,
        "square_far",
        (odd, square_kept),
        (b_prev, b_next, other_mid, own_left, own_right, near_lefts),
        [wide, slab, slab, ((2, 2, 2 * group, WIDE), BF16), rights],
    )
    far_prev, far_next = from_columns(out_next, out_prev)
    begun, right_mid_near = call(
        square_mid_start_body,
        "square_mid_start",
        (),
        (partner_near, own_left, own_right, near_lefts),
        [wide, rights],
    )
    s_mid, out_next, out_prev, right_mid_far = call(
        square_mid_body,
        "square_mid",
        (square_kept,),
        (other_far, own_left, far_lefts, begun),
        [wide, slab, slab, rights],
    )
    mid_prev, mid_next = from_columns(out_next, out_prev)
    (total,) = call(
        cube_own_body,
        "cube_own",
        (),
        (s_near, s_mid, s_far, own_right, right_near, right_far, right_mid_near, right_mid_far),
        [((3, side, WIDE), F32)],
    )
    for part, prev, after, right_side, right_mid in (
        (NEAR, near_prev, near_next, right_near, right_mid_near),
        (FAR, far_prev, far_next, right_far, right_mid_far),
    ):
        (total,) = call(
            lambda *refs, part=part: cube_side_body(part, *refs),
            ("cube_near", "cube_mid", "cube_far")[part],
            (),
            (prev, after, right_side, right_mid, total),
            [((3, side, WIDE), F32)],
        )
    (purified,) = call(
        finish_body,
        "finish",
        (odd, result_kept),
        (mid_prev, mid_next, own_right, s_near, s_mid, s_far, total),
        [((side, side), F32)],
    )
    return purified


def solution(mesh):
    return jax.shard_map(
        on_device,
        mesh=mesh,
        in_specs=(P("row", "col"), P("row", "col"), P("row", "col")),
        out_specs=P("row", "col"),
        check_vma=False,
    )
```

time: 141 us -> 61.9 us (0.44)
  matrix products: 40.2 us -> 0 us
  waiting for transfers between devices: 67.2 us -> 28.1 us
  local copies, waits for them, and re-layouts: 20.7 us -> 1.4 us
  Pallas kernels: 0 us -> 14.3 us
  starting transfers between devices: 10.8 us -> 17.9 us
    dot_general x18 -> x0, matrix products: 40.2 us -> none  [block_product(): jnp.dot(left_part[:, (col_step + 1) * group_rows:(col_step + 2) * group_r...]
    ppermute x6 -> x14, waiting for transfers between devices: 67.2 us -> 28.1 us  [the longest x4 14.6 us: on_rows(): lax.ppermute(value, 'row', [(i, (i + (even_step if i % 2 == 0 else -even_...]
    mul x7 -> x0, local copies, waits for them, and re-layouts: 20.7 us -> none  [mask_blocks(): block_grid = block_grid * kept_mask.astype(jnp.float32)[:, None, :, None]]
    pallas_call x0 -> x10, Pallas kernels: none -> 14.3 us  [call(): pl.pallas_call(body, out_shape=[jax.ShapeDtypeStruct(shape, kind) for sha...]
    ppermute x6 -> x14, starting transfers between devices: 10.8 us -> 17.9 us  [the longest x5 9.78 us: from_columns(): lax.ppermute(to_prev, 'col', down)]
  transfers between devices with their start and end apart: 6 -> 14, of which waited for: 4 -> 5; matrix products, arithmetic and copies ran while one was open for 26% -> 0% of each run, Pallas kernels for 0% -> 17%
where the time goes in v2:
time: 61.9 us; the launch traced here: 61.8 us
  waiting for transfers between devices  28.1 us (45%)
  starting transfers between devices  17.9 us (29%)
  Pallas kernels  14.3 us (23%)
  local copies, waits for them, and re-layouts  1.4 us (2%)
    ppermute x4, waiting for transfers between devices, on_rows(): lax.ppermute(value, 'row', [(i, (i + (even_step if i % 2 == 0 else -even_...  14.6 us
    pallas_call x10, Pallas kernels, call(): pl.pallas_call(body, out_shape=[jax.ShapeDtypeStruct(shape, kind) for sha...  14.3 us
    ppermute x5, waiting for transfers between devices, from_columns(): lax.ppermute(to_next, 'col', up)  13.5 us
    ppermute x5, starting transfers between devices, from_columns(): lax.ppermute(to_prev, 'col', down)  9.78 us
    ppermute x4, starting transfers between devices, on_rows(): lax.ppermute(value, 'row', [(i, (i + (even_step if i % 2 == 0 else -even_...  5.41 us
    ppermute x5, starting transfers between devices, from_columns(): lax.ppermute(to_next, 'col', up)  2.66 us
    unnamed x6, local copies, waits for them, and re-layouts  1.4 us
  transfers between devices with their start and end apart: 14, of which 5 were waited for; matrix products, arithmetic and copies ran while one was open for 0% of the time, Pallas kernels for 17%

profile of v2, /device:TPU:0, one launch (start us, length us, event | category | flops | bytes accessed | tf_op | source)
XLA Modules:
  0.0 61.8 jit_solution(12001347063964945225)
XLA Ops:
  0.0 0.0 copy-start.1
  0.0 0.0 copy-start
  0.0 1.4 %copy-done = f32[576,576]{1,0:T(8,128)S(1)} copy-done((f32[576,576]{1,0:T(8,128)S(1)}, f32[576,576]{1,0:T(8,128)}, u32[]{:S(2)}) %copy-start) | copy-done | bytes 1327128
  1.4 0.5 pack.1
  1.9 0.5 collective-permute-start.5
  2.4 4.1 %collective-permute-start.6 = (f32[1152,128]{1,0:T(8,128)S(1)}, f32[1152,128]{1,0:T(8,128)S(1)}, u32[]{:S(2)}, u32[]{:S(2)}) collective-permute-start(f32[1152,128]{1,0:T(8,128)S(1)} %get-tuple-element.37), channel_id=1, source_target_pairs={{0,7},{1,0},{2,1},{3,2},{4,3},{5,4},{6,5},{7,6},{8,15},{9,8},{10,9... | collective-permute-start | bytes 1769480 | tf_op jit(solution)/shard_map/ppermute | solution.py:253
  6.5 1.9 %collective-permute-start.3 = (f32[864,128]{1,0:T(8,128)S(1)}, f32[864,128]{1,0:T(8,128)S(1)}, u32[]{:S(2)}, u32[]{:S(2)}) collective-permute-start(f32[864,128]{1,0:T(8,128)S(1)} %get-tuple-element.34), channel_id=1, source_target_pairs={{0,8},{8,0},{16,24},{24,16},{1,9},{9,1},{17,25},{25,17},{2,10},{10... | collective-permute-start | bytes 1327112 | tf_op jit(solution)/shard_map/ppermute | solution.py:256
  8.4 0.1 collective-permute-start.7
  8.5 11.1 %collective-permute-done.3.mid = f32[864,128]{1,0:T(8,128)S(1)} collective-permute-done((f32[864,128]{1,0:T(8,128)S(1)}, f32[864,128]{1,0:T(8,128)S(1)}, u32[]{:S(2)}, u32[]{:S(2)}) %collective-permute-start.3) | collective-permute-done | bytes 442400 | tf_op jit(solution)/shard_map/ppermute | solution.py:256
  19.6 2.0 %collective-permute-start.4 = (f32[864,128]{1,0:T(8,128)S(1)}, f32[864,128]{1,0:T(8,128)S(1)}, u32[]{:S(2)}, u32[]{:S(2)}) collective-permute-start(f32[864,128]{1,0:T(8,128)S(1)} %collective-permute-done.3.mid), channel_id=1, source_target_pairs={{0,16},{8,24},{16,0},{24,8},{1,17},{9,25},{17,1},{25,9},{2,18},{10... | collective-permute-start | bytes 1327112 | tf_op jit(solution)/shard_map/ppermute | solution.py:256
  21.6 1.4 %collective-permute-start = (f32[864,128]{1,0:T(8,128)S(1)}, f32[864,128]{1,0:T(8,128)S(1)}, u32[]{:S(2)}, u32[]{:S(2)}) collective-permute-start(f32[864,128]{1,0:T(8,128)S(1)} %get-tuple-element.30), channel_id=1, source_target_pairs={{0,24},{8,16},{16,8},{24,0},{1,25},{9,17},{17,9},{25,1},{2,26},{10... | collective-permute-start | bytes 1327112 | tf_op jit(solution)/shard_map/ppermute | solution.py:256
  23.0 0.0 collective-permute-done.5.a_prev
  23.0 0.0 collective-permute-start.1
  23.0 0.0 collective-permute-done.6.a_next
  23.0 3.5 %collective-permute-start.2 = (f32[576,128]{1,0:T(8,128)S(1)}, f32[576,128]{1,0:T(8,128)S(1)}, u32[]{:S(2)}, u32[]{:S(2)}) collective-permute-start(f32[576,128]{1,0:T(8,128)S(1)} %get-tuple-element.33), channel_id=1, source_target_pairs={{0,7},{1,0},{2,1},{3,2},{4,3},{5,4},{6,5},{7,6},{8,15},{9,8},{10,9... | collective-permute-start | bytes 884744 | tf_op jit(solution)/shard_map/ppermute | solution.py:253
  26.6 0.3 prepare.1
  26.9 0.0 copy-done.1
  26.9 2.1 %square_near.1 = (f32[576,256]{1,0:T(8,128)S(1)}, f32[576,128]{1,0:T(8,128)S(1)}, f32[576,128]{1,0:T(8,128)S(1)}, bf16[2,2,2,384,256]{4,3,2,1,0:T(8,128)(2,1)S(1)}, bf16[2,768,256]{2,1,0:T(8,128)(2,1)S(1)}) custom-call(s32[1]{0:T(128)} %bitcast.odd, s32[9,9]{1,0:T(8,128)S(1)} %copy-done.1, f32[1152,128]{1,0:T(8,128)S(1)} %collective-permute-done.5.a_prev, ...), custom_call_target="tpu_custom_call" | custom-call | tf_op jit(solution)/shard_map/square_near/pallas_call | solution.py:229
  29.0 0.1 collective-permute-done.7.near
  29.1 0.0 collective-permute-start.12
  29.1 1.3 %square_mid_start.1 = (f32[576,256]{1,0:T(8,128)S(1)}, bf16[2,768,256]{2,1,0:T(8,128)(2,1)S(1)}) custom-call(f32[864,128]{1,0:T(8,128)S(1)} %collective-permute-done.7.near, bf16[2,3,576,256]{3,2,1,0:T(8,128)(2,1)S(1)} %get-tuple-element.31.own_left, bf16[2,3,768,256]{3,2,1,0:T(8,128)(2,1)S(1)} %get-tuple-element.35.own_right, ...), custom_call_target="tpu_custom_call" | custom-call | tf_op jit(solution)/shard_map/square_mid_start/pallas_call | solution.py:229
  30.4 3.4 %collective-permute-done.1.b_prev = f32[576,128]{1,0:T(8,128)S(1)} collective-permute-done((f32[576,128]{1,0:T(8,128)S(1)}, f32[576,128]{1,0:T(8,128)S(1)}, u32[]{:S(2)}, u32[]{:S(2)}) %collective-permute-start.1) | collective-permute-done | bytes 294944 | tf_op jit(solution)/shard_map/ppermute | solution.py:253
  33.8 0.2 collective-permute-start.13
  34.0 0.0 collective-permute-done.2.b_next
  34.0 3.4 %collective-permute-done.4.mid = f32[864,128]{1,0:T(8,128)S(1)} collective-permute-done((f32[864,128]{1,0:T(8,128)S(1)}, f32[864,128]{1,0:T(8,128)S(1)}, u32[]{:S(2)}, u32[]{:S(2)}) %collective-permute-start.4) | collective-permute-done | bytes 442400 | tf_op jit(solution)/shard_map/ppermute | solution.py:256
  37.4 2.0 %square_far.1 = (f32[576,256]{1,0:T(8,128)S(1)}, f32[576,128]{1,0:T(8,128)S(1)}, f32[576,128]{1,0:T(8,128)S(1)}, bf16[2,2,384,256]{3,2,1,0:T(8,128)(2,1)S(1)}, bf16[2,768,256]{2,1,0:T(8,128)(2,1)S(1)}) custom-call(s32[1]{0:T(128)} %bitcast.odd, s32[9,9]{1,0:T(8,128)S(1)} %copy-done.1, f32[576,128]{1,0:T(8,128)S(1)} %collective-permute-done.1.b_prev, ...), custom_call_target="tpu_custom_call" | custom-call | tf_op jit(solution)/shard_map/square_far/pallas_call | solution.py:229
  39.4 0.0 collective-permute-done.far
  39.5 1.5 %square_mid.1 = (f32[576,256]{1,0:T(8,128)S(1)}, f32[576,128]{1,0:T(8,128)S(1)}, f32[576,128]{1,0:T(8,128)S(1)}, bf16[2,768,256]{2,1,0:T(8,128)(2,1)S(1)}) custom-call(s32[9,9]{1,0:T(8,128)S(1)} %copy-done.1, f32[864,128]{1,0:T(8,128)S(1)} %collective-permute-done.far, bf16[2,3,576,256]{3,2,1,0:T(8,128)(2,1)S(1)} %get-tuple-element.31.own_left, ...), custom_call_target="tpu_custom_call" | custom-call | tf_op jit(solution)/shard_map/square_mid/pallas_call | solution.py:229
  41.0 0.1 collective-permute-start.8
  41.0 2.1 %collective-permute-start.10 = (f32[576,128]{1,0:T(8,128)S(1)}, f32[576,128]{1,0:T(8,128)S(1)}, u32[]{:S(2)}, u32[]{:S(2)}) collective-permute-start(f32[576,128]{1,0:T(8,128)S(1)} %get-tuple-element.47), channel_id=1, source_target_pairs={{0,1},{1,2},{2,3},{3,4},{4,5},{5,6},{6,7},{7,0},{8,9},{9,10},{10,1... | collective-permute-start | bytes 884744 | tf_op jit(solution)/shard_map/ppermute | solution.py:253
  43.1 1.5 %collective-permute-start.11 = (f32[576,128]{1,0:T(8,128)S(1)}, f32[576,128]{1,0:T(8,128)S(1)}, u32[]{:S(2)}, u32[]{:S(2)}) collective-permute-start(f32[576,128]{1,0:T(8,128)S(1)} %get-tuple-element.48), channel_id=1, source_target_pairs={{0,7},{1,0},{2,1},{3,2},{4,3},{5,4},{6,5},{7,6},{8,15},{9,8},{10,9... | collective-permute-start | bytes 884744 | tf_op jit(solution)/shard_map/ppermute | solution.py:253
  44.6 0.0 collective-permute-done.12.refs_0_
  44.6 0.4 collective-permute-start.9
  45.1 1.8 %cube_own.1.refs_4_ = f32[3,576,256]{2,1,0:T(8,128)S(1)} custom-call(f32[576,256]{1,0:T(8,128)S(1)} %get-tuple-element.44.near, f32[576,256]{1,0:T(8,128)S(1)} %get-tuple-element.45.mid, f32[576,256]{1,0:T(8,128)S(1)} %get-tuple-element.46.far, bf16[2,3,768,256]{3,2,1,0:T(8,128)(2,1)S(1)} %get-tuple-element.35.own_right, ...), custom_call_target="tpu_custom_call" | custom-call | tf_op jit(solution)/shard_map/cube_own/pallas_call | solution.py:229
  46.9 0.0 collective-permute-done.13.refs_1_
  46.9 0.8 %cube_near.1.refs_4_ = f32[3,576,256]{2,1,0:T(8,128)S(1)} custom-call(f32[576,128]{1,0:T(8,128)S(1)} %collective-permute-done.12.refs_0_, f32[576,128]{1,0:T(8,128)S(1)} %collective-permute-done.13.refs_1_, bf16[2,768,256]{2,1,0:T(8,128)(2,1)S(1)} %get-tuple-element.53.right_near.refs_2_, bf16[2,768,256]{2,1,0:T(8,128)(2,1)S(1)} %get-tuple-element.54.right_mid_near.refs_3_, ...), custom_call_target="tpu_custom_call" | custom-call | tf_op jit(solution)/shard_map/cube_near/pallas_call | solution.py:229
  47.7 0.0 copy-start.2
  47.7 10.1 %collective-permute-done.10.refs_0_ = f32[576,128]{1,0:T(8,128)S(1)} collective-permute-done((f32[576,128]{1,0:T(8,128)S(1)}, f32[576,128]{1,0:T(8,128)S(1)}, u32[]{:S(2)}, u32[]{:S(2)}) %collective-permute-start.10) | collective-permute-done | bytes 294944 | tf_op jit(solution)/shard_map/ppermute | solution.py:253
  57.8 0.0 collective-permute-done.11.refs_1_
  57.8 0.8 %cube_far.1.total = f32[3,576,256]{2,1,0:T(8,128)S(1)} custom-call(f32[576,128]{1,0:T(8,128)S(1)} %collective-permute-done.10.refs_0_, f32[576,128]{1,0:T(8,128)S(1)} %collective-permute-done.11.refs_1_, bf16[2,768,256]{2,1,0:T(8,128)(2,1)S(1)} %get-tuple-element.49.right_far.refs_2_, bf16[2,768,256]{2,1,0:T(8,128)(2,1)S(1)} %get-tuple-element.50.right_mid_far.refs_3_, ...), custom_call_target="tpu_custom_call" | custom-call | tf_op jit(solution)/shard_map/cube_far/pallas_call | solution.py:229
  58.6 0.0 collective-permute-done.8.from_prev
  58.6 0.0 collective-permute-done.9.from_next
  58.6 0.0 copy-done.2
  58.6 3.1 %finish.1 = f32[576,576]{1,0:T(8,128)} custom-call(s32[1]{0:T(128)} %bitcast.odd, s32[9,9]{1,0:T(8,128)S(1)} %copy-done.2, f32[576,128]{1,0:T(8,128)S(1)} %collective-permute-done.8.from_prev, f32[576,128]{1,0:T(8,128)S(1)} %collective-permute-done.9.from_next, bf16[2,3,768,256]{3,2,1,0:T(8,128)(2,1)S(1)} %get-tuple-element.35.own_right, ...), custom_call_target="tpu_custom_call" | custom-call | tf_op jit(solution)/shard_map/finish/pallas_call | solution.py:229
Async XLA Ops:
  0.0 26.9 %copy-start.1 = (s32[9,9]{1,0:T(8,128)S(1)}, s32[9,9]{1,0:T(8,128)}, u32[]{:S(2)}) copy-start(s32[9,9]{1,0:T(8,128)} %kept.6) | copy-start | bytes 976
  0.0 1.4 %copy-start = (f32[576,576]{1,0:T(8,128)S(1)}, f32[576,576]{1,0:T(8,128)}, u32[]{:S(2)}) copy-start(f32[576,576]{1,0:T(8,128)} %tile.3) | copy-start | bytes 3981316
  1.9 21.1 %collective-permute-start.5 = (f32[1152,128]{1,0:T(8,128)S(1)}, f32[1152,128]{1,0:T(8,128)S(1)}, u32[]{:S(2)}, u32[]{:S(2)}) collective-permute-start(f32[1152,128]{1,0:T(8,128)S(1)} %get-tuple-element.36), channel_id=1, source_target_pairs={{0,1},{1,2},{2,3},{3,4},{4,5},{5,6},{6,7},{7,0},{8,9},{9,10},{10,1... | collective-permute-start | bytes 1769480 | tf_op jit(solution)/shard_map/ppermute | solution.py:253
  2.4 20.6 %collective-permute-start.6 = (f32[1152,128]{1,0:T(8,128)S(1)}, f32[1152,128]{1,0:T(8,128)S(1)}, u32[]{:S(2)}, u32[]{:S(2)}) collective-permute-start(f32[1152,128]{1,0:T(8,128)S(1)} %get-tuple-element.37), channel_id=1, source_target_pairs={{0,7},{1,0},{2,1},{3,2},{4,3},{5,4},{6,5},{7,6},{8,15},{9,8},{10,9... | collective-permute-start | bytes 1769480 | tf_op jit(solution)/shard_map/ppermute | solution.py:253
  6.5 13.1 %collective-permute-start.3 = (f32[864,128]{1,0:T(8,128)S(1)}, f32[864,128]{1,0:T(8,128)S(1)}, u32[]{:S(2)}, u32[]{:S(2)}) collective-permute-start(f32[864,128]{1,0:T(8,128)S(1)} %get-tuple-element.34), channel_id=1, source_target_pairs={{0,8},{8,0},{16,24},{24,16},{1,9},{9,1},{17,25},{25,17},{2,10},{10... | collective-permute-start | bytes 1327112 | tf_op jit(solution)/shard_map/ppermute | solution.py:256
  8.4 20.7 %collective-permute-start.7 = (f32[864,128]{1,0:T(8,128)S(1)}, f32[864,128]{1,0:T(8,128)S(1)}, u32[]{:S(2)}, u32[]{:S(2)}) collective-permute-start(f32[864,128]{1,0:T(8,128)S(1)} %get-tuple-element.40), channel_id=1, source_target_pairs={{0,8},{8,0},{16,24},{24,16},{1,9},{9,1},{17,25},{25,17},{2,10},{10... | collective-permute-start | bytes 1327112 | tf_op jit(solution)/shard_map/ppermute | solution.py:256
  19.6 17.8 %collective-permute-start.4 = (f32[864,128]{1,0:T(8,128)S(1)}, f32[864,128]{1,0:T(8,128)S(1)}, u32[]{:S(2)}, u32[]{:S(2)}) collective-permute-start(f32[864,128]{1,0:T(8,128)S(1)} %collective-permute-done.3.mid), channel_id=1, source_target_pairs={{0,16},{8,24},{16,0},{24,8},{1,17},{9,25},{17,1},{25,9},{2,18},{10... | collective-permute-start | bytes 1327112 | tf_op jit(solution)/shard_map/ppermute | solution.py:256
  21.6 17.9 %collective-permute-start = (f32[864,128]{1,0:T(8,128)S(1)}, f32[864,128]{1,0:T(8,128)S(1)}, u32[]{:S(2)}, u32[]{:S(2)}) collective-permute-start(f32[864,128]{1,0:T(8,128)S(1)} %get-tuple-element.30), channel_id=1, source_target_pairs={{0,24},{8,16},{16,8},{24,0},{1,25},{9,17},{17,9},{25,1},{2,26},{10... | collective-permute-start | bytes 1327112 | tf_op jit(solution)/shard_map/ppermute | solution.py:256
  23.0 10.8 %collective-permute-start.1 = (f32[576,128]{1,0:T(8,128)S(1)}, f32[576,128]{1,0:T(8,128)S(1)}, u32[]{:S(2)}, u32[]{:S(2)}) collective-permute-start(f32[576,128]{1,0:T(8,128)S(1)} %get-tuple-element.32), channel_id=1, source_target_pairs={{0,1},{1,2},{2,3},{3,4},{4,5},{5,6},{6,7},{7,0},{8,9},{9,10},{10,1... | collective-permute-start | bytes 884744 | tf_op jit(solution)/shard_map/ppermute | solution.py:253
  23.0 11.0 %collective-permute-start.2 = (f32[576,128]{1,0:T(8,128)S(1)}, f32[576,128]{1,0:T(8,128)S(1)}, u32[]{:S(2)}, u32[]{:S(2)}) collective-permute-start(f32[576,128]{1,0:T(8,128)S(1)} %get-tuple-element.33), channel_id=1, source_target_pairs={{0,7},{1,0},{2,1},{3,2},{4,3},{5,4},{6,5},{7,6},{8,15},{9,8},{10,9... | collective-permute-start | bytes 884744 | tf_op jit(solution)/shard_map/ppermute | solution.py:253
  29.1 15.5 %collective-permute-start.12 = (f32[576,128]{1,0:T(8,128)S(1)}, f32[576,128]{1,0:T(8,128)S(1)}, u32[]{:S(2)}, u32[]{:S(2)}) collective-permute-start(f32[576,128]{1,0:T(8,128)S(1)} %get-tuple-element.51), channel_id=1, source_target_pairs={{0,1},{1,2},{2,3},{3,4},{4,5},{5,6},{6,7},{7,0},{8,9},{9,10},{10,1... | collective-permute-start | bytes 884744 | tf_op jit(solution)/shard_map/ppermute | solution.py:253
  33.8 13.1 %collective-permute-start.13 = (f32[576,128]{1,0:T(8,128)S(1)}, f32[576,128]{1,0:T(8,128)S(1)}, u32[]{:S(2)}, u32[]{:S(2)}) collective-permute-start(f32[576,128]{1,0:T(8,128)S(1)} %get-tuple-element.52), channel_id=1, source_target_pairs={{0,7},{1,0},{2,1},{3,2},{4,3},{5,4},{6,5},{7,6},{8,15},{9,8},{10,9... | collective-permute-start | bytes 884744 | tf_op jit(solution)/shard_map/ppermute | solution.py:253
  41.0 17.6 %collective-permute-start.8 = (f32[576,128]{1,0:T(8,128)S(1)}, f32[576,128]{1,0:T(8,128)S(1)}, u32[]{:S(2)}, u32[]{:S(2)}) collective-permute-start(f32[576,128]{1,0:T(8,128)S(1)} %get-tuple-element.42), channel_id=1, source_target_pairs={{0,1},{1,2},{2,3},{3,4},{4,5},{5,6},{6,7},{7,0},{8,9},{9,10},{10,1... | collective-permute-start | bytes 884744 | tf_op jit(solution)/shard_map/ppermute | solution.py:253
  41.0 16.8 %collective-permute-start.10 = (f32[576,128]{1,0:T(8,128)S(1)}, f32[576,128]{1,0:T(8,128)S(1)}, u32[]{:S(2)}, u32[]{:S(2)}) collective-permute-start(f32[576,128]{1,0:T(8,128)S(1)} %get-tuple-element.47), channel_id=1, source_target_pairs={{0,1},{1,2},{2,3},{3,4},{4,5},{5,6},{6,7},{7,0},{8,9},{9,10},{10,1... | collective-permute-start | bytes 884744 | tf_op jit(solution)/shard_map/ppermute | solution.py:253
  43.1 14.7 %collective-permute-start.11 = (f32[576,128]{1,0:T(8,128)S(1)}, f32[576,128]{1,0:T(8,128)S(1)}, u32[]{:S(2)}, u32[]{:S(2)}) collective-permute-start(f32[576,128]{1,0:T(8,128)S(1)} %get-tuple-element.48), channel_id=1, source_target_pairs={{0,7},{1,0},{2,1},{3,2},{4,3},{5,4},{6,5},{7,6},{8,15},{9,8},{10,9... | collective-permute-start | bytes 884744 | tf_op jit(solution)/shard_map/ppermute | solution.py:253
  44.6 14.0 %collective-permute-start.9 = (f32[576,128]{1,0:T(8,128)S(1)}, f32[576,128]{1,0:T(8,128)S(1)}, u32[]{:S(2)}, u32[]{:S(2)}) collective-permute-start(f32[576,128]{1,0:T(8,128)S(1)} %get-tuple-element.43), channel_id=1, source_target_pairs={{0,7},{1,0},{2,1},{3,2},{4,3},{5,4},{6,5},{7,6},{8,15},{9,8},{10,9... | collective-permute-start | bytes 884744 | tf_op jit(solution)/shard_map/ppermute | solution.py:253
  47.7 10.9 %copy-start.2 = (s32[9,9]{1,0:T(8,128)S(1)}, s32[9,9]{1,0:T(8,128)}, u32[]{:S(2)}) copy-start(s32[9,9]{1,0:T(8,128)} %kept.7) | copy-start | bytes 976

commit v3 on v2

--- a/solution.py
+++ b/solution.py
@@ -191,30 +191,41 @@
     store_sides(value, to_next, to_prev)
 
 
-def cube_own_body(near, mid, far, own_right, right_near, right_far, right_mid_near, right_mid_far, out):
+def cube_near_body(from_prev, from_next, s_near, s_far, own_right, right_near, right_far, right_mid, out):
+    lefts = [split(unfold(ref[...])) for ref in (from_prev, from_next)]
+    near, far = split(s_near[...]), split(s_far[...])
+    out[FAR] = passes([far], [right(right_far, 1)])
+    for part, ref, own in (
+        (NEAR, right_near, passes([near], [right(right_near, 1)])),
+        (MID, right_mid, passes([near], [right(right_mid, 1)])),
+    ):
+        before, after = (passes([lefts[k // 2]], [right(ref, k)]) for k in (0, 2))
+        out[part] = stacked(before, own, after)
+
+
+def cube_own_body(total, near, mid, far, own_right, right_mid_far, out):
     squares = [split(ref[...]) for ref in (near, mid, far)]
-    out[NEAR] = passes(squares[:2], [right(right_near, 1), right(own_right, 1, NEAR)])
-    out[MID] = passes(squares, [right(right_mid_near, 1), right(own_right, 1, MID), right(right_mid_far, 1)])
-    out[FAR] = passes(squares[1:], [right(own_right, 1, FAR), right(right_far, 1)])
-
-
-def cube_side_body(side, from_prev, from_next, right_side, right_mid, total, out):
+    rights = [right(own_right, 1, part) for part in range(3)]
+    out[NEAR] = 3.0 * near[...] - 2.0 * (total[NEAR] + passes(squares[1:2], rights[NEAR:MID]))
+    out[MID] = 3.0 * mid[...] - 2.0 * (total[MID] + passes(squares[1:], [rights[MID], right(right_mid_far, 1)]))
+    out[FAR] = 3.0 * far[...] - 2.0 * (total[FAR] + passes(squares[1:2], rights[FAR:]))
+
+
+def cube_far_body(from_prev, from_next, right_far, right_mid, base, out):
     lefts = [split(unfold(ref[...])) for ref in (from_prev, from_next)]
-    for part, ref in ((side, right_side), (MID, right_mid)):
-        before, after = (passes([lefts[k // 2]], [right(ref, k)]) for k in (0, 2))
-        out[part] = stacked(before, total[part], after)
-    rest = NEAR + FAR - side
-    out[rest] = total[rest]
-
-
-def finish_body(odd, kept, from_prev, from_next, own_right, near, mid, far, total, out):
+    out[NEAR] = base[NEAR]
+    for part, ref in ((FAR, right_far), (MID, right_mid)):
+        before, after = (-2.0 * passes([lefts[k // 2]], [right(ref, k)]) for k in (0, 2))
+        out[part] = stacked(before, base[part], after)
+
+
+def finish_body(odd, kept, from_prev, from_next, own_right, base, out):
     group = out.shape[0] // 3
     lefts = [split(unfold(ref[...])) for ref in (from_prev, from_next)]
     values = []
-    for part, square in enumerate((near, mid, far)):
-        before, after = (passes([lefts[k // 2]], [right(own_right, k, part)]) for k in (0, 2))
-        cubed = stacked(before, total[part], after)
-        values.append(masked(3.0 * square[...] - 2.0 * cubed, kept, first_block(odd, part)))
+    for part in range(3):
+        before, after = (-2.0 * passes([lefts[k // 2]], [right(own_right, k, part)]) for k in (0, 2))
+        values.append(masked(stacked(before, base[part], after), kept, first_block(odd, part)))
     is_odd = odd[0] == 1
     out[:, :group] = jnp.where(is_odd, values[NEAR], values[FAR])[:, :group]
     out[:, group : 2 * group] = values[MID][:, :group]
@@ -232,6 +243,7 @@
         in_specs=[SMEM] * len(scalars) + [VMEM] * len(arrays),
         out_specs=[VMEM] * len(outs),
         compiler_params=pltpu.CompilerParams(vmem_limit_bytes=24 << 20),
+        cost_estimate=pl.CostEstimate(flops=2000000000, transcendentals=0, bytes_accessed=10000000),
         name=name,
     )(*scalars, *arrays)
 
@@ -265,7 +277,6 @@
     b_prev, b_next = from_columns(b_next, b_prev)
     other_mid = on_rows(partner_mid, 2)
     partner_near = on_rows(near, 1)
-    other_far = on_rows(far, -1)
 
     own_left, own_right = call(
         prepare_body, "prepare", (odd,), (p_tiles,), [((2, 3, side, WIDE), BF16), ((2, 3, 3 * WIDE, WIDE), BF16)]
@@ -278,6 +289,8 @@
         [wide, slab, slab, ((2, 2, 2, 2 * group, WIDE), BF16), rights],
     )
     near_prev, near_next = from_columns(out_next, out_prev)
+    other_mid, far, near_lefts = lax.optimization_barrier((other_mid, far, near_lefts))
+    other_far = on_rows(far, -1)
     s_far, out_next, out_prev, far_lefts, right_far = call(
         square_far_body,
         "square_far",
@@ -293,6 +306,14 @@
         (partner_near, own_left, own_right, near_lefts),
         [wide, rights],
     )
+    (total,) = call(
+        cube_near_body,
+        "cube_near",
+        (),
+        (near_prev, near_next, s_near, s_far, own_right, right_near, right_far, right_mid_near),
+        [((3, side, WIDE), F32)],
+    )
+    total, other_far = lax.optimization_barrier((total, other_far))
     s_mid, out_next, out_prev, right_mid_far = call(
         square_mid_body,
         "square_mid",
@@ -301,29 +322,25 @@
         [wide, slab, slab, rights],
     )
     mid_prev, mid_next = from_columns(out_next, out_prev)
-    (total,) = call(
+    (base,) = call(
         cube_own_body,
         "cube_own",
         (),
-        (s_near, s_mid, s_far, own_right, right_near, right_far, right_mid_near, right_mid_far),
+        (total, s_near, s_mid, s_far, own_right, right_mid_far),
         [((3, side, WIDE), F32)],
     )
-    for part, prev, after, right_side, right_mid in (
-        (NEAR, near_prev, near_next, right_near, right_mid_near),
-        (FAR, far_prev, far_next, right_far, right_mid_far),
-    ):
-        (total,) = call(
-            lambda *refs, part=part: cube_side_body(part, *refs),
-            ("cube_near", "cube_mid", "cube_far")[part],
-            (),
-            (prev, after, right_side, right_mid, total),
-            [((3, side, WIDE), F32)],
-        )
+    (base,) = call(
+        cube_far_body,
+        "cube_far",
+        (),
+        (far_prev, far_next, right_far, right_mid_far, base),
+        [((3, side, WIDE), F32)],
+    )
     (purified,) = call(
         finish_body,
         "finish",
         (odd, result_kept),
-        (mid_prev, mid_next, own_right, s_near, s_mid, s_far, total),
+        (mid_prev, mid_next, own_right, base),
         [((side, side), F32)],
     )
     return purified

time: 61.9 us -> 57.1 us (0.922)
  waiting for transfers between devices: 28.1 us -> 17.2 us
  starting transfers between devices: 17.9 us -> 24.1 us
    ppermute x5, waiting for transfers between devices: 13.5 us -> 4.91 us  [from_columns(): lax.ppermute(to_next, 'col', up)]
    ppermute x5, starting transfers between devices: 9.78 us -> 13.8 us  [from_columns(): lax.ppermute(to_prev, 'col', down)]
    ppermute x4, starting transfers between devices: 5.41 us -> 9.21 us  [on_rows(): lax.ppermute(value, 'row', [(i, (i + (even_step if i % 2 == 0 else -even_...]
    ppermute x4, waiting for transfers between devices: 14.6 us -> 12.3 us  [on_rows(): lax.ppermute(value, 'row', [(i, (i + (even_step if i % 2 == 0 else -even_...]
    ppermute x5, starting transfers between devices: 2.66 us -> 1.11 us  [from_columns(): lax.ppermute(to_next, 'col', up)]
  transfers between devices with their start and end apart: 14 -> 14, of which waited for: 5 -> 4; matrix products, arithmetic and copies ran while one was open for 0% -> 0% of each run, Pallas kernels for 17% -> 19%
where the time goes in v3:
time: 57.1 us; the launch traced here: 56.9 us
  starting transfers between devices  24.1 us (42%)
  waiting for transfers between devices  17.2 us (30%)
  Pallas kernels  14.1 us (25%)
  local copies, waits for them, and re-layouts  1.38 us (2%)
    pallas_call x10, Pallas kernels, call(): pl.pallas_call(body, out_shape=[jax.ShapeDtypeStruct(shape, kind) for sha...  14.1 us
    ppermute x5, starting transfers between devices, from_columns(): lax.ppermute(to_prev, 'col', down)  13.8 us
    ppermute x4, waiting for transfers between devices, on_rows(): lax.ppermute(value, 'row', [(i, (i + (even_step if i % 2 == 0 else -even_...  12.3 us
    ppermute x4, starting transfers between devices, on_rows(): lax.ppermute(value, 'row', [(i, (i + (even_step if i % 2 == 0 else -even_...  9.21 us
    ppermute x5, waiting for transfers between devices, from_columns(): lax.ppermute(to_next, 'col', up)  4.91 us
    unnamed x6, local copies, waits for them, and re-layouts  1.38 us
  transfers between devices with their start and end apart: 14, of which 4 were waited for; matrix products, arithmetic and copies ran while one was open for 0% of the time, Pallas kernels for 19%

profile of v3, /device:TPU:0, one launch (start us, length us, event | category | flops | bytes accessed | tf_op | source)
XLA Modules:
  0.0 56.9 jit_solution(3150718122564737010)
XLA Ops:
  0.0 0.0 copy-start
  0.0 1.4 %copy-done = f32[576,576]{1,0:T(8,128)S(1)} copy-done((f32[576,576]{1,0:T(8,128)S(1)}, f32[576,576]{1,0:T(8,128)}, u32[]{:S(2)}) %copy-start) | copy-done | bytes 1327128
  1.4 0.5 pack.1
  1.9 0.5 collective-permute-start
  2.4 2.6 %collective-permute-start.2 = (f32[864,128]{1,0:T(8,128)S(1)}, f32[864,128]{1,0:T(8,128)S(1)}, u32[]{:S(2)}, u32[]{:S(2)}) collective-permute-start(f32[864,128]{1,0:T(8,128)S(1)} %get-tuple-element.37), channel_id=1, source_target_pairs={{0,8},{8,0},{16,24},{24,16},{1,9},{9,1},{17,25},{25,17},{2,10},{10... | collective-permute-start | bytes 1327112 | tf_op jit(solution)/shard_map/ppermute | solution.py:268
  5.0 3.2 %collective-permute-start.1 = (f32[1152,128]{1,0:T(8,128)S(1)}, f32[1152,128]{1,0:T(8,128)S(1)}, u32[]{:S(2)}, u32[]{:S(2)}) collective-permute-start(f32[1152,128]{1,0:T(8,128)S(1)} %get-tuple-element.36), channel_id=1, source_target_pairs={{0,7},{1,0},{2,1},{3,2},{4,3},{5,4},{6,5},{7,6},{8,15},{9,8},{10,9... | collective-permute-start | bytes 1769480 | tf_op jit(solution)/shard_map/ppermute | solution.py:265
  8.2 6.8 %collective-permute-done.2.mid = f32[864,128]{1,0:T(8,128)S(1)} collective-permute-done((f32[864,128]{1,0:T(8,128)S(1)}, f32[864,128]{1,0:T(8,128)S(1)}, u32[]{:S(2)}, u32[]{:S(2)}) %collective-permute-start.2) | collective-permute-done | bytes 442400 | tf_op jit(solution)/shard_map/ppermute | solution.py:268
  14.9 2.5 %collective-permute-start.7 = (f32[864,128]{1,0:T(8,128)S(1)}, f32[864,128]{1,0:T(8,128)S(1)}, u32[]{:S(2)}, u32[]{:S(2)}) collective-permute-start(f32[864,128]{1,0:T(8,128)S(1)} %collective-permute-done.2.mid), channel_id=1, source_target_pairs={{0,16},{8,24},{16,0},{24,8},{1,17},{9,25},{17,1},{25,9},{2,18},{10... | collective-permute-start | bytes 1327112 | tf_op jit(solution)/shard_map/ppermute | solution.py:268
  17.4 0.4 collective-permute-start.5
  17.9 3.1 %collective-permute-start.6 = (f32[576,128]{1,0:T(8,128)S(1)}, f32[576,128]{1,0:T(8,128)S(1)}, u32[]{:S(2)}, u32[]{:S(2)}) collective-permute-start(f32[576,128]{1,0:T(8,128)S(1)} %get-tuple-element.44), channel_id=1, source_target_pairs={{0,7},{1,0},{2,1},{3,2},{4,3},{5,4},{6,5},{7,6},{8,15},{9,8},{10,9... | collective-permute-start | bytes 884744 | tf_op jit(solution)/shard_map/ppermute | solution.py:265
  21.0 0.0 collective-permute-done.a_prev
  21.0 0.0 copy-start.1
  21.0 1.5 %collective-permute-start.8 = (f32[864,128]{1,0:T(8,128)S(1)}, f32[864,128]{1,0:T(8,128)S(1)}, u32[]{:S(2)}, u32[]{:S(2)}) collective-permute-start(f32[864,128]{1,0:T(8,128)S(1)} %get-tuple-element.52), channel_id=1, source_target_pairs={{0,8},{8,0},{16,24},{24,16},{1,9},{9,1},{17,25},{25,17},{2,10},{10... | collective-permute-start | bytes 1327112 | tf_op jit(solution)/shard_map/ppermute | solution.py:268
  22.5 0.3 prepare.1
  22.8 0.0 collective-permute-done.1.a_next
  22.8 0.0 copy-done.1
  22.8 2.1 %square_near.1 = (f32[576,256]{1,0:T(8,128)S(1)}, f32[576,128]{1,0:T(8,128)S(1)}, f32[576,128]{1,0:T(8,128)S(1)}, bf16[2,2,2,384,256]{4,3,2,1,0:T(8,128)(2,1)S(1)}, bf16[2,768,256]{2,1,0:T(8,128)(2,1)S(1)}) custom-call(s32[1]{0:T(128)} %bitcast.odd, s32[9,9]{1,0:T(8,128)S(1)} %copy-done.1, f32[1152,128]{1,0:T(8,128)S(1)} %collective-permute-done.a_prev, ...), custom_call_target="tpu_custom_call" | custom-call | flops 2000000000 | bytes 10000000 | tf_op jit(solution)/shard_map/square_near/pallas_call | solution.py:240
  24.9 0.1 collective-permute-start.3
  25.0 3.4 %collective-permute-done.7.mid = f32[864,128]{1,0:T(8,128)S(1)} collective-permute-done((f32[864,128]{1,0:T(8,128)S(1)}, f32[864,128]{1,0:T(8,128)S(1)}, u32[]{:S(2)}, u32[]{:S(2)}) %collective-permute-start.7) | collective-permute-done | bytes 442400 | tf_op jit(solution)/shard_map/ppermute | solution.py:268
  28.4 0.4 collective-permute-start.4
  28.9 0.0 collective-permute-done.5.b_prev
  28.9 2.6 %collective-permute-start.9 = (f32[864,128]{1,0:T(8,128)S(1)}, f32[864,128]{1,0:T(8,128)S(1)}, u32[]{:S(2)}, u32[]{:S(2)}) collective-permute-start(f32[864,128]{1,0:T(8,128)S(1)} %get-tuple-element.54), channel_id=1, source_target_pairs={{0,24},{8,16},{16,8},{24,0},{1,25},{9,17},{17,9},{25,1},{2,26},{10... | collective-permute-start | bytes 1327112 | tf_op jit(solution)/shard_map/ppermute | solution.py:268
  31.5 0.0 collective-permute-done.6.b_next
  31.5 2.0 %square_far.1 = (f32[576,256]{1,0:T(8,128)S(1)}, f32[576,128]{1,0:T(8,128)S(1)}, f32[576,128]{1,0:T(8,128)S(1)}, bf16[2,2,384,256]{3,2,1,0:T(8,128)(2,1)S(1)}, bf16[2,768,256]{2,1,0:T(8,128)(2,1)S(1)}) custom-call(s32[1]{0:T(128)} %bitcast.odd, s32[9,9]{1,0:T(8,128)S(1)} %copy-done.1, f32[576,128]{1,0:T(8,128)S(1)} %collective-permute-done.5.b_prev, ...), custom_call_target="tpu_custom_call" | custom-call | flops 2000000000 | bytes 10000000 | tf_op jit(solution)/shard_map/square_far/pallas_call | solution.py:240
  33.6 0.1 collective-permute-start.12
  33.6 0.0 collective-permute-done.8.near
  33.6 3.5 %collective-permute-start.13 = (f32[576,128]{1,0:T(8,128)S(1)}, f32[576,128]{1,0:T(8,128)S(1)}, u32[]{:S(2)}, u32[]{:S(2)}) collective-permute-start(f32[576,128]{1,0:T(8,128)S(1)} %get-tuple-element.61), channel_id=1, source_target_pairs={{0,7},{1,0},{2,1},{3,2},{4,3},{5,4},{6,5},{7,6},{8,15},{9,8},{10,9... | collective-permute-start | bytes 884744 | tf_op jit(solution)/shard_map/ppermute | solution.py:265
  37.2 1.3 %square_mid_start.1 = (f32[576,256]{1,0:T(8,128)S(1)}, bf16[2,768,256]{2,1,0:T(8,128)(2,1)S(1)}) custom-call(f32[864,128]{1,0:T(8,128)S(1)} %collective-permute-done.8.near, bf16[2,3,576,256]{3,2,1,0:T(8,128)(2,1)S(1)} %get-tuple-element.38.own_left, bf16[2,3,768,256]{3,2,1,0:T(8,128)(2,1)S(1)} %get-tuple-element.39.own_right, ...), custom_call_target="tpu_custom_call" | custom-call | flops 2000000000 | bytes 10000000 | tf_op jit(solution)/shard_map/square_mid_start/pallas_call | solution.py:240
  38.4 0.0 collective-permute-done.3.from_prev
  38.4 0.0 collective-permute-done.4.from_next
  38.5 1.5 %cube_near.1.total = f32[3,576,256]{2,1,0:T(8,128)S(1)} custom-call(f32[576,128]{1,0:T(8,128)S(1)} %collective-permute-done.3.from_prev, f32[576,128]{1,0:T(8,128)S(1)} %collective-permute-done.4.from_next, f32[576,256]{1,0:T(8,128)S(1)} %get-tuple-element.42.s_near.near, f32[576,256]{1,0:T(8,128)S(1)} %get-tuple-element.49.s_far.far, ...), custom_call_target="tpu_custom_call" | custom-call | flops 2000000000 | bytes 10000000 | tf_op jit(solution)/shard_map/cube_near/pallas_call | solution.py:240
  40.0 2.0 %collective-permute-done.9.far = f32[864,128]{1,0:T(8,128)S(1)} collective-permute-done((f32[864,128]{1,0:T(8,128)S(1)}, f32[864,128]{1,0:T(8,128)S(1)}, u32[]{:S(2)}, u32[]{:S(2)}) %collective-permute-start.9) | collective-permute-done | bytes 442400 | tf_op jit(solution)/shard_map/ppermute | solution.py:268
  42.0 1.5 %square_mid.1 = (f32[576,256]{1,0:T(8,128)S(1)}, f32[576,128]{1,0:T(8,128)S(1)}, f32[576,128]{1,0:T(8,128)S(1)}, bf16[2,768,256]{2,1,0:T(8,128)(2,1)S(1)}) custom-call(s32[9,9]{1,0:T(8,128)S(1)} %copy-done.1, f32[864,128]{1,0:T(8,128)S(1)} %collective-permute-done.9.far, bf16[2,3,576,256]{3,2,1,0:T(8,128)(2,1)S(1)} %get-tuple-element.38.own_left, ...), custom_call_target="tpu_custom_call" | custom-call | flops 2000000000 | bytes 10000000 | tf_op jit(solution)/shard_map/square_mid/pallas_call | solution.py:240
  43.5 0.1 collective-permute-start.10
  43.6 3.5 %collective-permute-start.11 = (f32[576,128]{1,0:T(8,128)S(1)}, f32[576,128]{1,0:T(8,128)S(1)}, u32[]{:S(2)}, u32[]{:S(2)}) collective-permute-start(f32[576,128]{1,0:T(8,128)S(1)} %get-tuple-element.59), channel_id=1, source_target_pairs={{0,7},{1,0},{2,1},{3,2},{4,3},{5,4},{6,5},{7,6},{8,15},{9,8},{10,9... | collective-permute-start | bytes 884744 | tf_op jit(solution)/shard_map/ppermute | solution.py:265
  47.1 1.1 %cube_own.1.base = f32[3,576,256]{2,1,0:T(8,128)S(1)} custom-call(f32[3,576,256]{2,1,0:T(8,128)S(1)} %cube_near.1.total, f32[576,256]{1,0:T(8,128)S(1)} %get-tuple-element.42.s_near.near, f32[576,256]{1,0:T(8,128)S(1)} %get-tuple-element.64.mid, f32[576,256]{1,0:T(8,128)S(1)} %get-tuple-element.49.s_far.far, ...), custom_call_target="tpu_custom_call" | custom-call | flops 2000000000 | bytes 10000000 | tf_op jit(solution)/shard_map/cube_own/pallas_call | solution.py:240
  48.3 0.0 copy-start.2
  48.3 0.0 collective-permute-done.12.from_prev
  48.3 0.0 collective-permute-done.13.from_next
  48.3 0.8 %cube_far.1.base = f32[3,576,256]{2,1,0:T(8,128)S(1)} custom-call(f32[576,128]{1,0:T(8,128)S(1)} %collective-permute-done.12.from_prev, f32[576,128]{1,0:T(8,128)S(1)} %collective-permute-done.13.from_next, bf16[2,768,256]{2,1,0:T(8,128)(2,1)S(1)} %get-tuple-element.51.right_far, bf16[2,768,256]{2,1,0:T(8,128)(2,1)S(1)} %get-tuple-element.62.right_mid_far.right_mid, ...), custom_call_target="tpu_custom_call" | custom-call | flops 2000000000 | bytes 10000000 | tf_op jit(solution)/shard_map/cube_far/pallas_call | solution.py:240
  49.1 4.9 %collective-permute-done.10.from_prev = f32[576,128]{1,0:T(8,128)S(1)} collective-permute-done((f32[576,128]{1,0:T(8,128)S(1)}, f32[576,128]{1,0:T(8,128)S(1)}, u32[]{:S(2)}, u32[]{:S(2)}) %collective-permute-start.10) | collective-permute-done | bytes 294944 | tf_op jit(solution)/shard_map/ppermute | solution.py:265
  54.0 0.0 collective-permute-done.11.from_next
  54.0 0.0 copy-done.2
  54.0 2.9 %finish.1 = f32[576,576]{1,0:T(8,128)} custom-call(s32[1]{0:T(128)} %bitcast.odd, s32[9,9]{1,0:T(8,128)S(1)} %copy-done.2, f32[576,128]{1,0:T(8,128)S(1)} %collective-permute-done.10.from_prev, f32[576,128]{1,0:T(8,128)S(1)} %collective-permute-done.11.from_next, bf16[2,3,768,256]{3,2,1,0:T(8,128)(2,1)S(1)} %get-tuple-element.39.own_right, ...), custom_call_target="tpu_custom_call" | custom-call | flops 2000000000 | bytes 10000000 | tf_op jit(solution)/shard_map/finish/pallas_call | solution.py:240
Async XLA Ops:
  0.0 1.4 %copy-start = (f32[576,576]{1,0:T(8,128)S(1)}, f32[576,576]{1,0:T(8,128)}, u32[]{:S(2)}) copy-start(f32[576,576]{1,0:T(8,128)} %tile.3) | copy-start | bytes 3981316
  1.9 19.1 %collective-permute-start = (f32[1152,128]{1,0:T(8,128)S(1)}, f32[1152,128]{1,0:T(8,128)S(1)}, u32[]{:S(2)}, u32[]{:S(2)}) collective-permute-start(f32[1152,128]{1,0:T(8,128)S(1)} %get-tuple-element.35), channel_id=1, source_target_pairs={{0,1},{1,2},{2,3},{3,4},{4,5},{5,6},{6,7},{7,0},{8,9},{9,10},{10,1... | collective-permute-start | bytes 1769480 | tf_op jit(solution)/shard_map/ppermute | solution.py:265
  2.4 12.5 %collective-permute-start.2 = (f32[864,128]{1,0:T(8,128)S(1)}, f32[864,128]{1,0:T(8,128)S(1)}, u32[]{:S(2)}, u32[]{:S(2)}) collective-permute-start(f32[864,128]{1,0:T(8,128)S(1)} %get-tuple-element.37), channel_id=1, source_target_pairs={{0,8},{8,0},{16,24},{24,16},{1,9},{9,1},{17,25},{25,17},{2,10},{10... | collective-permute-start | bytes 1327112 | tf_op jit(solution)/shard_map/ppermute | solution.py:268
  5.0 17.9 %collective-permute-start.1 = (f32[1152,128]{1,0:T(8,128)S(1)}, f32[1152,128]{1,0:T(8,128)S(1)}, u32[]{:S(2)}, u32[]{:S(2)}) collective-permute-start(f32[1152,128]{1,0:T(8,128)S(1)} %get-tuple-element.36), channel_id=1, source_target_pairs={{0,7},{1,0},{2,1},{3,2},{4,3},{5,4},{6,5},{7,6},{8,15},{9,8},{10,9... | collective-permute-start | bytes 1769480 | tf_op jit(solution)/shard_map/ppermute | solution.py:265
  14.9 13.5 %collective-permute-start.7 = (f32[864,128]{1,0:T(8,128)S(1)}, f32[864,128]{1,0:T(8,128)S(1)}, u32[]{:S(2)}, u32[]{:S(2)}) collective-permute-start(f32[864,128]{1,0:T(8,128)S(1)} %collective-permute-done.2.mid), channel_id=1, source_target_pairs={{0,16},{8,24},{16,0},{24,8},{1,17},{9,25},{17,1},{25,9},{2,18},{10... | collective-permute-start | bytes 1327112 | tf_op jit(solution)/shard_map/ppermute | solution.py:268
  17.4 11.4 %collective-permute-start.5 = (f32[576,128]{1,0:T(8,128)S(1)}, f32[576,128]{1,0:T(8,128)S(1)}, u32[]{:S(2)}, u32[]{:S(2)}) collective-permute-start(f32[576,128]{1,0:T(8,128)S(1)} %get-tuple-element.43), channel_id=1, source_target_pairs={{0,1},{1,2},{2,3},{3,4},{4,5},{5,6},{6,7},{7,0},{8,9},{9,10},{10,1... | collective-permute-start | bytes 884744 | tf_op jit(solution)/shard_map/ppermute | solution.py:265
  17.9 13.6 %collective-permute-start.6 = (f32[576,128]{1,0:T(8,128)S(1)}, f32[576,128]{1,0:T(8,128)S(1)}, u32[]{:S(2)}, u32[]{:S(2)}) collective-permute-start(f32[576,128]{1,0:T(8,128)S(1)} %get-tuple-element.44), channel_id=1, source_target_pairs={{0,7},{1,0},{2,1},{3,2},{4,3},{5,4},{6,5},{7,6},{8,15},{9,8},{10,9... | collective-permute-start | bytes 884744 | tf_op jit(solution)/shard_map/ppermute | solution.py:265
  21.0 1.8 %copy-start.1 = (s32[9,9]{1,0:T(8,128)S(1)}, s32[9,9]{1,0:T(8,128)}, u32[]{:S(2)}) copy-start(s32[9,9]{1,0:T(8,128)} %kept.6) | copy-start | bytes 976
  21.0 12.6 %collective-permute-start.8 = (f32[864,128]{1,0:T(8,128)S(1)}, f32[864,128]{1,0:T(8,128)S(1)}, u32[]{:S(2)}, u32[]{:S(2)}) collective-permute-start(f32[864,128]{1,0:T(8,128)S(1)} %get-tuple-element.52), channel_id=1, source_target_pairs={{0,8},{8,0},{16,24},{24,16},{1,9},{9,1},{17,25},{25,17},{2,10},{10... | collective-permute-start | bytes 1327112 | tf_op jit(solution)/shard_map/ppermute | solution.py:268
  24.9 13.5 %collective-permute-start.3 = (f32[576,128]{1,0:T(8,128)S(1)}, f32[576,128]{1,0:T(8,128)S(1)}, u32[]{:S(2)}, u32[]{:S(2)}) collective-permute-start(f32[576,128]{1,0:T(8,128)S(1)} %get-tuple-element.40), channel_id=1, source_target_pairs={{0,1},{1,2},{2,3},{3,4},{4,5},{5,6},{6,7},{7,0},{8,9},{9,10},{10,1... | collective-permute-start | bytes 884744 | tf_op jit(solution)/shard_map/ppermute | solution.py:265
  28.4 10.0 %collective-permute-start.4 = (f32[576,128]{1,0:T(8,128)S(1)}, f32[576,128]{1,0:T(8,128)S(1)}, u32[]{:S(2)}, u32[]{:S(2)}) collective-permute-start(f32[576,128]{1,0:T(8,128)S(1)} %get-tuple-element.41), channel_id=1, source_target_pairs={{0,7},{1,0},{2,1},{3,2},{4,3},{5,4},{6,5},{7,6},{8,15},{9,8},{10,9... | collective-permute-start | bytes 884744 | tf_op jit(solution)/shard_map/ppermute | solution.py:265
  28.9 13.1 %collective-permute-start.9 = (f32[864,128]{1,0:T(8,128)S(1)}, f32[864,128]{1,0:T(8,128)S(1)}, u32[]{:S(2)}, u32[]{:S(2)}) collective-permute-start(f32[864,128]{1,0:T(8,128)S(1)} %get-tuple-element.54), channel_id=1, source_target_pairs={{0,24},{8,16},{16,8},{24,0},{1,25},{9,17},{17,9},{25,1},{2,26},{10... | collective-permute-start | bytes 1327112 | tf_op jit(solution)/shard_map/ppermute | solution.py:268
  33.6 14.7 %collective-permute-start.12 = (f32[576,128]{1,0:T(8,128)S(1)}, f32[576,128]{1,0:T(8,128)S(1)}, u32[]{:S(2)}, u32[]{:S(2)}) collective-permute-start(f32[576,128]{1,0:T(8,128)S(1)} %get-tuple-element.60), channel_id=1, source_target_pairs={{0,1},{1,2},{2,3},{3,4},{4,5},{5,6},{6,7},{7,0},{8,9},{9,10},{10,1... | collective-permute-start | bytes 884744 | tf_op jit(solution)/shard_map/ppermute | solution.py:265
  33.6 14.7 %collective-permute-start.13 = (f32[576,128]{1,0:T(8,128)S(1)}, f32[576,128]{1,0:T(8,128)S(1)}, u32[]{:S(2)}, u32[]{:S(2)}) collective-permute-start(f32[576,128]{1,0:T(8,128)S(1)} %get-tuple-element.61), channel_id=1, source_target_pairs={{0,7},{1,0},{2,1},{3,2},{4,3},{5,4},{6,5},{7,6},{8,15},{9,8},{10,9... | collective-permute-start | bytes 884744 | tf_op jit(solution)/shard_map/ppermute | solution.py:265
  43.5 10.5 %collective-permute-start.10 = (f32[576,128]{1,0:T(8,128)S(1)}, f32[576,128]{1,0:T(8,128)S(1)}, u32[]{:S(2)}, u32[]{:S(2)}) collective-permute-start(f32[576,128]{1,0:T(8,128)S(1)} %get-tuple-element.58), channel_id=1, source_target_pairs={{0,1},{1,2},{2,3},{3,4},{4,5},{5,6},{6,7},{7,0},{8,9},{9,10},{10,1... | collective-permute-start | bytes 884744 | tf_op jit(solution)/shard_map/ppermute | solution.py:265
  43.6 10.4 %collective-permute-start.11 = (f32[576,128]{1,0:T(8,128)S(1)}, f32[576,128]{1,0:T(8,128)S(1)}, u32[]{:S(2)}, u32[]{:S(2)}) collective-permute-start(f32[576,128]{1,0:T(8,128)S(1)} %get-tuple-element.59), channel_id=1, source_target_pairs={{0,7},{1,0},{2,1},{3,2},{4,3},{5,4},{6,5},{7,6},{8,15},{9,8},{10,9... | collective-permute-start | bytes 884744 | tf_op jit(solution)/shard_map/ppermute | solution.py:265
  48.3 5.7 %copy-start.2 = (s32[9,9]{1,0:T(8,128)S(1)}, s32[9,9]{1,0:T(8,128)}, u32[]{:S(2)}) copy-start(s32[9,9]{1,0:T(8,128)} %kept.7) | copy-start | bytes 976

commit v4 on v0

v4 whole, which is shorter than its diff:
```python
import jax
import jax.numpy as jnp
from jax import lax
from jax.experimental import pallas as pl
from jax.experimental.pallas import tpu as pltpu
from jax.sharding import PartitionSpec as P

LANES = 128
WIDE = 256
F32 = jnp.float32
BF16 = jnp.bfloat16
NEAR, MID, FAR = range(3)
OWN, CHIP, LINK = range(3)


def place(info, who, group):
    above = (info[1] == 1) == (who == CHIP)
    return jnp.where(above, 0, group), jnp.where(above, 0, 2)


def shared_rows(info, who, group):
    return pl.ds(pl.multiple_of(place(info, who, group)[0], 64), 2 * group)


def low_half(rows):
    return lax.broadcasted_iota(jnp.int32, (rows, LANES), 1) < LANES // 2


def store_fold(out_ref, base, value):
    rows = value.shape[0]
    half = rows // 2
    tail = value[:, LANES:]
    out_ref[pl.ds(base, rows), :] = value[:, :LANES]
    out_ref[pl.ds(base + rows, half), :] = jnp.where(
        low_half(half), tail[:half], pltpu.roll(tail[half:], LANES // 2, 1)
    )


def unfold(packed):
    rows = packed.shape[0] * 2 // 3
    half = rows // 2
    tail = packed[rows:]
    keep = low_half(half)
    upper = jnp.where(keep, tail, 0.0)
    lower = jnp.where(keep, pltpu.roll(tail, LANES // 2, 1), 0.0)
    return jnp.concatenate([packed[:rows], jnp.concatenate([upper, lower], 0)], 1)


def tile_groups(info, tile_ref, at):
    keep = low_half(at.size)
    first = jnp.concatenate([tile_ref[at, 0:128], jnp.where(keep, tile_ref[at, 128:256], 0.0)], 1)
    one = pltpu.roll(tile_ref[at, 128:256], LANES // 2, 1)
    two = pltpu.roll(tile_ref[at, 256:384], LANES // 2, 1)
    middle = jnp.concatenate([jnp.where(keep, one, two), jnp.where(keep, two, 0.0)], 1)
    end = tile_ref[at, 512:576]
    last = jnp.concatenate([tile_ref[at, 384:512], jnp.concatenate([end, jnp.zeros_like(end)], 1)], 1)
    odd = info[0] == 1
    return jnp.where(odd, first, last), middle, jnp.where(odd, last, first)


def split(value):
    high = value.astype(BF16)
    return high, (value - high.astype(F32)).astype(BF16)


def store_left(out_ref, at, value):
    out_ref[(0,) + at], out_ref[(1,) + at] = split(value)


def store_right(out_ref, at, value):
    group = value.shape[0] // 3
    for half, part in enumerate(split(value)):
        for ky in range(3):
            out_ref[(half,) + at + (pl.ds(ky * WIDE, group),)] = part[ky * group : (ky + 1) * group]
            out_ref[(half,) + at + (pl.ds(ky * WIDE + group, WIDE - group),)] = jnp.zeros((WIDE - group, WIDE), BF16)


def left(ref, *at):
    return ref[(0,) + at], ref[(1,) + at]


def right(ref, info, who, *at):
    start = WIDE if who == OWN else pl.multiple_of(place(info, who, 0)[1] * WIDE, WIDE)
    rows = (pl.ds(start, WIDE),)
    return ref[(0,) + at + rows], ref[(1,) + at + rows]


def passes(lefts, rights):
    wide = [high for high, _ in lefts] + [low for _, low in lefts] + [high for high, _ in lefts]
    tall = [high for high, _ in rights] + [high for high, _ in rights] + [low for _, low in rights]
    return jnp.dot(jnp.concatenate(wide, 1), jnp.concatenate(tall, 0), preferred_element_type=F32)


def mask_at(info, part):
    return 3 if part == MID else jnp.where((info[0] == 1) == (part == NEAR), 0, 6)


def masked(value, kept_ref, start, first_row=0):
    lane = lax.broadcasted_iota(jnp.int32, (8, WIDE), 1)

    def flags(i):
        one, two, three = (kept_ref[first_row + i, start + j] for j in range(3))
        return jnp.where(lane < 64, one, jnp.where(lane < 128, two, three)).astype(F32)[:1]

    return jnp.concatenate([value[i * 64 : (i + 1) * 64] * flags(i) for i in range(value.shape[0] // 64)], 0)


def pack_body(info, tile, chip, link_a, link_b, mid, near, far):
    side = tile.shape[0]
    group = side // 3
    groups = tile_groups(info, tile, shared_rows(info, LINK, group))
    store_fold(link_a, 0, groups[MID])
    store_fold(link_a, 3 * group, groups[NEAR])
    store_fold(link_b, 0, groups[FAR])
    groups = tile_groups(info, tile, pl.ds(0, side))
    for out, part in ((mid, MID), (near, NEAR), (far, FAR)):
        store_fold(out, 0, groups[part])
    groups = tile_groups(info, tile, shared_rows(info, CHIP, group))
    for part in range(3):
        store_fold(chip, part * 3 * group, groups[part])


def prepare_body(info, tile, chip, own_left, own_right, chip_left):
    side = tile.shape[0]
    for part, value in enumerate(tile_groups(info, tile, pl.ds(0, side))):
        store_left(own_left, (part,), value)
        store_right(own_right, (part,), value)
        store_left(chip_left, (part,), unfold(chip[part * side : (part + 1) * side, :]))


def near_start_body(info, mid, own_left, own_right, chip_left, out, rights):
    group = mid.shape[0] * 2 // 9
    store_right(rights, (), unfold(mid[...]))
    for who, lefts in ((OWN, own_left), (CHIP, chip_left)):
        value = passes(
            [left(lefts, NEAR), left(lefts, MID)], [right(rights, info, who), right(own_right, info, who, NEAR)]
        )
        if who == OWN:
            out[...] = value
        else:
            out[shared_rows(info, who, group), :] += value


def near_body(info, kept, link_a, begun, own_right, right_near, out, link, link_left):
    group = link_a.shape[0] // 6
    for part, base in ((MID, 0), (NEAR, 3 * group)):
        store_left(link_left, (part,), unfold(link_a[base : base + 3 * group, :]))
    out[...] = begun[...]
    out[shared_rows(info, LINK, group), :] += passes(
        [left(link_left, NEAR), left(link_left, MID)],
        [right(right_near, info, LINK), right(own_right, info, LINK, NEAR)],
    )
    out[...] = masked(out[...], kept, mask_at(info, NEAR))
    store_fold(link, 0, out[shared_rows(info, LINK, group), :])


def far_start_body(info, own_left, own_right, chip_left, link_left, out):
    group = out.shape[0] // 3
    for who, lefts in ((OWN, own_left), (CHIP, chip_left), (LINK, link_left)):
        value = passes([left(lefts, MID)], [right(own_right, info, who, FAR)])
        if who == OWN:
            out[...] = value
        else:
            out[shared_rows(info, who, group), :] += value


def far_body(info, kept, link_b, mid, begun, near, own_left, chip_left, out, chip, link, link_left, rights):
    group = out.shape[0] // 3
    store_left(link_left, (), unfold(link_b[...]))
    store_right(rights, (), unfold(mid[...]))
    out[...] = begun[...] + passes([left(own_left, FAR)], [right(rights, info, OWN)])
    for who, factor in ((CHIP, left(chip_left, FAR)), (LINK, left(link_left))):
        out[shared_rows(info, who, group), :] += passes([factor], [right(rights, info, who)])
    out[...] = masked(out[...], kept, mask_at(info, FAR))
    store_fold(link, 0, out[shared_rows(info, LINK, group), :])
    store_fold(chip, 0, near[shared_rows(info, CHIP, group), :])
    store_fold(chip, 3 * group, out[shared_rows(info, CHIP, group), :])


def mid_start_body(info, near, own_left, own_right, chip_left, link_left, out, rights):
    group = out.shape[0] // 3
    store_right(rights, (), unfold(near[...]))
    for who, lefts in ((OWN, own_left), (CHIP, chip_left), (LINK, link_left)):
        value = passes(
            [left(lefts, NEAR), left(lefts, MID)], [right(rights, info, who), right(own_right, info, who, MID)]
        )
        if who == OWN:
            out[...] = value
        else:
            out[shared_rows(info, who, group), :] += value


def mid_body(info, kept, far, own_left, chip_left, link_left, begun, out, chip, link, rights):
    group = out.shape[0] // 3
    store_right(rights, (), unfold(far[...]))
    out[...] = begun[...] + passes([left(own_left, FAR)], [right(rights, info, OWN)])
    for who, factor in ((CHIP, left(chip_left, FAR)), (LINK, left(link_left))):
        out[shared_rows(info, who, group), :] += passes([factor], [right(rights, info, who)])
    out[...] = masked(out[...], kept, 3)
    store_fold(link, 0, out[shared_rows(info, LINK, group), :])
    store_fold(chip, 0, out[shared_rows(info, CHIP, group), :])


def cube_near_body(info, link, near, right_near, right_mid, out):
    group = near.shape[0] // 3
    own, other = split(near[...]), split(unfold(link[...]))
    out[FAR] = jnp.zeros(near.shape, F32)
    for part, ref in ((NEAR, right_near), (MID, right_mid)):
        out[part] = passes([own], [right(ref, info, OWN)])
        out[part, shared_rows(info, LINK, group), :] += passes([other], [right(ref, info, LINK)])


def cube_own_body(info, chip, total, near, mid, far, own_right, right_near, right_far, mid_near, mid_far, out):
    group = near.shape[0] // 3
    own_mid, own_far = split(mid[...]), split(far[...])
    chip_near, chip_far = (split(unfold(chip[at * 3 * group : (at + 1) * 3 * group, :])) for at in range(2))

    def add(part, square, own, other):
        out[part] = 3.0 * square[...] - 2.0 * (total[part] + passes(*own))
        out[part, shared_rows(info, CHIP, group), :] -= 2.0 * passes(*other)

    add(
        NEAR,
        near,
        ([own_mid], [right(own_right, info, OWN, NEAR)]),
        ([chip_near], [right(right_near, info, CHIP)]),
    )
    add(
        MID,
        mid,
        ([own_mid, own_far], [right(own_right, info, OWN, MID), right(mid_far, info, OWN)]),
        ([chip_near, chip_far], [right(mid_near, info, CHIP), right(mid_far, info, CHIP)]),
    )
    add(
        FAR,
        far,
        ([own_mid, own_far], [right(own_right, info, OWN, FAR), right(right_far, info, OWN)]),
        ([chip_far], [right(right_far, info, CHIP)]),
    )


def cube_far_body(info, kept, link, chip, own_right, right_far, mid_far, base, out):
    group = base.shape[1] // 3
    link_far, chip_mid = split(unfold(link[...])), split(unfold(chip[...]))
    out[...] = base[...]
    for part in range(3):
        out[part, shared_rows(info, CHIP, group), :] -= 2.0 * passes(
            [chip_mid], [right(own_right, info, CHIP, part)]
        )
    for part, ref in ((MID, mid_far), (FAR, right_far)):
        out[part, shared_rows(info, LINK, group), :] -= 2.0 * passes([link_far], [right(ref, info, LINK)])
    for part in range(3):
        out[part] = masked(out[part], kept, mask_at(info, part))


def finish_body(info, kept, link, own_right, base, out):
    group = out.shape[0] // 3
    link_mid = split(unfold(link[...]))
    at = shared_rows(info, LINK, group)
    first_row = place(info, LINK, 3)[0]
    values = []
    for part in range(3):
        value = -2.0 * passes([link_mid], [right(own_right, info, LINK, part)])
        values.append(base[part, at, :] + masked(value, kept, mask_at(info, part), first_row))
    odd = info[0] == 1

    def store(rows, near, mid, far):
        out[rows, :group] = jnp.where(odd, near, far)[:, :group]
        out[rows, group : 2 * group] = mid[:, :group]
        out[rows, 2 * group :] = jnp.where(odd, far, near)[:, :group]

    store(at, *values)
    rest = pl.ds(pl.multiple_of(2 * place(info, CHIP, group)[0], 64), group)
    store(rest, *(base[part, rest, :] for part in range(3)))


VMEM = pl.BlockSpec(memory_space=pltpu.VMEM)
SMEM = pl.BlockSpec(memory_space=pltpu.SMEM)


def call(body, name, scalars, arrays, outs):
    return pl.pallas_call(
        body,
        out_shape=[jax.ShapeDtypeStruct(shape, kind) for shape, kind in outs],
        in_specs=[SMEM] * len(scalars) + [VMEM] * len(arrays),
        out_specs=[VMEM] * len(outs),
        compiler_params=pltpu.CompilerParams(vmem_limit_bytes=24 << 20),
        cost_estimate=pl.CostEstimate(flops=4000000000, transcendentals=0, bytes_accessed=20000000),
        name=name,
    )(*scalars, *arrays)


def on_device(p_tiles, square_kept, result_kept):
    side = p_tiles.shape[0]
    group = side // 3
    n_row, n_col = lax.axis_size("row"), lax.axis_size("col")
    info = jnp.stack([lax.axis_index("row") % 2, lax.axis_index("col") % 2]).astype(jnp.int32)
    strip = ((3 * side // 2, LANES), F32)
    slab = ((3 * group, LANES), F32)
    two_slabs = ((6 * group, LANES), F32)
    three_slabs = ((9 * group, LANES), F32)
    wide = ((side, WIDE), F32)
    three_wide = ((3, side, WIDE), F32)
    rights = ((2, 3 * WIDE, WIDE), BF16)

    def exchange(value, axis, even_step):
        size = n_row if axis == "row" else n_col
        return lax.ppermute(
            value, axis, [(i, (i + (even_step if i % 2 == 0 else -even_step)) % size) for i in range(size)]
        )

    chip, link_a, link_b, mid, near, far = call(
        pack_body, "pack", (info,), (p_tiles,), [three_slabs, two_slabs, slab] + [strip] * 3
    )
    link_a = exchange(link_a, "col", -1)
    partner_mid = exchange(mid, "row", 1)
    chip = exchange(chip, "col", 1)
    chip, link_b, near = lax.optimization_barrier((chip, link_b, near))
    link_b = exchange(link_b, "col", -1)
    partner_near = exchange(near, "row", 1)
    other_mid = exchange(partner_mid, "row", 2)

    own_left, own_right, chip_left = call(
        prepare_body,
        "prepare",
        (info,),
        (p_tiles, chip),
        [((2, 3, side, WIDE), BF16), ((2, 3, 3 * WIDE, WIDE), BF16), ((2, 3, 2 * group, WIDE), BF16)],
    )
    begun, right_near = call(
        near_start_body, "near_start", (info,), (partner_mid, own_left, own_right, chip_left), [wide, rights]
    )
    s_near, near_link, link_left = call(
        near_body,
        "square_near",
        (info, square_kept),
        (link_a, begun, own_right, right_near),
        [wide, slab, ((2, 2, 2 * group, WIDE), BF16)],
    )
    near_link = exchange(near_link, "col", -1)
    (begun,) = call(
        far_start_body, "far_start", (info,), (own_left, own_right, chip_left, link_left), [wide]
    )
    other_mid, far, begun = lax.optimization_barrier((other_mid, far, begun))
    other_far = exchange(far, "row", -1)
    s_far, sides_chip, far_link, link_left_far, right_far = call(
        far_body,
        "square_far",
        (info, square_kept),
        (link_b, other_mid, begun, s_near, own_left, chip_left),
        [wide, two_slabs, slab, ((2, 2 * group, WIDE), BF16), rights],
    )
    far_link = exchange(far_link, "col", -1)
    sides_chip = exchange(sides_chip, "col", 1)
    begun, mid_near = call(
        mid_start_body,
        "mid_start",
        (info,),
        (partner_near, own_left, own_right, chip_left, link_left),
        [wide, rights],
    )
    (total,) = call(cube_near_body, "cube_near", (info,), (near_link, s_near, right_near, mid_near), [three_wide])
    total, other_far = lax.optimization_barrier((total, other_far))
    s_mid, mid_chip, mid_link, mid_far = call(
        mid_body,
        "square_mid",
        (info, square_kept),
        (other_far, own_left, chip_left, link_left_far, begun),
        [wide, slab, slab, rights],
    )
    mid_link = exchange(mid_link, "col", -1)
    mid_chip = exchange(mid_chip, "col", 1)
    (base,) = call(
        cube_own_body,
        "cube_own",
        (info,),
        (sides_chip, total, s_near, s_mid, s_far, own_right, right_near, right_far, mid_near, mid_far),
        [three_wide],
    )
    (base,) = call(
        cube_far_body,
        "cube_far",
        (info, result_kept),
        (far_link, mid_chip, own_right, right_far, mid_far, base),
        [three_wide],
    )
    (purified,) = call(
        finish_body, "finish", (info, result_kept), (mid_link, own_right, base), [((side, side), F32)]
    )
    return purified


def solution(mesh):
    return jax.shard_map(
        on_device,
        mesh=mesh,
        in_specs=(P("row", "col"), P("row", "col"), P("row", "col")),
        out_specs=P("row", "col"),
        check_vma=False,
    )
```

time: 141 us -> 57.4 us (0.41)
  waiting for transfers between devices: 67.2 us -> 15.2 us
  matrix products: 40.2 us -> 0 us
  Pallas kernels: 0 us -> 21.5 us
  local copies, waits for them, and re-layouts: 20.7 us -> 1.38 us
  starting transfers between devices: 10.8 us -> 19 us
    ppermute x6 -> x12, waiting for transfers between devices: 67.2 us -> 15.2 us  [exchange(): lax.ppermute(value, axis, [(i, (i + (even_step if i % 2 == 0 else -even_s...]
    dot_general x18 -> x0, matrix products: 40.2 us -> none  [block_product(): jnp.dot(left_part[:, (col_step + 1) * group_rows:(col_step + 2) * group_r...]
    pallas_call x0 -> x12, Pallas kernels: none -> 21.5 us  [call(): pl.pallas_call(body, out_shape=[jax.ShapeDtypeStruct(shape, kind) for sha...]
    mul x7 -> x0, local copies, waits for them, and re-layouts: 20.7 us -> none  [mask_blocks(): block_grid = block_grid * kept_mask.astype(jnp.float32)[:, None, :, None]]
    ppermute x6 -> x12, starting transfers between devices: 10.8 us -> 19 us  [exchange(): lax.ppermute(value, axis, [(i, (i + (even_step if i % 2 == 0 else -even_s...]
  transfers between devices with their start and end apart: 6 -> 12, of which waited for: 4 -> 4; matrix products, arithmetic and copies ran while one was open for 26% -> 0% of each run, Pallas kernels for 0% -> 31%
where the time goes in v4:
time: 57.4 us; the launch traced here: 57.2 us
  Pallas kernels  21.5 us (37%)
  starting transfers between devices  19 us (33%)
  waiting for transfers between devices  15.2 us (26%)
  local copies, waits for them, and re-layouts  1.38 us (2%)
    pallas_call x12, Pallas kernels, call(): pl.pallas_call(body, out_shape=[jax.ShapeDtypeStruct(shape, kind) for sha...  21.5 us
    ppermute x12, starting transfers between devices, exchange(): lax.ppermute(value, axis, [(i, (i + (even_step if i % 2 == 0 else -even_s...  19 us
    ppermute x12, waiting for transfers between devices, exchange(): lax.ppermute(value, axis, [(i, (i + (even_step if i % 2 == 0 else -even_s...  15.2 us
    unnamed x6, local copies, waits for them, and re-layouts  1.38 us
  transfers between devices with their start and end apart: 12, of which 4 were waited for; matrix products, arithmetic and copies ran while one was open for 0% of the time, Pallas kernels for 31%

profile of v4, /device:TPU:0, one launch (start us, length us, event | category | flops | bytes accessed | tf_op | source)
XLA Modules:
  0.0 57.2 jit_solution(3627667269948100710)
XLA Ops:
  0.0 0.1 pad_add_fusion.info
  0.1 0.0 copy-start
  0.1 1.4 %copy-done = f32[576,576]{1,0:T(8,128)S(1)} copy-done((f32[576,576]{1,0:T(8,128)S(1)}, f32[576,576]{1,0:T(8,128)}, u32[]{:S(2)}) %copy-start) | copy-done | bytes 1327128
  1.4 1.4 %pack.1 = (f32[1728,128]{1,0:T(8,128)S(1)}, f32[1152,128]{1,0:T(8,128)S(1)}, f32[576,128]{1,0:T(8,128)S(1)}, f32[864,128]{1,0:T(8,128)S(1)}, f32[864,128]{1,0:T(8,128)S(1)}, /*index=5*/f32[864,128]{1,0:T(8,128)S(1)}) custom-call(s32[2]{0:T(128)S(1)} %pad_add_fusion.info, f32[576,576]{1,0:T(8,128)S(1)} %copy-done), custom_call_target="tpu_custom_call" | custom-call | flops 4000000000 | bytes 20000000 | tf_op jit(solution)/shard_map/pack/pallas_call | solution.py:282
  2.9 0.5 collective-permute-start.2
  3.4 2.6 %collective-permute-start.1 = (f32[864,128]{1,0:T(8,128)S(1)}, f32[864,128]{1,0:T(8,128)S(1)}, u32[]{:S(2)}, u32[]{:S(2)}) collective-permute-start(f32[864,128]{1,0:T(8,128)S(1)} %get-tuple-element.39), channel_id=1, source_target_pairs={{0,8},{8,0},{16,24},{24,16},{1,9},{9,1},{17,25},{25,17},{2,10},{10... | collective-permute-start | bytes 1327112 | tf_op jit(solution)/shard_map/ppermute | solution.py:308
  5.9 3.4 %collective-permute-start = (f32[1152,128]{1,0:T(8,128)S(1)}, f32[1152,128]{1,0:T(8,128)S(1)}, u32[]{:S(2)}, u32[]{:S(2)}) collective-permute-start(f32[1152,128]{1,0:T(8,128)S(1)} %get-tuple-element.38), channel_id=1, source_target_pairs={{0,7},{1,2},{2,1},{3,4},{4,3},{5,6},{6,5},{7,0},{8,15},{9,10},{10,... | collective-permute-start | bytes 1769480 | tf_op jit(solution)/shard_map/ppermute | solution.py:308
  9.3 7.4 %collective-permute-done.1.mid = f32[864,128]{1,0:T(8,128)S(1)} collective-permute-done((f32[864,128]{1,0:T(8,128)S(1)}, f32[864,128]{1,0:T(8,128)S(1)}, u32[]{:S(2)}, u32[]{:S(2)}) %collective-permute-start.1) | collective-permute-done | bytes 442400 | tf_op jit(solution)/shard_map/ppermute | solution.py:308
  16.7 1.8 %collective-permute-start.5 = (f32[864,128]{1,0:T(8,128)S(1)}, f32[864,128]{1,0:T(8,128)S(1)}, u32[]{:S(2)}, u32[]{:S(2)}) collective-permute-start(f32[864,128]{1,0:T(8,128)S(1)} %collective-permute-done.1.mid), channel_id=1, source_target_pairs={{0,16},{8,24},{16,0},{24,8},{1,17},{9,25},{17,1},{25,9},{2,18},{10... | collective-permute-start | bytes 1327112 | tf_op jit(solution)/shard_map/ppermute | solution.py:308
  18.5 0.0 collective-permute-done.2.chip
  18.5 2.6 %collective-permute-start.7 = (f32[576,128]{1,0:T(8,128)S(1)}, f32[576,128]{1,0:T(8,128)S(1)}, u32[]{:S(2)}, u32[]{:S(2)}) collective-permute-start(f32[576,128]{1,0:T(8,128)S(1)} %get-tuple-element.57), channel_id=1, source_target_pairs={{0,7},{1,2},{2,1},{3,4},{4,3},{5,6},{6,5},{7,0},{8,15},{9,10},{10,... | collective-permute-start | bytes 884744 | tf_op jit(solution)/shard_map/ppermute | solution.py:308
  21.1 1.5 %collective-permute-start.4 = (f32[864,128]{1,0:T(8,128)S(1)}, f32[864,128]{1,0:T(8,128)S(1)}, u32[]{:S(2)}, u32[]{:S(2)}) collective-permute-start(f32[864,128]{1,0:T(8,128)S(1)} %get-tuple-element.51), channel_id=1, source_target_pairs={{0,8},{8,0},{16,24},{24,16},{1,9},{9,1},{17,25},{25,17},{2,10},{10... | collective-permute-start | bytes 1327112 | tf_op jit(solution)/shard_map/ppermute | solution.py:308
  22.6 1.0 %prepare.1 = (bf16[2,3,576,256]{3,2,1,0:T(8,128)(2,1)S(1)}, bf16[2,3,768,256]{3,2,1,0:T(8,128)(2,1)S(1)}, bf16[2,3,384,256]{3,2,1,0:T(8,128)(2,1)S(1)}) custom-call(s32[2]{0:T(128)S(1)} %pad_add_fusion.info, f32[576,576]{1,0:T(8,128)S(1)} %copy-done, f32[1728,128]{1,0:T(8,128)S(1)} %collective-permute-done.2.chip), custom_call_target="tpu_custom_call" | custom-call | flops 4000000000 | bytes 20000000 | tf_op jit(solution)/shard_map/prepare/pallas_call | solution.py:282
  23.6 0.0 copy-start.1
  23.6 1.6 %near_start.1 = (f32[576,256]{1,0:T(8,128)S(1)}, bf16[2,768,256]{2,1,0:T(8,128)(2,1)S(1)}) custom-call(s32[2]{0:T(128)S(1)} %pad_add_fusion.info, f32[864,128]{1,0:T(8,128)S(1)} %collective-permute-done.1.mid, bf16[2,3,576,256]{3,2,1,0:T(8,128)(2,1)S(1)} %get-tuple-element.44.own_left, bf16[2,3,768,256]{3,2,1,0:T(8,128)(2,1)S(1)} %get-tuple-element.45.own_right, ...), custom_call_target="tpu_custom_call" | custom-call | flops 4000000000 | bytes 20000000 | tf_op jit(solution)/shard_map/near_start/pallas_call | solution.py:282
  25.2 0.0 collective-permute-done.link_a
  25.2 0.0 copy-done.1
  25.2 1.4 %square_near.1 = (f32[576,256]{1,0:T(8,128)S(1)}, f32[576,128]{1,0:T(8,128)S(1)}, bf16[2,2,384,256]{3,2,1,0:T(8,128)(2,1)S(1)}) custom-call(s32[2]{0:T(128)S(1)} %pad_add_fusion.info, s32[9,9]{1,0:T(8,128)S(1)} %copy-done.1, f32[1152,128]{1,0:T(8,128)S(1)} %collective-permute-done.link_a, f32[576,256]{1,0:T(8,128)S(1)} %get-tuple-element.47.begun, ...), custom_call_target="tpu_custom_call" | custom-call | flops 4000000000 | bytes 20000000 | tf_op jit(solution)/shard_map/square_near/pallas_call | solution.py:282
  26.6 0.7 %collective-permute-start.3 = (f32[576,128]{1,0:T(8,128)S(1)}, f32[576,128]{1,0:T(8,128)S(1)}, u32[]{:S(2)}, u32[]{:S(2)}) collective-permute-start(f32[576,128]{1,0:T(8,128)S(1)} %get-tuple-element.49), channel_id=1, source_target_pairs={{0,7},{1,2},{2,1},{3,4},{4,3},{5,6},{6,5},{7,0},{8,15},{9,10},{10,... | collective-permute-start | bytes 884744 | tf_op jit(solution)/shard_map/ppermute | solution.py:308
  27.3 1.3 %far_start.1.begun = f32[576,256]{1,0:T(8,128)S(1)} custom-call(s32[2]{0:T(128)S(1)} %pad_add_fusion.info, bf16[2,3,576,256]{3,2,1,0:T(8,128)(2,1)S(1)} %get-tuple-element.44.own_left, bf16[2,3,768,256]{3,2,1,0:T(8,128)(2,1)S(1)} %get-tuple-element.45.own_right, bf16[2,3,384,256]{3,2,1,0:T(8,128)(2,1)S(1)} %get-tuple-element.46.chip_left, ...), custom_call_target="tpu_custom_call" | custom-call | flops 4000000000 | bytes 20000000 | tf_op jit(solution)/shard_map/far_start/pallas_call | solution.py:282
  28.6 0.0 collective-permute-done.5.mid
  28.6 2.5 %collective-permute-start.6 = (f32[864,128]{1,0:T(8,128)S(1)}, f32[864,128]{1,0:T(8,128)S(1)}, u32[]{:S(2)}, u32[]{:S(2)}) collective-permute-start(f32[864,128]{1,0:T(8,128)S(1)} %get-tuple-element.55), channel_id=1, source_target_pairs={{0,24},{8,16},{16,8},{24,0},{1,25},{9,17},{17,9},{25,1},{2,26},{10... | collective-permute-start | bytes 1327112 | tf_op jit(solution)/shard_map/ppermute | solution.py:308
  31.1 0.0 collective-permute-done.7.link_b
  31.2 1.9 %square_far.1 = (f32[576,256]{1,0:T(8,128)S(1)}, f32[1152,128]{1,0:T(8,128)S(1)}, f32[576,128]{1,0:T(8,128)S(1)}, bf16[2,384,256]{2,1,0:T(8,128)(2,1)S(1)}, bf16[2,768,256]{2,1,0:T(8,128)(2,1)S(1)}) custom-call(s32[2]{0:T(128)S(1)} %pad_add_fusion.info, s32[9,9]{1,0:T(8,128)S(1)} %copy-done.1, f32[576,128]{1,0:T(8,128)S(1)} %collective-permute-done.7.link_b, ...), custom_call_target="tpu_custom_call" | custom-call | flops 4000000000 | bytes 20000000 | tf_op jit(solution)/shard_map/square_far/pallas_call | solution.py:282
  33.0 1.8 %collective-permute-start.9 = (f32[576,128]{1,0:T(8,128)S(1)}, f32[576,128]{1,0:T(8,128)S(1)}, u32[]{:S(2)}, u32[]{:S(2)}) collective-permute-start(f32[576,128]{1,0:T(8,128)S(1)} %get-tuple-element.63), channel_id=1, source_target_pairs={{0,7},{1,2},{2,1},{3,4},{4,3},{5,6},{6,5},{7,0},{8,15},{9,10},{10,... | collective-permute-start | bytes 884744 | tf_op jit(solution)/shard_map/ppermute | solution.py:308
  34.8 0.0 collective-permute-start.11
  34.8 0.0 collective-permute-done.4.near
  34.8 2.0 %mid_start.1 = (f32[576,256]{1,0:T(8,128)S(1)}, bf16[2,768,256]{2,1,0:T(8,128)(2,1)S(1)}) custom-call(s32[2]{0:T(128)S(1)} %pad_add_fusion.info, f32[864,128]{1,0:T(8,128)S(1)} %collective-permute-done.4.near, bf16[2,3,576,256]{3,2,1,0:T(8,128)(2,1)S(1)} %get-tuple-element.44.own_left, bf16[2,3,768,256]{3,2,1,0:T(8,128)(2,1)S(1)} %get-tuple-element.45.own_right, ...), custom_call_target="tpu_custom_call" | custom-call | flops 4000000000 | bytes 20000000 | tf_op jit(solution)/shard_map/mid_start/pallas_call | solution.py:282
  36.7 0.3 collective-permute-done.3.link
  37.1 1.6 %cube_near.1.total = f32[3,576,256]{2,1,0:T(8,128)S(1)} custom-call(s32[2]{0:T(128)S(1)} %pad_add_fusion.info, f32[576,128]{1,0:T(8,128)S(1)} %collective-permute-done.3.link, f32[576,256]{1,0:T(8,128)S(1)} %get-tuple-element.50.near, bf16[2,768,256]{2,1,0:T(8,128)(2,1)S(1)} %get-tuple-element.48.right_near, ...), custom_call_target="tpu_custom_call" | custom-call | flops 4000000000 | bytes 20000000 | tf_op jit(solution)/shard_map/cube_near/pallas_call | solution.py:282
  38.7 3.0 %collective-permute-done.6.far = f32[864,128]{1,0:T(8,128)S(1)} collective-permute-done((f32[864,128]{1,0:T(8,128)S(1)}, f32[864,128]{1,0:T(8,128)S(1)}, u32[]{:S(2)}, u32[]{:S(2)}) %collective-permute-start.6) | collective-permute-done | bytes 442400 | tf_op jit(solution)/shard_map/ppermute | solution.py:308
  41.7 1.9 %square_mid.1 = (f32[576,256]{1,0:T(8,128)S(1)}, f32[576,128]{1,0:T(8,128)S(1)}, f32[576,128]{1,0:T(8,128)S(1)}, bf16[2,768,256]{2,1,0:T(8,128)(2,1)S(1)}) custom-call(s32[2]{0:T(128)S(1)} %pad_add_fusion.info, s32[9,9]{1,0:T(8,128)S(1)} %copy-done.1, f32[864,128]{1,0:T(8,128)S(1)} %collective-permute-done.6.far, ...), custom_call_target="tpu_custom_call" | custom-call | flops 4000000000 | bytes 20000000 | tf_op jit(solution)/shard_map/square_mid/pallas_call | solution.py:282
  43.6 1.7 %collective-permute-start.8 = (f32[576,128]{1,0:T(8,128)S(1)}, f32[576,128]{1,0:T(8,128)S(1)}, u32[]{:S(2)}, u32[]{:S(2)}) collective-permute-start(f32[576,128]{1,0:T(8,128)S(1)} %get-tuple-element.62), channel_id=1, source_target_pairs={{0,7},{1,2},{2,1},{3,4},{4,3},{5,6},{6,5},{7,0},{8,15},{9,10},{10,... | collective-permute-start | bytes 884744 | tf_op jit(solution)/shard_map/ppermute | solution.py:308
  45.2 0.0 collective-permute-start.10
  45.2 0.0 collective-permute-done.11.chip
  45.2 0.0 copy-start.2
  45.2 2.7 %cube_own.1.base = f32[3,576,256]{2,1,0:T(8,128)S(1)} custom-call(s32[2]{0:T(128)S(1)} %pad_add_fusion.info, f32[1152,128]{1,0:T(8,128)S(1)} %collective-permute-done.11.chip, f32[3,576,256]{2,1,0:T(8,128)S(1)} %cube_near.1.total, f32[576,256]{1,0:T(8,128)S(1)} %get-tuple-element.50.near, f32[576,256]{1,0:T(8,128)S(1)} %get-tuple-element.69.mid, ...), custom_call_target="tpu_custom_call" | custom-call | flops 4000000000 | bytes 20000000 | tf_op jit(solution)/shard_map/cube_own/pallas_call | solution.py:282
  48.0 0.0 collective-permute-done.9.link
  48.0 0.0 collective-permute-done.10.chip
  48.0 0.0 copy-done.2
  48.0 2.2 %cube_far.1.base = f32[3,576,256]{2,1,0:T(8,128)S(1)} custom-call(s32[2]{0:T(128)S(1)} %pad_add_fusion.info, s32[9,9]{1,0:T(8,128)S(1)} %copy-done.2, f32[576,128]{1,0:T(8,128)S(1)} %collective-permute-done.9.link, f32[576,128]{1,0:T(8,128)S(1)} %collective-permute-done.10.chip, bf16[2,3,768,256]{3,2,1,0:T(8,128)(2,1)S(1)} %get-tuple-element.45.own_right, ...), custom_call_target="tpu_custom_call" | custom-call | flops 4000000000 | bytes 20000000 | tf_op jit(solution)/shard_map/cube_far/pallas_call | solution.py:282
  50.2 4.5 %collective-permute-done.8.link = f32[576,128]{1,0:T(8,128)S(1)} collective-permute-done((f32[576,128]{1,0:T(8,128)S(1)}, f32[576,128]{1,0:T(8,128)S(1)}, u32[]{:S(2)}, u32[]{:S(2)}) %collective-permute-start.8) | collective-permute-done | bytes 294944 | tf_op jit(solution)/shard_map/ppermute | solution.py:308
  54.7 2.5 %finish.1 = f32[576,576]{1,0:T(8,128)} custom-call(s32[2]{0:T(128)S(1)} %pad_add_fusion.info, s32[9,9]{1,0:T(8,128)S(1)} %copy-done.2, f32[576,128]{1,0:T(8,128)S(1)} %collective-permute-done.8.link, bf16[2,3,768,256]{3,2,1,0:T(8,128)(2,1)S(1)} %get-tuple-element.45.own_right, f32[3,576,256]{2,1,0:T(8,128)S(1)} %cube_far.1.base), custom_call_target="tpu_custom_call" | custom-call | flops 4000000000 | bytes 20000000 | tf_op jit(solution)/shard_map/finish/pallas_call | solution.py:282
Async XLA Ops:
  0.1 1.4 %copy-start = (f32[576,576]{1,0:T(8,128)S(1)}, f32[576,576]{1,0:T(8,128)}, u32[]{:S(2)}) copy-start(f32[576,576]{1,0:T(8,128)} %tile.3) | copy-start | bytes 3981316
  2.9 15.6 %collective-permute-start.2 = (f32[1728,128]{1,0:T(8,128)S(1)}, f32[1728,128]{1,0:T(8,128)S(1)}, u32[]{:S(2)}, u32[]{:S(2)}) collective-permute-start(f32[1728,128]{1,0:T(8,128)S(1)} %get-tuple-element.40), channel_id=1, source_target_pairs={{0,1},{1,0},{2,3},{3,2},{4,5},{5,4},{6,7},{7,6},{8,9},{9,8},{10,11... | collective-permute-start | bytes 2654216 | tf_op jit(solution)/shard_map/ppermute | solution.py:308
  3.4 13.3 %collective-permute-start.1 = (f32[864,128]{1,0:T(8,128)S(1)}, f32[864,128]{1,0:T(8,128)S(1)}, u32[]{:S(2)}, u32[]{:S(2)}) collective-permute-start(f32[864,128]{1,0:T(8,128)S(1)} %get-tuple-element.39), channel_id=1, source_target_pairs={{0,8},{8,0},{16,24},{24,16},{1,9},{9,1},{17,25},{25,17},{2,10},{10... | collective-permute-start | bytes 1327112 | tf_op jit(solution)/shard_map/ppermute | solution.py:308
  5.9 19.2 %collective-permute-start = (f32[1152,128]{1,0:T(8,128)S(1)}, f32[1152,128]{1,0:T(8,128)S(1)}, u32[]{:S(2)}, u32[]{:S(2)}) collective-permute-start(f32[1152,128]{1,0:T(8,128)S(1)} %get-tuple-element.38), channel_id=1, source_target_pairs={{0,7},{1,2},{2,1},{3,4},{4,3},{5,6},{6,5},{7,0},{8,15},{9,10},{10,... | collective-permute-start | bytes 1769480 | tf_op jit(solution)/shard_map/ppermute | solution.py:308
  16.7 11.9 %collective-permute-start.5 = (f32[864,128]{1,0:T(8,128)S(1)}, f32[864,128]{1,0:T(8,128)S(1)}, u32[]{:S(2)}, u32[]{:S(2)}) collective-permute-start(f32[864,128]{1,0:T(8,128)S(1)} %collective-permute-done.1.mid), channel_id=1, source_target_pairs={{0,16},{8,24},{16,0},{24,8},{1,17},{9,25},{17,1},{25,9},{2,18},{10... | collective-permute-start | bytes 1327112 | tf_op jit(solution)/shard_map/ppermute | solution.py:308
  18.5 12.7 %collective-permute-start.7 = (f32[576,128]{1,0:T(8,128)S(1)}, f32[576,128]{1,0:T(8,128)S(1)}, u32[]{:S(2)}, u32[]{:S(2)}) collective-permute-start(f32[576,128]{1,0:T(8,128)S(1)} %get-tuple-element.57), channel_id=1, source_target_pairs={{0,7},{1,2},{2,1},{3,4},{4,3},{5,6},{6,5},{7,0},{8,15},{9,10},{10,... | collective-permute-start | bytes 884744 | tf_op jit(solution)/shard_map/ppermute | solution.py:308
  21.1 13.7 %collective-permute-start.4 = (f32[864,128]{1,0:T(8,128)S(1)}, f32[864,128]{1,0:T(8,128)S(1)}, u32[]{:S(2)}, u32[]{:S(2)}) collective-permute-start(f32[864,128]{1,0:T(8,128)S(1)} %get-tuple-element.51), channel_id=1, source_target_pairs={{0,8},{8,0},{16,24},{24,16},{1,9},{9,1},{17,25},{25,17},{2,10},{10... | collective-permute-start | bytes 1327112 | tf_op jit(solution)/shard_map/ppermute | solution.py:308
  23.6 1.6 %copy-start.1 = (s32[9,9]{1,0:T(8,128)S(1)}, s32[9,9]{1,0:T(8,128)}, u32[]{:S(2)}) copy-start(s32[9,9]{1,0:T(8,128)} %kept.7) | copy-start | bytes 976
  26.6 10.4 %collective-permute-start.3 = (f32[576,128]{1,0:T(8,128)S(1)}, f32[576,128]{1,0:T(8,128)S(1)}, u32[]{:S(2)}, u32[]{:S(2)}) collective-permute-start(f32[576,128]{1,0:T(8,128)S(1)} %get-tuple-element.49), channel_id=1, source_target_pairs={{0,7},{1,2},{2,1},{3,4},{4,3},{5,6},{6,5},{7,0},{8,15},{9,10},{10,... | collective-permute-start | bytes 884744 | tf_op jit(solution)/shard_map/ppermute | solution.py:308
  28.6 13.1 %collective-permute-start.6 = (f32[864,128]{1,0:T(8,128)S(1)}, f32[864,128]{1,0:T(8,128)S(1)}, u32[]{:S(2)}, u32[]{:S(2)}) collective-permute-start(f32[864,128]{1,0:T(8,128)S(1)} %get-tuple-element.55), channel_id=1, source_target_pairs={{0,24},{8,16},{16,8},{24,0},{1,25},{9,17},{17,9},{25,1},{2,26},{10... | collective-permute-start | bytes 1327112 | tf_op jit(solution)/shard_map/ppermute | solution.py:308
  33.0 15.0 %collective-permute-start.9 = (f32[576,128]{1,0:T(8,128)S(1)}, f32[576,128]{1,0:T(8,128)S(1)}, u32[]{:S(2)}, u32[]{:S(2)}) collective-permute-start(f32[576,128]{1,0:T(8,128)S(1)} %get-tuple-element.63), channel_id=1, source_target_pairs={{0,7},{1,2},{2,1},{3,4},{4,3},{5,6},{6,5},{7,0},{8,15},{9,10},{10,... | collective-permute-start | bytes 884744 | tf_op jit(solution)/shard_map/ppermute | solution.py:308
  34.8 10.5 %collective-permute-start.11 = (f32[1152,128]{1,0:T(8,128)S(1)}, f32[1152,128]{1,0:T(8,128)S(1)}, u32[]{:S(2)}, u32[]{:S(2)}) collective-permute-start(f32[1152,128]{1,0:T(8,128)S(1)} %get-tuple-element.67), channel_id=1, source_target_pairs={{0,1},{1,0},{2,3},{3,2},{4,5},{5,4},{6,7},{7,6},{8,9},{9,8},{10,11... | collective-permute-start | bytes 1769480 | tf_op jit(solution)/shard_map/ppermute | solution.py:308
  43.6 11.2 %collective-permute-start.8 = (f32[576,128]{1,0:T(8,128)S(1)}, f32[576,128]{1,0:T(8,128)S(1)}, u32[]{:S(2)}, u32[]{:S(2)}) collective-permute-start(f32[576,128]{1,0:T(8,128)S(1)} %get-tuple-element.62), channel_id=1, source_target_pairs={{0,7},{1,2},{2,1},{3,4},{4,3},{5,6},{6,5},{7,0},{8,15},{9,10},{10,... | collective-permute-start | bytes 884744 | tf_op jit(solution)/shard_map/ppermute | solution.py:308
  45.2 2.8 %collective-permute-start.10 = (f32[576,128]{1,0:T(8,128)S(1)}, f32[576,128]{1,0:T(8,128)S(1)}, u32[]{:S(2)}, u32[]{:S(2)}) collective-permute-start(f32[576,128]{1,0:T(8,128)S(1)} %get-tuple-element.64), channel_id=1, source_target_pairs={{0,1},{1,0},{2,3},{3,2},{4,5},{5,4},{6,7},{7,6},{8,9},{9,8},{10,11... | collective-permute-start | bytes 884744 | tf_op jit(solution)/shard_map/ppermute | solution.py:308
  45.2 2.8 %copy-start.2 = (s32[9,9]{1,0:T(8,128)S(1)}, s32[9,9]{1,0:T(8,128)}, u32[]{:S(2)}) copy-start(s32[9,9]{1,0:T(8,128)} %kept.9) | copy-start | bytes 976

commit v5 on v4

--- a/solution.py
+++ b/solution.py
@@ -210,46 +210,49 @@
         out[part, shared_rows(info, LINK, group), :] += passes([other], [right(ref, info, LINK)])
 
 
-def cube_own_body(info, chip, total, near, mid, far, own_right, right_near, right_far, mid_near, mid_far, out):
+def cube_own_body(info, chip, link, total, near, mid, far, own_right, right_near, right_far, mid_near, mid_far, out):
     group = near.shape[0] // 3
     own_mid, own_far = split(mid[...]), split(far[...])
     chip_near, chip_far = (split(unfold(chip[at * 3 * group : (at + 1) * 3 * group, :])) for at in range(2))
-
-    def add(part, square, own, other):
+    link_far = split(unfold(link[...]))
+
+    def add(part, square, own, from_chip, from_link):
         out[part] = 3.0 * square[...] - 2.0 * (total[part] + passes(*own))
-        out[part, shared_rows(info, CHIP, group), :] -= 2.0 * passes(*other)
+        out[part, shared_rows(info, CHIP, group), :] -= 2.0 * passes(*from_chip)
+        if from_link is not None:
+            out[part, shared_rows(info, LINK, group), :] -= 2.0 * passes([link_far], [from_link])
 
     add(
         NEAR,
         near,
         ([own_mid], [right(own_right, info, OWN, NEAR)]),
         ([chip_near], [right(right_near, info, CHIP)]),
+        None,
     )
     add(
         MID,
         mid,
         ([own_mid, own_far], [right(own_right, info, OWN, MID), right(mid_far, info, OWN)]),
         ([chip_near, chip_far], [right(mid_near, info, CHIP), right(mid_far, info, CHIP)]),
+        right(mid_far, info, LINK),
     )
     add(
         FAR,
         far,
         ([own_mid, own_far], [right(own_right, info, OWN, FAR), right(right_far, info, OWN)]),
         ([chip_far], [right(right_far, info, CHIP)]),
-    )
-
-
-def cube_far_body(info, kept, link, chip, own_right, right_far, mid_far, base, out):
+        right(right_far, info, LINK),
+    )
+
+
+def cube_chip_body(info, kept, chip, own_right, base, out):
     group = base.shape[1] // 3
-    link_far, chip_mid = split(unfold(link[...])), split(unfold(chip[...]))
-    out[...] = base[...]
+    chip_mid = split(unfold(chip[...]))
     for part in range(3):
+        out[part] = base[part]
         out[part, shared_rows(info, CHIP, group), :] -= 2.0 * passes(
             [chip_mid], [right(own_right, info, CHIP, part)]
         )
-    for part, ref in ((MID, mid_far), (FAR, right_far)):
-        out[part, shared_rows(info, LINK, group), :] -= 2.0 * passes([link_far], [right(ref, info, LINK)])
-    for part in range(3):
         out[part] = masked(out[part], kept, mask_at(info, part))
 
 
@@ -278,14 +281,14 @@
 SMEM = pl.BlockSpec(memory_space=pltpu.SMEM)
 
 
-def call(body, name, scalars, arrays, outs):
+def call(body, name, scalars, arrays, outs, work=4):
     return pl.pallas_call(
         body,
         out_shape=[jax.ShapeDtypeStruct(shape, kind) for shape, kind in outs],
         in_specs=[SMEM] * len(scalars) + [VMEM] * len(arrays),
         out_specs=[VMEM] * len(outs),
         compiler_params=pltpu.CompilerParams(vmem_limit_bytes=24 << 20),
-        cost_estimate=pl.CostEstimate(flops=4000000000, transcendentals=0, bytes_accessed=20000000),
+        cost_estimate=pl.CostEstimate(flops=work * 1000000000, transcendentals=0, bytes_accessed=work * 5000000),
         name=name,
     )(*scalars, *arrays)
 
@@ -318,8 +321,6 @@
     chip, link_b, near = lax.optimization_barrier((chip, link_b, near))
     link_b = exchange(link_b, "col", -1)
     partner_near = exchange(near, "row", 1)
-    other_mid = exchange(partner_mid, "row", 2)
-
     own_left, own_right, chip_left = call(
         prepare_body,
         "prepare",
@@ -327,6 +328,8 @@
         (p_tiles, chip),
         [((2, 3, side, WIDE), BF16), ((2, 3, 3 * WIDE, WIDE), BF16), ((2, 3, 2 * group, WIDE), BF16)],
     )
+    partner_mid, own_left = lax.optimization_barrier((partner_mid, own_left))
+    other_mid = exchange(partner_mid, "row", 2)
     begun, right_near = call(
         near_start_body, "near_start", (info,), (partner_mid, own_left, own_right, chip_left), [wide, rights]
     )
@@ -341,7 +344,7 @@
     (begun,) = call(
         far_start_body, "far_start", (info,), (own_left, own_right, chip_left, link_left), [wide]
     )
-    other_mid, far, begun = lax.optimization_barrier((other_mid, far, begun))
+    far, begun = lax.optimization_barrier((far, begun))
     other_far = exchange(far, "row", -1)
     s_far, sides_chip, far_link, link_left_far, right_far = call(
         far_body,
@@ -367,6 +370,7 @@
         (info, square_kept),
         (other_far, own_left, chip_left, link_left_far, begun),
         [wide, slab, slab, rights],
+        work=0,
     )
     mid_link = exchange(mid_link, "col", -1)
     mid_chip = exchange(mid_chip, "col", 1)
@@ -374,14 +378,14 @@
         cube_own_body,
         "cube_own",
         (info,),
-        (sides_chip, total, s_near, s_mid, s_far, own_right, right_near, right_far, mid_near, mid_far),
+        (sides_chip, far_link, total, s_near, s_mid, s_far, own_right, right_near, right_far, mid_near, mid_far),
         [three_wide],
     )
     (base,) = call(
-        cube_far_body,
-        "cube_far",
+        cube_chip_body,
+        "cube_chip",
         (info, result_kept),
-        (far_link, mid_chip, own_right, right_far, mid_far, base),
+        (mid_chip, own_right, base),
         [three_wide],
     )
     (purified,) = call(

time: 57.4 us -> 60.5 us (1.054)
  starting transfers between devices: 19 us -> 24.4 us
  waiting for transfers between devices: 15.2 us -> 12.8 us
    ppermute x12, starting transfers between devices: 19 us -> 24.4 us  [exchange(): lax.ppermute(value, axis, [(i, (i + (even_step if i % 2 == 0 else -even_s...]
    ppermute x12, waiting for transfers between devices: 15.2 us -> 12.8 us  [exchange(): lax.ppermute(value, axis, [(i, (i + (even_step if i % 2 == 0 else -even_s...]
  transfers between devices with their start and end apart: 12 -> 12, of which waited for: 4 -> 4; matrix products, arithmetic and copies ran while one was open for 0% -> 0% of each run, Pallas kernels for 31% -> 29%
where the time goes in v5:
time: 60.5 us; the launch traced here: 60.4 us
  starting transfers between devices  24.4 us (40%)
  Pallas kernels  21.6 us (36%)
  waiting for transfers between devices  12.8 us (21%)
  local copies, waits for them, and re-layouts  1.38 us (2%)
    ppermute x12, starting transfers between devices, exchange(): lax.ppermute(value, axis, [(i, (i + (even_step if i % 2 == 0 else -even_s...  24.4 us
    pallas_call x12, Pallas kernels, call(): pl.pallas_call(body, out_shape=[jax.ShapeDtypeStruct(shape, kind) for sha...  21.6 us
    ppermute x12, waiting for transfers between devices, exchange(): lax.ppermute(value, axis, [(i, (i + (even_step if i % 2 == 0 else -even_s...  12.8 us
    unnamed x6, local copies, waits for them, and re-layouts  1.38 us
  transfers between devices with their start and end apart: 12, of which 4 were waited for; matrix products, arithmetic and copies ran while one was open for 0% of the time, Pallas kernels for 29%

profile of v5, /device:TPU:0, one launch (start us, length us, event | category | flops | bytes accessed | tf_op | source)
XLA Modules:
  0.0 60.4 jit_solution(2868891889674669662)
XLA Ops:
  0.0 0.1 pad_add_fusion.info
  0.1 0.0 copy-start.1
  0.1 1.4 %copy-done.1 = f32[576,576]{1,0:T(8,128)S(1)} copy-done((f32[576,576]{1,0:T(8,128)S(1)}, f32[576,576]{1,0:T(8,128)}, u32[]{:S(2)}) %copy-start.1) | copy-done | bytes 1327128
  1.4 1.4 %pack.1 = (f32[1728,128]{1,0:T(8,128)S(1)}, f32[1152,128]{1,0:T(8,128)S(1)}, f32[576,128]{1,0:T(8,128)S(1)}, f32[864,128]{1,0:T(8,128)S(1)}, f32[864,128]{1,0:T(8,128)S(1)}, /*index=5*/f32[864,128]{1,0:T(8,128)S(1)}) custom-call(s32[2]{0:T(128)S(1)} %pad_add_fusion.info, f32[576,576]{1,0:T(8,128)S(1)} %copy-done.1), custom_call_target="tpu_custom_call" | custom-call | flops 4000000000 | bytes 20000000 | tf_op jit(solution)/shard_map/pack/pallas_call | solution.py:285
  2.8 0.5 collective-permute-start.2
  3.4 2.6 %collective-permute-start.1 = (f32[864,128]{1,0:T(8,128)S(1)}, f32[864,128]{1,0:T(8,128)S(1)}, u32[]{:S(2)}, u32[]{:S(2)}) collective-permute-start(f32[864,128]{1,0:T(8,128)S(1)} %get-tuple-element.40), channel_id=1, source_target_pairs={{0,8},{8,0},{16,24},{24,16},{1,9},{9,1},{17,25},{25,17},{2,10},{10... | collective-permute-start | bytes 1327112 | tf_op jit(solution)/shard_map/ppermute | solution.py:311
  5.9 3.4 %collective-permute-start = (f32[1152,128]{1,0:T(8,128)S(1)}, f32[1152,128]{1,0:T(8,128)S(1)}, u32[]{:S(2)}, u32[]{:S(2)}) collective-permute-start(f32[1152,128]{1,0:T(8,128)S(1)} %get-tuple-element.39), channel_id=1, source_target_pairs={{0,7},{1,2},{2,1},{3,4},{4,3},{5,6},{6,5},{7,0},{8,15},{9,10},{10,... | collective-permute-start | bytes 1769480 | tf_op jit(solution)/shard_map/ppermute | solution.py:311
  9.3 0.0 collective-permute-done.2.chip
  9.3 0.8 %collective-permute-start.6 = (f32[576,128]{1,0:T(8,128)S(1)}, f32[576,128]{1,0:T(8,128)S(1)}, u32[]{:S(2)}, u32[]{:S(2)}) collective-permute-start(f32[576,128]{1,0:T(8,128)S(1)} %get-tuple-element.60), channel_id=1, source_target_pairs={{0,7},{1,2},{2,1},{3,4},{4,3},{5,6},{6,5},{7,0},{8,15},{9,10},{10,... | collective-permute-start | bytes 884744 | tf_op jit(solution)/shard_map/ppermute | solution.py:311
  10.1 1.5 %collective-permute-start.4 = (f32[864,128]{1,0:T(8,128)S(1)}, f32[864,128]{1,0:T(8,128)S(1)}, u32[]{:S(2)}, u32[]{:S(2)}) collective-permute-start(f32[864,128]{1,0:T(8,128)S(1)} %get-tuple-element.54), channel_id=1, source_target_pairs={{0,8},{8,0},{16,24},{24,16},{1,9},{9,1},{17,25},{25,17},{2,10},{10... | collective-permute-start | bytes 1327112 | tf_op jit(solution)/shard_map/ppermute | solution.py:311
  11.6 1.0 %prepare.1 = (bf16[2,3,576,256]{3,2,1,0:T(8,128)(2,1)S(1)}, bf16[2,3,768,256]{3,2,1,0:T(8,128)(2,1)S(1)}, bf16[2,3,384,256]{3,2,1,0:T(8,128)(2,1)S(1)}) custom-call(s32[2]{0:T(128)S(1)} %pad_add_fusion.info, f32[576,576]{1,0:T(8,128)S(1)} %copy-done.1, f32[1728,128]{1,0:T(8,128)S(1)} %collective-permute-done.2.chip), custom_call_target="tpu_custom_call" | custom-call | flops 4000000000 | bytes 20000000 | tf_op jit(solution)/shard_map/prepare/pallas_call | solution.py:285
  12.7 4.3 %collective-permute-done.1.mid = f32[864,128]{1,0:T(8,128)S(1)} collective-permute-done((f32[864,128]{1,0:T(8,128)S(1)}, f32[864,128]{1,0:T(8,128)S(1)}, u32[]{:S(2)}, u32[]{:S(2)}) %collective-permute-start.1) | collective-permute-done | bytes 442400 | tf_op jit(solution)/shard_map/ppermute | solution.py:311
  17.0 2.0 %collective-permute-start.7 = (f32[864,128]{1,0:T(8,128)S(1)}, f32[864,128]{1,0:T(8,128)S(1)}, u32[]{:S(2)}, u32[]{:S(2)}) collective-permute-start(f32[864,128]{1,0:T(8,128)S(1)} %collective-permute-done.1.mid), channel_id=1, source_target_pairs={{0,16},{8,24},{16,0},{24,8},{1,17},{9,25},{17,1},{25,9},{2,18},{10... | collective-permute-start | bytes 1327112 | tf_op jit(solution)/shard_map/ppermute | solution.py:311
  18.9 0.0 copy-start
  18.9 1.6 %near_start.1 = (f32[576,256]{1,0:T(8,128)S(1)}, bf16[2,768,256]{2,1,0:T(8,128)(2,1)S(1)}) custom-call(s32[2]{0:T(128)S(1)} %pad_add_fusion.info, f32[864,128]{1,0:T(8,128)S(1)} %collective-permute-done.1.mid, bf16[2,3,576,256]{3,2,1,0:T(8,128)(2,1)S(1)} %get-tuple-element.47.own_left, bf16[2,3,768,256]{3,2,1,0:T(8,128)(2,1)S(1)} %get-tuple-element.48.own_right, ...), custom_call_target="tpu_custom_call" | custom-call | flops 4000000000 | bytes 20000000 | tf_op jit(solution)/shard_map/near_start/pallas_call | solution.py:285
  20.5 2.6 %collective-permute-done.link_a = f32[1152,128]{1,0:T(8,128)S(1)} collective-permute-done((f32[1152,128]{1,0:T(8,128)S(1)}, f32[1152,128]{1,0:T(8,128)S(1)}, u32[]{:S(2)}, u32[]{:S(2)}) %collective-permute-start) | collective-permute-done | bytes 589856 | tf_op jit(solution)/shard_map/ppermute | solution.py:311
  23.1 0.0 copy-done
  23.1 1.4 %square_near.1 = (f32[576,256]{1,0:T(8,128)S(1)}, f32[576,128]{1,0:T(8,128)S(1)}, bf16[2,2,384,256]{3,2,1,0:T(8,128)(2,1)S(1)}) custom-call(s32[2]{0:T(128)S(1)} %pad_add_fusion.info, s32[9,9]{1,0:T(8,128)S(1)} %copy-done, f32[1152,128]{1,0:T(8,128)S(1)} %collective-permute-done.link_a, f32[576,256]{1,0:T(8,128)S(1)} %get-tuple-element.50.begun, ...), custom_call_target="tpu_custom_call" | custom-call | flops 4000000000 | bytes 20000000 | tf_op jit(solution)/shard_map/square_near/pallas_call | solution.py:285
  24.5 3.7 %collective-permute-start.3 = (f32[576,128]{1,0:T(8,128)S(1)}, f32[576,128]{1,0:T(8,128)S(1)}, u32[]{:S(2)}, u32[]{:S(2)}) collective-permute-start(f32[576,128]{1,0:T(8,128)S(1)} %get-tuple-element.52), channel_id=1, source_target_pairs={{0,7},{1,2},{2,1},{3,4},{4,3},{5,6},{6,5},{7,0},{8,15},{9,10},{10,... | collective-permute-start | bytes 884744 | tf_op jit(solution)/shard_map/ppermute | solution.py:311
  28.3 1.3 %far_start.1.begun = f32[576,256]{1,0:T(8,128)S(1)} custom-call(s32[2]{0:T(128)S(1)} %pad_add_fusion.info, bf16[2,3,576,256]{3,2,1,0:T(8,128)(2,1)S(1)} %get-tuple-element.47.own_left, bf16[2,3,768,256]{3,2,1,0:T(8,128)(2,1)S(1)} %get-tuple-element.48.own_right, bf16[2,3,384,256]{3,2,1,0:T(8,128)(2,1)S(1)} %get-tuple-element.49.chip_left, ...), custom_call_target="tpu_custom_call" | custom-call | flops 4000000000 | bytes 20000000 | tf_op jit(solution)/shard_map/far_start/pallas_call | solution.py:285
  29.5 1.5 %collective-permute-start.5 = (f32[864,128]{1,0:T(8,128)S(1)}, f32[864,128]{1,0:T(8,128)S(1)}, u32[]{:S(2)}, u32[]{:S(2)}) collective-permute-start(f32[864,128]{1,0:T(8,128)S(1)} %get-tuple-element.58), channel_id=1, source_target_pairs={{0,24},{8,16},{16,8},{24,0},{1,25},{9,17},{17,9},{25,1},{2,26},{10... | collective-permute-start | bytes 1327112 | tf_op jit(solution)/shard_map/ppermute | solution.py:311
  31.1 0.0 collective-permute-done.6.link_b
  31.1 2.3 %collective-permute-done.7.mid = f32[864,128]{1,0:T(8,128)S(1)} collective-permute-done((f32[864,128]{1,0:T(8,128)S(1)}, f32[864,128]{1,0:T(8,128)S(1)}, u32[]{:S(2)}, u32[]{:S(2)}) %collective-permute-start.7) | collective-permute-done | bytes 442400 | tf_op jit(solution)/shard_map/ppermute | solution.py:311
  33.4 1.9 %square_far.1 = (f32[576,256]{1,0:T(8,128)S(1)}, f32[1152,128]{1,0:T(8,128)S(1)}, f32[576,128]{1,0:T(8,128)S(1)}, bf16[2,384,256]{2,1,0:T(8,128)(2,1)S(1)}, bf16[2,768,256]{2,1,0:T(8,128)(2,1)S(1)}) custom-call(s32[2]{0:T(128)S(1)} %pad_add_fusion.info, s32[9,9]{1,0:T(8,128)S(1)} %copy-done, f32[576,128]{1,0:T(8,128)S(1)} %collective-permute-done.6.link_b, ...), custom_call_target="tpu_custom_call" | custom-call | flops 4000000000 | bytes 20000000 | tf_op jit(solution)/shard_map/square_far/pallas_call | solution.py:285
  35.2 0.1 collective-permute-start.11
  35.3 6.5 %collective-permute-start.10 = (f32[1152,128]{1,0:T(8,128)S(1)}, f32[1152,128]{1,0:T(8,128)S(1)}, u32[]{:S(2)}, u32[]{:S(2)}) collective-permute-start(f32[1152,128]{1,0:T(8,128)S(1)} %get-tuple-element.66), channel_id=1, source_target_pairs={{0,1},{1,0},{2,3},{3,2},{4,5},{5,4},{6,7},{7,6},{8,9},{9,8},{10,11... | collective-permute-start | bytes 1769480 | tf_op jit(solution)/shard_map/ppermute | solution.py:311
  41.8 0.0 collective-permute-done.4.near
  41.8 2.0 %mid_start.1 = (f32[576,256]{1,0:T(8,128)S(1)}, bf16[2,768,256]{2,1,0:T(8,128)(2,1)S(1)}) custom-call(s32[2]{0:T(128)S(1)} %pad_add_fusion.info, f32[864,128]{1,0:T(8,128)S(1)} %collective-permute-done.4.near, bf16[2,3,576,256]{3,2,1,0:T(8,128)(2,1)S(1)} %get-tuple-element.47.own_left, bf16[2,3,768,256]{3,2,1,0:T(8,128)(2,1)S(1)} %get-tuple-element.48.own_right, ...), custom_call_target="tpu_custom_call" | custom-call | flops 4000000000 | bytes 20000000 | tf_op jit(solution)/shard_map/mid_start/pallas_call | solution.py:285
  43.8 0.0 collective-permute-done.3.link
  43.8 1.6 %cube_near.1.total = f32[3,576,256]{2,1,0:T(8,128)S(1)} custom-call(s32[2]{0:T(128)S(1)} %pad_add_fusion.info, f32[576,128]{1,0:T(8,128)S(1)} %collective-permute-done.3.link, f32[576,256]{1,0:T(8,128)S(1)} %get-tuple-element.53.near, bf16[2,768,256]{2,1,0:T(8,128)(2,1)S(1)} %get-tuple-element.51.right_near, ...), custom_call_target="tpu_custom_call" | custom-call | flops 4000000000 | bytes 20000000 | tf_op jit(solution)/shard_map/cube_near/pallas_call | solution.py:285
  45.4 0.0 collective-permute-done.5.far
  45.4 1.9 %square_mid.1 = (f32[576,256]{1,0:T(8,128)S(1)}, f32[576,128]{1,0:T(8,128)S(1)}, f32[576,128]{1,0:T(8,128)S(1)}, bf16[2,768,256]{2,1,0:T(8,128)(2,1)S(1)}) custom-call(s32[2]{0:T(128)S(1)} %pad_add_fusion.info, s32[9,9]{1,0:T(8,128)S(1)} %copy-done, f32[864,128]{1,0:T(8,128)S(1)} %collective-permute-done.5.far, ...), custom_call_target="tpu_custom_call" | custom-call | tf_op jit(solution)/shard_map/square_mid/pallas_call | solution.py:285
  47.3 0.1 collective-permute-start.8
  47.4 1.7 %collective-permute-start.9 = (f32[576,128]{1,0:T(8,128)S(1)}, f32[576,128]{1,0:T(8,128)S(1)}, u32[]{:S(2)}, u32[]{:S(2)}) collective-permute-start(f32[576,128]{1,0:T(8,128)S(1)} %get-tuple-element.65), channel_id=1, source_target_pairs={{0,1},{1,0},{2,3},{3,2},{4,5},{5,4},{6,7},{7,6},{8,9},{9,8},{10,11... | collective-permute-start | bytes 884744 | tf_op jit(solution)/shard_map/ppermute | solution.py:311
  49.1 0.0 collective-permute-done.11.link
  49.1 0.0 collective-permute-done.10.chip
  49.1 0.0 copy-start.2
  49.1 3.3 %cube_own.1.base = f32[3,576,256]{2,1,0:T(8,128)S(1)} custom-call(s32[2]{0:T(128)S(1)} %pad_add_fusion.info, f32[1152,128]{1,0:T(8,128)S(1)} %collective-permute-done.10.chip, f32[576,128]{1,0:T(8,128)S(1)} %collective-permute-done.11.link, f32[3,576,256]{2,1,0:T(8,128)S(1)} %cube_near.1.total, f32[576,256]{1,0:T(8,128)S(1)} %get-tuple-element.53.near, ...), custom_call_target="tpu_custom_call" | custom-call | flops 4000000000 | bytes 20000000 | tf_op jit(solution)/shard_map/cube_own/pallas_call | solution.py:285
  52.4 0.0 collective-permute-done.9.chip
  52.4 0.0 copy-done.2
  52.4 1.8 %cube_chip.1.base = f32[3,576,256]{2,1,0:T(8,128)S(1)} custom-call(s32[2]{0:T(128)S(1)} %pad_add_fusion.info, s32[9,9]{1,0:T(8,128)S(1)} %copy-done.2, f32[576,128]{1,0:T(8,128)S(1)} %collective-permute-done.9.chip, bf16[2,3,768,256]{3,2,1,0:T(8,128)(2,1)S(1)} %get-tuple-element.48.own_right, f32[3,576,256]{2,1,0:T(8,128)S(1)} %cube_own.1.base), custom_call_target="tpu_custom_call" | custom-call | flops 4000000000 | bytes 20000000 | tf_op jit(solution)/shard_map/cube_chip/pallas_call | solution.py:285
  54.2 3.7 %collective-permute-done.8.link = f32[576,128]{1,0:T(8,128)S(1)} collective-permute-done((f32[576,128]{1,0:T(8,128)S(1)}, f32[576,128]{1,0:T(8,128)S(1)}, u32[]{:S(2)}, u32[]{:S(2)}) %collective-permute-start.8) | collective-permute-done | bytes 294944 | tf_op jit(solution)/shard_map/ppermute | solution.py:311
  57.8 2.5 %finish.1 = f32[576,576]{1,0:T(8,128)} custom-call(s32[2]{0:T(128)S(1)} %pad_add_fusion.info, s32[9,9]{1,0:T(8,128)S(1)} %copy-done.2, f32[576,128]{1,0:T(8,128)S(1)} %collective-permute-done.8.link, bf16[2,3,768,256]{3,2,1,0:T(8,128)(2,1)S(1)} %get-tuple-element.48.own_right, f32[3,576,256]{2,1,0:T(8,128)S(1)} %cube_chip.1.base), custom_call_target="tpu_custom_call" | custom-call | flops 4000000000 | bytes 20000000 | tf_op jit(solution)/shard_map/finish/pallas_call | solution.py:285
Async XLA Ops:
  0.1 1.4 %copy-start.1 = (f32[576,576]{1,0:T(8,128)S(1)}, f32[576,576]{1,0:T(8,128)}, u32[]{:S(2)}) copy-start(f32[576,576]{1,0:T(8,128)} %tile.3) | copy-start | bytes 3981316
  2.8 6.5 %collective-permute-start.2 = (f32[1728,128]{1,0:T(8,128)S(1)}, f32[1728,128]{1,0:T(8,128)S(1)}, u32[]{:S(2)}, u32[]{:S(2)}) collective-permute-start(f32[1728,128]{1,0:T(8,128)S(1)} %get-tuple-element.41), channel_id=1, source_target_pairs={{0,1},{1,0},{2,3},{3,2},{4,5},{5,4},{6,7},{7,6},{8,9},{9,8},{10,11... | collective-permute-start | bytes 2654216 | tf_op jit(solution)/shard_map/ppermute | solution.py:311
  3.4 13.6 %collective-permute-start.1 = (f32[864,128]{1,0:T(8,128)S(1)}, f32[864,128]{1,0:T(8,128)S(1)}, u32[]{:S(2)}, u32[]{:S(2)}) collective-permute-start(f32[864,128]{1,0:T(8,128)S(1)} %get-tuple-element.40), channel_id=1, source_target_pairs={{0,8},{8,0},{16,24},{24,16},{1,9},{9,1},{17,25},{25,17},{2,10},{10... | collective-permute-start | bytes 1327112 | tf_op jit(solution)/shard_map/ppermute | solution.py:311
  5.9 17.2 %collective-permute-start = (f32[1152,128]{1,0:T(8,128)S(1)}, f32[1152,128]{1,0:T(8,128)S(1)}, u32[]{:S(2)}, u32[]{:S(2)}) collective-permute-start(f32[1152,128]{1,0:T(8,128)S(1)} %get-tuple-element.39), channel_id=1, source_target_pairs={{0,7},{1,2},{2,1},{3,4},{4,3},{5,6},{6,5},{7,0},{8,15},{9,10},{10,... | collective-permute-start | bytes 1769480 | tf_op jit(solution)/shard_map/ppermute | solution.py:311
  9.3 21.8 %collective-permute-start.6 = (f32[576,128]{1,0:T(8,128)S(1)}, f32[576,128]{1,0:T(8,128)S(1)}, u32[]{:S(2)}, u32[]{:S(2)}) collective-permute-start(f32[576,128]{1,0:T(8,128)S(1)} %get-tuple-element.60), channel_id=1, source_target_pairs={{0,7},{1,2},{2,1},{3,4},{4,3},{5,6},{6,5},{7,0},{8,15},{9,10},{10,... | collective-permute-start | bytes 884744 | tf_op jit(solution)/shard_map/ppermute | solution.py:311
  10.1 31.7 %collective-permute-start.4 = (f32[864,128]{1,0:T(8,128)S(1)}, f32[864,128]{1,0:T(8,128)S(1)}, u32[]{:S(2)}, u32[]{:S(2)}) collective-permute-start(f32[864,128]{1,0:T(8,128)S(1)} %get-tuple-element.54), channel_id=1, source_target_pairs={{0,8},{8,0},{16,24},{24,16},{1,9},{9,1},{17,25},{25,17},{2,10},{10... | collective-permute-start | bytes 1327112 | tf_op jit(solution)/shard_map/ppermute | solution.py:311
  17.0 16.4 %collective-permute-start.7 = (f32[864,128]{1,0:T(8,128)S(1)}, f32[864,128]{1,0:T(8,128)S(1)}, u32[]{:S(2)}, u32[]{:S(2)}) collective-permute-start(f32[864,128]{1,0:T(8,128)S(1)} %collective-permute-done.1.mid), channel_id=1, source_target_pairs={{0,16},{8,24},{16,0},{24,8},{1,17},{9,25},{17,1},{25,9},{2,18},{10... | collective-permute-start | bytes 1327112 | tf_op jit(solution)/shard_map/ppermute | solution.py:311
  18.9 4.2 %copy-start = (s32[9,9]{1,0:T(8,128)S(1)}, s32[9,9]{1,0:T(8,128)}, u32[]{:S(2)}) copy-start(s32[9,9]{1,0:T(8,128)} %kept.7) | copy-start | bytes 976
  24.5 19.3 %collective-permute-start.3 = (f32[576,128]{1,0:T(8,128)S(1)}, f32[576,128]{1,0:T(8,128)S(1)}, u32[]{:S(2)}, u32[]{:S(2)}) collective-permute-start(f32[576,128]{1,0:T(8,128)S(1)} %get-tuple-element.52), channel_id=1, source_target_pairs={{0,7},{1,2},{2,1},{3,4},{4,3},{5,6},{6,5},{7,0},{8,15},{9,10},{10,... | collective-permute-start | bytes 884744 | tf_op jit(solution)/shard_map/ppermute | solution.py:311
  29.5 15.9 %collective-permute-start.5 = (f32[864,128]{1,0:T(8,128)S(1)}, f32[864,128]{1,0:T(8,128)S(1)}, u32[]{:S(2)}, u32[]{:S(2)}) collective-permute-start(f32[864,128]{1,0:T(8,128)S(1)} %get-tuple-element.58), channel_id=1, source_target_pairs={{0,24},{8,16},{16,8},{24,0},{1,25},{9,17},{17,9},{25,1},{2,26},{10... | collective-permute-start | bytes 1327112 | tf_op jit(solution)/shard_map/ppermute | solution.py:311
  35.2 13.8 %collective-permute-start.11 = (f32[576,128]{1,0:T(8,128)S(1)}, f32[576,128]{1,0:T(8,128)S(1)}, u32[]{:S(2)}, u32[]{:S(2)}) collective-permute-start(f32[576,128]{1,0:T(8,128)S(1)} %get-tuple-element.67), channel_id=1, source_target_pairs={{0,7},{1,2},{2,1},{3,4},{4,3},{5,6},{6,5},{7,0},{8,15},{9,10},{10,... | collective-permute-start | bytes 884744 | tf_op jit(solution)/shard_map/ppermute | solution.py:311
  35.3 13.8 %collective-permute-start.10 = (f32[1152,128]{1,0:T(8,128)S(1)}, f32[1152,128]{1,0:T(8,128)S(1)}, u32[]{:S(2)}, u32[]{:S(2)}) collective-permute-start(f32[1152,128]{1,0:T(8,128)S(1)} %get-tuple-element.66), channel_id=1, source_target_pairs={{0,1},{1,0},{2,3},{3,2},{4,5},{5,4},{6,7},{7,6},{8,9},{9,8},{10,11... | collective-permute-start | bytes 1769480 | tf_op jit(solution)/shard_map/ppermute | solution.py:311
  47.3 10.5 %collective-permute-start.8 = (f32[576,128]{1,0:T(8,128)S(1)}, f32[576,128]{1,0:T(8,128)S(1)}, u32[]{:S(2)}, u32[]{:S(2)}) collective-permute-start(f32[576,128]{1,0:T(8,128)S(1)} %get-tuple-element.64), channel_id=1, source_target_pairs={{0,7},{1,2},{2,1},{3,4},{4,3},{5,6},{6,5},{7,0},{8,15},{9,10},{10,... | collective-permute-start | bytes 884744 | tf_op jit(solution)/shard_map/ppermute | solution.py:311
  47.4 5.0 %collective-permute-start.9 = (f32[576,128]{1,0:T(8,128)S(1)}, f32[576,128]{1,0:T(8,128)S(1)}, u32[]{:S(2)}, u32[]{:S(2)}) collective-permute-start(f32[576,128]{1,0:T(8,128)S(1)} %get-tuple-element.65), channel_id=1, source_target_pairs={{0,1},{1,0},{2,3},{3,2},{4,5},{5,4},{6,7},{7,6},{8,9},{9,8},{10,11... | collective-permute-start | bytes 884744 | tf_op jit(solution)/shard_map/ppermute | solution.py:311
  49.1 3.3 %copy-start.2 = (s32[9,9]{1,0:T(8,128)S(1)}, s32[9,9]{1,0:T(8,128)}, u32[]{:S(2)}) copy-start(s32[9,9]{1,0:T(8,128)} %kept.9) | copy-start | bytes 976

commit v6 on v5

--- a/solution.py
+++ b/solution.py
@@ -317,6 +317,7 @@
     )
     link_a = exchange(link_a, "col", -1)
     partner_mid = exchange(mid, "row", 1)
+    passed_far = exchange(far, "row", -2)
     chip = exchange(chip, "col", 1)
     chip, link_b, near = lax.optimization_barrier((chip, link_b, near))
     link_b = exchange(link_b, "col", -1)
@@ -333,6 +334,8 @@
     begun, right_near = call(
         near_start_body, "near_start", (info,), (partner_mid, own_left, own_right, chip_left), [wide, rights]
     )
+    passed_far, begun = lax.optimization_barrier((passed_far, begun))
+    other_far = exchange(passed_far, "row", 1)
     s_near, near_link, link_left = call(
         near_body,
         "square_near",
@@ -344,8 +347,6 @@
     (begun,) = call(
         far_start_body, "far_start", (info,), (own_left, own_right, chip_left, link_left), [wide]
     )
-    far, begun = lax.optimization_barrier((far, begun))
-    other_far = exchange(far, "row", -1)
     s_far, sides_chip, far_link, link_left_far, right_far = call(
         far_body,
         "square_far",

time: 60.5 us -> 53.9 us (0.89)
  waiting for transfers between devices: 12.8 us -> 8.57 us
  starting transfers between devices: 24.4 us -> 21.6 us
    ppermute x12 -> x13, waiting for transfers between devices: 12.8 us -> 8.57 us  [exchange(): lax.ppermute(value, axis, [(i, (i + (even_step if i % 2 == 0 else -even_s...]
    ppermute x12 -> x13, starting transfers between devices: 24.4 us -> 21.6 us  [exchange(): lax.ppermute(value, axis, [(i, (i + (even_step if i % 2 == 0 else -even_s...]
  transfers between devices with their start and end apart: 12 -> 13, of which waited for: 4 -> 4; matrix products, arithmetic and copies ran while one was open for 0% -> 0% of each run, Pallas kernels for 29% -> 33%
where the time goes in v6:
time: 53.9 us; the launch traced here: 53.3 us
  Pallas kernels  21.6 us (40%)
  starting transfers between devices  21.6 us (40%)
  waiting for transfers between devices  8.57 us (16%)
  local copies, waits for them, and re-layouts  1.38 us (3%)
    pallas_call x12, Pallas kernels, call(): pl.pallas_call(body, out_shape=[jax.ShapeDtypeStruct(shape, kind) for sha...  21.6 us
    ppermute x13, starting transfers between devices, exchange(): lax.ppermute(value, axis, [(i, (i + (even_step if i % 2 == 0 else -even_s...  21.6 us
    ppermute x13, waiting for transfers between devices, exchange(): lax.ppermute(value, axis, [(i, (i + (even_step if i % 2 == 0 else -even_s...  8.57 us
    unnamed x6, local copies, waits for them, and re-layouts  1.38 us
  transfers between devices with their start and end apart: 13, of which 4 were waited for; matrix products, arithmetic and copies ran while one was open for 0% of the time, Pallas kernels for 33%

profile of v6, /device:TPU:0, one launch (start us, length us, event | category | flops | bytes accessed | tf_op | source)
XLA Modules:
  0.0 53.3 jit_solution(14881675604575897762)
XLA Ops:
  0.0 0.1 pad_add_fusion.info
  0.1 0.0 copy-start.1
  0.1 1.4 %copy-done.1 = f32[576,576]{1,0:T(8,128)S(1)} copy-done((f32[576,576]{1,0:T(8,128)S(1)}, f32[576,576]{1,0:T(8,128)}, u32[]{:S(2)}) %copy-start.1) | copy-done | bytes 1327128
  1.4 1.4 %pack.1 = (f32[1728,128]{1,0:T(8,128)S(1)}, f32[1152,128]{1,0:T(8,128)S(1)}, f32[576,128]{1,0:T(8,128)S(1)}, f32[864,128]{1,0:T(8,128)S(1)}, f32[864,128]{1,0:T(8,128)S(1)}, /*index=5*/f32[864,128]{1,0:T(8,128)S(1)}) custom-call(s32[2]{0:T(128)S(1)} %pad_add_fusion.info, f32[576,576]{1,0:T(8,128)S(1)} %copy-done.1), custom_call_target="tpu_custom_call" | custom-call | flops 4000000000 | bytes 20000000 | tf_op jit(solution)/shard_map/pack/pallas_call | solution.py:285
  2.8 0.5 collective-permute-start.3
  3.4 2.6 %collective-permute-start.2 = (f32[864,128]{1,0:T(8,128)S(1)}, f32[864,128]{1,0:T(8,128)S(1)}, u32[]{:S(2)}, u32[]{:S(2)}) collective-permute-start(f32[864,128]{1,0:T(8,128)S(1)} %get-tuple-element.41), channel_id=1, source_target_pairs={{0,8},{8,0},{16,24},{24,16},{1,9},{9,1},{17,25},{25,17},{2,10},{10... | collective-permute-start | bytes 1327112 | tf_op jit(solution)/shard_map/ppermute | solution.py:311
  5.9 1.5 %collective-permute-start.1 = (f32[864,128]{1,0:T(8,128)S(1)}, f32[864,128]{1,0:T(8,128)S(1)}, u32[]{:S(2)}, u32[]{:S(2)}) collective-permute-start(f32[864,128]{1,0:T(8,128)S(1)} %get-tuple-element.40), channel_id=1, source_target_pairs={{0,16},{8,24},{16,0},{24,8},{1,17},{9,25},{17,1},{25,9},{2,18},{10... | collective-permute-start | bytes 1327112 | tf_op jit(solution)/shard_map/ppermute | solution.py:311
  7.5 3.1 %collective-permute-start = (f32[1152,128]{1,0:T(8,128)S(1)}, f32[1152,128]{1,0:T(8,128)S(1)}, u32[]{:S(2)}, u32[]{:S(2)}) collective-permute-start(f32[1152,128]{1,0:T(8,128)S(1)} %get-tuple-element.39), channel_id=1, source_target_pairs={{0,7},{1,2},{2,1},{3,4},{4,3},{5,6},{6,5},{7,0},{8,15},{9,10},{10,... | collective-permute-start | bytes 1769480 | tf_op jit(solution)/shard_map/ppermute | solution.py:311
  10.5 0.0 collective-permute-done.3.chip
  10.5 0.5 collective-permute-start.7
  11.0 0.6 %collective-permute-start.5 = (f32[864,128]{1,0:T(8,128)S(1)}, f32[864,128]{1,0:T(8,128)S(1)}, u32[]{:S(2)}, u32[]{:S(2)}) collective-permute-start(f32[864,128]{1,0:T(8,128)S(1)} %get-tuple-element.56), channel_id=1, source_target_pairs={{0,8},{8,0},{16,24},{24,16},{1,9},{9,1},{17,25},{25,17},{2,10},{10... | collective-permute-start | bytes 1327112 | tf_op jit(solution)/shard_map/ppermute | solution.py:311
  11.6 1.0 %prepare.1 = (bf16[2,3,576,256]{3,2,1,0:T(8,128)(2,1)S(1)}, bf16[2,3,768,256]{3,2,1,0:T(8,128)(2,1)S(1)}, bf16[2,3,384,256]{3,2,1,0:T(8,128)(2,1)S(1)}) custom-call(s32[2]{0:T(128)S(1)} %pad_add_fusion.info, f32[576,576]{1,0:T(8,128)S(1)} %copy-done.1, f32[1728,128]{1,0:T(8,128)S(1)} %collective-permute-done.3.chip), custom_call_target="tpu_custom_call" | custom-call | flops 4000000000 | bytes 20000000 | tf_op jit(solution)/shard_map/prepare/pallas_call | solution.py:285
  12.7 4.3 %collective-permute-done.2.mid = f32[864,128]{1,0:T(8,128)S(1)} collective-permute-done((f32[864,128]{1,0:T(8,128)S(1)}, f32[864,128]{1,0:T(8,128)S(1)}, u32[]{:S(2)}, u32[]{:S(2)}) %collective-permute-start.2) | collective-permute-done | bytes 442400 | tf_op jit(solution)/shard_map/ppermute | solution.py:311
  17.0 2.0 %collective-permute-start.8 = (f32[864,128]{1,0:T(8,128)S(1)}, f32[864,128]{1,0:T(8,128)S(1)}, u32[]{:S(2)}, u32[]{:S(2)}) collective-permute-start(f32[864,128]{1,0:T(8,128)S(1)} %collective-permute-done.2.mid), channel_id=1, source_target_pairs={{0,16},{8,24},{16,0},{24,8},{1,17},{9,25},{17,1},{25,9},{2,18},{10... | collective-permute-start | bytes 1327112 | tf_op jit(solution)/shard_map/ppermute | solution.py:311
  18.9 0.0 copy-start
  18.9 1.6 %near_start.1 = (f32[576,256]{1,0:T(8,128)S(1)}, bf16[2,768,256]{2,1,0:T(8,128)(2,1)S(1)}) custom-call(s32[2]{0:T(128)S(1)} %pad_add_fusion.info, f32[864,128]{1,0:T(8,128)S(1)} %collective-permute-done.2.mid, bf16[2,3,576,256]{3,2,1,0:T(8,128)(2,1)S(1)} %get-tuple-element.48.own_left, bf16[2,3,768,256]{3,2,1,0:T(8,128)(2,1)S(1)} %get-tuple-element.49.own_right, ...), custom_call_target="tpu_custom_call" | custom-call | flops 4000000000 | bytes 20000000 | tf_op jit(solution)/shard_map/near_start/pallas_call | solution.py:285
  20.5 0.0 collective-permute-done.1
  20.5 1.6 %collective-permute-start.6 = (f32[864,128]{1,0:T(8,128)S(1)}, f32[864,128]{1,0:T(8,128)S(1)}, u32[]{:S(2)}, u32[]{:S(2)}) collective-permute-start(f32[864,128]{1,0:T(8,128)S(1)} %collective-permute-done.1), channel_id=1, source_target_pairs={{0,8},{8,0},{16,24},{24,16},{1,9},{9,1},{17,25},{25,17},{2,10},{10... | collective-permute-start | bytes 1327112 | tf_op jit(solution)/shard_map/ppermute | solution.py:311
  22.1 2.6 %collective-permute-done.link_a = f32[1152,128]{1,0:T(8,128)S(1)} collective-permute-done((f32[1152,128]{1,0:T(8,128)S(1)}, f32[1152,128]{1,0:T(8,128)S(1)}, u32[]{:S(2)}, u32[]{:S(2)}) %collective-permute-start) | collective-permute-done | bytes 589856 | tf_op jit(solution)/shard_map/ppermute | solution.py:311
  24.6 0.0 copy-done
  24.6 1.4 %square_near.1 = (f32[576,256]{1,0:T(8,128)S(1)}, f32[576,128]{1,0:T(8,128)S(1)}, bf16[2,2,384,256]{3,2,1,0:T(8,128)(2,1)S(1)}) custom-call(s32[2]{0:T(128)S(1)} %pad_add_fusion.info, s32[9,9]{1,0:T(8,128)S(1)} %copy-done, f32[1152,128]{1,0:T(8,128)S(1)} %collective-permute-done.link_a, f32[576,256]{1,0:T(8,128)S(1)} %get-tuple-element.52.begun, ...), custom_call_target="tpu_custom_call" | custom-call | flops 4000000000 | bytes 20000000 | tf_op jit(solution)/shard_map/square_near/pallas_call | solution.py:285
  26.0 3.5 %collective-permute-start.4 = (f32[576,128]{1,0:T(8,128)S(1)}, f32[576,128]{1,0:T(8,128)S(1)}, u32[]{:S(2)}, u32[]{:S(2)}) collective-permute-start(f32[576,128]{1,0:T(8,128)S(1)} %get-tuple-element.54), channel_id=1, source_target_pairs={{0,7},{1,2},{2,1},{3,4},{4,3},{5,6},{6,5},{7,0},{8,15},{9,10},{10,... | collective-permute-start | bytes 884744 | tf_op jit(solution)/shard_map/ppermute | solution.py:311
  29.5 1.3 %far_start.1.begun = f32[576,256]{1,0:T(8,128)S(1)} custom-call(s32[2]{0:T(128)S(1)} %pad_add_fusion.info, bf16[2,3,576,256]{3,2,1,0:T(8,128)(2,1)S(1)} %get-tuple-element.48.own_left, bf16[2,3,768,256]{3,2,1,0:T(8,128)(2,1)S(1)} %get-tuple-element.49.own_right, bf16[2,3,384,256]{3,2,1,0:T(8,128)(2,1)S(1)} %get-tuple-element.50.chip_left, ...), custom_call_target="tpu_custom_call" | custom-call | flops 4000000000 | bytes 20000000 | tf_op jit(solution)/shard_map/far_start/pallas_call | solution.py:285
  30.8 0.2 collective-permute-done.7.link_b
  30.9 0.0 collective-permute-done.8.mid
  30.9 1.9 %square_far.1 = (f32[576,256]{1,0:T(8,128)S(1)}, f32[1152,128]{1,0:T(8,128)S(1)}, f32[576,128]{1,0:T(8,128)S(1)}, bf16[2,384,256]{2,1,0:T(8,128)(2,1)S(1)}, bf16[2,768,256]{2,1,0:T(8,128)(2,1)S(1)}) custom-call(s32[2]{0:T(128)S(1)} %pad_add_fusion.info, s32[9,9]{1,0:T(8,128)S(1)} %copy-done, f32[576,128]{1,0:T(8,128)S(1)} %collective-permute-done.7.link_b, ...), custom_call_target="tpu_custom_call" | custom-call | flops 4000000000 | bytes 20000000 | tf_op jit(solution)/shard_map/square_far/pallas_call | solution.py:285
  32.8 3.5 %collective-permute-start.12 = (f32[576,128]{1,0:T(8,128)S(1)}, f32[576,128]{1,0:T(8,128)S(1)}, u32[]{:S(2)}, u32[]{:S(2)}) collective-permute-start(f32[576,128]{1,0:T(8,128)S(1)} %get-tuple-element.67), channel_id=1, source_target_pairs={{0,7},{1,2},{2,1},{3,4},{4,3},{5,6},{6,5},{7,0},{8,15},{9,10},{10,... | collective-permute-start | bytes 884744 | tf_op jit(solution)/shard_map/ppermute | solution.py:311
  36.3 0.0 collective-permute-start.11
  36.3 0.0 collective-permute-done.5.near
  36.3 2.0 %mid_start.1 = (f32[576,256]{1,0:T(8,128)S(1)}, bf16[2,768,256]{2,1,0:T(8,128)(2,1)S(1)}) custom-call(s32[2]{0:T(128)S(1)} %pad_add_fusion.info, f32[864,128]{1,0:T(8,128)S(1)} %collective-permute-done.5.near, bf16[2,3,576,256]{3,2,1,0:T(8,128)(2,1)S(1)} %get-tuple-element.48.own_left, bf16[2,3,768,256]{3,2,1,0:T(8,128)(2,1)S(1)} %get-tuple-element.49.own_right, ...), custom_call_target="tpu_custom_call" | custom-call | flops 4000000000 | bytes 20000000 | tf_op jit(solution)/shard_map/mid_start/pallas_call | solution.py:285
  38.3 0.0 collective-permute-done.4.link
  38.3 1.6 %cube_near.1.total = f32[3,576,256]{2,1,0:T(8,128)S(1)} custom-call(s32[2]{0:T(128)S(1)} %pad_add_fusion.info, f32[576,128]{1,0:T(8,128)S(1)} %collective-permute-done.4.link, f32[576,256]{1,0:T(8,128)S(1)} %get-tuple-element.55.near, bf16[2,768,256]{2,1,0:T(8,128)(2,1)S(1)} %get-tuple-element.53.right_near, ...), custom_call_target="tpu_custom_call" | custom-call | flops 4000000000 | bytes 20000000 | tf_op jit(solution)/shard_map/cube_near/pallas_call | solution.py:285
  39.9 0.0 collective-permute-done.6.far
  39.9 1.9 %square_mid.1 = (f32[576,256]{1,0:T(8,128)S(1)}, f32[576,128]{1,0:T(8,128)S(1)}, f32[576,128]{1,0:T(8,128)S(1)}, bf16[2,768,256]{2,1,0:T(8,128)(2,1)S(1)}) custom-call(s32[2]{0:T(128)S(1)} %pad_add_fusion.info, s32[9,9]{1,0:T(8,128)S(1)} %copy-done, f32[864,128]{1,0:T(8,128)S(1)} %collective-permute-done.6.far, ...), custom_call_target="tpu_custom_call" | custom-call | tf_op jit(solution)/shard_map/square_mid/pallas_call | solution.py:285
  41.8 2.3 %collective-permute-start.9 = (f32[576,128]{1,0:T(8,128)S(1)}, f32[576,128]{1,0:T(8,128)S(1)}, u32[]{:S(2)}, u32[]{:S(2)}) collective-permute-start(f32[576,128]{1,0:T(8,128)S(1)} %get-tuple-element.64), channel_id=1, source_target_pairs={{0,7},{1,2},{2,1},{3,4},{4,3},{5,6},{6,5},{7,0},{8,15},{9,10},{10,... | collective-permute-start | bytes 884744 | tf_op jit(solution)/shard_map/ppermute | solution.py:311
  44.1 0.0 collective-permute-start.10
  44.1 0.0 collective-permute-done.12.link
  44.1 0.0 collective-permute-done.11.chip
  44.1 0.0 copy-start.2
  44.1 3.3 %cube_own.1.base = f32[3,576,256]{2,1,0:T(8,128)S(1)} custom-call(s32[2]{0:T(128)S(1)} %pad_add_fusion.info, f32[1152,128]{1,0:T(8,128)S(1)} %collective-permute-done.11.chip, f32[576,128]{1,0:T(8,128)S(1)} %collective-permute-done.12.link, f32[3,576,256]{2,1,0:T(8,128)S(1)} %cube_near.1.total, f32[576,256]{1,0:T(8,128)S(1)} %get-tuple-element.55.near, ...), custom_call_target="tpu_custom_call" | custom-call | flops 4000000000 | bytes 20000000 | tf_op jit(solution)/shard_map/cube_own/pallas_call | solution.py:285
  47.5 0.0 collective-permute-done.10.chip
  47.5 0.0 copy-done.2
  47.5 1.8 %cube_chip.1.base = f32[3,576,256]{2,1,0:T(8,128)S(1)} custom-call(s32[2]{0:T(128)S(1)} %pad_add_fusion.info, s32[9,9]{1,0:T(8,128)S(1)} %copy-done.2, f32[576,128]{1,0:T(8,128)S(1)} %collective-permute-done.10.chip, bf16[2,3,768,256]{3,2,1,0:T(8,128)(2,1)S(1)} %get-tuple-element.49.own_right, f32[3,576,256]{2,1,0:T(8,128)S(1)} %cube_own.1.base), custom_call_target="tpu_custom_call" | custom-call | flops 4000000000 | bytes 20000000 | tf_op jit(solution)/shard_map/cube_chip/pallas_call | solution.py:285
  49.3 1.5 %collective-permute-done.9.link = f32[576,128]{1,0:T(8,128)S(1)} collective-permute-done((f32[576,128]{1,0:T(8,128)S(1)}, f32[576,128]{1,0:T(8,128)S(1)}, u32[]{:S(2)}, u32[]{:S(2)}) %collective-permute-start.9) | collective-permute-done | bytes 294944 | tf_op jit(solution)/shard_map/ppermute | solution.py:311
  50.8 2.5 %finish.1 = f32[576,576]{1,0:T(8,128)} custom-call(s32[2]{0:T(128)S(1)} %pad_add_fusion.info, s32[9,9]{1,0:T(8,128)S(1)} %copy-done.2, f32[576,128]{1,0:T(8,128)S(1)} %collective-permute-done.9.link, bf16[2,3,768,256]{3,2,1,0:T(8,128)(2,1)S(1)} %get-tuple-element.49.own_right, f32[3,576,256]{2,1,0:T(8,128)S(1)} %cube_chip.1.base), custom_call_target="tpu_custom_call" | custom-call | flops 4000000000 | bytes 20000000 | tf_op jit(solution)/shard_map/finish/pallas_call | solution.py:285
Async XLA Ops:
  0.1 1.4 %copy-start.1 = (f32[576,576]{1,0:T(8,128)S(1)}, f32[576,576]{1,0:T(8,128)}, u32[]{:S(2)}) copy-start(f32[576,576]{1,0:T(8,128)} %tile.3) | copy-start | bytes 3981316
  2.8 7.7 %collective-permute-start.3 = (f32[1728,128]{1,0:T(8,128)S(1)}, f32[1728,128]{1,0:T(8,128)S(1)}, u32[]{:S(2)}, u32[]{:S(2)}) collective-permute-start(f32[1728,128]{1,0:T(8,128)S(1)} %get-tuple-element.42), channel_id=1, source_target_pairs={{0,1},{1,0},{2,3},{3,2},{4,5},{5,4},{6,7},{7,6},{8,9},{9,8},{10,11... | collective-permute-start | bytes 2654216 | tf_op jit(solution)/shard_map/ppermute | solution.py:311
  3.4 13.6 %collective-permute-start.2 = (f32[864,128]{1,0:T(8,128)S(1)}, f32[864,128]{1,0:T(8,128)S(1)}, u32[]{:S(2)}, u32[]{:S(2)}) collective-permute-start(f32[864,128]{1,0:T(8,128)S(1)} %get-tuple-element.41), channel_id=1, source_target_pairs={{0,8},{8,0},{16,24},{24,16},{1,9},{9,1},{17,25},{25,17},{2,10},{10... | collective-permute-start | bytes 1327112 | tf_op jit(solution)/shard_map/ppermute | solution.py:311
  5.9 14.6 %collective-permute-start.1 = (f32[864,128]{1,0:T(8,128)S(1)}, f32[864,128]{1,0:T(8,128)S(1)}, u32[]{:S(2)}, u32[]{:S(2)}) collective-permute-start(f32[864,128]{1,0:T(8,128)S(1)} %get-tuple-element.40), channel_id=1, source_target_pairs={{0,16},{8,24},{16,0},{24,8},{1,17},{9,25},{17,1},{25,9},{2,18},{10... | collective-permute-start | bytes 1327112 | tf_op jit(solution)/shard_map/ppermute | solution.py:311
  7.5 17.2 %collective-permute-start = (f32[1152,128]{1,0:T(8,128)S(1)}, f32[1152,128]{1,0:T(8,128)S(1)}, u32[]{:S(2)}, u32[]{:S(2)}) collective-permute-start(f32[1152,128]{1,0:T(8,128)S(1)} %get-tuple-element.39), channel_id=1, source_target_pairs={{0,7},{1,2},{2,1},{3,4},{4,3},{5,6},{6,5},{7,0},{8,15},{9,10},{10,... | collective-permute-start | bytes 1769480 | tf_op jit(solution)/shard_map/ppermute | solution.py:311
  10.5 20.4 %collective-permute-start.7 = (f32[576,128]{1,0:T(8,128)S(1)}, f32[576,128]{1,0:T(8,128)S(1)}, u32[]{:S(2)}, u32[]{:S(2)}) collective-permute-start(f32[576,128]{1,0:T(8,128)S(1)} %get-tuple-element.61), channel_id=1, source_target_pairs={{0,7},{1,2},{2,1},{3,4},{4,3},{5,6},{6,5},{7,0},{8,15},{9,10},{10,... | collective-permute-start | bytes 884744 | tf_op jit(solution)/shard_map/ppermute | solution.py:311
  11.0 25.3 %collective-permute-start.5 = (f32[864,128]{1,0:T(8,128)S(1)}, f32[864,128]{1,0:T(8,128)S(1)}, u32[]{:S(2)}, u32[]{:S(2)}) collective-permute-start(f32[864,128]{1,0:T(8,128)S(1)} %get-tuple-element.56), channel_id=1, source_target_pairs={{0,8},{8,0},{16,24},{24,16},{1,9},{9,1},{17,25},{25,17},{2,10},{10... | collective-permute-start | bytes 1327112 | tf_op jit(solution)/shard_map/ppermute | solution.py:311
  17.0 14.0 %collective-permute-start.8 = (f32[864,128]{1,0:T(8,128)S(1)}, f32[864,128]{1,0:T(8,128)S(1)}, u32[]{:S(2)}, u32[]{:S(2)}) collective-permute-start(f32[864,128]{1,0:T(8,128)S(1)} %collective-permute-done.2.mid), channel_id=1, source_target_pairs={{0,16},{8,24},{16,0},{24,8},{1,17},{9,25},{17,1},{25,9},{2,18},{10... | collective-permute-start | bytes 1327112 | tf_op jit(solution)/shard_map/ppermute | solution.py:311
  18.9 5.7 %copy-start = (s32[9,9]{1,0:T(8,128)S(1)}, s32[9,9]{1,0:T(8,128)}, u32[]{:S(2)}) copy-start(s32[9,9]{1,0:T(8,128)} %kept.7) | copy-start | bytes 976
  20.5 19.4 %collective-permute-start.6 = (f32[864,128]{1,0:T(8,128)S(1)}, f32[864,128]{1,0:T(8,128)S(1)}, u32[]{:S(2)}, u32[]{:S(2)}) collective-permute-start(f32[864,128]{1,0:T(8,128)S(1)} %collective-permute-done.1), channel_id=1, source_target_pairs={{0,8},{8,0},{16,24},{24,16},{1,9},{9,1},{17,25},{25,17},{2,10},{10... | collective-permute-start | bytes 1327112 | tf_op jit(solution)/shard_map/ppermute | solution.py:311
  26.0 12.2 %collective-permute-start.4 = (f32[576,128]{1,0:T(8,128)S(1)}, f32[576,128]{1,0:T(8,128)S(1)}, u32[]{:S(2)}, u32[]{:S(2)}) collective-permute-start(f32[576,128]{1,0:T(8,128)S(1)} %get-tuple-element.54), channel_id=1, source_target_pairs={{0,7},{1,2},{2,1},{3,4},{4,3},{5,6},{6,5},{7,0},{8,15},{9,10},{10,... | collective-permute-start | bytes 884744 | tf_op jit(solution)/shard_map/ppermute | solution.py:311
  32.8 11.3 %collective-permute-start.12 = (f32[576,128]{1,0:T(8,128)S(1)}, f32[576,128]{1,0:T(8,128)S(1)}, u32[]{:S(2)}, u32[]{:S(2)}) collective-permute-start(f32[576,128]{1,0:T(8,128)S(1)} %get-tuple-element.67), channel_id=1, source_target_pairs={{0,7},{1,2},{2,1},{3,4},{4,3},{5,6},{6,5},{7,0},{8,15},{9,10},{10,... | collective-permute-start | bytes 884744 | tf_op jit(solution)/shard_map/ppermute | solution.py:311
  36.3 7.8 %collective-permute-start.11 = (f32[1152,128]{1,0:T(8,128)S(1)}, f32[1152,128]{1,0:T(8,128)S(1)}, u32[]{:S(2)}, u32[]{:S(2)}) collective-permute-start(f32[1152,128]{1,0:T(8,128)S(1)} %get-tuple-element.66), channel_id=1, source_target_pairs={{0,1},{1,0},{2,3},{3,2},{4,5},{5,4},{6,7},{7,6},{8,9},{9,8},{10,11... | collective-permute-start | bytes 1769480 | tf_op jit(solution)/shard_map/ppermute | solution.py:311
  41.8 9.0 %collective-permute-start.9 = (f32[576,128]{1,0:T(8,128)S(1)}, f32[576,128]{1,0:T(8,128)S(1)}, u32[]{:S(2)}, u32[]{:S(2)}) collective-permute-start(f32[576,128]{1,0:T(8,128)S(1)} %get-tuple-element.64), channel_id=1, source_target_pairs={{0,7},{1,2},{2,1},{3,4},{4,3},{5,6},{6,5},{7,0},{8,15},{9,10},{10,... | collective-permute-start | bytes 884744 | tf_op jit(solution)/shard_map/ppermute | solution.py:311
  44.1 3.3 %collective-permute-start.10 = (f32[576,128]{1,0:T(8,128)S(1)}, f32[576,128]{1,0:T(8,128)S(1)}, u32[]{:S(2)}, u32[]{:S(2)}) collective-permute-start(f32[576,128]{1,0:T(8,128)S(1)} %get-tuple-element.65), channel_id=1, source_target_pairs={{0,1},{1,0},{2,3},{3,2},{4,5},{5,4},{6,7},{7,6},{8,9},{9,8},{10,11... | collective-permute-start | bytes 884744 | tf_op jit(solution)/shard_map/ppermute | solution.py:311
  44.1 3.3 %copy-start.2 = (s32[9,9]{1,0:T(8,128)S(1)}, s32[9,9]{1,0:T(8,128)}, u32[]{:S(2)}) copy-start(s32[9,9]{1,0:T(8,128)} %kept.9) | copy-start | bytes 976

commit v7 on v6

--- a/solution.py
+++ b/solution.py
@@ -11,6 +11,7 @@
 BF16 = jnp.bfloat16
 NEAR, MID, FAR = range(3)
 OWN, CHIP, LINK = range(3)
+COPIES = 6
 
 
 def place(info, who, group):
@@ -105,16 +106,30 @@
     return jnp.concatenate([value[i * 64 : (i + 1) * 64] * flags(i) for i in range(value.shape[0] // 64)], 0)
 
 
-def pack_body(info, tile, chip, link_a, link_b, mid, near, far):
+def pack_link_body(info, source, tile, link_a, sems):
     side = tile.shape[0]
     group = side // 3
+    step = side // COPIES
+    copies = [
+        pltpu.make_async_copy(source.at[pl.ds(i * step, step), :], tile.at[pl.ds(i * step, step), :], sems.at[i])
+        for i in range(COPIES)
+    ]
+    for copy in copies:
+        copy.start()
+    for copy in copies:
+        copy.wait()
     groups = tile_groups(info, tile, shared_rows(info, LINK, group))
     store_fold(link_a, 0, groups[MID])
     store_fold(link_a, 3 * group, groups[NEAR])
-    store_fold(link_b, 0, groups[FAR])
+
+
+def pack_body(info, tile, chip, link_b, mid, near, far):
+    side = tile.shape[0]
+    group = side // 3
     groups = tile_groups(info, tile, pl.ds(0, side))
     for out, part in ((mid, MID), (near, NEAR), (far, FAR)):
         store_fold(out, 0, groups[part])
+    store_fold(link_b, 0, tile_groups(info, tile, shared_rows(info, LINK, group))[FAR])
     groups = tile_groups(info, tile, shared_rows(info, CHIP, group))
     for part in range(3):
         store_fold(chip, part * 3 * group, groups[part])
@@ -154,17 +169,18 @@
     store_fold(link, 0, out[shared_rows(info, LINK, group), :])
 
 
-def far_start_body(info, own_left, own_right, chip_left, link_left, out):
-    group = out.shape[0] // 3
-    for who, lefts in ((OWN, own_left), (CHIP, chip_left), (LINK, link_left)):
-        value = passes([left(lefts, MID)], [right(own_right, info, who, FAR)])
-        if who == OWN:
-            out[...] = value
-        else:
-            out[shared_rows(info, who, group), :] += value
-
-
-def far_body(info, kept, link_b, mid, begun, near, own_left, chip_left, out, chip, link, link_left, rights):
+def middle_products_body(info, own_left, own_right, chip_left, link_left, far, mid):
+    group = far.shape[0] // 3
+    for out, part in ((far, FAR), (mid, MID)):
+        for who, lefts in ((OWN, own_left), (CHIP, chip_left), (LINK, link_left)):
+            value = passes([left(lefts, MID)], [right(own_right, info, who, part)])
+            if who == OWN:
+                out[...] = value
+            else:
+                out[shared_rows(info, who, group), :] += value
+
+
+def far_body(info, kept, link_b, mid, begun, own_left, chip_left, out, link, link_left, rights):
     group = out.shape[0] // 3
     store_left(link_left, (), unfold(link_b[...]))
     store_right(rights, (), unfold(mid[...]))
@@ -173,21 +189,16 @@
         out[shared_rows(info, who, group), :] += passes([factor], [right(rights, info, who)])
     out[...] = masked(out[...], kept, mask_at(info, FAR))
     store_fold(link, 0, out[shared_rows(info, LINK, group), :])
-    store_fold(chip, 0, near[shared_rows(info, CHIP, group), :])
-    store_fold(chip, 3 * group, out[shared_rows(info, CHIP, group), :])
-
-
-def mid_start_body(info, near, own_left, own_right, chip_left, link_left, out, rights):
+
+
+def mid_start_body(info, near, begun, own_left, chip_left, link_left, s_near, s_far, out, sides, rights):
     group = out.shape[0] // 3
+    store_fold(sides, 0, s_near[shared_rows(info, CHIP, group), :])
+    store_fold(sides, 3 * group, s_far[shared_rows(info, CHIP, group), :])
     store_right(rights, (), unfold(near[...]))
-    for who, lefts in ((OWN, own_left), (CHIP, chip_left), (LINK, link_left)):
-        value = passes(
-            [left(lefts, NEAR), left(lefts, MID)], [right(rights, info, who), right(own_right, info, who, MID)]
-        )
-        if who == OWN:
-            out[...] = value
-        else:
-            out[shared_rows(info, who, group), :] += value
+    out[...] = begun[...] + passes([left(own_left, NEAR)], [right(rights, info, OWN)])
+    for who, lefts in ((CHIP, chip_left), (LINK, link_left)):
+        out[shared_rows(info, who, group), :] += passes([left(lefts, NEAR)], [right(rights, info, who)])
 
 
 def mid_body(info, kept, far, own_left, chip_left, link_left, begun, out, chip, link, rights):
@@ -201,92 +212,90 @@
     store_fold(chip, 0, out[shared_rows(info, CHIP, group), :])
 
 
-def cube_near_body(info, link, near, right_near, right_mid, out):
+def cube_near_body(info, link, near, far, right_near, right_far, right_mid, out):
     group = near.shape[0] // 3
     own, other = split(near[...]), split(unfold(link[...]))
-    out[FAR] = jnp.zeros(near.shape, F32)
+    out[FAR] = passes([split(far[...])], [right(right_far, info, OWN)])
     for part, ref in ((NEAR, right_near), (MID, right_mid)):
         out[part] = passes([own], [right(ref, info, OWN)])
         out[part, shared_rows(info, LINK, group), :] += passes([other], [right(ref, info, LINK)])
 
 
-def cube_own_body(info, chip, link, total, near, mid, far, own_right, right_near, right_far, mid_near, mid_far, out):
+def cube_own_body(info, link, total, near, mid, far, own_right, right_far, mid_far, out):
     group = near.shape[0] // 3
     own_mid, own_far = split(mid[...]), split(far[...])
-    chip_near, chip_far = (split(unfold(chip[at * 3 * group : (at + 1) * 3 * group, :])) for at in range(2))
     link_far = split(unfold(link[...]))
-
-    def add(part, square, own, from_chip, from_link):
-        out[part] = 3.0 * square[...] - 2.0 * (total[part] + passes(*own))
-        out[part, shared_rows(info, CHIP, group), :] -= 2.0 * passes(*from_chip)
-        if from_link is not None:
-            out[part, shared_rows(info, LINK, group), :] -= 2.0 * passes([link_far], [from_link])
-
-    add(
-        NEAR,
-        near,
-        ([own_mid], [right(own_right, info, OWN, NEAR)]),
-        ([chip_near], [right(right_near, info, CHIP)]),
-        None,
-    )
-    add(
-        MID,
-        mid,
-        ([own_mid, own_far], [right(own_right, info, OWN, MID), right(mid_far, info, OWN)]),
-        ([chip_near, chip_far], [right(mid_near, info, CHIP), right(mid_far, info, CHIP)]),
-        right(mid_far, info, LINK),
-    )
-    add(
-        FAR,
-        far,
-        ([own_mid, own_far], [right(own_right, info, OWN, FAR), right(right_far, info, OWN)]),
-        ([chip_far], [right(right_far, info, CHIP)]),
-        right(right_far, info, LINK),
-    )
-
-
-def cube_chip_body(info, kept, chip, own_right, base, out):
+    rights = [right(own_right, info, OWN, part) for part in range(3)]
+    out[NEAR] = 3.0 * near[...] - 2.0 * (total[NEAR] + passes([own_mid], rights[NEAR:MID]))
+    out[MID] = 3.0 * mid[...] - 2.0 * (total[MID] + passes([own_mid, own_far], [rights[MID], right(mid_far, info, OWN)]))
+    out[FAR] = 3.0 * far[...] - 2.0 * (total[FAR] + passes([own_mid], rights[FAR:]))
+    for part, ref in ((MID, mid_far), (FAR, right_far)):
+        out[part, shared_rows(info, LINK, group), :] -= 2.0 * passes([link_far], [right(ref, info, LINK)])
+
+
+def cube_chip_body(info, kept, sides, chip, own_right, right_near, right_far, mid_near, mid_far, base, out):
     group = base.shape[1] // 3
-    chip_mid = split(unfold(chip[...]))
-    for part in range(3):
+    at = shared_rows(info, CHIP, group)
+    chips = [split(unfold(value)) for value in (sides[: 3 * group, :], chip[...], sides[3 * group :, :])]
+    own = [right(own_right, info, CHIP, part) for part in range(3)]
+    products = (
+        (chips[:2], [right(right_near, info, CHIP), own[NEAR]]),
+        (chips, [right(mid_near, info, CHIP), own[MID], right(mid_far, info, CHIP)]),
+        (chips[1:], [own[FAR], right(right_far, info, CHIP)]),
+    )
+    for part, factors in enumerate(products):
         out[part] = base[part]
-        out[part, shared_rows(info, CHIP, group), :] -= 2.0 * passes(
-            [chip_mid], [right(own_right, info, CHIP, part)]
-        )
+        out[part, at, :] -= 2.0 * passes(*factors)
         out[part] = masked(out[part], kept, mask_at(info, part))
 
 
-def finish_body(info, kept, link, own_right, base, out):
-    group = out.shape[0] // 3
+def finish_body(info, kept, link, own_right, base, out, tile, sems):
+    group = tile.shape[0] // 3
+    odd = info[0] == 1
+    start = place(info, LINK, group)[0]
+    first_row = place(info, LINK, 3)[0]
+
+    def send(k, row, near, mid, far):
+        rows = pl.ds(pl.multiple_of(row, 64), group)
+        tile[rows, :group] = jnp.where(odd, near, far)[:, :group]
+        tile[rows, group : 2 * group] = mid[:, :group]
+        tile[rows, 2 * group :] = jnp.where(odd, far, near)[:, :group]
+        copy = pltpu.make_async_copy(tile.at[rows, :], out.at[rows, :], sems.at[k])
+        copy.start()
+        return copy
+
+    rest = pl.multiple_of(2 * place(info, CHIP, group)[0], 64)
+    copies = [send(0, rest, *(base[part, pl.ds(rest, group), :] for part in range(3)))]
     link_mid = split(unfold(link[...]))
-    at = shared_rows(info, LINK, group)
-    first_row = place(info, LINK, 3)[0]
     values = []
     for part in range(3):
         value = -2.0 * passes([link_mid], [right(own_right, info, LINK, part)])
-        values.append(base[part, at, :] + masked(value, kept, mask_at(info, part), first_row))
-    odd = info[0] == 1
-
-    def store(rows, near, mid, far):
-        out[rows, :group] = jnp.where(odd, near, far)[:, :group]
-        out[rows, group : 2 * group] = mid[:, :group]
-        out[rows, 2 * group :] = jnp.where(odd, far, near)[:, :group]
-
-    store(at, *values)
-    rest = pl.ds(pl.multiple_of(2 * place(info, CHIP, group)[0], 64), group)
-    store(rest, *(base[part, rest, :] for part in range(3)))
+        values.append(masked(value, kept, mask_at(info, part), first_row))
+    for k in range(2):
+        row = pl.multiple_of(start + k * group, 64)
+        copies.append(
+            send(
+                k + 1,
+                row,
+                *(base[part, pl.ds(row, group), :] + values[part][k * group : (k + 1) * group] for part in range(3)),
+            )
+        )
+    for copy in copies:
+        copy.wait()
 
 
 VMEM = pl.BlockSpec(memory_space=pltpu.VMEM)
 SMEM = pl.BlockSpec(memory_space=pltpu.SMEM)
-
-
-def call(body, name, scalars, arrays, outs, work=4):
+ANY = pl.BlockSpec(memory_space=pl.ANY)
+
+
+def call(body, name, scalars, arrays, outs, work=4, source=VMEM, target=VMEM, scratch=()):
     return pl.pallas_call(
         body,
         out_shape=[jax.ShapeDtypeStruct(shape, kind) for shape, kind in outs],
-        in_specs=[SMEM] * len(scalars) + [VMEM] * len(arrays),
-        out_specs=[VMEM] * len(outs),
+        in_specs=[SMEM] * len(scalars) + [source] * len(arrays),
+        out_specs=[target] * len(outs),
+        scratch_shapes=scratch,
         compiler_params=pltpu.CompilerParams(vmem_limit_bytes=24 << 20),
         cost_estimate=pl.CostEstimate(flops=work * 1000000000, transcendentals=0, bytes_accessed=work * 5000000),
         name=name,
@@ -312,8 +321,17 @@
             value, axis, [(i, (i + (even_step if i % 2 == 0 else -even_step)) % size) for i in range(size)]
         )
 
-    chip, link_a, link_b, mid, near, far = call(
-        pack_body, "pack", (info,), (p_tiles,), [three_slabs, two_slabs, slab] + [strip] * 3
+    tile, link_a = call(
+        pack_link_body,
+        "pack_link",
+        (info,),
+        (p_tiles,),
+        [((side, side), F32), two_slabs],
+        source=ANY,
+        scratch=[pltpu.SemaphoreType.DMA((COPIES,))],
+    )
+    chip, link_b, mid, near, far = call(
+        pack_body, "pack", (info,), (tile,), [three_slabs, slab] + [strip] * 3
     )
     link_a = exchange(link_a, "col", -1)
     partner_mid = exchange(mid, "row", 1)
@@ -322,11 +340,12 @@
     chip, link_b, near = lax.optimization_barrier((chip, link_b, near))
     link_b = exchange(link_b, "col", -1)
     partner_near = exchange(near, "row", 1)
+
     own_left, own_right, chip_left = call(
         prepare_body,
         "prepare",
         (info,),
-        (p_tiles, chip),
+        (tile, chip),
         [((2, 3, side, WIDE), BF16), ((2, 3, 3 * WIDE, WIDE), BF16), ((2, 3, 2 * group, WIDE), BF16)],
     )
     partner_mid, own_left = lax.optimization_barrier((partner_mid, own_left))
@@ -334,8 +353,6 @@
     begun, right_near = call(
         near_start_body, "near_start", (info,), (partner_mid, own_left, own_right, chip_left), [wide, rights]
     )
-    passed_far, begun = lax.optimization_barrier((passed_far, begun))
-    other_far = exchange(passed_far, "row", 1)
     s_near, near_link, link_left = call(
         near_body,
         "square_near",
@@ -344,26 +361,34 @@
         [wide, slab, ((2, 2, 2 * group, WIDE), BF16)],
     )
     near_link = exchange(near_link, "col", -1)
-    (begun,) = call(
-        far_start_body, "far_start", (info,), (own_left, own_right, chip_left, link_left), [wide]
-    )
-    s_far, sides_chip, far_link, link_left_far, right_far = call(
+    passed_far, link_left = lax.optimization_barrier((passed_far, link_left))
+    other_far = exchange(passed_far, "row", 1)
+    begun, begun_mid = call(
+        middle_products_body, "middle_products", (info,), (own_left, own_right, chip_left, link_left), [wide] * 2
+    )
+    s_far, far_link, link_left_far, right_far = call(
         far_body,
         "square_far",
         (info, square_kept),
-        (link_b, other_mid, begun, s_near, own_left, chip_left),
-        [wide, two_slabs, slab, ((2, 2 * group, WIDE), BF16), rights],
+        (link_b, other_mid, begun, own_left, chip_left),
+        [wide, slab, ((2, 2 * group, WIDE), BF16), rights],
     )
     far_link = exchange(far_link, "col", -1)
-    sides_chip = exchange(sides_chip, "col", 1)
-    begun, mid_near = call(
+    partner_near, link_left_far = lax.optimization_barrier((partner_near, link_left_far))
+    begun, sides_chip, mid_near = call(
         mid_start_body,
         "mid_start",
         (info,),
-        (partner_near, own_left, own_right, chip_left, link_left),
-        [wide, rights],
-    )
-    (total,) = call(cube_near_body, "cube_near", (info,), (near_link, s_near, right_near, mid_near), [three_wide])
+        (partner_near, begun_mid, own_left, chip_left, link_left, s_near, s_far),
+        [wide, two_slabs, rights],
+    )
+    (total,) = call(
+        cube_near_body,
+        "cube_near",
+        (info,),
+        (near_link, s_near, s_far, right_near, right_far, mid_near),
+        [three_wide],
+    )
     total, other_far = lax.optimization_barrier((total, other_far))
     s_mid, mid_chip, mid_link, mid_far = call(
         mid_body,
@@ -374,23 +399,30 @@
         work=0,
     )
     mid_link = exchange(mid_link, "col", -1)
+    sides_chip = exchange(sides_chip, "col", 1)
     mid_chip = exchange(mid_chip, "col", 1)
     (base,) = call(
         cube_own_body,
         "cube_own",
         (info,),
-        (sides_chip, far_link, total, s_near, s_mid, s_far, own_right, right_near, right_far, mid_near, mid_far),
+        (far_link, total, s_near, s_mid, s_far, own_right, right_far, mid_far),
         [three_wide],
     )
     (base,) = call(
         cube_chip_body,
         "cube_chip",
         (info, result_kept),
-        (mid_chip, own_right, base),
+        (sides_chip, mid_chip, own_right, right_near, right_far, mid_near, mid_far, base),
         [three_wide],
     )
     (purified,) = call(
-        finish_body, "finish", (info, result_kept), (mid_link, own_right, base), [((side, side), F32)]
+        finish_body,
+        "finish",
+        (info, result_kept),
+        (mid_link, own_right, base),
+        [((side, side), F32)],
+        target=ANY,
+        scratch=[pltpu.VMEM((side, side), F32), pltpu.SemaphoreType.DMA((3,))],
     )
     return purified
 

time: 53.9 us -> 54.8 us (1.017)
  starting transfers between devices: 21.6 us -> 19.2 us
  Pallas kernels: 21.6 us -> 23.5 us
  waiting for transfers between devices: 8.57 us -> 10.4 us
    ppermute x13, starting transfers between devices: 21.6 us -> 19.2 us  [exchange(): lax.ppermute(value, axis, [(i, (i + (even_step if i % 2 == 0 else -even_s...]
    pallas_call x12 -> x13, Pallas kernels: 21.6 us -> 23.5 us  [call(): pl.pallas_call(body, out_shape=[jax.ShapeDtypeStruct(shape, kind) for sha...]
    ppermute x13, waiting for transfers between devices: 8.57 us -> 10.4 us  [exchange(): lax.ppermute(value, axis, [(i, (i + (even_step if i % 2 == 0 else -even_s...]
  transfers between devices with their start and end apart: 13 -> 13, of which waited for: 4 -> 4; matrix products, arithmetic and copies ran while one was open for 0% -> 0% of each run, Pallas kernels for 33% -> 31%
where the time goes in v7:
time: 54.8 us; the launch traced here: 54.7 us
  Pallas kernels  23.5 us (43%)
  starting transfers between devices  19.2 us (35%)
  waiting for transfers between devices  10.4 us (19%)
  local copies, waits for them, and re-layouts  1.38 us (3%)
    pallas_call x13, Pallas kernels, call(): pl.pallas_call(body, out_shape=[jax.ShapeDtypeStruct(shape, kind) for sha...  23.5 us
    ppermute x13, starting transfers between devices, exchange(): lax.ppermute(value, axis, [(i, (i + (even_step if i % 2 == 0 else -even_s...  19.2 us
    ppermute x13, waiting for transfers between devices, exchange(): lax.ppermute(value, axis, [(i, (i + (even_step if i % 2 == 0 else -even_s...  10.4 us
    unnamed x6, local copies, waits for them, and re-layouts  1.38 us
  transfers between devices with their start and end apart: 13, of which 4 were waited for; matrix products, arithmetic and copies ran while one was open for 0% of the time, Pallas kernels for 31%

profile of v7, /device:TPU:0, one launch (start us, length us, event | category | flops | bytes accessed | tf_op | source)
XLA Modules:
  0.0 54.7 jit_solution(16712967488743014652)
XLA Ops:
  0.0 0.1 pad_add_fusion.info
  0.1 0.0 copy-start.1
  0.1 1.4 %copy-done.1 = f32[576,576]{1,0:T(8,128)S(1)} copy-done((f32[576,576]{1,0:T(8,128)S(1)}, f32[576,576]{1,0:T(8,128)}, u32[]{:S(2)}) %copy-start.1) | copy-done | bytes 1327128
  1.4 2.8 %pack_link.1 = (f32[576,576]{1,0:T(8,128)S(1)}, f32[1152,128]{1,0:T(8,128)S(1)}) custom-call(s32[2]{0:T(128)S(1)} %pad_add_fusion.info, f32[576,576]{1,0:T(8,128)S(1)} %copy-done.1), custom_call_target="tpu_custom_call" | custom-call | flops 4000000000 | bytes 20000000 | tf_op jit(solution)/shard_map/pack_link/pallas_call | solution.py:293
  4.2 1.2 %pack.1 = (f32[1728,128]{1,0:T(8,128)S(1)}, f32[576,128]{1,0:T(8,128)S(1)}, f32[864,128]{1,0:T(8,128)S(1)}, f32[864,128]{1,0:T(8,128)S(1)}, f32[864,128]{1,0:T(8,128)S(1)}) custom-call(s32[2]{0:T(128)S(1)} %pad_add_fusion.info, f32[576,576]{1,0:T(8,128)S(1)} %get-tuple-element.45.tile), custom_call_target="tpu_custom_call" | custom-call | flops 4000000000 | bytes 20000000 | tf_op jit(solution)/shard_map/pack/pallas_call | solution.py:293
  5.4 0.5 collective-permute-start.2
  6.0 2.6 %collective-permute-start.1 = (f32[864,128]{1,0:T(8,128)S(1)}, f32[864,128]{1,0:T(8,128)S(1)}, u32[]{:S(2)}, u32[]{:S(2)}) collective-permute-start(f32[864,128]{1,0:T(8,128)S(1)} %get-tuple-element.46), channel_id=1, source_target_pairs={{0,8},{8,0},{16,24},{24,16},{1,9},{9,1},{17,25},{25,17},{2,10},{10... | collective-permute-start | bytes 1327112 | tf_op jit(solution)/shard_map/ppermute | solution.py:320
  8.5 3.4 %collective-permute-start = (f32[1152,128]{1,0:T(8,128)S(1)}, f32[1152,128]{1,0:T(8,128)S(1)}, u32[]{:S(2)}, u32[]{:S(2)}) collective-permute-start(f32[1152,128]{1,0:T(8,128)S(1)} %get-tuple-element.44), channel_id=1, source_target_pairs={{0,7},{1,2},{2,1},{3,4},{4,3},{5,6},{6,5},{7,0},{8,15},{9,10},{10,... | collective-permute-start | bytes 1769480 | tf_op jit(solution)/shard_map/ppermute | solution.py:320
  11.9 1.5 %collective-permute-start.6 = (f32[864,128]{1,0:T(8,128)S(1)}, f32[864,128]{1,0:T(8,128)S(1)}, u32[]{:S(2)}, u32[]{:S(2)}) collective-permute-start(f32[864,128]{1,0:T(8,128)S(1)} %get-tuple-element.61), channel_id=1, source_target_pairs={{0,16},{8,24},{16,0},{24,8},{1,17},{9,25},{17,1},{25,9},{2,18},{10... | collective-permute-start | bytes 1327112 | tf_op jit(solution)/shard_map/ppermute | solution.py:320
  13.4 0.0 collective-permute-done.2.chip
  13.4 0.0 collective-permute-start.4
  13.4 0.8 %collective-permute-start.7 = (f32[864,128]{1,0:T(8,128)S(1)}, f32[864,128]{1,0:T(8,128)S(1)}, u32[]{:S(2)}, u32[]{:S(2)}) collective-permute-start(f32[864,128]{1,0:T(8,128)S(1)} %get-tuple-element.67), channel_id=1, source_target_pairs={{0,8},{8,0},{16,24},{24,16},{1,9},{9,1},{17,25},{25,17},{2,10},{10... | collective-permute-start | bytes 1327112 | tf_op jit(solution)/shard_map/ppermute | solution.py:320
  14.2 1.0 %prepare.1 = (bf16[2,3,576,256]{3,2,1,0:T(8,128)(2,1)S(1)}, bf16[2,3,768,256]{3,2,1,0:T(8,128)(2,1)S(1)}, bf16[2,3,384,256]{3,2,1,0:T(8,128)(2,1)S(1)}) custom-call(s32[2]{0:T(128)S(1)} %pad_add_fusion.info, f32[576,576]{1,0:T(8,128)S(1)} %get-tuple-element.45.tile, f32[1728,128]{1,0:T(8,128)S(1)} %collective-permute-done.2.chip), custom_call_target="tpu_custom_call" | custom-call | flops 4000000000 | bytes 20000000 | tf_op jit(solution)/shard_map/prepare/pallas_call | solution.py:293
  15.2 4.3 %collective-permute-done.1.mid = f32[864,128]{1,0:T(8,128)S(1)} collective-permute-done((f32[864,128]{1,0:T(8,128)S(1)}, f32[864,128]{1,0:T(8,128)S(1)}, u32[]{:S(2)}, u32[]{:S(2)}) %collective-permute-start.1) | collective-permute-done | bytes 442400 | tf_op jit(solution)/shard_map/ppermute | solution.py:320
  19.5 2.0 %collective-permute-start.5 = (f32[864,128]{1,0:T(8,128)S(1)}, f32[864,128]{1,0:T(8,128)S(1)}, u32[]{:S(2)}, u32[]{:S(2)}) collective-permute-start(f32[864,128]{1,0:T(8,128)S(1)} %collective-permute-done.1.mid), channel_id=1, source_target_pairs={{0,16},{8,24},{16,0},{24,8},{1,17},{9,25},{17,1},{25,9},{2,18},{10... | collective-permute-start | bytes 1327112 | tf_op jit(solution)/shard_map/ppermute | solution.py:320
  21.5 0.0 copy-start
  21.5 1.6 %near_start.1 = (f32[576,256]{1,0:T(8,128)S(1)}, bf16[2,768,256]{2,1,0:T(8,128)(2,1)S(1)}) custom-call(s32[2]{0:T(128)S(1)} %pad_add_fusion.info, f32[864,128]{1,0:T(8,128)S(1)} %collective-permute-done.1.mid, bf16[2,3,576,256]{3,2,1,0:T(8,128)(2,1)S(1)} %get-tuple-element.53.own_left, bf16[2,3,768,256]{3,2,1,0:T(8,128)(2,1)S(1)} %get-tuple-element.54.own_right, ...), custom_call_target="tpu_custom_call" | custom-call | flops 4000000000 | bytes 20000000 | tf_op jit(solution)/shard_map/near_start/pallas_call | solution.py:293
  23.1 2.6 %collective-permute-done.link_a = f32[1152,128]{1,0:T(8,128)S(1)} collective-permute-done((f32[1152,128]{1,0:T(8,128)S(1)}, f32[1152,128]{1,0:T(8,128)S(1)}, u32[]{:S(2)}, u32[]{:S(2)}) %collective-permute-start) | collective-permute-done | bytes 589856 | tf_op jit(solution)/shard_map/ppermute | solution.py:320
  25.7 0.0 copy-done
  25.7 1.4 %square_near.1 = (f32[576,256]{1,0:T(8,128)S(1)}, f32[576,128]{1,0:T(8,128)S(1)}, bf16[2,2,384,256]{3,2,1,0:T(8,128)(2,1)S(1)}) custom-call(s32[2]{0:T(128)S(1)} %pad_add_fusion.info, s32[9,9]{1,0:T(8,128)S(1)} %copy-done, f32[1152,128]{1,0:T(8,128)S(1)} %collective-permute-done.link_a, f32[576,256]{1,0:T(8,128)S(1)} %get-tuple-element.56.begun, ...), custom_call_target="tpu_custom_call" | custom-call | flops 4000000000 | bytes 20000000 | tf_op jit(solution)/shard_map/square_near/pallas_call | solution.py:293
  27.1 0.0 collective-permute-done.6
  27.1 3.8 %collective-permute-start.3 = (f32[576,128]{1,0:T(8,128)S(1)}, f32[576,128]{1,0:T(8,128)S(1)}, u32[]{:S(2)}, u32[]{:S(2)}) collective-permute-start(f32[576,128]{1,0:T(8,128)S(1)} %get-tuple-element.58), channel_id=1, source_target_pairs={{0,7},{1,2},{2,1},{3,4},{4,3},{5,6},{6,5},{7,0},{8,15},{9,10},{10,... | collective-permute-start | bytes 884744 | tf_op jit(solution)/shard_map/ppermute | solution.py:320
  30.9 0.5 collective-permute-start.8
  31.4 1.9 %middle_products.1 = (f32[576,256]{1,0:T(8,128)S(1)}, f32[576,256]{1,0:T(8,128)S(1)}) custom-call(s32[2]{0:T(128)S(1)} %pad_add_fusion.info, bf16[2,3,576,256]{3,2,1,0:T(8,128)(2,1)S(1)} %get-tuple-element.53.own_left, bf16[2,3,768,256]{3,2,1,0:T(8,128)(2,1)S(1)} %get-tuple-element.54.own_right, bf16[2,3,384,256]{3,2,1,0:T(8,128)(2,1)S(1)} %get-tuple-element.55.chip_left, ...), custom_call_target="tpu_custom_call" | custom-call | flops 4000000000 | bytes 20000000 | tf_op jit(solution)/shard_map/middle_products/pallas_call | solution.py:293
  33.3 0.0 collective-permute-done.4.link_b
  33.3 0.0 collective-permute-done.5.mid
  33.3 1.8 %square_far.1 = (f32[576,256]{1,0:T(8,128)S(1)}, f32[576,128]{1,0:T(8,128)S(1)}, bf16[2,384,256]{2,1,0:T(8,128)(2,1)S(1)}, bf16[2,768,256]{2,1,0:T(8,128)(2,1)S(1)}) custom-call(s32[2]{0:T(128)S(1)} %pad_add_fusion.info, s32[9,9]{1,0:T(8,128)S(1)} %copy-done, f32[576,128]{1,0:T(8,128)S(1)} %collective-permute-done.4.link_b, ...), custom_call_target="tpu_custom_call" | custom-call | flops 4000000000 | bytes 20000000 | tf_op jit(solution)/shard_map/square_far/pallas_call | solution.py:293
  35.2 0.0 collective-permute-done.7.near
  35.2 2.4 %collective-permute-start.12 = (f32[576,128]{1,0:T(8,128)S(1)}, f32[576,128]{1,0:T(8,128)S(1)}, u32[]{:S(2)}, u32[]{:S(2)}) collective-permute-start(f32[576,128]{1,0:T(8,128)S(1)} %get-tuple-element.80), channel_id=1, source_target_pairs={{0,7},{1,2},{2,1},{3,4},{4,3},{5,6},{6,5},{7,0},{8,15},{9,10},{10,... | collective-permute-start | bytes 884744 | tf_op jit(solution)/shard_map/ppermute | solution.py:320
  37.6 1.4 %mid_start.1 = (f32[576,256]{1,0:T(8,128)S(1)}, f32[1152,128]{1,0:T(8,128)S(1)}, bf16[2,768,256]{2,1,0:T(8,128)(2,1)S(1)}) custom-call(s32[2]{0:T(128)S(1)} %pad_add_fusion.info, f32[864,128]{1,0:T(8,128)S(1)} %collective-permute-done.7.near, f32[576,256]{1,0:T(8,128)S(1)} %get-tuple-element.70.begun, ...), custom_call_target="tpu_custom_call" | custom-call | flops 4000000000 | bytes 20000000 | tf_op jit(solution)/shard_map/mid_start/pallas_call | solution.py:293
  39.0 0.1 collective-permute-start.10
  39.1 0.0 collective-permute-done.3.link
  39.1 1.8 %cube_near.1.total = f32[3,576,256]{2,1,0:T(8,128)S(1)} custom-call(s32[2]{0:T(128)S(1)} %pad_add_fusion.info, f32[576,128]{1,0:T(8,128)S(1)} %collective-permute-done.3.link, f32[576,256]{1,0:T(8,128)S(1)} %get-tuple-element.59.s_near.near, f32[576,256]{1,0:T(8,128)S(1)} %get-tuple-element.65.s_far.far, ...), custom_call_target="tpu_custom_call" | custom-call | flops 4000000000 | bytes 20000000 | tf_op jit(solution)/shard_map/cube_near/pallas_call | solution.py:293
  40.9 0.0 collective-permute-done.8.far
  40.9 1.9 %square_mid.1 = (f32[576,256]{1,0:T(8,128)S(1)}, f32[576,128]{1,0:T(8,128)S(1)}, f32[576,128]{1,0:T(8,128)S(1)}, bf16[2,768,256]{2,1,0:T(8,128)(2,1)S(1)}) custom-call(s32[2]{0:T(128)S(1)} %pad_add_fusion.info, s32[9,9]{1,0:T(8,128)S(1)} %copy-done, f32[864,128]{1,0:T(8,128)S(1)} %collective-permute-done.8.far, ...), custom_call_target="tpu_custom_call" | custom-call | tf_op jit(solution)/shard_map/square_mid/pallas_call | solution.py:293
  42.8 1.6 %collective-permute-start.9 = (f32[576,128]{1,0:T(8,128)S(1)}, f32[576,128]{1,0:T(8,128)S(1)}, u32[]{:S(2)}, u32[]{:S(2)}) collective-permute-start(f32[576,128]{1,0:T(8,128)S(1)} %get-tuple-element.76), channel_id=1, source_target_pairs={{0,7},{1,2},{2,1},{3,4},{4,3},{5,6},{6,5},{7,0},{8,15},{9,10},{10,... | collective-permute-start | bytes 884744 | tf_op jit(solution)/shard_map/ppermute | solution.py:320
  44.4 0.0 collective-permute-start.11
  44.4 0.5 collective-permute-done.12.link
  44.9 0.0 copy-start.2
  44.9 2.1 %cube_own.1.base = f32[3,576,256]{2,1,0:T(8,128)S(1)} custom-call(s32[2]{0:T(128)S(1)} %pad_add_fusion.info, f32[576,128]{1,0:T(8,128)S(1)} %collective-permute-done.12.link, f32[3,576,256]{2,1,0:T(8,128)S(1)} %cube_near.1.total, f32[576,256]{1,0:T(8,128)S(1)} %get-tuple-element.59.s_near.near, f32[576,256]{1,0:T(8,128)S(1)} %get-tuple-element.82.mid, ...), custom_call_target="tpu_custom_call" | custom-call | flops 4000000000 | bytes 20000000 | tf_op jit(solution)/shard_map/cube_own/pallas_call | solution.py:293
  47.0 0.0 collective-permute-done.11.chip
  47.0 0.0 collective-permute-done.10.sides
  47.0 0.0 copy-done.2
  47.0 2.4 %cube_chip.1.base = f32[3,576,256]{2,1,0:T(8,128)S(1)} custom-call(s32[2]{0:T(128)S(1)} %pad_add_fusion.info, s32[9,9]{1,0:T(8,128)S(1)} %copy-done.2, f32[1152,128]{1,0:T(8,128)S(1)} %collective-permute-done.10.sides, f32[576,128]{1,0:T(8,128)S(1)} %collective-permute-done.11.chip, bf16[2,3,768,256]{3,2,1,0:T(8,128)(2,1)S(1)} %get-tuple-element.54.own_right, ...), custom_call_target="tpu_custom_call" | custom-call | flops 4000000000 | bytes 20000000 | tf_op jit(solution)/shard_map/cube_chip/pallas_call | solution.py:293
  49.4 2.9 %collective-permute-done.9.link = f32[576,128]{1,0:T(8,128)S(1)} collective-permute-done((f32[576,128]{1,0:T(8,128)S(1)}, f32[576,128]{1,0:T(8,128)S(1)}, u32[]{:S(2)}, u32[]{:S(2)}) %collective-permute-start.9) | collective-permute-done | bytes 294944 | tf_op jit(solution)/shard_map/ppermute | solution.py:320
  52.4 2.3 %finish.1 = f32[576,576]{1,0:T(8,128)} custom-call(s32[2]{0:T(128)S(1)} %pad_add_fusion.info, s32[9,9]{1,0:T(8,128)S(1)} %copy-done.2, f32[576,128]{1,0:T(8,128)S(1)} %collective-permute-done.9.link, bf16[2,3,768,256]{3,2,1,0:T(8,128)(2,1)S(1)} %get-tuple-element.54.own_right, f32[3,576,256]{2,1,0:T(8,128)S(1)} %cube_chip.1.base), custom_call_target="tpu_custom_call" | custom-call | flops 4000000000 | bytes 20000000 | tf_op jit(solution)/shard_map/finish/pallas_call | solution.py:293
Async XLA Ops:
  0.1 1.4 %copy-start.1 = (f32[576,576]{1,0:T(8,128)S(1)}, f32[576,576]{1,0:T(8,128)}, u32[]{:S(2)}) copy-start(f32[576,576]{1,0:T(8,128)} %source.1) | copy-start | bytes 3981316
  5.4 8.0 %collective-permute-start.2 = (f32[1728,128]{1,0:T(8,128)S(1)}, f32[1728,128]{1,0:T(8,128)S(1)}, u32[]{:S(2)}, u32[]{:S(2)}) collective-permute-start(f32[1728,128]{1,0:T(8,128)S(1)} %get-tuple-element.47), channel_id=1, source_target_pairs={{0,1},{1,0},{2,3},{3,2},{4,5},{5,4},{6,7},{7,6},{8,9},{9,8},{10,11... | collective-permute-start | bytes 2654216 | tf_op jit(solution)/shard_map/ppermute | solution.py:320
  6.0 13.6 %collective-permute-start.1 = (f32[864,128]{1,0:T(8,128)S(1)}, f32[864,128]{1,0:T(8,128)S(1)}, u32[]{:S(2)}, u32[]{:S(2)}) collective-permute-start(f32[864,128]{1,0:T(8,128)S(1)} %get-tuple-element.46), channel_id=1, source_target_pairs={{0,8},{8,0},{16,24},{24,16},{1,9},{9,1},{17,25},{25,17},{2,10},{10... | collective-permute-start | bytes 1327112 | tf_op jit(solution)/shard_map/ppermute | solution.py:320
  8.5 17.2 %collective-permute-start = (f32[1152,128]{1,0:T(8,128)S(1)}, f32[1152,128]{1,0:T(8,128)S(1)}, u32[]{:S(2)}, u32[]{:S(2)}) collective-permute-start(f32[1152,128]{1,0:T(8,128)S(1)} %get-tuple-element.44), channel_id=1, source_target_pairs={{0,7},{1,2},{2,1},{3,4},{4,3},{5,6},{6,5},{7,0},{8,15},{9,10},{10,... | collective-permute-start | bytes 1769480 | tf_op jit(solution)/shard_map/ppermute | solution.py:320
  11.9 15.2 %collective-permute-start.6 = (f32[864,128]{1,0:T(8,128)S(1)}, f32[864,128]{1,0:T(8,128)S(1)}, u32[]{:S(2)}, u32[]{:S(2)}) collective-permute-start(f32[864,128]{1,0:T(8,128)S(1)} %get-tuple-element.61), channel_id=1, source_target_pairs={{0,16},{8,24},{16,0},{24,8},{1,17},{9,25},{17,1},{25,9},{2,18},{10... | collective-permute-start | bytes 1327112 | tf_op jit(solution)/shard_map/ppermute | solution.py:320
  13.4 19.9 %collective-permute-start.4 = (f32[576,128]{1,0:T(8,128)S(1)}, f32[576,128]{1,0:T(8,128)S(1)}, u32[]{:S(2)}, u32[]{:S(2)}) collective-permute-start(f32[576,128]{1,0:T(8,128)S(1)} %get-tuple-element.60), channel_id=1, source_target_pairs={{0,7},{1,2},{2,1},{3,4},{4,3},{5,6},{6,5},{7,0},{8,15},{9,10},{10,... | collective-permute-start | bytes 884744 | tf_op jit(solution)/shard_map/ppermute | solution.py:320
  13.4 21.7 %collective-permute-start.7 = (f32[864,128]{1,0:T(8,128)S(1)}, f32[864,128]{1,0:T(8,128)S(1)}, u32[]{:S(2)}, u32[]{:S(2)}) collective-permute-start(f32[864,128]{1,0:T(8,128)S(1)} %get-tuple-element.67), channel_id=1, source_target_pairs={{0,8},{8,0},{16,24},{24,16},{1,9},{9,1},{17,25},{25,17},{2,10},{10... | collective-permute-start | bytes 1327112 | tf_op jit(solution)/shard_map/ppermute | solution.py:320
  19.5 13.8 %collective-permute-start.5 = (f32[864,128]{1,0:T(8,128)S(1)}, f32[864,128]{1,0:T(8,128)S(1)}, u32[]{:S(2)}, u32[]{:S(2)}) collective-permute-start(f32[864,128]{1,0:T(8,128)S(1)} %collective-permute-done.1.mid), channel_id=1, source_target_pairs={{0,16},{8,24},{16,0},{24,8},{1,17},{9,25},{17,1},{25,9},{2,18},{10... | collective-permute-start | bytes 1327112 | tf_op jit(solution)/shard_map/ppermute | solution.py:320
  21.5 4.2 %copy-start = (s32[9,9]{1,0:T(8,128)S(1)}, s32[9,9]{1,0:T(8,128)}, u32[]{:S(2)}) copy-start(s32[9,9]{1,0:T(8,128)} %kept.7) | copy-start | bytes 976
  27.1 12.0 %collective-permute-start.3 = (f32[576,128]{1,0:T(8,128)S(1)}, f32[576,128]{1,0:T(8,128)S(1)}, u32[]{:S(2)}, u32[]{:S(2)}) collective-permute-start(f32[576,128]{1,0:T(8,128)S(1)} %get-tuple-element.58), channel_id=1, source_target_pairs={{0,7},{1,2},{2,1},{3,4},{4,3},{5,6},{6,5},{7,0},{8,15},{9,10},{10,... | collective-permute-start | bytes 884744 | tf_op jit(solution)/shard_map/ppermute | solution.py:320
  30.9 10.0 %collective-permute-start.8 = (f32[864,128]{1,0:T(8,128)S(1)}, f32[864,128]{1,0:T(8,128)S(1)}, u32[]{:S(2)}, u32[]{:S(2)}) collective-permute-start(f32[864,128]{1,0:T(8,128)S(1)} %collective-permute-done.6), channel_id=1, source_target_pairs={{0,8},{8,0},{16,24},{24,16},{1,9},{9,1},{17,25},{25,17},{2,10},{10... | collective-permute-start | bytes 1327112 | tf_op jit(solution)/shard_map/ppermute | solution.py:320
  35.2 9.8 %collective-permute-start.12 = (f32[576,128]{1,0:T(8,128)S(1)}, f32[576,128]{1,0:T(8,128)S(1)}, u32[]{:S(2)}, u32[]{:S(2)}) collective-permute-start(f32[576,128]{1,0:T(8,128)S(1)} %get-tuple-element.80), channel_id=1, source_target_pairs={{0,7},{1,2},{2,1},{3,4},{4,3},{5,6},{6,5},{7,0},{8,15},{9,10},{10,... | collective-permute-start | bytes 884744 | tf_op jit(solution)/shard_map/ppermute | solution.py:320
  39.0 8.0 %collective-permute-start.10 = (f32[1152,128]{1,0:T(8,128)S(1)}, f32[1152,128]{1,0:T(8,128)S(1)}, u32[]{:S(2)}, u32[]{:S(2)}) collective-permute-start(f32[1152,128]{1,0:T(8,128)S(1)} %get-tuple-element.77), channel_id=1, source_target_pairs={{0,1},{1,0},{2,3},{3,2},{4,5},{5,4},{6,7},{7,6},{8,9},{9,8},{10,11... | collective-permute-start | bytes 1769480 | tf_op jit(solution)/shard_map/ppermute | solution.py:320
  42.8 9.6 %collective-permute-start.9 = (f32[576,128]{1,0:T(8,128)S(1)}, f32[576,128]{1,0:T(8,128)S(1)}, u32[]{:S(2)}, u32[]{:S(2)}) collective-permute-start(f32[576,128]{1,0:T(8,128)S(1)} %get-tuple-element.76), channel_id=1, source_target_pairs={{0,7},{1,2},{2,1},{3,4},{4,3},{5,6},{6,5},{7,0},{8,15},{9,10},{10,... | collective-permute-start | bytes 884744 | tf_op jit(solution)/shard_map/ppermute | solution.py:320
  44.4 2.6 %collective-permute-start.11 = (f32[576,128]{1,0:T(8,128)S(1)}, f32[576,128]{1,0:T(8,128)S(1)}, u32[]{:S(2)}, u32[]{:S(2)}) collective-permute-start(f32[576,128]{1,0:T(8,128)S(1)} %get-tuple-element.78), channel_id=1, source_target_pairs={{0,1},{1,0},{2,3},{3,2},{4,5},{5,4},{6,7},{7,6},{8,9},{9,8},{10,11... | collective-permute-start | bytes 884744 | tf_op jit(solution)/shard_map/ppermute | solution.py:320
  44.9 2.1 %copy-start.2 = (s32[9,9]{1,0:T(8,128)S(1)}, s32[9,9]{1,0:T(8,128)}, u32[]{:S(2)}) copy-start(s32[9,9]{1,0:T(8,128)} %kept.9) | copy-start | bytes 976

commit v8 on v7

--- a/solution.py
+++ b/solution.py
@@ -1,3 +1,5 @@
+import functools
+
 import jax
 import jax.numpy as jnp
 from jax import lax
@@ -11,7 +13,6 @@
 BF16 = jnp.bfloat16
 NEAR, MID, FAR = range(3)
 OWN, CHIP, LINK = range(3)
-COPIES = 6
 
 
 def place(info, who, group):
@@ -106,33 +107,24 @@
     return jnp.concatenate([value[i * 64 : (i + 1) * 64] * flags(i) for i in range(value.shape[0] // 64)], 0)
 
 
-def pack_link_body(info, source, tile, link_a, sems):
+def pack_first_body(info, tile, mid, link_a, chip):
     side = tile.shape[0]
     group = side // 3
-    step = side // COPIES
-    copies = [
-        pltpu.make_async_copy(source.at[pl.ds(i * step, step), :], tile.at[pl.ds(i * step, step), :], sems.at[i])
-        for i in range(COPIES)
-    ]
-    for copy in copies:
-        copy.start()
-    for copy in copies:
-        copy.wait()
+    store_fold(mid, 0, tile_groups(info, tile, pl.ds(0, side))[MID])
     groups = tile_groups(info, tile, shared_rows(info, LINK, group))
     store_fold(link_a, 0, groups[MID])
     store_fold(link_a, 3 * group, groups[NEAR])
-
-
-def pack_body(info, tile, chip, link_b, mid, near, far):
-    side = tile.shape[0]
-    group = side // 3
-    groups = tile_groups(info, tile, pl.ds(0, side))
-    for out, part in ((mid, MID), (near, NEAR), (far, FAR)):
-        store_fold(out, 0, groups[part])
-    store_fold(link_b, 0, tile_groups(info, tile, shared_rows(info, LINK, group))[FAR])
     groups = tile_groups(info, tile, shared_rows(info, CHIP, group))
     for part in range(3):
         store_fold(chip, part * 3 * group, groups[part])
+
+
+def pack_rest_body(info, tile, link_b, near, far):
+    side = tile.shape[0]
+    groups = tile_groups(info, tile, pl.ds(0, side))
+    store_fold(near, 0, groups[NEAR])
+    store_fold(far, 0, groups[FAR])
+    store_fold(link_b, 0, tile_groups(info, tile, shared_rows(info, LINK, side // 3))[FAR])
 
 
 def prepare_body(info, tile, chip, own_left, own_right, chip_left):
@@ -201,14 +193,16 @@
         out[shared_rows(info, who, group), :] += passes([left(lefts, NEAR)], [right(rights, info, who)])
 
 
-def mid_body(info, kept, far, own_left, chip_left, link_left, begun, out, chip, link, rights):
+def mid_body(info, kept, far, own_left, chip_left, link_left, begun, out, chip, link_first, link_second, rights):
     group = out.shape[0] // 3
     store_right(rights, (), unfold(far[...]))
     out[...] = begun[...] + passes([left(own_left, FAR)], [right(rights, info, OWN)])
     for who, factor in ((CHIP, left(chip_left, FAR)), (LINK, left(link_left))):
         out[shared_rows(info, who, group), :] += passes([factor], [right(rights, info, who)])
     out[...] = masked(out[...], kept, 3)
-    store_fold(link, 0, out[shared_rows(info, LINK, group), :])
+    start = place(info, LINK, group)[0]
+    for k, link in enumerate((link_first, link_second)):
+        store_fold(link, 0, out[pl.ds(pl.multiple_of(start + k * group, 64), group), :])
     store_fold(chip, 0, out[shared_rows(info, CHIP, group), :])
 
 
@@ -233,7 +227,18 @@
         out[part, shared_rows(info, LINK, group), :] -= 2.0 * passes([link_far], [right(ref, info, LINK)])
 
 
-def cube_chip_body(info, kept, sides, chip, own_right, right_near, right_far, mid_near, mid_far, base, out):
+def send_rows(info, tile, out, sem, row, near, mid, far):
+    odd = info[0] == 1
+    group = near.shape[0]
+    tile[:, :group] = jnp.where(odd, near, far)[:, :group]
+    tile[:, group : 2 * group] = mid[:, :group]
+    tile[:, 2 * group :] = jnp.where(odd, far, near)[:, :group]
+    copy = pltpu.make_async_copy(tile, out.at[pl.ds(row, group), :], sem)
+    copy.start()
+    return copy
+
+
+def cube_chip_body(info, kept, sides, chip, own_right, right_near, right_far, mid_near, mid_far, base, out, result, tile, sem):
     group = base.shape[1] // 3
     at = shared_rows(info, CHIP, group)
     chips = [split(unfold(value)) for value in (sides[: 3 * group, :], chip[...], sides[3 * group :, :])]
@@ -247,41 +252,21 @@
         out[part] = base[part]
         out[part, at, :] -= 2.0 * passes(*factors)
         out[part] = masked(out[part], kept, mask_at(info, part))
-
-
-def finish_body(info, kept, link, own_right, base, out, tile, sems):
-    group = tile.shape[0] // 3
-    odd = info[0] == 1
-    start = place(info, LINK, group)[0]
-    first_row = place(info, LINK, 3)[0]
-
-    def send(k, row, near, mid, far):
-        rows = pl.ds(pl.multiple_of(row, 64), group)
-        tile[rows, :group] = jnp.where(odd, near, far)[:, :group]
-        tile[rows, group : 2 * group] = mid[:, :group]
-        tile[rows, 2 * group :] = jnp.where(odd, far, near)[:, :group]
-        copy = pltpu.make_async_copy(tile.at[rows, :], out.at[rows, :], sems.at[k])
-        copy.start()
-        return copy
-
     rest = pl.multiple_of(2 * place(info, CHIP, group)[0], 64)
-    copies = [send(0, rest, *(base[part, pl.ds(rest, group), :] for part in range(3)))]
+    send_rows(info, tile, result, sem, rest, *(out[part, pl.ds(rest, group), :] for part in range(3))).wait()
+
+
+def finish_body(half, info, kept, link, own_right, base, begun, result, tile, sem):
+    del begun
+    group = tile.shape[0]
+    row = pl.multiple_of(place(info, LINK, group)[0] + half * group, 64)
+    first_row = place(info, LINK, 3)[0] + 3 * half
     link_mid = split(unfold(link[...]))
     values = []
     for part in range(3):
         value = -2.0 * passes([link_mid], [right(own_right, info, LINK, part)])
-        values.append(masked(value, kept, mask_at(info, part), first_row))
-    for k in range(2):
-        row = pl.multiple_of(start + k * group, 64)
-        copies.append(
-            send(
-                k + 1,
-                row,
-                *(base[part, pl.ds(row, group), :] + values[part][k * group : (k + 1) * group] for part in range(3)),
-            )
-        )
-    for copy in copies:
-        copy.wait()
+        values.append(base[part, pl.ds(row, group), :] + masked(value, kept, mask_at(info, part), first_row))
+    send_rows(info, tile, result, sem, row, *values).wait()
 
 
 VMEM = pl.BlockSpec(memory_space=pltpu.VMEM)
@@ -289,17 +274,19 @@
 ANY = pl.BlockSpec(memory_space=pl.ANY)
 
 
-def call(body, name, scalars, arrays, outs, work=4, source=VMEM, target=VMEM, scratch=()):
+def call(body, name, scalars, arrays, outs, work=4, result=False, begun=(), scratch=()):
+    count = len(scalars) + len(arrays)
     return pl.pallas_call(
         body,
         out_shape=[jax.ShapeDtypeStruct(shape, kind) for shape, kind in outs],
-        in_specs=[SMEM] * len(scalars) + [source] * len(arrays),
-        out_specs=[target] * len(outs),
+        in_specs=[SMEM] * len(scalars) + [VMEM] * len(arrays) + [ANY] * len(begun),
+        out_specs=[VMEM] * (len(outs) - result) + [ANY] * result,
         scratch_shapes=scratch,
+        input_output_aliases={count: len(outs) - 1} if begun else {},
         compiler_params=pltpu.CompilerParams(vmem_limit_bytes=24 << 20),
         cost_estimate=pl.CostEstimate(flops=work * 1000000000, transcendentals=0, bytes_accessed=work * 5000000),
         name=name,
-    )(*scalars, *arrays)
+    )(*scalars, *arrays, *begun)
 
 
 def on_device(p_tiles, square_kept, result_kept):
@@ -309,6 +296,7 @@
     info = jnp.stack([lax.axis_index("row") % 2, lax.axis_index("col") % 2]).astype(jnp.int32)
     strip = ((3 * side // 2, LANES), F32)
     slab = ((3 * group, LANES), F32)
+    half_slab = ((3 * group // 2, LANES), F32)
     two_slabs = ((6 * group, LANES), F32)
     three_slabs = ((9 * group, LANES), F32)
     wide = ((side, WIDE), F32)
@@ -321,31 +309,23 @@
             value, axis, [(i, (i + (even_step if i % 2 == 0 else -even_step)) % size) for i in range(size)]
         )
 
-    tile, link_a = call(
-        pack_link_body,
-        "pack_link",
-        (info,),
-        (p_tiles,),
-        [((side, side), F32), two_slabs],
-        source=ANY,
-        scratch=[pltpu.SemaphoreType.DMA((COPIES,))],
-    )
-    chip, link_b, mid, near, far = call(
-        pack_body, "pack", (info,), (tile,), [three_slabs, slab] + [strip] * 3
+    mid, link_a, chip = call(
+        pack_first_body, "pack_first", (info,), (p_tiles,), [strip, two_slabs, three_slabs]
     )
     link_a = exchange(link_a, "col", -1)
     partner_mid = exchange(mid, "row", 1)
+    chip = exchange(chip, "col", 1)
+    chip, tile = lax.optimization_barrier((chip, p_tiles))
+    link_b, near, far = call(pack_rest_body, "pack_rest", (info,), (tile,), [slab, strip, strip])
+    partner_near = exchange(near, "row", 1)
+    link_b = exchange(link_b, "col", -1)
     passed_far = exchange(far, "row", -2)
-    chip = exchange(chip, "col", 1)
-    chip, link_b, near = lax.optimization_barrier((chip, link_b, near))
-    link_b = exchange(link_b, "col", -1)
-    partner_near = exchange(near, "row", 1)
 
     own_left, own_right, chip_left = call(
         prepare_body,
         "prepare",
         (info,),
-        (tile, chip),
+        (p_tiles, chip),
         [((2, 3, side, WIDE), BF16), ((2, 3, 3 * WIDE, WIDE), BF16), ((2, 3, 2 * group, WIDE), BF16)],
     )
     partner_mid, own_left = lax.optimization_barrier((partner_mid, own_left))
@@ -390,16 +370,18 @@
         [three_wide],
     )
     total, other_far = lax.optimization_barrier((total, other_far))
-    s_mid, mid_chip, mid_link, mid_far = call(
+    s_mid, mid_chip, link_first, link_second, mid_far = call(
         mid_body,
         "square_mid",
         (info, square_kept),
         (other_far, own_left, chip_left, link_left_far, begun),
-        [wide, slab, slab, rights],
+        [wide, slab, half_slab, half_slab, rights],
         work=0,
     )
-    mid_link = exchange(mid_link, "col", -1)
+    link_first = exchange(link_first, "col", -1)
     sides_chip = exchange(sides_chip, "col", 1)
+    link_second, sides_chip = lax.optimization_barrier((link_second, sides_chip))
+    link_second = exchange(link_second, "col", -1)
     mid_chip = exchange(mid_chip, "col", 1)
     (base,) = call(
         cube_own_body,
@@ -408,22 +390,28 @@
         (far_link, total, s_near, s_mid, s_far, own_right, right_far, mid_far),
         [three_wide],
     )
-    (base,) = call(
+    result = ((side, side), F32)
+    row_scratch = [pltpu.VMEM((group, side), F32), pltpu.SemaphoreType.DMA(())]
+    base, purified = call(
         cube_chip_body,
         "cube_chip",
         (info, result_kept),
         (sides_chip, mid_chip, own_right, right_near, right_far, mid_near, mid_far, base),
-        [three_wide],
-    )
-    (purified,) = call(
-        finish_body,
-        "finish",
-        (info, result_kept),
-        (mid_link, own_right, base),
-        [((side, side), F32)],
-        target=ANY,
-        scratch=[pltpu.VMEM((side, side), F32), pltpu.SemaphoreType.DMA((3,))],
-    )
+        [three_wide, result],
+        result=True,
+        scratch=row_scratch,
+    )
+    for half, link in enumerate((link_first, link_second)):
+        (purified,) = call(
+            functools.partial(finish_body, half),
+            ("finish_first", "finish_second")[half],
+            (info, result_kept),
+            (link, own_right, base),
+            [result],
+            result=True,
+            begun=(purified,),
+            scratch=row_scratch,
+        )
     return purified
 
 

time: 54.8 us -> 54.4 us (level)
  waiting for transfers between devices: 10.4 us -> 6.21 us
  starting transfers between devices: 19.2 us -> 22.5 us
    ppermute x13 -> x14, waiting for transfers between devices: 10.4 us -> 6.21 us  [exchange(): lax.ppermute(value, axis, [(i, (i + (even_step if i % 2 == 0 else -even_s...]
    ppermute x13 -> x14, starting transfers between devices: 19.2 us -> 22.5 us  [exchange(): lax.ppermute(value, axis, [(i, (i + (even_step if i % 2 == 0 else -even_s...]
    pallas_call x13 -> x14, Pallas kernels: 23.5 us -> 24 us  [call(): pl.pallas_call(body, out_shape=[jax.ShapeDtypeStruct(shape, kind) for sha...]
  transfers between devices with their start and end apart: 13 -> 14, of which waited for: 4 -> 4; matrix products, arithmetic and copies ran while one was open for 0% -> 0% of each run, Pallas kernels for 31% -> 38%
where the time goes in v8:
time: 54.4 us; the launch traced here: 54.3 us
  Pallas kernels  24 us (44%)
  starting transfers between devices  22.5 us (41%)
  waiting for transfers between devices  6.21 us (11%)
  local copies, waits for them, and re-layouts  1.38 us (3%)
    pallas_call x14, Pallas kernels, call(): pl.pallas_call(body, out_shape=[jax.ShapeDtypeStruct(shape, kind) for sha...  24 us
    ppermute x14, starting transfers between devices, exchange(): lax.ppermute(value, axis, [(i, (i + (even_step if i % 2 == 0 else -even_s...  22.5 us
    ppermute x14, waiting for transfers between devices, exchange(): lax.ppermute(value, axis, [(i, (i + (even_step if i % 2 == 0 else -even_s...  6.21 us
    unnamed x6, local copies, waits for them, and re-layouts  1.38 us
  transfers between devices with their start and end apart: 14, of which 4 were waited for; matrix products, arithmetic and copies ran while one was open for 0% of the time, Pallas kernels for 38%

profile of v8, /device:TPU:0, one launch (start us, length us, event | category | flops | bytes accessed | tf_op | source)
XLA Modules:
  0.0 54.3 jit_solution(17999994129332363988)
XLA Ops:
  0.0 0.1 pad_add_fusion.info
  0.1 0.0 copy-start.1
  0.1 1.4 %copy-done.1 = f32[576,576]{1,0:T(8,128)S(1)} copy-done((f32[576,576]{1,0:T(8,128)S(1)}, f32[576,576]{1,0:T(8,128)}, u32[]{:S(2)}) %copy-start.1) | copy-done | bytes 1327128
  1.4 1.2 %pack_first.1 = (f32[864,128]{1,0:T(8,128)S(1)}, f32[1152,128]{1,0:T(8,128)S(1)}, f32[1728,128]{1,0:T(8,128)S(1)}) custom-call(s32[2]{0:T(128)S(1)} %pad_add_fusion.info, f32[576,576]{1,0:T(8,128)S(1)} %copy-done.1), custom_call_target="tpu_custom_call" | custom-call | flops 4000000000 | bytes 20000000 | tf_op jit(solution)/shard_map/pack_first/pallas_call | solution.py:279
  2.7 0.5 collective-permute-start.2
  3.2 2.6 %collective-permute-start.1 = (f32[864,128]{1,0:T(8,128)S(1)}, f32[864,128]{1,0:T(8,128)S(1)}, u32[]{:S(2)}, u32[]{:S(2)}) collective-permute-start(f32[864,128]{1,0:T(8,128)S(1)} %get-tuple-element.48), channel_id=1, source_target_pairs={{0,8},{8,0},{16,24},{24,16},{1,9},{9,1},{17,25},{25,17},{2,10},{10... | collective-permute-start | bytes 1327112 | tf_op jit(solution)/shard_map/ppermute | solution.py:308
  5.8 3.4 %collective-permute-start = (f32[1152,128]{1,0:T(8,128)S(1)}, f32[1152,128]{1,0:T(8,128)S(1)}, u32[]{:S(2)}, u32[]{:S(2)}) collective-permute-start(f32[1152,128]{1,0:T(8,128)S(1)} %get-tuple-element.47), channel_id=1, source_target_pairs={{0,7},{1,2},{2,1},{3,4},{4,3},{5,6},{6,5},{7,0},{8,15},{9,10},{10,... | collective-permute-start | bytes 1769480 | tf_op jit(solution)/shard_map/ppermute | solution.py:308
  9.1 0.0 collective-permute-done.2.chip
  9.1 0.8 %pack_rest.1 = (f32[576,128]{1,0:T(8,128)S(1)}, f32[864,128]{1,0:T(8,128)S(1)}, f32[864,128]{1,0:T(8,128)S(1)}) custom-call(s32[2]{0:T(128)S(1)} %pad_add_fusion.info, f32[576,576]{1,0:T(8,128)S(1)} %copy-done.1), custom_call_target="tpu_custom_call" | custom-call | flops 4000000000 | bytes 20000000 | tf_op jit(solution)/shard_map/pack_rest/pallas_call | solution.py:279
  9.9 0.9 %collective-permute-start.4 = (f32[576,128]{1,0:T(8,128)S(1)}, f32[576,128]{1,0:T(8,128)S(1)}, u32[]{:S(2)}, u32[]{:S(2)}) collective-permute-start(f32[576,128]{1,0:T(8,128)S(1)} %get-tuple-element.61), channel_id=1, source_target_pairs={{0,7},{1,2},{2,1},{3,4},{4,3},{5,6},{6,5},{7,0},{8,15},{9,10},{10,... | collective-permute-start | bytes 884744 | tf_op jit(solution)/shard_map/ppermute | solution.py:308
  10.8 1.5 %collective-permute-start.6 = (f32[864,128]{1,0:T(8,128)S(1)}, f32[864,128]{1,0:T(8,128)S(1)}, u32[]{:S(2)}, u32[]{:S(2)}) collective-permute-start(f32[864,128]{1,0:T(8,128)S(1)} %get-tuple-element.62), channel_id=1, source_target_pairs={{0,16},{8,24},{16,0},{24,8},{1,17},{9,25},{17,1},{25,9},{2,18},{10... | collective-permute-start | bytes 1327112 | tf_op jit(solution)/shard_map/ppermute | solution.py:308
  12.3 1.5 %collective-permute-start.7 = (f32[864,128]{1,0:T(8,128)S(1)}, f32[864,128]{1,0:T(8,128)S(1)}, u32[]{:S(2)}, u32[]{:S(2)}) collective-permute-start(f32[864,128]{1,0:T(8,128)S(1)} %get-tuple-element.68), channel_id=1, source_target_pairs={{0,8},{8,0},{16,24},{24,16},{1,9},{9,1},{17,25},{25,17},{2,10},{10... | collective-permute-start | bytes 1327112 | tf_op jit(solution)/shard_map/ppermute | solution.py:308
  13.8 1.0 %prepare.1 = (bf16[2,3,576,256]{3,2,1,0:T(8,128)(2,1)S(1)}, bf16[2,3,768,256]{3,2,1,0:T(8,128)(2,1)S(1)}, bf16[2,3,384,256]{3,2,1,0:T(8,128)(2,1)S(1)}) custom-call(s32[2]{0:T(128)S(1)} %pad_add_fusion.info, f32[576,576]{1,0:T(8,128)S(1)} %copy-done.1, f32[1728,128]{1,0:T(8,128)S(1)} %collective-permute-done.2.chip), custom_call_target="tpu_custom_call" | custom-call | flops 4000000000 | bytes 20000000 | tf_op jit(solution)/shard_map/prepare/pallas_call | solution.py:279
  14.8 1.9 %collective-permute-done.1.mid = f32[864,128]{1,0:T(8,128)S(1)} collective-permute-done((f32[864,128]{1,0:T(8,128)S(1)}, f32[864,128]{1,0:T(8,128)S(1)}, u32[]{:S(2)}, u32[]{:S(2)}) %collective-permute-start.1) | collective-permute-done | bytes 442400 | tf_op jit(solution)/shard_map/ppermute | solution.py:308
  16.8 2.0 %collective-permute-start.5 = (f32[864,128]{1,0:T(8,128)S(1)}, f32[864,128]{1,0:T(8,128)S(1)}, u32[]{:S(2)}, u32[]{:S(2)}) collective-permute-start(f32[864,128]{1,0:T(8,128)S(1)} %collective-permute-done.1.mid), channel_id=1, source_target_pairs={{0,16},{8,24},{16,0},{24,8},{1,17},{9,25},{17,1},{25,9},{2,18},{10... | collective-permute-start | bytes 1327112 | tf_op jit(solution)/shard_map/ppermute | solution.py:308
  18.8 0.0 copy-start
  18.8 1.6 %near_start.1 = (f32[576,256]{1,0:T(8,128)S(1)}, bf16[2,768,256]{2,1,0:T(8,128)(2,1)S(1)}) custom-call(s32[2]{0:T(128)S(1)} %pad_add_fusion.info, f32[864,128]{1,0:T(8,128)S(1)} %collective-permute-done.1.mid, bf16[2,3,576,256]{3,2,1,0:T(8,128)(2,1)S(1)} %get-tuple-element.53.own_left, bf16[2,3,768,256]{3,2,1,0:T(8,128)(2,1)S(1)} %get-tuple-element.54.own_right, ...), custom_call_target="tpu_custom_call" | custom-call | flops 4000000000 | bytes 20000000 | tf_op jit(solution)/shard_map/near_start/pallas_call | solution.py:279
  20.3 2.6 %collective-permute-done.link_a = f32[1152,128]{1,0:T(8,128)S(1)} collective-permute-done((f32[1152,128]{1,0:T(8,128)S(1)}, f32[1152,128]{1,0:T(8,128)S(1)}, u32[]{:S(2)}, u32[]{:S(2)}) %collective-permute-start) | collective-permute-done | bytes 589856 | tf_op jit(solution)/shard_map/ppermute | solution.py:308
  22.9 0.0 copy-done
  22.9 1.4 %square_near.1 = (f32[576,256]{1,0:T(8,128)S(1)}, f32[576,128]{1,0:T(8,128)S(1)}, bf16[2,2,384,256]{3,2,1,0:T(8,128)(2,1)S(1)}) custom-call(s32[2]{0:T(128)S(1)} %pad_add_fusion.info, s32[9,9]{1,0:T(8,128)S(1)} %copy-done, f32[1152,128]{1,0:T(8,128)S(1)} %collective-permute-done.link_a, f32[576,256]{1,0:T(8,128)S(1)} %get-tuple-element.56.begun, ...), custom_call_target="tpu_custom_call" | custom-call | flops 4000000000 | bytes 20000000 | tf_op jit(solution)/shard_map/square_near/pallas_call | solution.py:279
  24.4 3.7 %collective-permute-start.3 = (f32[576,128]{1,0:T(8,128)S(1)}, f32[576,128]{1,0:T(8,128)S(1)}, u32[]{:S(2)}, u32[]{:S(2)}) collective-permute-start(f32[576,128]{1,0:T(8,128)S(1)} %get-tuple-element.58), channel_id=1, source_target_pairs={{0,7},{1,2},{2,1},{3,4},{4,3},{5,6},{6,5},{7,0},{8,15},{9,10},{10,... | collective-permute-start | bytes 884744 | tf_op jit(solution)/shard_map/ppermute | solution.py:308
  28.1 0.0 collective-permute-done.6
  28.1 0.5 collective-permute-start.8
  28.6 1.9 %middle_products.1 = (f32[576,256]{1,0:T(8,128)S(1)}, f32[576,256]{1,0:T(8,128)S(1)}) custom-call(s32[2]{0:T(128)S(1)} %pad_add_fusion.info, bf16[2,3,576,256]{3,2,1,0:T(8,128)(2,1)S(1)} %get-tuple-element.53.own_left, bf16[2,3,768,256]{3,2,1,0:T(8,128)(2,1)S(1)} %get-tuple-element.54.own_right, bf16[2,3,384,256]{3,2,1,0:T(8,128)(2,1)S(1)} %get-tuple-element.55.chip_left, ...), custom_call_target="tpu_custom_call" | custom-call | flops 4000000000 | bytes 20000000 | tf_op jit(solution)/shard_map/middle_products/pallas_call | solution.py:279
  30.5 0.0 collective-permute-done.4.link_b
  30.5 0.2 collective-permute-done.5.mid
  30.7 1.8 %square_far.1 = (f32[576,256]{1,0:T(8,128)S(1)}, f32[576,128]{1,0:T(8,128)S(1)}, bf16[2,384,256]{2,1,0:T(8,128)(2,1)S(1)}, bf16[2,768,256]{2,1,0:T(8,128)(2,1)S(1)}) custom-call(s32[2]{0:T(128)S(1)} %pad_add_fusion.info, s32[9,9]{1,0:T(8,128)S(1)} %copy-done, f32[576,128]{1,0:T(8,128)S(1)} %collective-permute-done.4.link_b, ...), custom_call_target="tpu_custom_call" | custom-call | flops 4000000000 | bytes 20000000 | tf_op jit(solution)/shard_map/square_far/pallas_call | solution.py:279
  32.5 0.0 collective-permute-done.7.near
  32.5 3.6 %collective-permute-start.12 = (f32[576,128]{1,0:T(8,128)S(1)}, f32[576,128]{1,0:T(8,128)S(1)}, u32[]{:S(2)}, u32[]{:S(2)}) collective-permute-start(f32[576,128]{1,0:T(8,128)S(1)} %get-tuple-element.83), channel_id=1, source_target_pairs={{0,7},{1,2},{2,1},{3,4},{4,3},{5,6},{6,5},{7,0},{8,15},{9,10},{10,... | collective-permute-start | bytes 884744 | tf_op jit(solution)/shard_map/ppermute | solution.py:308
  36.1 1.4 %mid_start.1 = (f32[576,256]{1,0:T(8,128)S(1)}, f32[1152,128]{1,0:T(8,128)S(1)}, bf16[2,768,256]{2,1,0:T(8,128)(2,1)S(1)}) custom-call(s32[2]{0:T(128)S(1)} %pad_add_fusion.info, f32[864,128]{1,0:T(8,128)S(1)} %collective-permute-done.7.near, f32[576,256]{1,0:T(8,128)S(1)} %get-tuple-element.71.begun, ...), custom_call_target="tpu_custom_call" | custom-call | flops 4000000000 | bytes 20000000 | tf_op jit(solution)/shard_map/mid_start/pallas_call | solution.py:279
  37.5 0.1 collective-permute-start.9
  37.6 0.0 collective-permute-done.3.link
  37.6 1.8 %cube_near.1.total = f32[3,576,256]{2,1,0:T(8,128)S(1)} custom-call(s32[2]{0:T(128)S(1)} %pad_add_fusion.info, f32[576,128]{1,0:T(8,128)S(1)} %collective-permute-done.3.link, f32[576,256]{1,0:T(8,128)S(1)} %get-tuple-element.59.s_near.near, f32[576,256]{1,0:T(8,128)S(1)} %get-tuple-element.66.s_far.far, ...), custom_call_target="tpu_custom_call" | custom-call | flops 4000000000 | bytes 20000000 | tf_op jit(solution)/shard_map/cube_near/pallas_call | solution.py:279
  39.4 0.0 collective-permute-done.8.far
  39.4 1.9 %square_mid.1 = (f32[576,256]{1,0:T(8,128)S(1)}, f32[576,128]{1,0:T(8,128)S(1)}, f32[288,128]{1,0:T(8,128)S(1)}, f32[288,128]{1,0:T(8,128)S(1)}, bf16[2,768,256]{2,1,0:T(8,128)(2,1)S(1)}) custom-call(s32[2]{0:T(128)S(1)} %pad_add_fusion.info, s32[9,9]{1,0:T(8,128)S(1)} %copy-done, f32[864,128]{1,0:T(8,128)S(1)} %collective-permute-done.8.far, ...), custom_call_target="tpu_custom_call" | custom-call | tf_op jit(solution)/shard_map/square_mid/pallas_call | solution.py:279
  41.3 0.3 collective-permute-start.13
  41.6 0.3 collective-permute-start.11
  41.9 1.5 %collective-permute-done.12.link = f32[576,128]{1,0:T(8,128)S(1)} collective-permute-done((f32[576,128]{1,0:T(8,128)S(1)}, f32[576,128]{1,0:T(8,128)S(1)}, u32[]{:S(2)}, u32[]{:S(2)}) %collective-permute-start.12) | collective-permute-done | bytes 294944 | tf_op jit(solution)/shard_map/ppermute | solution.py:308
  43.4 2.1 %cube_own.1.base = f32[3,576,256]{2,1,0:T(8,128)S(1)} custom-call(s32[2]{0:T(128)S(1)} %pad_add_fusion.info, f32[576,128]{1,0:T(8,128)S(1)} %collective-permute-done.12.link, f32[3,576,256]{2,1,0:T(8,128)S(1)} %cube_near.1.total, f32[576,256]{1,0:T(8,128)S(1)} %get-tuple-element.59.s_near.near, f32[576,256]{1,0:T(8,128)S(1)} %get-tuple-element.85.mid, ...), custom_call_target="tpu_custom_call" | custom-call | flops 4000000000 | bytes 20000000 | tf_op jit(solution)/shard_map/cube_own/pallas_call | solution.py:279
  45.5 0.0 collective-permute-done.9.sides
  45.5 1.6 %collective-permute-start.10 = (f32[288,128]{1,0:T(8,128)S(1)}, f32[288,128]{1,0:T(8,128)S(1)}, u32[]{:S(2)}, u32[]{:S(2)}) collective-permute-start(f32[288,128]{1,0:T(8,128)S(1)} %get-tuple-element.79), channel_id=1, source_target_pairs={{0,7},{1,2},{2,1},{3,4},{4,3},{5,6},{6,5},{7,0},{8,15},{9,10},{10,... | collective-permute-start | bytes 442376 | tf_op jit(solution)/shard_map/ppermute | solution.py:308
  47.1 0.0 collective-permute-done.11.chip
  47.1 0.0 copy-done.2
  47.1 3.3 %cube_chip.1 = (f32[3,576,256]{2,1,0:T(8,128)S(1)}, f32[576,576]{1,0:T(8,128)}) custom-call(s32[2]{0:T(128)S(1)} %pad_add_fusion.info, s32[9,9]{1,0:T(8,128)S(1)} %copy-done.2, f32[1152,128]{1,0:T(8,128)S(1)} %collective-permute-done.9.sides, f32[576,128]{1,0:T(8,128)S(1)} %collective-permute-done.11.chip, ...), custom_call_target="tpu_custom_call" | custom-call | flops 4000000000 | bytes 20000000 | tf_op jit(solution)/shard_map/cube_chip/pallas_call | solution.py:279
  50.4 0.0 collective-permute-done.13.link
  50.4 1.9 %finish_first.1.begun = f32[576,576]{1,0:T(8,128)} custom-call(s32[2]{0:T(128)S(1)} %pad_add_fusion.info, s32[9,9]{1,0:T(8,128)S(1)} %copy-done.2, f32[288,128]{1,0:T(8,128)S(1)} %collective-permute-done.13.link, bf16[2,3,768,256]{3,2,1,0:T(8,128)(2,1)S(1)} %get-tuple-element.54.own_right, ...), custom_call_target="tpu_custom_call", output_to_operand_aliasing={{}: (5, {})} | custom-call | flops 4000000000 | bytes 20000000 | tf_op jit(solution)/shard_map/finish_first/pallas_call | solution.py:279
  52.3 0.0 collective-permute-done.10.link
  52.4 1.9 %finish_second.1 = f32[576,576]{1,0:T(8,128)} custom-call(s32[2]{0:T(128)S(1)} %pad_add_fusion.info, s32[9,9]{1,0:T(8,128)S(1)} %copy-done.2, f32[288,128]{1,0:T(8,128)S(1)} %collective-permute-done.10.link, bf16[2,3,768,256]{3,2,1,0:T(8,128)(2,1)S(1)} %get-tuple-element.54.own_right, ...), custom_call_target="tpu_custom_call", output_to_operand_aliasing={{}: (5, {})} | custom-call | flops 4000000000 | bytes 20000000 | tf_op jit(solution)/shard_map/finish_second/pallas_call | solution.py:279
  (1 shorter events, 0.0 us)
Async XLA Ops:
  0.1 1.4 %copy-start.1 = (f32[576,576]{1,0:T(8,128)S(1)}, f32[576,576]{1,0:T(8,128)}, u32[]{:S(2)}) copy-start(f32[576,576]{1,0:T(8,128)} %tile.4) | copy-start | bytes 3981316
  2.7 6.5 %collective-permute-start.2 = (f32[1728,128]{1,0:T(8,128)S(1)}, f32[1728,128]{1,0:T(8,128)S(1)}, u32[]{:S(2)}, u32[]{:S(2)}) collective-permute-start(f32[1728,128]{1,0:T(8,128)S(1)} %get-tuple-element.49), channel_id=1, source_target_pairs={{0,1},{1,0},{2,3},{3,2},{4,5},{5,4},{6,7},{7,6},{8,9},{9,8},{10,11... | collective-permute-start | bytes 2654216 | tf_op jit(solution)/shard_map/ppermute | solution.py:308
  3.2 13.6 %collective-permute-start.1 = (f32[864,128]{1,0:T(8,128)S(1)}, f32[864,128]{1,0:T(8,128)S(1)}, u32[]{:S(2)}, u32[]{:S(2)}) collective-permute-start(f32[864,128]{1,0:T(8,128)S(1)} %get-tuple-element.48), channel_id=1, source_target_pairs={{0,8},{8,0},{16,24},{24,16},{1,9},{9,1},{17,25},{25,17},{2,10},{10... | collective-permute-start | bytes 1327112 | tf_op jit(solution)/shard_map/ppermute | solution.py:308
  5.8 17.2 %collective-permute-start = (f32[1152,128]{1,0:T(8,128)S(1)}, f32[1152,128]{1,0:T(8,128)S(1)}, u32[]{:S(2)}, u32[]{:S(2)}) collective-permute-start(f32[1152,128]{1,0:T(8,128)S(1)} %get-tuple-element.47), channel_id=1, source_target_pairs={{0,7},{1,2},{2,1},{3,4},{4,3},{5,6},{6,5},{7,0},{8,15},{9,10},{10,... | collective-permute-start | bytes 1769480 | tf_op jit(solution)/shard_map/ppermute | solution.py:308
  9.9 20.6 %collective-permute-start.4 = (f32[576,128]{1,0:T(8,128)S(1)}, f32[576,128]{1,0:T(8,128)S(1)}, u32[]{:S(2)}, u32[]{:S(2)}) collective-permute-start(f32[576,128]{1,0:T(8,128)S(1)} %get-tuple-element.61), channel_id=1, source_target_pairs={{0,7},{1,2},{2,1},{3,4},{4,3},{5,6},{6,5},{7,0},{8,15},{9,10},{10,... | collective-permute-start | bytes 884744 | tf_op jit(solution)/shard_map/ppermute | solution.py:308
  10.8 17.3 %collective-permute-start.6 = (f32[864,128]{1,0:T(8,128)S(1)}, f32[864,128]{1,0:T(8,128)S(1)}, u32[]{:S(2)}, u32[]{:S(2)}) collective-permute-start(f32[864,128]{1,0:T(8,128)S(1)} %get-tuple-element.62), channel_id=1, source_target_pairs={{0,16},{8,24},{16,0},{24,8},{1,17},{9,25},{17,1},{25,9},{2,18},{10... | collective-permute-start | bytes 1327112 | tf_op jit(solution)/shard_map/ppermute | solution.py:308
  12.3 20.2 %collective-permute-start.7 = (f32[864,128]{1,0:T(8,128)S(1)}, f32[864,128]{1,0:T(8,128)S(1)}, u32[]{:S(2)}, u32[]{:S(2)}) collective-permute-start(f32[864,128]{1,0:T(8,128)S(1)} %get-tuple-element.68), channel_id=1, source_target_pairs={{0,8},{8,0},{16,24},{24,16},{1,9},{9,1},{17,25},{25,17},{2,10},{10... | collective-permute-start | bytes 1327112 | tf_op jit(solution)/shard_map/ppermute | solution.py:308
  16.8 13.9 %collective-permute-start.5 = (f32[864,128]{1,0:T(8,128)S(1)}, f32[864,128]{1,0:T(8,128)S(1)}, u32[]{:S(2)}, u32[]{:S(2)}) collective-permute-start(f32[864,128]{1,0:T(8,128)S(1)} %collective-permute-done.1.mid), channel_id=1, source_target_pairs={{0,16},{8,24},{16,0},{24,8},{1,17},{9,25},{17,1},{25,9},{2,18},{10... | collective-permute-start | bytes 1327112 | tf_op jit(solution)/shard_map/ppermute | solution.py:308
  18.8 4.2 %copy-start = (s32[9,9]{1,0:T(8,128)S(1)}, s32[9,9]{1,0:T(8,128)}, u32[]{:S(2)}) copy-start(s32[9,9]{1,0:T(8,128)} %kept.8) | copy-start | bytes 976
  24.4 13.3 %collective-permute-start.3 = (f32[576,128]{1,0:T(8,128)S(1)}, f32[576,128]{1,0:T(8,128)S(1)}, u32[]{:S(2)}, u32[]{:S(2)}) collective-permute-start(f32[576,128]{1,0:T(8,128)S(1)} %get-tuple-element.58), channel_id=1, source_target_pairs={{0,7},{1,2},{2,1},{3,4},{4,3},{5,6},{6,5},{7,0},{8,15},{9,10},{10,... | collective-permute-start | bytes 884744 | tf_op jit(solution)/shard_map/ppermute | solution.py:308
  28.1 11.3 %collective-permute-start.8 = (f32[864,128]{1,0:T(8,128)S(1)}, f32[864,128]{1,0:T(8,128)S(1)}, u32[]{:S(2)}, u32[]{:S(2)}) collective-permute-start(f32[864,128]{1,0:T(8,128)S(1)} %collective-permute-done.6), channel_id=1, source_target_pairs={{0,8},{8,0},{16,24},{24,16},{1,9},{9,1},{17,25},{25,17},{2,10},{10... | collective-permute-start | bytes 1327112 | tf_op jit(solution)/shard_map/ppermute | solution.py:308
  32.5 10.8 %collective-permute-start.12 = (f32[576,128]{1,0:T(8,128)S(1)}, f32[576,128]{1,0:T(8,128)S(1)}, u32[]{:S(2)}, u32[]{:S(2)}) collective-permute-start(f32[576,128]{1,0:T(8,128)S(1)} %get-tuple-element.83), channel_id=1, source_target_pairs={{0,7},{1,2},{2,1},{3,4},{4,3},{5,6},{6,5},{7,0},{8,15},{9,10},{10,... | collective-permute-start | bytes 884744 | tf_op jit(solution)/shard_map/ppermute | solution.py:308
  37.5 7.9 %collective-permute-start.9 = (f32[1152,128]{1,0:T(8,128)S(1)}, f32[1152,128]{1,0:T(8,128)S(1)}, u32[]{:S(2)}, u32[]{:S(2)}) collective-permute-start(f32[1152,128]{1,0:T(8,128)S(1)} %get-tuple-element.78), channel_id=1, source_target_pairs={{0,1},{1,0},{2,3},{3,2},{4,5},{5,4},{6,7},{7,6},{8,9},{9,8},{10,11... | collective-permute-start | bytes 1769480 | tf_op jit(solution)/shard_map/ppermute | solution.py:308
  41.3 9.1 %collective-permute-start.13 = (f32[288,128]{1,0:T(8,128)S(1)}, f32[288,128]{1,0:T(8,128)S(1)}, u32[]{:S(2)}, u32[]{:S(2)}) collective-permute-start(f32[288,128]{1,0:T(8,128)S(1)} %get-tuple-element.87), channel_id=1, source_target_pairs={{0,7},{1,2},{2,1},{3,4},{4,3},{5,6},{6,5},{7,0},{8,15},{9,10},{10,... | collective-permute-start | bytes 442376 | tf_op jit(solution)/shard_map/ppermute | solution.py:308
  41.6 5.5 %collective-permute-start.11 = (f32[576,128]{1,0:T(8,128)S(1)}, f32[576,128]{1,0:T(8,128)S(1)}, u32[]{:S(2)}, u32[]{:S(2)}) collective-permute-start(f32[576,128]{1,0:T(8,128)S(1)} %get-tuple-element.81), channel_id=1, source_target_pairs={{0,1},{1,0},{2,3},{3,2},{4,5},{5,4},{6,7},{7,6},{8,9},{9,8},{10,11... | collective-permute-start | bytes 884744 | tf_op jit(solution)/shard_map/ppermute | solution.py:308
  43.4 3.7 %copy-start.2 = (s32[9,9]{1,0:T(8,128)S(1)}, s32[9,9]{1,0:T(8,128)}, u32[]{:S(2)}) copy-start(s32[9,9]{1,0:T(8,128)} %kept.11) | copy-start | bytes 976
  45.5 6.9 %collective-permute-start.10 = (f32[288,128]{1,0:T(8,128)S(1)}, f32[288,128]{1,0:T(8,128)S(1)}, u32[]{:S(2)}, u32[]{:S(2)}) collective-permute-start(f32[288,128]{1,0:T(8,128)S(1)} %get-tuple-element.79), channel_id=1, source_target_pairs={{0,7},{1,2},{2,1},{3,4},{4,3},{5,6},{6,5},{7,0},{8,15},{9,10},{10,... | collective-permute-start | bytes 442376 | tf_op jit(solution)/shard_map/ppermute | solution.py:308

commit v9 on v8

--- a/solution.py
+++ b/solution.py
@@ -1,5 +1,3 @@
-import functools
-
 import jax
 import jax.numpy as jnp
 from jax import lax
@@ -172,7 +170,7 @@
                 out[shared_rows(info, who, group), :] += value
 
 
-def far_body(info, kept, link_b, mid, begun, own_left, chip_left, out, link, link_left, rights):
+def far_body(info, kept, link_b, mid, begun, s_near, own_left, chip_left, out, link, sides, link_left, rights):
     group = out.shape[0] // 3
     store_left(link_left, (), unfold(link_b[...]))
     store_right(rights, (), unfold(mid[...]))
@@ -181,28 +179,26 @@
         out[shared_rows(info, who, group), :] += passes([factor], [right(rights, info, who)])
     out[...] = masked(out[...], kept, mask_at(info, FAR))
     store_fold(link, 0, out[shared_rows(info, LINK, group), :])
-
-
-def mid_start_body(info, near, begun, own_left, chip_left, link_left, s_near, s_far, out, sides, rights):
+    store_fold(sides, 0, s_near[shared_rows(info, CHIP, group), :])
+    store_fold(sides, 3 * group, out[shared_rows(info, CHIP, group), :])
+
+
+def mid_start_body(info, near, begun, own_left, chip_left, link_left, out, rights):
     group = out.shape[0] // 3
-    store_fold(sides, 0, s_near[shared_rows(info, CHIP, group), :])
-    store_fold(sides, 3 * group, s_far[shared_rows(info, CHIP, group), :])
     store_right(rights, (), unfold(near[...]))
     out[...] = begun[...] + passes([left(own_left, NEAR)], [right(rights, info, OWN)])
     for who, lefts in ((CHIP, chip_left), (LINK, link_left)):
         out[shared_rows(info, who, group), :] += passes([left(lefts, NEAR)], [right(rights, info, who)])
 
 
-def mid_body(info, kept, far, own_left, chip_left, link_left, begun, out, chip, link_first, link_second, rights):
+def mid_body(info, kept, far, own_left, chip_left, link_left, begun, out, chip, link, rights):
     group = out.shape[0] // 3
     store_right(rights, (), unfold(far[...]))
     out[...] = begun[...] + passes([left(own_left, FAR)], [right(rights, info, OWN)])
     for who, factor in ((CHIP, left(chip_left, FAR)), (LINK, left(link_left))):
         out[shared_rows(info, who, group), :] += passes([factor], [right(rights, info, who)])
     out[...] = masked(out[...], kept, 3)
-    start = place(info, LINK, group)[0]
-    for k, link in enumerate((link_first, link_second)):
-        store_fold(link, 0, out[pl.ds(pl.multiple_of(start + k * group, 64), group), :])
+    store_fold(link, 0, out[shared_rows(info, LINK, group), :])
     store_fold(chip, 0, out[shared_rows(info, CHIP, group), :])
 
 
@@ -240,7 +236,9 @@
 
 def cube_chip_body(info, kept, sides, chip, own_right, right_near, right_far, mid_near, mid_far, base, out, result, tile, sem):
     group = base.shape[1] // 3
-    at = shared_rows(info, CHIP, group)
+    chip_start = place(info, CHIP, group)[0]
+    rest = pl.multiple_of(2 * chip_start, 64)
+    link_only = pl.multiple_of(2 * (group - chip_start), 64)
     chips = [split(unfold(value)) for value in (sides[: 3 * group, :], chip[...], sides[3 * group :, :])]
     own = [right(own_right, info, CHIP, part) for part in range(3)]
     products = (
@@ -249,24 +247,38 @@
         (chips[1:], [own[FAR], right(right_far, info, CHIP)]),
     )
     for part, factors in enumerate(products):
-        out[part] = base[part]
-        out[part, at, :] -= 2.0 * passes(*factors)
-        out[part] = masked(out[part], kept, mask_at(info, part))
-    rest = pl.multiple_of(2 * place(info, CHIP, group)[0], 64)
-    send_rows(info, tile, result, sem, rest, *(out[part, pl.ds(rest, group), :] for part in range(3))).wait()
-
-
-def finish_body(half, info, kept, link, own_right, base, begun, result, tile, sem):
+        out[part, shared_rows(info, CHIP, group), :] = base[part, shared_rows(info, CHIP, group), :] - 2.0 * passes(*factors)
+
+    def finished(row):
+        at = pl.ds(row, group)
+        return [masked(out[part, at, :], kept, mask_at(info, part), row // 64) for part in range(3)]
+
+    copy = send_rows(info, tile, result, sem, rest, *finished(rest))
+    for part in range(3):
+        out[part, pl.ds(link_only, group), :] = base[part, pl.ds(link_only, group), :]
+    for row in (group, link_only):
+        for part, value in enumerate(finished(row)):
+            out[part, pl.ds(row, group), :] = value
+    copy.wait()
+
+
+def finish_body(info, kept, link, own_right, base, begun, result, tile, sem):
     del begun
-    group = tile.shape[0]
-    row = pl.multiple_of(place(info, LINK, group)[0] + half * group, 64)
-    first_row = place(info, LINK, 3)[0] + 3 * half
-    link_mid = split(unfold(link[...]))
-    values = []
-    for part in range(3):
-        value = -2.0 * passes([link_mid], [right(own_right, info, LINK, part)])
-        values.append(base[part, pl.ds(row, group), :] + masked(value, kept, mask_at(info, part), first_row))
-    send_rows(info, tile, result, sem, row, *values).wait()
+    group = tile.shape[1]
+    start, first_row = place(info, LINK, group)[0], place(info, LINK, 3)[0]
+    link_mid = unfold(link[...])
+    copies = []
+    for half in range(2):
+        factor = split(link_mid[half * group : (half + 1) * group])
+        row = pl.multiple_of(start + half * group, 64)
+        values = []
+        for part in range(3):
+            value = -2.0 * passes([factor], [right(own_right, info, LINK, part)])
+            value = masked(value, kept, mask_at(info, part), first_row + 3 * half)
+            values.append(base[part, pl.ds(row, group), :] + value)
+        copies.append(send_rows(info, tile.at[half], result, sem.at[half], row, *values))
+    for copy in copies:
+        copy.wait()
 
 
 VMEM = pl.BlockSpec(memory_space=pltpu.VMEM)
@@ -296,7 +308,6 @@
     info = jnp.stack([lax.axis_index("row") % 2, lax.axis_index("col") % 2]).astype(jnp.int32)
     strip = ((3 * side // 2, LANES), F32)
     slab = ((3 * group, LANES), F32)
-    half_slab = ((3 * group // 2, LANES), F32)
     two_slabs = ((6 * group, LANES), F32)
     three_slabs = ((9 * group, LANES), F32)
     wide = ((side, WIDE), F32)
@@ -346,22 +357,23 @@
     begun, begun_mid = call(
         middle_products_body, "middle_products", (info,), (own_left, own_right, chip_left, link_left), [wide] * 2
     )
-    s_far, far_link, link_left_far, right_far = call(
+    begun_mid, mid_near = call(
+        mid_start_body,
+        "mid_start",
+        (info,),
+        (partner_near, begun_mid, own_left, chip_left, link_left),
+        [wide, rights],
+    )
+    begun, begun_mid = lax.optimization_barrier((begun, begun_mid))
+    s_far, far_link, sides_chip, link_left_far, right_far = call(
         far_body,
         "square_far",
         (info, square_kept),
-        (link_b, other_mid, begun, own_left, chip_left),
-        [wide, slab, ((2, 2 * group, WIDE), BF16), rights],
+        (link_b, other_mid, begun, s_near, own_left, chip_left),
+        [wide, slab, two_slabs, ((2, 2 * group, WIDE), BF16), rights],
     )
     far_link = exchange(far_link, "col", -1)
-    partner_near, link_left_far = lax.optimization_barrier((partner_near, link_left_far))
-    begun, sides_chip, mid_near = call(
-        mid_start_body,
-        "mid_start",
-        (info,),
-        (partner_near, begun_mid, own_left, chip_left, link_left, s_near, s_far),
-        [wide, two_slabs, rights],
-    )
+    sides_chip = exchange(sides_chip, "col", 1)
     (total,) = call(
         cube_near_body,
         "cube_near",
@@ -370,18 +382,15 @@
         [three_wide],
     )
     total, other_far = lax.optimization_barrier((total, other_far))
-    s_mid, mid_chip, link_first, link_second, mid_far = call(
+    s_mid, mid_chip, mid_link, mid_far = call(
         mid_body,
         "square_mid",
         (info, square_kept),
-        (other_far, own_left, chip_left, link_left_far, begun),
-        [wide, slab, half_slab, half_slab, rights],
+        (other_far, own_left, chip_left, link_left_far, begun_mid),
+        [wide, slab, slab, rights],
         work=0,
     )
-    link_first = exchange(link_first, "col", -1)
-    sides_chip = exchange(sides_chip, "col", 1)
-    link_second, sides_chip = lax.optimization_barrier((link_second, sides_chip))
-    link_second = exchange(link_second, "col", -1)
+    mid_link = exchange(mid_link, "col", -1)
     mid_chip = exchange(mid_chip, "col", 1)
     (base,) = call(
         cube_own_body,
@@ -391,7 +400,6 @@
         [three_wide],
     )
     result = ((side, side), F32)
-    row_scratch = [pltpu.VMEM((group, side), F32), pltpu.SemaphoreType.DMA(())]
     base, purified = call(
         cube_chip_body,
         "cube_chip",
@@ -399,19 +407,18 @@
         (sides_chip, mid_chip, own_right, right_near, right_far, mid_near, mid_far, base),
         [three_wide, result],
         result=True,
-        scratch=row_scratch,
-    )
-    for half, link in enumerate((link_first, link_second)):
-        (purified,) = call(
-            functools.partial(finish_body, half),
-            ("finish_first", "finish_second")[half],
-            (info, result_kept),
-            (link, own_right, base),
-            [result],
-            result=True,
-            begun=(purified,),
-            scratch=row_scratch,
-        )
+        scratch=[pltpu.VMEM((group, side), F32), pltpu.SemaphoreType.DMA(())],
+    )
+    (purified,) = call(
+        finish_body,
+        "finish",
+        (info, result_kept),
+        (mid_link, own_right, base),
+        [result],
+        result=True,
+        begun=(purified,),
+        scratch=[pltpu.VMEM((2, group, side), F32), pltpu.SemaphoreType.DMA((2,))],
+    )
     return purified
 
 

time: 54.4 us -> 52.8 us (0.971)
  waiting for transfers between devices: 6.21 us -> 8.05 us
  starting transfers between devices: 22.5 us -> 20.7 us
  Pallas kernels: 24 us -> 22.3 us
    ppermute x14 -> x13, waiting for transfers between devices: 6.21 us -> 8.05 us  [exchange(): lax.ppermute(value, axis, [(i, (i + (even_step if i % 2 == 0 else -even_s...]
    ppermute x14 -> x13, starting transfers between devices: 22.5 us -> 20.7 us  [exchange(): lax.ppermute(value, axis, [(i, (i + (even_step if i % 2 == 0 else -even_s...]
    pallas_call x14 -> x13, Pallas kernels: 24 us -> 22.3 us  [call(): pl.pallas_call(body, out_shape=[jax.ShapeDtypeStruct(shape, kind) for sha...]
  transfers between devices with their start and end apart: 14 -> 13, of which waited for: 4 -> 4; matrix products, arithmetic and copies ran while one was open for 0% -> 0% of each run, Pallas kernels for 38% -> 36%
where the time goes in v9:
time: 52.8 us; the launch traced here: 52.7 us
  Pallas kernels  22.3 us (42%)
  starting transfers between devices  20.7 us (39%)
  waiting for transfers between devices  8.05 us (15%)
  local copies, waits for them, and re-layouts  1.38 us (3%)
    pallas_call x13, Pallas kernels, call(): pl.pallas_call(body, out_shape=[jax.ShapeDtypeStruct(shape, kind) for sha...  22.3 us
    ppermute x13, starting transfers between devices, exchange(): lax.ppermute(value, axis, [(i, (i + (even_step if i % 2 == 0 else -even_s...  20.7 us
    ppermute x13, waiting for transfers between devices, exchange(): lax.ppermute(value, axis, [(i, (i + (even_step if i % 2 == 0 else -even_s...  8.05 us
    unnamed x6, local copies, waits for them, and re-layouts  1.38 us
  transfers between devices with their start and end apart: 13, of which 4 were waited for; matrix products, arithmetic and copies ran while one was open for 0% of the time, Pallas kernels for 36%

profile of v9, /device:TPU:0, one launch (start us, length us, event | category | flops | bytes accessed | tf_op | source)
XLA Modules:
  0.0 52.7 jit_solution(18352073549011463500)
XLA Ops:
  0.0 0.1 pad_add_fusion.info
  0.1 0.0 copy-start.1
  0.1 1.4 %copy-done.1 = f32[576,576]{1,0:T(8,128)S(1)} copy-done((f32[576,576]{1,0:T(8,128)S(1)}, f32[576,576]{1,0:T(8,128)}, u32[]{:S(2)}) %copy-start.1) | copy-done | bytes 1327128
  1.4 1.2 %pack_first.1 = (f32[864,128]{1,0:T(8,128)S(1)}, f32[1152,128]{1,0:T(8,128)S(1)}, f32[1728,128]{1,0:T(8,128)S(1)}) custom-call(s32[2]{0:T(128)S(1)} %pad_add_fusion.info, f32[576,576]{1,0:T(8,128)S(1)} %copy-done.1), custom_call_target="tpu_custom_call" | custom-call | flops 4000000000 | bytes 20000000 | tf_op jit(solution)/shard_map/pack_first/pallas_call | solution.py:291
  2.7 0.5 collective-permute-start.2
  3.2 2.6 %collective-permute-start.1 = (f32[864,128]{1,0:T(8,128)S(1)}, f32[864,128]{1,0:T(8,128)S(1)}, u32[]{:S(2)}, u32[]{:S(2)}) collective-permute-start(f32[864,128]{1,0:T(8,128)S(1)} %get-tuple-element.45), channel_id=1, source_target_pairs={{0,8},{8,0},{16,24},{24,16},{1,9},{9,1},{17,25},{25,17},{2,10},{10... | collective-permute-start | bytes 1327112 | tf_op jit(solution)/shard_map/ppermute | solution.py:319
  5.8 3.4 %collective-permute-start = (f32[1152,128]{1,0:T(8,128)S(1)}, f32[1152,128]{1,0:T(8,128)S(1)}, u32[]{:S(2)}, u32[]{:S(2)}) collective-permute-start(f32[1152,128]{1,0:T(8,128)S(1)} %get-tuple-element.44), channel_id=1, source_target_pairs={{0,7},{1,2},{2,1},{3,4},{4,3},{5,6},{6,5},{7,0},{8,15},{9,10},{10,... | collective-permute-start | bytes 1769480 | tf_op jit(solution)/shard_map/ppermute | solution.py:319
  9.1 0.0 collective-permute-done.2.chip
  9.1 0.8 %pack_rest.1 = (f32[576,128]{1,0:T(8,128)S(1)}, f32[864,128]{1,0:T(8,128)S(1)}, f32[864,128]{1,0:T(8,128)S(1)}) custom-call(s32[2]{0:T(128)S(1)} %pad_add_fusion.info, f32[576,576]{1,0:T(8,128)S(1)} %copy-done.1), custom_call_target="tpu_custom_call" | custom-call | flops 4000000000 | bytes 20000000 | tf_op jit(solution)/shard_map/pack_rest/pallas_call | solution.py:291
  9.9 0.9 %collective-permute-start.4 = (f32[576,128]{1,0:T(8,128)S(1)}, f32[576,128]{1,0:T(8,128)S(1)}, u32[]{:S(2)}, u32[]{:S(2)}) collective-permute-start(f32[576,128]{1,0:T(8,128)S(1)} %get-tuple-element.58), channel_id=1, source_target_pairs={{0,7},{1,2},{2,1},{3,4},{4,3},{5,6},{6,5},{7,0},{8,15},{9,10},{10,... | collective-permute-start | bytes 884744 | tf_op jit(solution)/shard_map/ppermute | solution.py:319
  10.8 1.5 %collective-permute-start.6 = (f32[864,128]{1,0:T(8,128)S(1)}, f32[864,128]{1,0:T(8,128)S(1)}, u32[]{:S(2)}, u32[]{:S(2)}) collective-permute-start(f32[864,128]{1,0:T(8,128)S(1)} %get-tuple-element.59), channel_id=1, source_target_pairs={{0,16},{8,24},{16,0},{24,8},{1,17},{9,25},{17,1},{25,9},{2,18},{10... | collective-permute-start | bytes 1327112 | tf_op jit(solution)/shard_map/ppermute | solution.py:319
  12.3 1.5 %collective-permute-start.7 = (f32[864,128]{1,0:T(8,128)S(1)}, f32[864,128]{1,0:T(8,128)S(1)}, u32[]{:S(2)}, u32[]{:S(2)}) collective-permute-start(f32[864,128]{1,0:T(8,128)S(1)} %get-tuple-element.63), channel_id=1, source_target_pairs={{0,8},{8,0},{16,24},{24,16},{1,9},{9,1},{17,25},{25,17},{2,10},{10... | collective-permute-start | bytes 1327112 | tf_op jit(solution)/shard_map/ppermute | solution.py:319
  13.8 1.0 %prepare.1 = (bf16[2,3,576,256]{3,2,1,0:T(8,128)(2,1)S(1)}, bf16[2,3,768,256]{3,2,1,0:T(8,128)(2,1)S(1)}, bf16[2,3,384,256]{3,2,1,0:T(8,128)(2,1)S(1)}) custom-call(s32[2]{0:T(128)S(1)} %pad_add_fusion.info, f32[576,576]{1,0:T(8,128)S(1)} %copy-done.1, f32[1728,128]{1,0:T(8,128)S(1)} %collective-permute-done.2.chip), custom_call_target="tpu_custom_call" | custom-call | flops 4000000000 | bytes 20000000 | tf_op jit(solution)/shard_map/prepare/pallas_call | solution.py:291
  14.8 1.9 %collective-permute-done.1.mid = f32[864,128]{1,0:T(8,128)S(1)} collective-permute-done((f32[864,128]{1,0:T(8,128)S(1)}, f32[864,128]{1,0:T(8,128)S(1)}, u32[]{:S(2)}, u32[]{:S(2)}) %collective-permute-start.1) | collective-permute-done | bytes 442400 | tf_op jit(solution)/shard_map/ppermute | solution.py:319
  16.8 2.0 %collective-permute-start.5 = (f32[864,128]{1,0:T(8,128)S(1)}, f32[864,128]{1,0:T(8,128)S(1)}, u32[]{:S(2)}, u32[]{:S(2)}) collective-permute-start(f32[864,128]{1,0:T(8,128)S(1)} %collective-permute-done.1.mid), channel_id=1, source_target_pairs={{0,16},{8,24},{16,0},{24,8},{1,17},{9,25},{17,1},{25,9},{2,18},{10... | collective-permute-start | bytes 1327112 | tf_op jit(solution)/shard_map/ppermute | solution.py:319
  18.8 0.0 copy-start
  18.8 1.6 %near_start.1 = (f32[576,256]{1,0:T(8,128)S(1)}, bf16[2,768,256]{2,1,0:T(8,128)(2,1)S(1)}) custom-call(s32[2]{0:T(128)S(1)} %pad_add_fusion.info, f32[864,128]{1,0:T(8,128)S(1)} %collective-permute-done.1.mid, bf16[2,3,576,256]{3,2,1,0:T(8,128)(2,1)S(1)} %get-tuple-element.50.own_left, bf16[2,3,768,256]{3,2,1,0:T(8,128)(2,1)S(1)} %get-tuple-element.51.own_right, ...), custom_call_target="tpu_custom_call" | custom-call | flops 4000000000 | bytes 20000000 | tf_op jit(solution)/shard_map/near_start/pallas_call | solution.py:291
  20.3 2.6 %collective-permute-done.link_a = f32[1152,128]{1,0:T(8,128)S(1)} collective-permute-done((f32[1152,128]{1,0:T(8,128)S(1)}, f32[1152,128]{1,0:T(8,128)S(1)}, u32[]{:S(2)}, u32[]{:S(2)}) %collective-permute-start) | collective-permute-done | bytes 589856 | tf_op jit(solution)/shard_map/ppermute | solution.py:319
  22.9 0.0 copy-done
  22.9 1.4 %square_near.1 = (f32[576,256]{1,0:T(8,128)S(1)}, f32[576,128]{1,0:T(8,128)S(1)}, bf16[2,2,384,256]{3,2,1,0:T(8,128)(2,1)S(1)}) custom-call(s32[2]{0:T(128)S(1)} %pad_add_fusion.info, s32[9,9]{1,0:T(8,128)S(1)} %copy-done, f32[1152,128]{1,0:T(8,128)S(1)} %collective-permute-done.link_a, f32[576,256]{1,0:T(8,128)S(1)} %get-tuple-element.53.begun, ...), custom_call_target="tpu_custom_call" | custom-call | flops 4000000000 | bytes 20000000 | tf_op jit(solution)/shard_map/square_near/pallas_call | solution.py:291
  24.4 3.7 %collective-permute-start.3 = (f32[576,128]{1,0:T(8,128)S(1)}, f32[576,128]{1,0:T(8,128)S(1)}, u32[]{:S(2)}, u32[]{:S(2)}) collective-permute-start(f32[576,128]{1,0:T(8,128)S(1)} %get-tuple-element.55), channel_id=1, source_target_pairs={{0,7},{1,2},{2,1},{3,4},{4,3},{5,6},{6,5},{7,0},{8,15},{9,10},{10,... | collective-permute-start | bytes 884744 | tf_op jit(solution)/shard_map/ppermute | solution.py:319
  28.1 0.0 collective-permute-done.6
  28.1 0.5 %collective-permute-start.8 = (f32[864,128]{1,0:T(8,128)S(1)}, f32[864,128]{1,0:T(8,128)S(1)}, u32[]{:S(2)}, u32[]{:S(2)}) collective-permute-start(f32[864,128]{1,0:T(8,128)S(1)} %collective-permute-done.6), channel_id=1, source_target_pairs={{0,8},{8,0},{16,24},{24,16},{1,9},{9,1},{17,25},{25,17},{2,10},{10... | collective-permute-start | bytes 1327112 | tf_op jit(solution)/shard_map/ppermute | solution.py:319
  28.6 1.9 %middle_products.1 = (f32[576,256]{1,0:T(8,128)S(1)}, f32[576,256]{1,0:T(8,128)S(1)}) custom-call(s32[2]{0:T(128)S(1)} %pad_add_fusion.info, bf16[2,3,576,256]{3,2,1,0:T(8,128)(2,1)S(1)} %get-tuple-element.50.own_left, bf16[2,3,768,256]{3,2,1,0:T(8,128)(2,1)S(1)} %get-tuple-element.51.own_right, bf16[2,3,384,256]{3,2,1,0:T(8,128)(2,1)S(1)} %get-tuple-element.52.chip_left, ...), custom_call_target="tpu_custom_call" | custom-call | flops 4000000000 | bytes 20000000 | tf_op jit(solution)/shard_map/middle_products/pallas_call | solution.py:291
  30.5 0.0 collective-permute-done.7.near
  30.5 1.4 %mid_start.1 = (f32[576,256]{1,0:T(8,128)S(1)}, bf16[2,768,256]{2,1,0:T(8,128)(2,1)S(1)}) custom-call(s32[2]{0:T(128)S(1)} %pad_add_fusion.info, f32[864,128]{1,0:T(8,128)S(1)} %collective-permute-done.7.near, f32[576,256]{1,0:T(8,128)S(1)} %get-tuple-element.64.begun, bf16[2,3,576,256]{3,2,1,0:T(8,128)(2,1)S(1)} %get-tuple-element.50.own_left, ...), custom_call_target="tpu_custom_call" | custom-call | flops 4000000000 | bytes 20000000 | tf_op jit(solution)/shard_map/mid_start/pallas_call | solution.py:291
  31.9 0.0 collective-permute-done.4.link_b
  31.9 0.0 collective-permute-done.5.mid
  32.0 1.9 %square_far.1 = (f32[576,256]{1,0:T(8,128)S(1)}, f32[576,128]{1,0:T(8,128)S(1)}, f32[1152,128]{1,0:T(8,128)S(1)}, bf16[2,384,256]{2,1,0:T(8,128)(2,1)S(1)}, bf16[2,768,256]{2,1,0:T(8,128)(2,1)S(1)}) custom-call(s32[2]{0:T(128)S(1)} %pad_add_fusion.info, s32[9,9]{1,0:T(8,128)S(1)} %copy-done, f32[576,128]{1,0:T(8,128)S(1)} %collective-permute-done.4.link_b, ...), custom_call_target="tpu_custom_call" | custom-call | flops 4000000000 | bytes 20000000 | tf_op jit(solution)/shard_map/square_far/pallas_call | solution.py:291
  33.8 2.3 %collective-permute-start.12 = (f32[576,128]{1,0:T(8,128)S(1)}, f32[576,128]{1,0:T(8,128)S(1)}, u32[]{:S(2)}, u32[]{:S(2)}) collective-permute-start(f32[576,128]{1,0:T(8,128)S(1)} %get-tuple-element.78), channel_id=1, source_target_pairs={{0,7},{1,2},{2,1},{3,4},{4,3},{5,6},{6,5},{7,0},{8,15},{9,10},{10,... | collective-permute-start | bytes 884744 | tf_op jit(solution)/shard_map/ppermute | solution.py:319
  36.1 0.0 collective-permute-start.10
  36.1 0.0 collective-permute-done.3.link
  36.1 1.8 %cube_near.1.total = f32[3,576,256]{2,1,0:T(8,128)S(1)} custom-call(s32[2]{0:T(128)S(1)} %pad_add_fusion.info, f32[576,128]{1,0:T(8,128)S(1)} %collective-permute-done.3.link, f32[576,256]{1,0:T(8,128)S(1)} %get-tuple-element.56.s_near.near, f32[576,256]{1,0:T(8,128)S(1)} %get-tuple-element.67.far, bf16[2,768,256]{2,1,0:T(8,128)(2,1)S(1)} %get-tuple-element.54.right_near, ...), custom_call_target="tpu_custom_call" | custom-call | flops 4000000000 | bytes 20000000 | tf_op jit(solution)/shard_map/cube_near/pallas_call | solution.py:291
  37.9 0.0 collective-permute-done.8.far
  37.9 1.9 %square_mid.1 = (f32[576,256]{1,0:T(8,128)S(1)}, f32[576,128]{1,0:T(8,128)S(1)}, f32[576,128]{1,0:T(8,128)S(1)}, bf16[2,768,256]{2,1,0:T(8,128)(2,1)S(1)}) custom-call(s32[2]{0:T(128)S(1)} %pad_add_fusion.info, s32[9,9]{1,0:T(8,128)S(1)} %copy-done, f32[864,128]{1,0:T(8,128)S(1)} %collective-permute-done.8.far, ...), custom_call_target="tpu_custom_call" | custom-call | tf_op jit(solution)/shard_map/square_mid/pallas_call | solution.py:291
  39.8 1.8 %collective-permute-start.9 = (f32[576,128]{1,0:T(8,128)S(1)}, f32[576,128]{1,0:T(8,128)S(1)}, u32[]{:S(2)}, u32[]{:S(2)}) collective-permute-start(f32[576,128]{1,0:T(8,128)S(1)} %get-tuple-element.74), channel_id=1, source_target_pairs={{0,7},{1,2},{2,1},{3,4},{4,3},{5,6},{6,5},{7,0},{8,15},{9,10},{10,... | collective-permute-start | bytes 884744 | tf_op jit(solution)/shard_map/ppermute | solution.py:319
  41.6 0.0 collective-permute-start.11
  41.6 3.4 %collective-permute-done.12.link = f32[576,128]{1,0:T(8,128)S(1)} collective-permute-done((f32[576,128]{1,0:T(8,128)S(1)}, f32[576,128]{1,0:T(8,128)S(1)}, u32[]{:S(2)}, u32[]{:S(2)}) %collective-permute-start.12) | collective-permute-done | bytes 294944 | tf_op jit(solution)/shard_map/ppermute | solution.py:319
  45.0 0.0 copy-start.2
  45.0 2.1 %cube_own.1.base = f32[3,576,256]{2,1,0:T(8,128)S(1)} custom-call(s32[2]{0:T(128)S(1)} %pad_add_fusion.info, f32[576,128]{1,0:T(8,128)S(1)} %collective-permute-done.12.link, f32[3,576,256]{2,1,0:T(8,128)S(1)} %cube_near.1.total, f32[576,256]{1,0:T(8,128)S(1)} %get-tuple-element.56.s_near.near, f32[576,256]{1,0:T(8,128)S(1)} %get-tuple-element.80.mid, ...), custom_call_target="tpu_custom_call" | custom-call | flops 4000000000 | bytes 20000000 | tf_op jit(solution)/shard_map/cube_own/pallas_call | solution.py:291
  47.1 0.0 collective-permute-done.10.sides
  47.1 0.0 collective-permute-done.11.chip
  47.2 0.0 copy-done.2
  47.2 3.2 %cube_chip.1 = (f32[3,576,256]{2,1,0:T(8,128)S(1)}, f32[576,576]{1,0:T(8,128)}) custom-call(s32[2]{0:T(128)S(1)} %pad_add_fusion.info, s32[9,9]{1,0:T(8,128)S(1)} %copy-done.2, f32[1152,128]{1,0:T(8,128)S(1)} %collective-permute-done.10.sides, f32[576,128]{1,0:T(8,128)S(1)} %collective-permute-done.11.chip, ...), custom_call_target="tpu_custom_call" | custom-call | flops 4000000000 | bytes 20000000 | tf_op jit(solution)/shard_map/cube_chip/pallas_call | solution.py:291
  50.3 0.1 collective-permute-done.9.link
  50.5 2.2 %finish.1 = f32[576,576]{1,0:T(8,128)} custom-call(s32[2]{0:T(128)S(1)} %pad_add_fusion.info, s32[9,9]{1,0:T(8,128)S(1)} %copy-done.2, f32[576,128]{1,0:T(8,128)S(1)} %collective-permute-done.9.link, bf16[2,3,768,256]{3,2,1,0:T(8,128)(2,1)S(1)} %get-tuple-element.51.own_right, ...), custom_call_target="tpu_custom_call", output_to_operand_aliasing={{}: (5, {})} | custom-call | flops 4000000000 | bytes 20000000 | tf_op jit(solution)/shard_map/finish/pallas_call | solution.py:291
Async XLA Ops:
  0.1 1.4 %copy-start.1 = (f32[576,576]{1,0:T(8,128)S(1)}, f32[576,576]{1,0:T(8,128)}, u32[]{:S(2)}) copy-start(f32[576,576]{1,0:T(8,128)} %tile.4) | copy-start | bytes 3981316
  2.7 6.5 %collective-permute-start.2 = (f32[1728,128]{1,0:T(8,128)S(1)}, f32[1728,128]{1,0:T(8,128)S(1)}, u32[]{:S(2)}, u32[]{:S(2)}) collective-permute-start(f32[1728,128]{1,0:T(8,128)S(1)} %get-tuple-element.46), channel_id=1, source_target_pairs={{0,1},{1,0},{2,3},{3,2},{4,5},{5,4},{6,7},{7,6},{8,9},{9,8},{10,11... | collective-permute-start | bytes 2654216 | tf_op jit(solution)/shard_map/ppermute | solution.py:319
  3.2 13.6 %collective-permute-start.1 = (f32[864,128]{1,0:T(8,128)S(1)}, f32[864,128]{1,0:T(8,128)S(1)}, u32[]{:S(2)}, u32[]{:S(2)}) collective-permute-start(f32[864,128]{1,0:T(8,128)S(1)} %get-tuple-element.45), channel_id=1, source_target_pairs={{0,8},{8,0},{16,24},{24,16},{1,9},{9,1},{17,25},{25,17},{2,10},{10... | collective-permute-start | bytes 1327112 | tf_op jit(solution)/shard_map/ppermute | solution.py:319
  5.8 17.2 %collective-permute-start = (f32[1152,128]{1,0:T(8,128)S(1)}, f32[1152,128]{1,0:T(8,128)S(1)}, u32[]{:S(2)}, u32[]{:S(2)}) collective-permute-start(f32[1152,128]{1,0:T(8,128)S(1)} %get-tuple-element.44), channel_id=1, source_target_pairs={{0,7},{1,2},{2,1},{3,4},{4,3},{5,6},{6,5},{7,0},{8,15},{9,10},{10,... | collective-permute-start | bytes 1769480 | tf_op jit(solution)/shard_map/ppermute | solution.py:319
  9.9 22.0 %collective-permute-start.4 = (f32[576,128]{1,0:T(8,128)S(1)}, f32[576,128]{1,0:T(8,128)S(1)}, u32[]{:S(2)}, u32[]{:S(2)}) collective-permute-start(f32[576,128]{1,0:T(8,128)S(1)} %get-tuple-element.58), channel_id=1, source_target_pairs={{0,7},{1,2},{2,1},{3,4},{4,3},{5,6},{6,5},{7,0},{8,15},{9,10},{10,... | collective-permute-start | bytes 884744 | tf_op jit(solution)/shard_map/ppermute | solution.py:319
  10.8 17.3 %collective-permute-start.6 = (f32[864,128]{1,0:T(8,128)S(1)}, f32[864,128]{1,0:T(8,128)S(1)}, u32[]{:S(2)}, u32[]{:S(2)}) collective-permute-start(f32[864,128]{1,0:T(8,128)S(1)} %get-tuple-element.59), channel_id=1, source_target_pairs={{0,16},{8,24},{16,0},{24,8},{1,17},{9,25},{17,1},{25,9},{2,18},{10... | collective-permute-start | bytes 1327112 | tf_op jit(solution)/shard_map/ppermute | solution.py:319
  12.3 18.2 %collective-permute-start.7 = (f32[864,128]{1,0:T(8,128)S(1)}, f32[864,128]{1,0:T(8,128)S(1)}, u32[]{:S(2)}, u32[]{:S(2)}) collective-permute-start(f32[864,128]{1,0:T(8,128)S(1)} %get-tuple-element.63), channel_id=1, source_target_pairs={{0,8},{8,0},{16,24},{24,16},{1,9},{9,1},{17,25},{25,17},{2,10},{10... | collective-permute-start | bytes 1327112 | tf_op jit(solution)/shard_map/ppermute | solution.py:319
  16.8 15.2 %collective-permute-start.5 = (f32[864,128]{1,0:T(8,128)S(1)}, f32[864,128]{1,0:T(8,128)S(1)}, u32[]{:S(2)}, u32[]{:S(2)}) collective-permute-start(f32[864,128]{1,0:T(8,128)S(1)} %collective-permute-done.1.mid), channel_id=1, source_target_pairs={{0,16},{8,24},{16,0},{24,8},{1,17},{9,25},{17,1},{25,9},{2,18},{10... | collective-permute-start | bytes 1327112 | tf_op jit(solution)/shard_map/ppermute | solution.py:319
  18.8 4.2 %copy-start = (s32[9,9]{1,0:T(8,128)S(1)}, s32[9,9]{1,0:T(8,128)}, u32[]{:S(2)}) copy-start(s32[9,9]{1,0:T(8,128)} %kept.7) | copy-start | bytes 976
  24.4 11.8 %collective-permute-start.3 = (f32[576,128]{1,0:T(8,128)S(1)}, f32[576,128]{1,0:T(8,128)S(1)}, u32[]{:S(2)}, u32[]{:S(2)}) collective-permute-start(f32[576,128]{1,0:T(8,128)S(1)} %get-tuple-element.55), channel_id=1, source_target_pairs={{0,7},{1,2},{2,1},{3,4},{4,3},{5,6},{6,5},{7,0},{8,15},{9,10},{10,... | collective-permute-start | bytes 884744 | tf_op jit(solution)/shard_map/ppermute | solution.py:319
  28.1 9.8 %collective-permute-start.8 = (f32[864,128]{1,0:T(8,128)S(1)}, f32[864,128]{1,0:T(8,128)S(1)}, u32[]{:S(2)}, u32[]{:S(2)}) collective-permute-start(f32[864,128]{1,0:T(8,128)S(1)} %collective-permute-done.6), channel_id=1, source_target_pairs={{0,8},{8,0},{16,24},{24,16},{1,9},{9,1},{17,25},{25,17},{2,10},{10... | collective-permute-start | bytes 1327112 | tf_op jit(solution)/shard_map/ppermute | solution.py:319
  33.8 11.2 %collective-permute-start.12 = (f32[576,128]{1,0:T(8,128)S(1)}, f32[576,128]{1,0:T(8,128)S(1)}, u32[]{:S(2)}, u32[]{:S(2)}) collective-permute-start(f32[576,128]{1,0:T(8,128)S(1)} %get-tuple-element.78), channel_id=1, source_target_pairs={{0,7},{1,2},{2,1},{3,4},{4,3},{5,6},{6,5},{7,0},{8,15},{9,10},{10,... | collective-permute-start | bytes 884744 | tf_op jit(solution)/shard_map/ppermute | solution.py:319
  36.1 11.0 %collective-permute-start.10 = (f32[1152,128]{1,0:T(8,128)S(1)}, f32[1152,128]{1,0:T(8,128)S(1)}, u32[]{:S(2)}, u32[]{:S(2)}) collective-permute-start(f32[1152,128]{1,0:T(8,128)S(1)} %get-tuple-element.75), channel_id=1, source_target_pairs={{0,1},{1,0},{2,3},{3,2},{4,5},{5,4},{6,7},{7,6},{8,9},{9,8},{10,11... | collective-permute-start | bytes 1769480 | tf_op jit(solution)/shard_map/ppermute | solution.py:319
  39.8 10.6 %collective-permute-start.9 = (f32[576,128]{1,0:T(8,128)S(1)}, f32[576,128]{1,0:T(8,128)S(1)}, u32[]{:S(2)}, u32[]{:S(2)}) collective-permute-start(f32[576,128]{1,0:T(8,128)S(1)} %get-tuple-element.74), channel_id=1, source_target_pairs={{0,7},{1,2},{2,1},{3,4},{4,3},{5,6},{6,5},{7,0},{8,15},{9,10},{10,... | collective-permute-start | bytes 884744 | tf_op jit(solution)/shard_map/ppermute | solution.py:319
  41.6 5.5 %collective-permute-start.11 = (f32[576,128]{1,0:T(8,128)S(1)}, f32[576,128]{1,0:T(8,128)S(1)}, u32[]{:S(2)}, u32[]{:S(2)}) collective-permute-start(f32[576,128]{1,0:T(8,128)S(1)} %get-tuple-element.76), channel_id=1, source_target_pairs={{0,1},{1,0},{2,3},{3,2},{4,5},{5,4},{6,7},{7,6},{8,9},{9,8},{10,11... | collective-permute-start | bytes 884744 | tf_op jit(solution)/shard_map/ppermute | solution.py:319
  45.0 2.2 %copy-start.2 = (s32[9,9]{1,0:T(8,128)S(1)}, s32[9,9]{1,0:T(8,128)}, u32[]{:S(2)}) copy-start(s32[9,9]{1,0:T(8,128)} %kept.9) | copy-start | bytes 976

commit v10 on v9

--- a/solution.py
+++ b/solution.py
@@ -159,15 +159,18 @@
     store_fold(link, 0, out[shared_rows(info, LINK, group), :])
 
 
-def middle_products_body(info, own_left, own_right, chip_left, link_left, far, mid):
+def middle_products_body(info, own_left, own_right, chip_left, far, mid):
     group = far.shape[0] // 3
     for out, part in ((far, FAR), (mid, MID)):
-        for who, lefts in ((OWN, own_left), (CHIP, chip_left), (LINK, link_left)):
-            value = passes([left(lefts, MID)], [right(own_right, info, who, part)])
-            if who == OWN:
-                out[...] = value
-            else:
-                out[shared_rows(info, who, group), :] += value
+        out[...] = passes([left(own_left, MID)], [right(own_right, info, OWN, part)])
+        out[shared_rows(info, CHIP, group), :] += passes([left(chip_left, MID)], [right(own_right, info, CHIP, part)])
+
+
+def middle_link_body(info, own_right, link_left, begun_far, begun_mid, far, mid):
+    group = far.shape[0] // 3
+    for out, begun, part in ((far, begun_far, FAR), (mid, begun_mid, MID)):
+        out[...] = begun[...]
+        out[shared_rows(info, LINK, group), :] += passes([left(link_left, MID)], [right(own_right, info, LINK, part)])
 
 
 def far_body(info, kept, link_b, mid, begun, s_near, own_left, chip_left, out, link, sides, link_left, rights):
@@ -339,7 +342,10 @@
         (p_tiles, chip),
         [((2, 3, side, WIDE), BF16), ((2, 3, 3 * WIDE, WIDE), BF16), ((2, 3, 2 * group, WIDE), BF16)],
     )
-    partner_mid, own_left = lax.optimization_barrier((partner_mid, own_left))
+    begun_far, begun_mid = call(
+        middle_products_body, "middle_products", (info,), (own_left, own_right, chip_left), [wide] * 2
+    )
+    partner_mid, own_left, begun_mid = lax.optimization_barrier((partner_mid, own_left, begun_mid))
     other_mid = exchange(partner_mid, "row", 2)
     begun, right_near = call(
         near_start_body, "near_start", (info,), (partner_mid, own_left, own_right, chip_left), [wide, rights]
@@ -354,8 +360,8 @@
     near_link = exchange(near_link, "col", -1)
     passed_far, link_left = lax.optimization_barrier((passed_far, link_left))
     other_far = exchange(passed_far, "row", 1)
-    begun, begun_mid = call(
-        middle_products_body, "middle_products", (info,), (own_left, own_right, chip_left, link_left), [wide] * 2
+    begun_far, begun_mid = call(
+        middle_link_body, "middle_link", (info,), (own_right, link_left, begun_far, begun_mid), [wide] * 2
     )
     begun_mid, mid_near = call(
         mid_start_body,
@@ -364,16 +370,17 @@
         (partner_near, begun_mid, own_left, chip_left, link_left),
         [wide, rights],
     )
-    begun, begun_mid = lax.optimization_barrier((begun, begun_mid))
+    begun_far, begun_mid = lax.optimization_barrier((begun_far, begun_mid))
     s_far, far_link, sides_chip, link_left_far, right_far = call(
         far_body,
         "square_far",
         (info, square_kept),
-        (link_b, other_mid, begun, s_near, own_left, chip_left),
+        (link_b, other_mid, begun_far, s_near, own_left, chip_left),
         [wide, slab, two_slabs, ((2, 2 * group, WIDE), BF16), rights],
     )
     far_link = exchange(far_link, "col", -1)
     sides_chip = exchange(sides_chip, "col", 1)
+    near_link, other_far = lax.optimization_barrier((near_link, other_far))
     (total,) = call(
         cube_near_body,
         "cube_near",

time: 52.8 us -> 53.3 us (level)
  waiting for transfers between devices: 8.05 us -> 5.34 us
  starting transfers between devices: 20.7 us -> 23.1 us
  Pallas kernels: 22.3 us -> 23.1 us
    ppermute x13, waiting for transfers between devices: 8.05 us -> 5.34 us  [exchange(): lax.ppermute(value, axis, [(i, (i + (even_step if i % 2 == 0 else -even_s...]
    ppermute x13, starting transfers between devices: 20.7 us -> 23.1 us  [exchange(): lax.ppermute(value, axis, [(i, (i + (even_step if i % 2 == 0 else -even_s...]
    pallas_call x13 -> x14, Pallas kernels: 22.3 us -> 23.1 us  [call(): pl.pallas_call(body, out_shape=[jax.ShapeDtypeStruct(shape, kind) for sha...]
  transfers between devices with their start and end apart: 13 -> 13, of which waited for: 4 -> 5; matrix products, arithmetic and copies ran while one was open for 0% -> 0% of each run, Pallas kernels for 36% -> 37%
where the time goes in v10:
time: 53.3 us; the launch traced here: 53.1 us
  Pallas kernels  23.1 us (43%)
  starting transfers between devices  23.1 us (43%)
  waiting for transfers between devices  5.34 us (10%)
  local copies, waits for them, and re-layouts  1.38 us (3%)
    ppermute x13, starting transfers between devices, exchange(): lax.ppermute(value, axis, [(i, (i + (even_step if i % 2 == 0 else -even_s...  23.1 us
    pallas_call x14, Pallas kernels, call(): pl.pallas_call(body, out_shape=[jax.ShapeDtypeStruct(shape, kind) for sha...  23.1 us
    ppermute x13, waiting for transfers between devices, exchange(): lax.ppermute(value, axis, [(i, (i + (even_step if i % 2 == 0 else -even_s...  5.34 us
    unnamed x6, local copies, waits for them, and re-layouts  1.38 us
  transfers between devices with their start and end apart: 13, of which 5 were waited for; matrix products, arithmetic and copies ran while one was open for 0% of the time, Pallas kernels for 37%

profile of v10, /device:TPU:0, one launch (start us, length us, event | category | flops | bytes accessed | tf_op | source)
XLA Modules:
  0.0 53.1 jit_solution(2264601303463350074)
XLA Ops:
  0.0 0.1 pad_add_fusion.info
  0.1 0.0 copy-start.1
  0.1 1.4 %copy-done.1 = f32[576,576]{1,0:T(8,128)S(1)} copy-done((f32[576,576]{1,0:T(8,128)S(1)}, f32[576,576]{1,0:T(8,128)}, u32[]{:S(2)}) %copy-start.1) | copy-done | bytes 1327128
  1.4 1.2 %pack_first.1 = (f32[864,128]{1,0:T(8,128)S(1)}, f32[1152,128]{1,0:T(8,128)S(1)}, f32[1728,128]{1,0:T(8,128)S(1)}) custom-call(s32[2]{0:T(128)S(1)} %pad_add_fusion.info, f32[576,576]{1,0:T(8,128)S(1)} %copy-done.1), custom_call_target="tpu_custom_call" | custom-call | flops 4000000000 | bytes 20000000 | tf_op jit(solution)/shard_map/pack_first/pallas_call | solution.py:294
  2.7 0.5 collective-permute-start.2
  3.2 2.6 %collective-permute-start.1 = (f32[864,128]{1,0:T(8,128)S(1)}, f32[864,128]{1,0:T(8,128)S(1)}, u32[]{:S(2)}, u32[]{:S(2)}) collective-permute-start(f32[864,128]{1,0:T(8,128)S(1)} %get-tuple-element.50), channel_id=1, source_target_pairs={{0,8},{8,0},{16,24},{24,16},{1,9},{9,1},{17,25},{25,17},{2,10},{10... | collective-permute-start | bytes 1327112 | tf_op jit(solution)/shard_map/ppermute | solution.py:322
  5.8 3.4 %collective-permute-start = (f32[1152,128]{1,0:T(8,128)S(1)}, f32[1152,128]{1,0:T(8,128)S(1)}, u32[]{:S(2)}, u32[]{:S(2)}) collective-permute-start(f32[1152,128]{1,0:T(8,128)S(1)} %get-tuple-element.49), channel_id=1, source_target_pairs={{0,7},{1,2},{2,1},{3,4},{4,3},{5,6},{6,5},{7,0},{8,15},{9,10},{10,... | collective-permute-start | bytes 1769480 | tf_op jit(solution)/shard_map/ppermute | solution.py:322
  9.1 0.0 collective-permute-done.2.chip
  9.1 0.8 %pack_rest.1 = (f32[576,128]{1,0:T(8,128)S(1)}, f32[864,128]{1,0:T(8,128)S(1)}, f32[864,128]{1,0:T(8,128)S(1)}) custom-call(s32[2]{0:T(128)S(1)} %pad_add_fusion.info, f32[576,576]{1,0:T(8,128)S(1)} %copy-done.1), custom_call_target="tpu_custom_call" | custom-call | flops 4000000000 | bytes 20000000 | tf_op jit(solution)/shard_map/pack_rest/pallas_call | solution.py:294
  9.9 0.9 %collective-permute-start.6 = (f32[576,128]{1,0:T(8,128)S(1)}, f32[576,128]{1,0:T(8,128)S(1)}, u32[]{:S(2)}, u32[]{:S(2)}) collective-permute-start(f32[576,128]{1,0:T(8,128)S(1)} %get-tuple-element.68), channel_id=1, source_target_pairs={{0,7},{1,2},{2,1},{3,4},{4,3},{5,6},{6,5},{7,0},{8,15},{9,10},{10,... | collective-permute-start | bytes 884744 | tf_op jit(solution)/shard_map/ppermute | solution.py:322
  10.8 1.5 %collective-permute-start.4 = (f32[864,128]{1,0:T(8,128)S(1)}, f32[864,128]{1,0:T(8,128)S(1)}, u32[]{:S(2)}, u32[]{:S(2)}) collective-permute-start(f32[864,128]{1,0:T(8,128)S(1)} %get-tuple-element.63), channel_id=1, source_target_pairs={{0,16},{8,24},{16,0},{24,8},{1,17},{9,25},{17,1},{25,9},{2,18},{10... | collective-permute-start | bytes 1327112 | tf_op jit(solution)/shard_map/ppermute | solution.py:322
  12.3 1.5 %collective-permute-start.8 = (f32[864,128]{1,0:T(8,128)S(1)}, f32[864,128]{1,0:T(8,128)S(1)}, u32[]{:S(2)}, u32[]{:S(2)}) collective-permute-start(f32[864,128]{1,0:T(8,128)S(1)} %get-tuple-element.73), channel_id=1, source_target_pairs={{0,8},{8,0},{16,24},{24,16},{1,9},{9,1},{17,25},{25,17},{2,10},{10... | collective-permute-start | bytes 1327112 | tf_op jit(solution)/shard_map/ppermute | solution.py:322
  13.8 1.0 %prepare.1 = (bf16[2,3,576,256]{3,2,1,0:T(8,128)(2,1)S(1)}, bf16[2,3,768,256]{3,2,1,0:T(8,128)(2,1)S(1)}, bf16[2,3,384,256]{3,2,1,0:T(8,128)(2,1)S(1)}) custom-call(s32[2]{0:T(128)S(1)} %pad_add_fusion.info, f32[576,576]{1,0:T(8,128)S(1)} %copy-done.1, f32[1728,128]{1,0:T(8,128)S(1)} %collective-permute-done.2.chip), custom_call_target="tpu_custom_call" | custom-call | flops 4000000000 | bytes 20000000 | tf_op jit(solution)/shard_map/prepare/pallas_call | solution.py:294
  14.8 1.6 %middle_products.1 = (f32[576,256]{1,0:T(8,128)S(1)}, f32[576,256]{1,0:T(8,128)S(1)}) custom-call(s32[2]{0:T(128)S(1)} %pad_add_fusion.info, bf16[2,3,576,256]{3,2,1,0:T(8,128)(2,1)S(1)} %get-tuple-element.58.own_left, bf16[2,3,768,256]{3,2,1,0:T(8,128)(2,1)S(1)} %get-tuple-element.54.own_right, bf16[2,3,384,256]{3,2,1,0:T(8,128)(2,1)S(1)} %get-tuple-element.55.chip_left), custom_call_target="tpu_custom_call" | custom-call | flops 4000000000 | bytes 20000000 | tf_op jit(solution)/shard_map/middle_products/pallas_call | solution.py:294
  16.4 0.3 collective-permute-done.1.mid
  16.8 0.0 copy-start
  16.8 2.0 %collective-permute-start.7 = (f32[864,128]{1,0:T(8,128)S(1)}, f32[864,128]{1,0:T(8,128)S(1)}, u32[]{:S(2)}, u32[]{:S(2)}) collective-permute-start(f32[864,128]{1,0:T(8,128)S(1)} %collective-permute-done.1.mid), channel_id=1, source_target_pairs={{0,16},{8,24},{16,0},{24,8},{1,17},{9,25},{17,1},{25,9},{2,18},{10... | collective-permute-start | bytes 1327112 | tf_op jit(solution)/shard_map/ppermute | solution.py:322
  18.8 1.6 %near_start.1 = (f32[576,256]{1,0:T(8,128)S(1)}, bf16[2,768,256]{2,1,0:T(8,128)(2,1)S(1)}) custom-call(s32[2]{0:T(128)S(1)} %pad_add_fusion.info, f32[864,128]{1,0:T(8,128)S(1)} %collective-permute-done.1.mid, bf16[2,3,576,256]{3,2,1,0:T(8,128)(2,1)S(1)} %get-tuple-element.58.own_left, bf16[2,3,768,256]{3,2,1,0:T(8,128)(2,1)S(1)} %get-tuple-element.54.own_right, ...), custom_call_target="tpu_custom_call" | custom-call | flops 4000000000 | bytes 20000000 | tf_op jit(solution)/shard_map/near_start/pallas_call | solution.py:294
  20.3 2.6 %collective-permute-done.link_a = f32[1152,128]{1,0:T(8,128)S(1)} collective-permute-done((f32[1152,128]{1,0:T(8,128)S(1)}, f32[1152,128]{1,0:T(8,128)S(1)}, u32[]{:S(2)}, u32[]{:S(2)}) %collective-permute-start) | collective-permute-done | bytes 589856 | tf_op jit(solution)/shard_map/ppermute | solution.py:322
  22.9 0.0 copy-done
  22.9 1.4 %square_near.1 = (f32[576,256]{1,0:T(8,128)S(1)}, f32[576,128]{1,0:T(8,128)S(1)}, bf16[2,2,384,256]{3,2,1,0:T(8,128)(2,1)S(1)}) custom-call(s32[2]{0:T(128)S(1)} %pad_add_fusion.info, s32[9,9]{1,0:T(8,128)S(1)} %copy-done, f32[1152,128]{1,0:T(8,128)S(1)} %collective-permute-done.link_a, f32[576,256]{1,0:T(8,128)S(1)} %get-tuple-element.59.begun, ...), custom_call_target="tpu_custom_call" | custom-call | flops 4000000000 | bytes 20000000 | tf_op jit(solution)/shard_map/square_near/pallas_call | solution.py:294
  24.4 3.7 %collective-permute-start.3 = (f32[576,128]{1,0:T(8,128)S(1)}, f32[576,128]{1,0:T(8,128)S(1)}, u32[]{:S(2)}, u32[]{:S(2)}) collective-permute-start(f32[576,128]{1,0:T(8,128)S(1)} %get-tuple-element.61), channel_id=1, source_target_pairs={{0,7},{1,2},{2,1},{3,4},{4,3},{5,6},{6,5},{7,0},{8,15},{9,10},{10,... | collective-permute-start | bytes 884744 | tf_op jit(solution)/shard_map/ppermute | solution.py:322
  28.1 0.0 collective-permute-done.4
  28.1 0.5 collective-permute-start.5
  28.6 1.0 %middle_link.1 = (f32[576,256]{1,0:T(8,128)S(1)}, f32[576,256]{1,0:T(8,128)S(1)}) custom-call(s32[2]{0:T(128)S(1)} %pad_add_fusion.info, bf16[2,3,768,256]{3,2,1,0:T(8,128)(2,1)S(1)} %get-tuple-element.54.own_right, bf16[2,2,384,256]{3,2,1,0:T(8,128)(2,1)S(1)} %get-tuple-element.69.link_left, f32[576,256]{1,0:T(8,128)S(1)} %get-tuple-element.70.begun_far, ...), custom_call_target="tpu_custom_call" | custom-call | flops 4000000000 | bytes 20000000 | tf_op jit(solution)/shard_map/middle_link/pallas_call | solution.py:294
  29.7 0.0 collective-permute-done.8.near
  29.7 1.4 %mid_start.1 = (f32[576,256]{1,0:T(8,128)S(1)}, bf16[2,768,256]{2,1,0:T(8,128)(2,1)S(1)}) custom-call(s32[2]{0:T(128)S(1)} %pad_add_fusion.info, f32[864,128]{1,0:T(8,128)S(1)} %collective-permute-done.8.near, f32[576,256]{1,0:T(8,128)S(1)} %get-tuple-element.74.begun, bf16[2,3,576,256]{3,2,1,0:T(8,128)(2,1)S(1)} %get-tuple-element.58.own_left, ...), custom_call_target="tpu_custom_call" | custom-call | flops 4000000000 | bytes 20000000 | tf_op jit(solution)/shard_map/mid_start/pallas_call | solution.py:294
  31.1 0.0 collective-permute-done.6.link_b
  31.1 0.0 collective-permute-done.7.mid
  31.1 1.9 %square_far.1 = (f32[576,256]{1,0:T(8,128)S(1)}, f32[576,128]{1,0:T(8,128)S(1)}, f32[1152,128]{1,0:T(8,128)S(1)}, bf16[2,384,256]{2,1,0:T(8,128)(2,1)S(1)}, bf16[2,768,256]{2,1,0:T(8,128)(2,1)S(1)}) custom-call(s32[2]{0:T(128)S(1)} %pad_add_fusion.info, s32[9,9]{1,0:T(8,128)S(1)} %copy-done, f32[576,128]{1,0:T(8,128)S(1)} %collective-permute-done.6.link_b, ...), custom_call_target="tpu_custom_call" | custom-call | flops 4000000000 | bytes 20000000 | tf_op jit(solution)/shard_map/square_far/pallas_call | solution.py:294
  33.0 3.2 %collective-permute-start.12 = (f32[576,128]{1,0:T(8,128)S(1)}, f32[576,128]{1,0:T(8,128)S(1)}, u32[]{:S(2)}, u32[]{:S(2)}) collective-permute-start(f32[576,128]{1,0:T(8,128)S(1)} %get-tuple-element.88), channel_id=1, source_target_pairs={{0,7},{1,2},{2,1},{3,4},{4,3},{5,6},{6,5},{7,0},{8,15},{9,10},{10,... | collective-permute-start | bytes 884744 | tf_op jit(solution)/shard_map/ppermute | solution.py:322
  36.1 0.0 collective-permute-start.10
  36.1 0.0 collective-permute-done.3.link
  36.1 0.3 collective-permute-done.5.far
  36.4 1.8 %cube_near.1.total = f32[3,576,256]{2,1,0:T(8,128)S(1)} custom-call(s32[2]{0:T(128)S(1)} %pad_add_fusion.info, f32[576,128]{1,0:T(8,128)S(1)} %collective-permute-done.3.link, f32[576,256]{1,0:T(8,128)S(1)} %get-tuple-element.67.s_near.near, f32[576,256]{1,0:T(8,128)S(1)} %get-tuple-element.77.far, bf16[2,768,256]{2,1,0:T(8,128)(2,1)S(1)} %get-tuple-element.60.right_near, ...), custom_call_target="tpu_custom_call" | custom-call | flops 4000000000 | bytes 20000000 | tf_op jit(solution)/shard_map/cube_near/pallas_call | solution.py:294
  38.2 1.9 %square_mid.1 = (f32[576,256]{1,0:T(8,128)S(1)}, f32[576,128]{1,0:T(8,128)S(1)}, f32[576,128]{1,0:T(8,128)S(1)}, bf16[2,768,256]{2,1,0:T(8,128)(2,1)S(1)}) custom-call(s32[2]{0:T(128)S(1)} %pad_add_fusion.info, s32[9,9]{1,0:T(8,128)S(1)} %copy-done, f32[864,128]{1,0:T(8,128)S(1)} %collective-permute-done.5.far, ...), custom_call_target="tpu_custom_call" | custom-call | tf_op jit(solution)/shard_map/square_mid/pallas_call | solution.py:294
  40.1 3.3 %collective-permute-start.9 = (f32[576,128]{1,0:T(8,128)S(1)}, f32[576,128]{1,0:T(8,128)S(1)}, u32[]{:S(2)}, u32[]{:S(2)}) collective-permute-start(f32[576,128]{1,0:T(8,128)S(1)} %get-tuple-element.84), channel_id=1, source_target_pairs={{0,7},{1,2},{2,1},{3,4},{4,3},{5,6},{6,5},{7,0},{8,15},{9,10},{10,... | collective-permute-start | bytes 884744 | tf_op jit(solution)/shard_map/ppermute | solution.py:322
  43.4 0.0 collective-permute-start.11
  43.4 0.8 %collective-permute-done.12.link = f32[576,128]{1,0:T(8,128)S(1)} collective-permute-done((f32[576,128]{1,0:T(8,128)S(1)}, f32[576,128]{1,0:T(8,128)S(1)}, u32[]{:S(2)}, u32[]{:S(2)}) %collective-permute-start.12) | collective-permute-done | bytes 294944 | tf_op jit(solution)/shard_map/ppermute | solution.py:322
  44.2 0.0 copy-start.2
  44.2 2.1 %cube_own.1.base = f32[3,576,256]{2,1,0:T(8,128)S(1)} custom-call(s32[2]{0:T(128)S(1)} %pad_add_fusion.info, f32[576,128]{1,0:T(8,128)S(1)} %collective-permute-done.12.link, f32[3,576,256]{2,1,0:T(8,128)S(1)} %cube_near.1.total, f32[576,256]{1,0:T(8,128)S(1)} %get-tuple-element.67.s_near.near, f32[576,256]{1,0:T(8,128)S(1)} %get-tuple-element.90.mid, ...), custom_call_target="tpu_custom_call" | custom-call | flops 4000000000 | bytes 20000000 | tf_op jit(solution)/shard_map/cube_own/pallas_call | solution.py:294
  46.3 0.0 collective-permute-done.10.sides
  46.3 0.0 collective-permute-done.11.chip
  46.3 0.0 copy-done.2
  46.4 3.2 %cube_chip.1 = (f32[3,576,256]{2,1,0:T(8,128)S(1)}, f32[576,576]{1,0:T(8,128)}) custom-call(s32[2]{0:T(128)S(1)} %pad_add_fusion.info, s32[9,9]{1,0:T(8,128)S(1)} %copy-done.2, f32[1152,128]{1,0:T(8,128)S(1)} %collective-permute-done.10.sides, f32[576,128]{1,0:T(8,128)S(1)} %collective-permute-done.11.chip, ...), custom_call_target="tpu_custom_call" | custom-call | flops 4000000000 | bytes 20000000 | tf_op jit(solution)/shard_map/cube_chip/pallas_call | solution.py:294
  49.6 1.3 %collective-permute-done.9.link = f32[576,128]{1,0:T(8,128)S(1)} collective-permute-done((f32[576,128]{1,0:T(8,128)S(1)}, f32[576,128]{1,0:T(8,128)S(1)}, u32[]{:S(2)}, u32[]{:S(2)}) %collective-permute-start.9) | collective-permute-done | bytes 294944 | tf_op jit(solution)/shard_map/ppermute | solution.py:322
  50.9 2.2 %finish.1 = f32[576,576]{1,0:T(8,128)} custom-call(s32[2]{0:T(128)S(1)} %pad_add_fusion.info, s32[9,9]{1,0:T(8,128)S(1)} %copy-done.2, f32[576,128]{1,0:T(8,128)S(1)} %collective-permute-done.9.link, bf16[2,3,768,256]{3,2,1,0:T(8,128)(2,1)S(1)} %get-tuple-element.54.own_right, ...), custom_call_target="tpu_custom_call", output_to_operand_aliasing={{}: (5, {})} | custom-call | flops 4000000000 | bytes 20000000 | tf_op jit(solution)/shard_map/finish/pallas_call | solution.py:294
Async XLA Ops:
  0.1 1.4 %copy-start.1 = (f32[576,576]{1,0:T(8,128)S(1)}, f32[576,576]{1,0:T(8,128)}, u32[]{:S(2)}) copy-start(f32[576,576]{1,0:T(8,128)} %tile.4) | copy-start | bytes 3981316
  2.7 6.5 %collective-permute-start.2 = (f32[1728,128]{1,0:T(8,128)S(1)}, f32[1728,128]{1,0:T(8,128)S(1)}, u32[]{:S(2)}, u32[]{:S(2)}) collective-permute-start(f32[1728,128]{1,0:T(8,128)S(1)} %get-tuple-element.51), channel_id=1, source_target_pairs={{0,1},{1,0},{2,3},{3,2},{4,5},{5,4},{6,7},{7,6},{8,9},{9,8},{10,11... | collective-permute-start | bytes 2654216 | tf_op jit(solution)/shard_map/ppermute | solution.py:322
  3.2 13.6 %collective-permute-start.1 = (f32[864,128]{1,0:T(8,128)S(1)}, f32[864,128]{1,0:T(8,128)S(1)}, u32[]{:S(2)}, u32[]{:S(2)}) collective-permute-start(f32[864,128]{1,0:T(8,128)S(1)} %get-tuple-element.50), channel_id=1, source_target_pairs={{0,8},{8,0},{16,24},{24,16},{1,9},{9,1},{17,25},{25,17},{2,10},{10... | collective-permute-start | bytes 1327112 | tf_op jit(solution)/shard_map/ppermute | solution.py:322
  5.8 17.2 %collective-permute-start = (f32[1152,128]{1,0:T(8,128)S(1)}, f32[1152,128]{1,0:T(8,128)S(1)}, u32[]{:S(2)}, u32[]{:S(2)}) collective-permute-start(f32[1152,128]{1,0:T(8,128)S(1)} %get-tuple-element.49), channel_id=1, source_target_pairs={{0,7},{1,2},{2,1},{3,4},{4,3},{5,6},{6,5},{7,0},{8,15},{9,10},{10,... | collective-permute-start | bytes 1769480 | tf_op jit(solution)/shard_map/ppermute | solution.py:322
  9.9 21.2 %collective-permute-start.6 = (f32[576,128]{1,0:T(8,128)S(1)}, f32[576,128]{1,0:T(8,128)S(1)}, u32[]{:S(2)}, u32[]{:S(2)}) collective-permute-start(f32[576,128]{1,0:T(8,128)S(1)} %get-tuple-element.68), channel_id=1, source_target_pairs={{0,7},{1,2},{2,1},{3,4},{4,3},{5,6},{6,5},{7,0},{8,15},{9,10},{10,... | collective-permute-start | bytes 884744 | tf_op jit(solution)/shard_map/ppermute | solution.py:322
  10.8 17.3 %collective-permute-start.4 = (f32[864,128]{1,0:T(8,128)S(1)}, f32[864,128]{1,0:T(8,128)S(1)}, u32[]{:S(2)}, u32[]{:S(2)}) collective-permute-start(f32[864,128]{1,0:T(8,128)S(1)} %get-tuple-element.63), channel_id=1, source_target_pairs={{0,16},{8,24},{16,0},{24,8},{1,17},{9,25},{17,1},{25,9},{2,18},{10... | collective-permute-start | bytes 1327112 | tf_op jit(solution)/shard_map/ppermute | solution.py:322
  12.3 17.3 %collective-permute-start.8 = (f32[864,128]{1,0:T(8,128)S(1)}, f32[864,128]{1,0:T(8,128)S(1)}, u32[]{:S(2)}, u32[]{:S(2)}) collective-permute-start(f32[864,128]{1,0:T(8,128)S(1)} %get-tuple-element.73), channel_id=1, source_target_pairs={{0,8},{8,0},{16,24},{24,16},{1,9},{9,1},{17,25},{25,17},{2,10},{10... | collective-permute-start | bytes 1327112 | tf_op jit(solution)/shard_map/ppermute | solution.py:322
  16.8 6.1 %copy-start = (s32[9,9]{1,0:T(8,128)S(1)}, s32[9,9]{1,0:T(8,128)}, u32[]{:S(2)}) copy-start(s32[9,9]{1,0:T(8,128)} %kept.7) | copy-start | bytes 976
  16.8 14.3 %collective-permute-start.7 = (f32[864,128]{1,0:T(8,128)S(1)}, f32[864,128]{1,0:T(8,128)S(1)}, u32[]{:S(2)}, u32[]{:S(2)}) collective-permute-start(f32[864,128]{1,0:T(8,128)S(1)} %collective-permute-done.1.mid), channel_id=1, source_target_pairs={{0,16},{8,24},{16,0},{24,8},{1,17},{9,25},{17,1},{25,9},{2,18},{10... | collective-permute-start | bytes 1327112 | tf_op jit(solution)/shard_map/ppermute | solution.py:322
  24.4 11.8 %collective-permute-start.3 = (f32[576,128]{1,0:T(8,128)S(1)}, f32[576,128]{1,0:T(8,128)S(1)}, u32[]{:S(2)}, u32[]{:S(2)}) collective-permute-start(f32[576,128]{1,0:T(8,128)S(1)} %get-tuple-element.61), channel_id=1, source_target_pairs={{0,7},{1,2},{2,1},{3,4},{4,3},{5,6},{6,5},{7,0},{8,15},{9,10},{10,... | collective-permute-start | bytes 884744 | tf_op jit(solution)/shard_map/ppermute | solution.py:322
  28.1 8.3 %collective-permute-start.5 = (f32[864,128]{1,0:T(8,128)S(1)}, f32[864,128]{1,0:T(8,128)S(1)}, u32[]{:S(2)}, u32[]{:S(2)}) collective-permute-start(f32[864,128]{1,0:T(8,128)S(1)} %collective-permute-done.4), channel_id=1, source_target_pairs={{0,8},{8,0},{16,24},{24,16},{1,9},{9,1},{17,25},{25,17},{2,10},{10... | collective-permute-start | bytes 1327112 | tf_op jit(solution)/shard_map/ppermute | solution.py:322
  33.0 11.2 %collective-permute-start.12 = (f32[576,128]{1,0:T(8,128)S(1)}, f32[576,128]{1,0:T(8,128)S(1)}, u32[]{:S(2)}, u32[]{:S(2)}) collective-permute-start(f32[576,128]{1,0:T(8,128)S(1)} %get-tuple-element.88), channel_id=1, source_target_pairs={{0,7},{1,2},{2,1},{3,4},{4,3},{5,6},{6,5},{7,0},{8,15},{9,10},{10,... | collective-permute-start | bytes 884744 | tf_op jit(solution)/shard_map/ppermute | solution.py:322
  36.1 10.2 %collective-permute-start.10 = (f32[1152,128]{1,0:T(8,128)S(1)}, f32[1152,128]{1,0:T(8,128)S(1)}, u32[]{:S(2)}, u32[]{:S(2)}) collective-permute-start(f32[1152,128]{1,0:T(8,128)S(1)} %get-tuple-element.85), channel_id=1, source_target_pairs={{0,1},{1,0},{2,3},{3,2},{4,5},{5,4},{6,7},{7,6},{8,9},{9,8},{10,11... | collective-permute-start | bytes 1769480 | tf_op jit(solution)/shard_map/ppermute | solution.py:322
  40.1 10.8 %collective-permute-start.9 = (f32[576,128]{1,0:T(8,128)S(1)}, f32[576,128]{1,0:T(8,128)S(1)}, u32[]{:S(2)}, u32[]{:S(2)}) collective-permute-start(f32[576,128]{1,0:T(8,128)S(1)} %get-tuple-element.84), channel_id=1, source_target_pairs={{0,7},{1,2},{2,1},{3,4},{4,3},{5,6},{6,5},{7,0},{8,15},{9,10},{10,... | collective-permute-start | bytes 884744 | tf_op jit(solution)/shard_map/ppermute | solution.py:322
  43.4 2.9 %collective-permute-start.11 = (f32[576,128]{1,0:T(8,128)S(1)}, f32[576,128]{1,0:T(8,128)S(1)}, u32[]{:S(2)}, u32[]{:S(2)}) collective-permute-start(f32[576,128]{1,0:T(8,128)S(1)} %get-tuple-element.86), channel_id=1, source_target_pairs={{0,1},{1,0},{2,3},{3,2},{4,5},{5,4},{6,7},{7,6},{8,9},{9,8},{10,11... | collective-permute-start | bytes 884744 | tf_op jit(solution)/shard_map/ppermute | solution.py:322
  44.2 2.2 %copy-start.2 = (s32[9,9]{1,0:T(8,128)S(1)}, s32[9,9]{1,0:T(8,128)}, u32[]{:S(2)}) copy-start(s32[9,9]{1,0:T(8,128)} %kept.9) | copy-start | bytes 976

commit v11 on v9

--- a/solution.py
+++ b/solution.py
@@ -105,8 +105,16 @@
     return jnp.concatenate([value[i * 64 : (i + 1) * 64] * flags(i) for i in range(value.shape[0] // 64)], 0)
 
 
-def pack_first_body(info, tile, mid, link_a, chip):
+def pack_first_body(info, source, mid, link_a, chip, tile, sems):
     side = tile.shape[0]
+    copies = [
+        pltpu.make_async_copy(source.at[pl.ds(i * side // 3, side // 3), :], tile.at[pl.ds(i * side // 3, side // 3), :], sems.at[i])
+        for i in range(3)
+    ]
+    for copy in copies:
+        copy.start()
+    for copy in copies:
+        copy.wait()
     group = side // 3
     store_fold(mid, 0, tile_groups(info, tile, pl.ds(0, side))[MID])
     groups = tile_groups(info, tile, shared_rows(info, LINK, group))
@@ -284,21 +292,22 @@
 VMEM = pl.BlockSpec(memory_space=pltpu.VMEM)
 SMEM = pl.BlockSpec(memory_space=pltpu.SMEM)
 ANY = pl.BlockSpec(memory_space=pl.ANY)
-
-
-def call(body, name, scalars, arrays, outs, work=4, result=False, begun=(), scratch=()):
+HBM = pl.BlockSpec(memory_space=pltpu.HBM)
+
+
+def call(body, name, scalars, arrays, outs, work=4, result=False, begun=(), unmoved=(), scratch=()):
     count = len(scalars) + len(arrays)
     return pl.pallas_call(
         body,
         out_shape=[jax.ShapeDtypeStruct(shape, kind) for shape, kind in outs],
-        in_specs=[SMEM] * len(scalars) + [VMEM] * len(arrays) + [ANY] * len(begun),
+        in_specs=[SMEM] * len(scalars) + [VMEM] * len(arrays) + [ANY] * len(begun) + [HBM] * len(unmoved),
         out_specs=[VMEM] * (len(outs) - result) + [ANY] * result,
         scratch_shapes=scratch,
         input_output_aliases={count: len(outs) - 1} if begun else {},
         compiler_params=pltpu.CompilerParams(vmem_limit_bytes=24 << 20),
         cost_estimate=pl.CostEstimate(flops=work * 1000000000, transcendentals=0, bytes_accessed=work * 5000000),
         name=name,
-    )(*scalars, *arrays, *begun)
+    )(*scalars, *arrays, *begun, *unmoved)
 
 
 def on_device(p_tiles, square_kept, result_kept):
@@ -321,7 +330,13 @@
         )
 
     mid, link_a, chip = call(
-        pack_first_body, "pack_first", (info,), (p_tiles,), [strip, two_slabs, three_slabs]
+        pack_first_body,
+        "pack_first",
+        (info,),
+        (),
+        [strip, two_slabs, three_slabs],
+        unmoved=(pltpu.with_memory_space_constraint(p_tiles, pltpu.HBM),),
+        scratch=[pltpu.VMEM((side, side), F32), pltpu.SemaphoreType.DMA((3,))],
     )
     link_a = exchange(link_a, "col", -1)
     partner_mid = exchange(mid, "row", 1)

time: 52.8 us -> 52.8 us (level)
  Pallas kernels: 22.3 us -> 23.8 us
  local copies, waits for them, and re-layouts: 1.38 us -> 0.01 us
    pallas_call x13, Pallas kernels: 22.3 us -> 23.8 us  [call(): pl.pallas_call(body, out_shape=[jax.ShapeDtypeStruct(shape, kind) for sha...]
    unnamed x6, local copies, waits for them, and re-layouts: 1.38 us -> 0.01 us
where the time goes in v11:
time: 52.8 us; the launch traced here: 52.7 us
  Pallas kernels  23.8 us (45%)
  starting transfers between devices  20.7 us (39%)
  waiting for transfers between devices  8 us (15%)
    pallas_call x13, Pallas kernels, call(): pl.pallas_call(body, out_shape=[jax.ShapeDtypeStruct(shape, kind) for sha...  23.8 us
    ppermute x13, starting transfers between devices, exchange(): lax.ppermute(value, axis, [(i, (i + (even_step if i % 2 == 0 else -even_s...  20.7 us
    ppermute x13, waiting for transfers between devices, exchange(): lax.ppermute(value, axis, [(i, (i + (even_step if i % 2 == 0 else -even_s...  8 us
  transfers between devices with their start and end apart: 13, of which 4 were waited for; matrix products, arithmetic and copies ran while one was open for 0% of the time, Pallas kernels for 36%

profile of v11, /device:TPU:0, one launch (start us, length us, event | category | flops | bytes accessed | tf_op | source)
XLA Modules:
  0.0 52.7 jit_solution(11346960869949875907)
XLA Ops:
  0.0 0.1 pad_add_fusion.info
  0.1 0.0 copy-start.1
  0.1 2.6 %pack_first.1 = (f32[864,128]{1,0:T(8,128)S(1)}, f32[1152,128]{1,0:T(8,128)S(1)}, f32[1728,128]{1,0:T(8,128)S(1)}) custom-call(s32[2]{0:T(128)S(1)} %pad_add_fusion.info, f32[576,576]{1,0:T(8,128)} %tile.2), custom_call_target="tpu_custom_call" | custom-call | flops 4000000000 | bytes 20000000 | tf_op jit(solution)/shard_map/pack_first/pallas_call | solution.py:300
  2.7 0.5 collective-permute-start.2
  3.2 2.6 %collective-permute-start.1 = (f32[864,128]{1,0:T(8,128)S(1)}, f32[864,128]{1,0:T(8,128)S(1)}, u32[]{:S(2)}, u32[]{:S(2)}) collective-permute-start(f32[864,128]{1,0:T(8,128)S(1)} %get-tuple-element.45), channel_id=1, source_target_pairs={{0,8},{8,0},{16,24},{24,16},{1,9},{9,1},{17,25},{25,17},{2,10},{10... | collective-permute-start | bytes 1327112 | tf_op jit(solution)/shard_map/ppermute | solution.py:328
  5.8 3.4 %collective-permute-start = (f32[1152,128]{1,0:T(8,128)S(1)}, f32[1152,128]{1,0:T(8,128)S(1)}, u32[]{:S(2)}, u32[]{:S(2)}) collective-permute-start(f32[1152,128]{1,0:T(8,128)S(1)} %get-tuple-element.44), channel_id=1, source_target_pairs={{0,7},{1,2},{2,1},{3,4},{4,3},{5,6},{6,5},{7,0},{8,15},{9,10},{10,... | collective-permute-start | bytes 1769480 | tf_op jit(solution)/shard_map/ppermute | solution.py:328
  9.1 0.0 collective-permute-done.2.chip
  9.1 0.0 copy-done.1
  9.1 0.8 %pack_rest.1 = (f32[576,128]{1,0:T(8,128)S(1)}, f32[864,128]{1,0:T(8,128)S(1)}, f32[864,128]{1,0:T(8,128)S(1)}) custom-call(s32[2]{0:T(128)S(1)} %pad_add_fusion.info, f32[576,576]{1,0:T(8,128)S(1)} %copy-done.1), custom_call_target="tpu_custom_call" | custom-call | flops 4000000000 | bytes 20000000 | tf_op jit(solution)/shard_map/pack_rest/pallas_call | solution.py:300
  9.9 0.9 %collective-permute-start.4 = (f32[576,128]{1,0:T(8,128)S(1)}, f32[576,128]{1,0:T(8,128)S(1)}, u32[]{:S(2)}, u32[]{:S(2)}) collective-permute-start(f32[576,128]{1,0:T(8,128)S(1)} %get-tuple-element.58), channel_id=1, source_target_pairs={{0,7},{1,2},{2,1},{3,4},{4,3},{5,6},{6,5},{7,0},{8,15},{9,10},{10,... | collective-permute-start | bytes 884744 | tf_op jit(solution)/shard_map/ppermute | solution.py:328
  10.8 1.5 %collective-permute-start.6 = (f32[864,128]{1,0:T(8,128)S(1)}, f32[864,128]{1,0:T(8,128)S(1)}, u32[]{:S(2)}, u32[]{:S(2)}) collective-permute-start(f32[864,128]{1,0:T(8,128)S(1)} %get-tuple-element.59), channel_id=1, source_target_pairs={{0,16},{8,24},{16,0},{24,8},{1,17},{9,25},{17,1},{25,9},{2,18},{10... | collective-permute-start | bytes 1327112 | tf_op jit(solution)/shard_map/ppermute | solution.py:328
  12.3 1.5 %collective-permute-start.7 = (f32[864,128]{1,0:T(8,128)S(1)}, f32[864,128]{1,0:T(8,128)S(1)}, u32[]{:S(2)}, u32[]{:S(2)}) collective-permute-start(f32[864,128]{1,0:T(8,128)S(1)} %get-tuple-element.63), channel_id=1, source_target_pairs={{0,8},{8,0},{16,24},{24,16},{1,9},{9,1},{17,25},{25,17},{2,10},{10... | collective-permute-start | bytes 1327112 | tf_op jit(solution)/shard_map/ppermute | solution.py:328
  13.8 1.0 %prepare.1 = (bf16[2,3,576,256]{3,2,1,0:T(8,128)(2,1)S(1)}, bf16[2,3,768,256]{3,2,1,0:T(8,128)(2,1)S(1)}, bf16[2,3,384,256]{3,2,1,0:T(8,128)(2,1)S(1)}) custom-call(s32[2]{0:T(128)S(1)} %pad_add_fusion.info, f32[576,576]{1,0:T(8,128)S(1)} %copy-done.1, f32[1728,128]{1,0:T(8,128)S(1)} %collective-permute-done.2.chip), custom_call_target="tpu_custom_call" | custom-call | flops 4000000000 | bytes 20000000 | tf_op jit(solution)/shard_map/prepare/pallas_call | solution.py:300
  14.9 1.9 %collective-permute-done.1.mid = f32[864,128]{1,0:T(8,128)S(1)} collective-permute-done((f32[864,128]{1,0:T(8,128)S(1)}, f32[864,128]{1,0:T(8,128)S(1)}, u32[]{:S(2)}, u32[]{:S(2)}) %collective-permute-start.1) | collective-permute-done | bytes 442400 | tf_op jit(solution)/shard_map/ppermute | solution.py:328
  16.8 2.0 %collective-permute-start.5 = (f32[864,128]{1,0:T(8,128)S(1)}, f32[864,128]{1,0:T(8,128)S(1)}, u32[]{:S(2)}, u32[]{:S(2)}) collective-permute-start(f32[864,128]{1,0:T(8,128)S(1)} %collective-permute-done.1.mid), channel_id=1, source_target_pairs={{0,16},{8,24},{16,0},{24,8},{1,17},{9,25},{17,1},{25,9},{2,18},{10... | collective-permute-start | bytes 1327112 | tf_op jit(solution)/shard_map/ppermute | solution.py:328
  18.8 0.0 copy-start
  18.8 1.6 %near_start.1 = (f32[576,256]{1,0:T(8,128)S(1)}, bf16[2,768,256]{2,1,0:T(8,128)(2,1)S(1)}) custom-call(s32[2]{0:T(128)S(1)} %pad_add_fusion.info, f32[864,128]{1,0:T(8,128)S(1)} %collective-permute-done.1.mid, bf16[2,3,576,256]{3,2,1,0:T(8,128)(2,1)S(1)} %get-tuple-element.50.own_left, bf16[2,3,768,256]{3,2,1,0:T(8,128)(2,1)S(1)} %get-tuple-element.51.own_right, ...), custom_call_target="tpu_custom_call" | custom-call | flops 4000000000 | bytes 20000000 | tf_op jit(solution)/shard_map/near_start/pallas_call | solution.py:300
  20.3 2.6 %collective-permute-done.link_a = f32[1152,128]{1,0:T(8,128)S(1)} collective-permute-done((f32[1152,128]{1,0:T(8,128)S(1)}, f32[1152,128]{1,0:T(8,128)S(1)}, u32[]{:S(2)}, u32[]{:S(2)}) %collective-permute-start) | collective-permute-done | bytes 589856 | tf_op jit(solution)/shard_map/ppermute | solution.py:328
  22.9 0.0 copy-done
  22.9 1.4 %square_near.1 = (f32[576,256]{1,0:T(8,128)S(1)}, f32[576,128]{1,0:T(8,128)S(1)}, bf16[2,2,384,256]{3,2,1,0:T(8,128)(2,1)S(1)}) custom-call(s32[2]{0:T(128)S(1)} %pad_add_fusion.info, s32[9,9]{1,0:T(8,128)S(1)} %copy-done, f32[1152,128]{1,0:T(8,128)S(1)} %collective-permute-done.link_a, f32[576,256]{1,0:T(8,128)S(1)} %get-tuple-element.53.begun, ...), custom_call_target="tpu_custom_call" | custom-call | flops 4000000000 | bytes 20000000 | tf_op jit(solution)/shard_map/square_near/pallas_call | solution.py:300
  24.4 3.7 %collective-permute-start.3 = (f32[576,128]{1,0:T(8,128)S(1)}, f32[576,128]{1,0:T(8,128)S(1)}, u32[]{:S(2)}, u32[]{:S(2)}) collective-permute-start(f32[576,128]{1,0:T(8,128)S(1)} %get-tuple-element.55), channel_id=1, source_target_pairs={{0,7},{1,2},{2,1},{3,4},{4,3},{5,6},{6,5},{7,0},{8,15},{9,10},{10,... | collective-permute-start | bytes 884744 | tf_op jit(solution)/shard_map/ppermute | solution.py:328
  28.1 0.0 collective-permute-done.6
  28.1 0.5 %collective-permute-start.8 = (f32[864,128]{1,0:T(8,128)S(1)}, f32[864,128]{1,0:T(8,128)S(1)}, u32[]{:S(2)}, u32[]{:S(2)}) collective-permute-start(f32[864,128]{1,0:T(8,128)S(1)} %collective-permute-done.6), channel_id=1, source_target_pairs={{0,8},{8,0},{16,24},{24,16},{1,9},{9,1},{17,25},{25,17},{2,10},{10... | collective-permute-start | bytes 1327112 | tf_op jit(solution)/shard_map/ppermute | solution.py:328
  28.6 1.9 %middle_products.1 = (f32[576,256]{1,0:T(8,128)S(1)}, f32[576,256]{1,0:T(8,128)S(1)}) custom-call(s32[2]{0:T(128)S(1)} %pad_add_fusion.info, bf16[2,3,576,256]{3,2,1,0:T(8,128)(2,1)S(1)} %get-tuple-element.50.own_left, bf16[2,3,768,256]{3,2,1,0:T(8,128)(2,1)S(1)} %get-tuple-element.51.own_right, bf16[2,3,384,256]{3,2,1,0:T(8,128)(2,1)S(1)} %get-tuple-element.52.chip_left, ...), custom_call_target="tpu_custom_call" | custom-call | flops 4000000000 | bytes 20000000 | tf_op jit(solution)/shard_map/middle_products/pallas_call | solution.py:300
  30.5 0.0 collective-permute-done.7.near
  30.5 1.4 %mid_start.1 = (f32[576,256]{1,0:T(8,128)S(1)}, bf16[2,768,256]{2,1,0:T(8,128)(2,1)S(1)}) custom-call(s32[2]{0:T(128)S(1)} %pad_add_fusion.info, f32[864,128]{1,0:T(8,128)S(1)} %collective-permute-done.7.near, f32[576,256]{1,0:T(8,128)S(1)} %get-tuple-element.64.begun, bf16[2,3,576,256]{3,2,1,0:T(8,128)(2,1)S(1)} %get-tuple-element.50.own_left, ...), custom_call_target="tpu_custom_call" | custom-call | flops 4000000000 | bytes 20000000 | tf_op jit(solution)/shard_map/mid_start/pallas_call | solution.py:300
  31.9 0.0 collective-permute-done.4.link_b
  31.9 0.0 collective-permute-done.5.mid
  31.9 1.9 %square_far.1 = (f32[576,256]{1,0:T(8,128)S(1)}, f32[576,128]{1,0:T(8,128)S(1)}, f32[1152,128]{1,0:T(8,128)S(1)}, bf16[2,384,256]{2,1,0:T(8,128)(2,1)S(1)}, bf16[2,768,256]{2,1,0:T(8,128)(2,1)S(1)}) custom-call(s32[2]{0:T(128)S(1)} %pad_add_fusion.info, s32[9,9]{1,0:T(8,128)S(1)} %copy-done, f32[576,128]{1,0:T(8,128)S(1)} %collective-permute-done.4.link_b, ...), custom_call_target="tpu_custom_call" | custom-call | flops 4000000000 | bytes 20000000 | tf_op jit(solution)/shard_map/square_far/pallas_call | solution.py:300
  33.8 2.3 %collective-permute-start.12 = (f32[576,128]{1,0:T(8,128)S(1)}, f32[576,128]{1,0:T(8,128)S(1)}, u32[]{:S(2)}, u32[]{:S(2)}) collective-permute-start(f32[576,128]{1,0:T(8,128)S(1)} %get-tuple-element.78), channel_id=1, source_target_pairs={{0,7},{1,2},{2,1},{3,4},{4,3},{5,6},{6,5},{7,0},{8,15},{9,10},{10,... | collective-permute-start | bytes 884744 | tf_op jit(solution)/shard_map/ppermute | solution.py:328
  36.1 0.0 collective-permute-start.10
  36.1 0.0 collective-permute-done.3.link
  36.1 1.8 %cube_near.1.total = f32[3,576,256]{2,1,0:T(8,128)S(1)} custom-call(s32[2]{0:T(128)S(1)} %pad_add_fusion.info, f32[576,128]{1,0:T(8,128)S(1)} %collective-permute-done.3.link, f32[576,256]{1,0:T(8,128)S(1)} %get-tuple-element.56.s_near.near, f32[576,256]{1,0:T(8,128)S(1)} %get-tuple-element.67.far, bf16[2,768,256]{2,1,0:T(8,128)(2,1)S(1)} %get-tuple-element.54.right_near, ...), custom_call_target="tpu_custom_call" | custom-call | flops 4000000000 | bytes 20000000 | tf_op jit(solution)/shard_map/cube_near/pallas_call | solution.py:300
  38.0 0.0 collective-permute-done.8.far
  38.0 1.9 %square_mid.1 = (f32[576,256]{1,0:T(8,128)S(1)}, f32[576,128]{1,0:T(8,128)S(1)}, f32[576,128]{1,0:T(8,128)S(1)}, bf16[2,768,256]{2,1,0:T(8,128)(2,1)S(1)}) custom-call(s32[2]{0:T(128)S(1)} %pad_add_fusion.info, s32[9,9]{1,0:T(8,128)S(1)} %copy-done, f32[864,128]{1,0:T(8,128)S(1)} %collective-permute-done.8.far, ...), custom_call_target="tpu_custom_call" | custom-call | tf_op jit(solution)/shard_map/square_mid/pallas_call | solution.py:300
  39.8 1.8 %collective-permute-start.9 = (f32[576,128]{1,0:T(8,128)S(1)}, f32[576,128]{1,0:T(8,128)S(1)}, u32[]{:S(2)}, u32[]{:S(2)}) collective-permute-start(f32[576,128]{1,0:T(8,128)S(1)} %get-tuple-element.74), channel_id=1, source_target_pairs={{0,7},{1,2},{2,1},{3,4},{4,3},{5,6},{6,5},{7,0},{8,15},{9,10},{10,... | collective-permute-start | bytes 884744 | tf_op jit(solution)/shard_map/ppermute | solution.py:328
  41.6 0.0 collective-permute-start.11
  41.6 3.4 %collective-permute-done.12.link = f32[576,128]{1,0:T(8,128)S(1)} collective-permute-done((f32[576,128]{1,0:T(8,128)S(1)}, f32[576,128]{1,0:T(8,128)S(1)}, u32[]{:S(2)}, u32[]{:S(2)}) %collective-permute-start.12) | collective-permute-done | bytes 294944 | tf_op jit(solution)/shard_map/ppermute | solution.py:328
  45.0 0.0 copy-start.2
  45.0 2.2 %cube_own.1.base = f32[3,576,256]{2,1,0:T(8,128)S(1)} custom-call(s32[2]{0:T(128)S(1)} %pad_add_fusion.info, f32[576,128]{1,0:T(8,128)S(1)} %collective-permute-done.12.link, f32[3,576,256]{2,1,0:T(8,128)S(1)} %cube_near.1.total, f32[576,256]{1,0:T(8,128)S(1)} %get-tuple-element.56.s_near.near, f32[576,256]{1,0:T(8,128)S(1)} %get-tuple-element.80.mid, ...), custom_call_target="tpu_custom_call" | custom-call | flops 4000000000 | bytes 20000000 | tf_op jit(solution)/shard_map/cube_own/pallas_call | solution.py:300
  47.2 0.0 collective-permute-done.10.sides
  47.2 0.0 collective-permute-done.11.chip
  47.2 0.0 copy-done.2
  47.2 3.2 %cube_chip.1 = (f32[3,576,256]{2,1,0:T(8,128)S(1)}, f32[576,576]{1,0:T(8,128)}) custom-call(s32[2]{0:T(128)S(1)} %pad_add_fusion.info, s32[9,9]{1,0:T(8,128)S(1)} %copy-done.2, f32[1152,128]{1,0:T(8,128)S(1)} %collective-permute-done.10.sides, f32[576,128]{1,0:T(8,128)S(1)} %collective-permute-done.11.chip, ...), custom_call_target="tpu_custom_call" | custom-call | flops 4000000000 | bytes 20000000 | tf_op jit(solution)/shard_map/cube_chip/pallas_call | solution.py:300
  50.4 0.1 collective-permute-done.9.link
  50.5 2.2 %finish.1 = f32[576,576]{1,0:T(8,128)} custom-call(s32[2]{0:T(128)S(1)} %pad_add_fusion.info, s32[9,9]{1,0:T(8,128)S(1)} %copy-done.2, f32[576,128]{1,0:T(8,128)S(1)} %collective-permute-done.9.link, bf16[2,3,768,256]{3,2,1,0:T(8,128)(2,1)S(1)} %get-tuple-element.51.own_right, ...), custom_call_target="tpu_custom_call", output_to_operand_aliasing={{}: (5, {})} | custom-call | flops 4000000000 | bytes 20000000 | tf_op jit(solution)/shard_map/finish/pallas_call | solution.py:300
Async XLA Ops:
  0.1 9.1 %copy-start.1 = (f32[576,576]{1,0:T(8,128)S(1)}, f32[576,576]{1,0:T(8,128)}, u32[]{:S(2)}) copy-start(f32[576,576]{1,0:T(8,128)} %tile.2) | copy-start | bytes 3981316
  2.7 6.5 %collective-permute-start.2 = (f32[1728,128]{1,0:T(8,128)S(1)}, f32[1728,128]{1,0:T(8,128)S(1)}, u32[]{:S(2)}, u32[]{:S(2)}) collective-permute-start(f32[1728,128]{1,0:T(8,128)S(1)} %get-tuple-element.46), channel_id=1, source_target_pairs={{0,1},{1,0},{2,3},{3,2},{4,5},{5,4},{6,7},{7,6},{8,9},{9,8},{10,11... | collective-permute-start | bytes 2654216 | tf_op jit(solution)/shard_map/ppermute | solution.py:328
  3.2 13.6 %collective-permute-start.1 = (f32[864,128]{1,0:T(8,128)S(1)}, f32[864,128]{1,0:T(8,128)S(1)}, u32[]{:S(2)}, u32[]{:S(2)}) collective-permute-start(f32[864,128]{1,0:T(8,128)S(1)} %get-tuple-element.45), channel_id=1, source_target_pairs={{0,8},{8,0},{16,24},{24,16},{1,9},{9,1},{17,25},{25,17},{2,10},{10... | collective-permute-start | bytes 1327112 | tf_op jit(solution)/shard_map/ppermute | solution.py:328
  5.8 17.2 %collective-permute-start = (f32[1152,128]{1,0:T(8,128)S(1)}, f32[1152,128]{1,0:T(8,128)S(1)}, u32[]{:S(2)}, u32[]{:S(2)}) collective-permute-start(f32[1152,128]{1,0:T(8,128)S(1)} %get-tuple-element.44), channel_id=1, source_target_pairs={{0,7},{1,2},{2,1},{3,4},{4,3},{5,6},{6,5},{7,0},{8,15},{9,10},{10,... | collective-permute-start | bytes 1769480 | tf_op jit(solution)/shard_map/ppermute | solution.py:328
  9.9 22.0 %collective-permute-start.4 = (f32[576,128]{1,0:T(8,128)S(1)}, f32[576,128]{1,0:T(8,128)S(1)}, u32[]{:S(2)}, u32[]{:S(2)}) collective-permute-start(f32[576,128]{1,0:T(8,128)S(1)} %get-tuple-element.58), channel_id=1, source_target_pairs={{0,7},{1,2},{2,1},{3,4},{4,3},{5,6},{6,5},{7,0},{8,15},{9,10},{10,... | collective-permute-start | bytes 884744 | tf_op jit(solution)/shard_map/ppermute | solution.py:328
  10.8 17.3 %collective-permute-start.6 = (f32[864,128]{1,0:T(8,128)S(1)}, f32[864,128]{1,0:T(8,128)S(1)}, u32[]{:S(2)}, u32[]{:S(2)}) collective-permute-start(f32[864,128]{1,0:T(8,128)S(1)} %get-tuple-element.59), channel_id=1, source_target_pairs={{0,16},{8,24},{16,0},{24,8},{1,17},{9,25},{17,1},{25,9},{2,18},{10... | collective-permute-start | bytes 1327112 | tf_op jit(solution)/shard_map/ppermute | solution.py:328
  12.3 18.2 %collective-permute-start.7 = (f32[864,128]{1,0:T(8,128)S(1)}, f32[864,128]{1,0:T(8,128)S(1)}, u32[]{:S(2)}, u32[]{:S(2)}) collective-permute-start(f32[864,128]{1,0:T(8,128)S(1)} %get-tuple-element.63), channel_id=1, source_target_pairs={{0,8},{8,0},{16,24},{24,16},{1,9},{9,1},{17,25},{25,17},{2,10},{10... | collective-permute-start | bytes 1327112 | tf_op jit(solution)/shard_map/ppermute | solution.py:328
  16.8 15.2 %collective-permute-start.5 = (f32[864,128]{1,0:T(8,128)S(1)}, f32[864,128]{1,0:T(8,128)S(1)}, u32[]{:S(2)}, u32[]{:S(2)}) collective-permute-start(f32[864,128]{1,0:T(8,128)S(1)} %collective-permute-done.1.mid), channel_id=1, source_target_pairs={{0,16},{8,24},{16,0},{24,8},{1,17},{9,25},{17,1},{25,9},{2,18},{10... | collective-permute-start | bytes 1327112 | tf_op jit(solution)/shard_map/ppermute | solution.py:328
  18.8 4.2 %copy-start = (s32[9,9]{1,0:T(8,128)S(1)}, s32[9,9]{1,0:T(8,128)}, u32[]{:S(2)}) copy-start(s32[9,9]{1,0:T(8,128)} %kept.7) | copy-start | bytes 976
  24.4 11.8 %collective-permute-start.3 = (f32[576,128]{1,0:T(8,128)S(1)}, f32[576,128]{1,0:T(8,128)S(1)}, u32[]{:S(2)}, u32[]{:S(2)}) collective-permute-start(f32[576,128]{1,0:T(8,128)S(1)} %get-tuple-element.55), channel_id=1, source_target_pairs={{0,7},{1,2},{2,1},{3,4},{4,3},{5,6},{6,5},{7,0},{8,15},{9,10},{10,... | collective-permute-start | bytes 884744 | tf_op jit(solution)/shard_map/ppermute | solution.py:328
  28.1 9.9 %collective-permute-start.8 = (f32[864,128]{1,0:T(8,128)S(1)}, f32[864,128]{1,0:T(8,128)S(1)}, u32[]{:S(2)}, u32[]{:S(2)}) collective-permute-start(f32[864,128]{1,0:T(8,128)S(1)} %collective-permute-done.6), channel_id=1, source_target_pairs={{0,8},{8,0},{16,24},{24,16},{1,9},{9,1},{17,25},{25,17},{2,10},{10... | collective-permute-start | bytes 1327112 | tf_op jit(solution)/shard_map/ppermute | solution.py:328
  33.8 11.2 %collective-permute-start.12 = (f32[576,128]{1,0:T(8,128)S(1)}, f32[576,128]{1,0:T(8,128)S(1)}, u32[]{:S(2)}, u32[]{:S(2)}) collective-permute-start(f32[576,128]{1,0:T(8,128)S(1)} %get-tuple-element.78), channel_id=1, source_target_pairs={{0,7},{1,2},{2,1},{3,4},{4,3},{5,6},{6,5},{7,0},{8,15},{9,10},{10,... | collective-permute-start | bytes 884744 | tf_op jit(solution)/shard_map/ppermute | solution.py:328
  36.1 11.0 %collective-permute-start.10 = (f32[1152,128]{1,0:T(8,128)S(1)}, f32[1152,128]{1,0:T(8,128)S(1)}, u32[]{:S(2)}, u32[]{:S(2)}) collective-permute-start(f32[1152,128]{1,0:T(8,128)S(1)} %get-tuple-element.75), channel_id=1, source_target_pairs={{0,1},{1,0},{2,3},{3,2},{4,5},{5,4},{6,7},{7,6},{8,9},{9,8},{10,11... | collective-permute-start | bytes 1769480 | tf_op jit(solution)/shard_map/ppermute | solution.py:328
  39.8 10.6 %collective-permute-start.9 = (f32[576,128]{1,0:T(8,128)S(1)}, f32[576,128]{1,0:T(8,128)S(1)}, u32[]{:S(2)}, u32[]{:S(2)}) collective-permute-start(f32[576,128]{1,0:T(8,128)S(1)} %get-tuple-element.74), channel_id=1, source_target_pairs={{0,7},{1,2},{2,1},{3,4},{4,3},{5,6},{6,5},{7,0},{8,15},{9,10},{10,... | collective-permute-start | bytes 884744 | tf_op jit(solution)/shard_map/ppermute | solution.py:328
  41.6 5.6 %collective-permute-start.11 = (f32[576,128]{1,0:T(8,128)S(1)}, f32[576,128]{1,0:T(8,128)S(1)}, u32[]{:S(2)}, u32[]{:S(2)}) collective-permute-start(f32[576,128]{1,0:T(8,128)S(1)} %get-tuple-element.76), channel_id=1, source_target_pairs={{0,1},{1,0},{2,3},{3,2},{4,5},{5,4},{6,7},{7,6},{8,9},{9,8},{10,11... | collective-permute-start | bytes 884744 | tf_op jit(solution)/shard_map/ppermute | solution.py:328
  45.0 2.2 %copy-start.2 = (s32[9,9]{1,0:T(8,128)S(1)}, s32[9,9]{1,0:T(8,128)}, u32[]{:S(2)}) copy-start(s32[9,9]{1,0:T(8,128)} %kept.9) | copy-start | bytes 976

commit v12 on v11

--- a/solution.py
+++ b/solution.py
@@ -107,22 +107,44 @@
 
 def pack_first_body(info, source, mid, link_a, chip, tile, sems):
     side = tile.shape[0]
+    group = side // 3
     copies = [
-        pltpu.make_async_copy(source.at[pl.ds(i * side // 3, side // 3), :], tile.at[pl.ds(i * side // 3, side // 3), :], sems.at[i])
+        pltpu.make_async_copy(source.at[pl.ds(i * group, group), :], tile.at[pl.ds(i * group, group), :], sems.at[i])
         for i in range(3)
     ]
     for copy in copies:
         copy.start()
-    for copy in copies:
+    slabs = (
+        (CHIP, ((chip, 0, NEAR), (chip, 3 * group, MID), (chip, 6 * group, FAR))),
+        (LINK, ((link_a, 0, MID), (link_a, 3 * group, NEAR))),
+    )
+    tails = []
+    for i, copy in enumerate(copies):
         copy.wait()
-    group = side // 3
-    store_fold(mid, 0, tile_groups(info, tile, pl.ds(0, side))[MID])
-    groups = tile_groups(info, tile, shared_rows(info, LINK, group))
-    store_fold(link_a, 0, groups[MID])
-    store_fold(link_a, 3 * group, groups[NEAR])
-    groups = tile_groups(info, tile, shared_rows(info, CHIP, group))
-    for part in range(3):
-        store_fold(chip, part * 3 * group, groups[part])
+        parts = tile_groups(info, tile, pl.ds(i * group, group))
+        mid[pl.ds(i * group, group), :] = parts[MID][:, :LANES]
+        tails.append(parts[MID][:, LANES:])
+        for who, targets in slabs:
+            first = place(info, who, 1)[0]
+            for half in range(2):
+                if 0 <= i - half <= 1:
+
+                    @pl.when(first == i - half)
+                    def _(targets=targets, half=half, parts=parts):
+                        for ref, base, part in targets:
+                            ref[pl.ds(base + half * group, group), :] = parts[part][:, :LANES]
+                            tail = parts[part][:, LANES:]
+                            if half == 0:
+                                ref[pl.ds(base + 2 * group, group), : LANES // 2] = tail[:, : LANES // 2]
+                            else:
+                                turned = pltpu.roll(tail, LANES // 2, 1)
+                                ref[pl.ds(base + 2 * group, group), LANES // 2 :] = turned[:, LANES // 2 :]
+
+    tail = jnp.concatenate(tails, 0)
+    middle = side // 2
+    mid[pl.ds(side, middle), :] = jnp.where(
+        low_half(middle), tail[:middle], pltpu.roll(tail[middle:], LANES // 2, 1)
+    )
 
 
 def pack_rest_body(info, tile, link_b, near, far):

time: 52.8 us -> 52.7 us (level)
  no operation moved by 1% of the time
where the time goes in v12:
time: 52.7 us; the launch traced here: 52.5 us
  Pallas kernels  23.6 us (45%)
  starting transfers between devices  20.7 us (39%)
  waiting for transfers between devices  8 us (15%)
    pallas_call x13, Pallas kernels, call(): pl.pallas_call(body, out_shape=[jax.ShapeDtypeStruct(shape, kind) for sha...  23.6 us
    ppermute x13, starting transfers between devices, exchange(): lax.ppermute(value, axis, [(i, (i + (even_step if i % 2 == 0 else -even_s...  20.7 us
    ppermute x13, waiting for transfers between devices, exchange(): lax.ppermute(value, axis, [(i, (i + (even_step if i % 2 == 0 else -even_s...  8 us
  transfers between devices with their start and end apart: 13, of which 4 were waited for; matrix products, arithmetic and copies ran while one was open for 0% of the time, Pallas kernels for 36%

profile of v12, /device:TPU:0, one launch (start us, length us, event | category | flops | bytes accessed | tf_op | source)
XLA Modules:
  0.0 52.5 jit_solution(3813888275028511745)
XLA Ops:
  0.0 0.1 pad_add_fusion.info
  0.1 0.0 copy-start.1
  0.1 2.4 %pack_first.1 = (f32[864,128]{1,0:T(8,128)S(1)}, f32[1152,128]{1,0:T(8,128)S(1)}, f32[1728,128]{1,0:T(8,128)S(1)}) custom-call(s32[2]{0:T(128)S(1)} %pad_add_fusion.info, f32[576,576]{1,0:T(8,128)} %tile.2), custom_call_target="tpu_custom_call" | custom-call | flops 4000000000 | bytes 20000000 | tf_op jit(solution)/shard_map/pack_first/pallas_call | solution.py:322
  2.5 0.5 %collective-permute-start.2 = (f32[1728,128]{1,0:T(8,128)S(1)}, f32[1728,128]{1,0:T(8,128)S(1)}, u32[]{:S(2)}, u32[]{:S(2)}) collective-permute-start(f32[1728,128]{1,0:T(8,128)S(1)} %get-tuple-element.46), channel_id=1, source_target_pairs={{0,1},{1,0},{2,3},{3,2},{4,5},{5,4},{6,7},{7,6},{8,9},{9,8},{10,11... | collective-permute-start | bytes 2654216 | tf_op jit(solution)/shard_map/ppermute | solution.py:350
  3.0 2.6 %collective-permute-start.1 = (f32[864,128]{1,0:T(8,128)S(1)}, f32[864,128]{1,0:T(8,128)S(1)}, u32[]{:S(2)}, u32[]{:S(2)}) collective-permute-start(f32[864,128]{1,0:T(8,128)S(1)} %get-tuple-element.45), channel_id=1, source_target_pairs={{0,8},{8,0},{16,24},{24,16},{1,9},{9,1},{17,25},{25,17},{2,10},{10... | collective-permute-start | bytes 1327112 | tf_op jit(solution)/shard_map/ppermute | solution.py:350
  5.6 3.4 %collective-permute-start = (f32[1152,128]{1,0:T(8,128)S(1)}, f32[1152,128]{1,0:T(8,128)S(1)}, u32[]{:S(2)}, u32[]{:S(2)}) collective-permute-start(f32[1152,128]{1,0:T(8,128)S(1)} %get-tuple-element.44), channel_id=1, source_target_pairs={{0,7},{1,2},{2,1},{3,4},{4,3},{5,6},{6,5},{7,0},{8,15},{9,10},{10,... | collective-permute-start | bytes 1769480 | tf_op jit(solution)/shard_map/ppermute | solution.py:350
  9.0 0.0 collective-permute-done.2.chip
  9.0 0.0 copy-done.1
  9.0 0.8 %pack_rest.1 = (f32[576,128]{1,0:T(8,128)S(1)}, f32[864,128]{1,0:T(8,128)S(1)}, f32[864,128]{1,0:T(8,128)S(1)}) custom-call(s32[2]{0:T(128)S(1)} %pad_add_fusion.info, f32[576,576]{1,0:T(8,128)S(1)} %copy-done.1), custom_call_target="tpu_custom_call" | custom-call | flops 4000000000 | bytes 20000000 | tf_op jit(solution)/shard_map/pack_rest/pallas_call | solution.py:322
  9.8 0.9 %collective-permute-start.4 = (f32[576,128]{1,0:T(8,128)S(1)}, f32[576,128]{1,0:T(8,128)S(1)}, u32[]{:S(2)}, u32[]{:S(2)}) collective-permute-start(f32[576,128]{1,0:T(8,128)S(1)} %get-tuple-element.58), channel_id=1, source_target_pairs={{0,7},{1,2},{2,1},{3,4},{4,3},{5,6},{6,5},{7,0},{8,15},{9,10},{10,... | collective-permute-start | bytes 884744 | tf_op jit(solution)/shard_map/ppermute | solution.py:350
  10.6 1.5 %collective-permute-start.6 = (f32[864,128]{1,0:T(8,128)S(1)}, f32[864,128]{1,0:T(8,128)S(1)}, u32[]{:S(2)}, u32[]{:S(2)}) collective-permute-start(f32[864,128]{1,0:T(8,128)S(1)} %get-tuple-element.59), channel_id=1, source_target_pairs={{0,16},{8,24},{16,0},{24,8},{1,17},{9,25},{17,1},{25,9},{2,18},{10... | collective-permute-start | bytes 1327112 | tf_op jit(solution)/shard_map/ppermute | solution.py:350
  12.2 1.5 %collective-permute-start.7 = (f32[864,128]{1,0:T(8,128)S(1)}, f32[864,128]{1,0:T(8,128)S(1)}, u32[]{:S(2)}, u32[]{:S(2)}) collective-permute-start(f32[864,128]{1,0:T(8,128)S(1)} %get-tuple-element.63), channel_id=1, source_target_pairs={{0,8},{8,0},{16,24},{24,16},{1,9},{9,1},{17,25},{25,17},{2,10},{10... | collective-permute-start | bytes 1327112 | tf_op jit(solution)/shard_map/ppermute | solution.py:350
  13.7 1.0 %prepare.1 = (bf16[2,3,576,256]{3,2,1,0:T(8,128)(2,1)S(1)}, bf16[2,3,768,256]{3,2,1,0:T(8,128)(2,1)S(1)}, bf16[2,3,384,256]{3,2,1,0:T(8,128)(2,1)S(1)}) custom-call(s32[2]{0:T(128)S(1)} %pad_add_fusion.info, f32[576,576]{1,0:T(8,128)S(1)} %copy-done.1, f32[1728,128]{1,0:T(8,128)S(1)} %collective-permute-done.2.chip), custom_call_target="tpu_custom_call" | custom-call | flops 4000000000 | bytes 20000000 | tf_op jit(solution)/shard_map/prepare/pallas_call | solution.py:322
  14.7 1.9 %collective-permute-done.1.mid = f32[864,128]{1,0:T(8,128)S(1)} collective-permute-done((f32[864,128]{1,0:T(8,128)S(1)}, f32[864,128]{1,0:T(8,128)S(1)}, u32[]{:S(2)}, u32[]{:S(2)}) %collective-permute-start.1) | collective-permute-done | bytes 442400 | tf_op jit(solution)/shard_map/ppermute | solution.py:350
  16.6 2.0 %collective-permute-start.5 = (f32[864,128]{1,0:T(8,128)S(1)}, f32[864,128]{1,0:T(8,128)S(1)}, u32[]{:S(2)}, u32[]{:S(2)}) collective-permute-start(f32[864,128]{1,0:T(8,128)S(1)} %collective-permute-done.1.mid), channel_id=1, source_target_pairs={{0,16},{8,24},{16,0},{24,8},{1,17},{9,25},{17,1},{25,9},{2,18},{10... | collective-permute-start | bytes 1327112 | tf_op jit(solution)/shard_map/ppermute | solution.py:350
  18.6 0.0 copy-start
  18.6 1.6 %near_start.1 = (f32[576,256]{1,0:T(8,128)S(1)}, bf16[2,768,256]{2,1,0:T(8,128)(2,1)S(1)}) custom-call(s32[2]{0:T(128)S(1)} %pad_add_fusion.info, f32[864,128]{1,0:T(8,128)S(1)} %collective-permute-done.1.mid, bf16[2,3,576,256]{3,2,1,0:T(8,128)(2,1)S(1)} %get-tuple-element.50.own_left, bf16[2,3,768,256]{3,2,1,0:T(8,128)(2,1)S(1)} %get-tuple-element.51.own_right, ...), custom_call_target="tpu_custom_call" | custom-call | flops 4000000000 | bytes 20000000 | tf_op jit(solution)/shard_map/near_start/pallas_call | solution.py:322
  20.2 2.6 %collective-permute-done.link_a = f32[1152,128]{1,0:T(8,128)S(1)} collective-permute-done((f32[1152,128]{1,0:T(8,128)S(1)}, f32[1152,128]{1,0:T(8,128)S(1)}, u32[]{:S(2)}, u32[]{:S(2)}) %collective-permute-start) | collective-permute-done | bytes 589856 | tf_op jit(solution)/shard_map/ppermute | solution.py:350
  22.8 0.0 copy-done
  22.8 1.4 %square_near.1 = (f32[576,256]{1,0:T(8,128)S(1)}, f32[576,128]{1,0:T(8,128)S(1)}, bf16[2,2,384,256]{3,2,1,0:T(8,128)(2,1)S(1)}) custom-call(s32[2]{0:T(128)S(1)} %pad_add_fusion.info, s32[9,9]{1,0:T(8,128)S(1)} %copy-done, f32[1152,128]{1,0:T(8,128)S(1)} %collective-permute-done.link_a, f32[576,256]{1,0:T(8,128)S(1)} %get-tuple-element.53.begun, ...), custom_call_target="tpu_custom_call" | custom-call | flops 4000000000 | bytes 20000000 | tf_op jit(solution)/shard_map/square_near/pallas_call | solution.py:322
  24.2 3.7 %collective-permute-start.3 = (f32[576,128]{1,0:T(8,128)S(1)}, f32[576,128]{1,0:T(8,128)S(1)}, u32[]{:S(2)}, u32[]{:S(2)}) collective-permute-start(f32[576,128]{1,0:T(8,128)S(1)} %get-tuple-element.55), channel_id=1, source_target_pairs={{0,7},{1,2},{2,1},{3,4},{4,3},{5,6},{6,5},{7,0},{8,15},{9,10},{10,... | collective-permute-start | bytes 884744 | tf_op jit(solution)/shard_map/ppermute | solution.py:350
  27.9 0.0 collective-permute-done.6
  27.9 0.5 %collective-permute-start.8 = (f32[864,128]{1,0:T(8,128)S(1)}, f32[864,128]{1,0:T(8,128)S(1)}, u32[]{:S(2)}, u32[]{:S(2)}) collective-permute-start(f32[864,128]{1,0:T(8,128)S(1)} %collective-permute-done.6), channel_id=1, source_target_pairs={{0,8},{8,0},{16,24},{24,16},{1,9},{9,1},{17,25},{25,17},{2,10},{10... | collective-permute-start | bytes 1327112 | tf_op jit(solution)/shard_map/ppermute | solution.py:350
  28.5 1.9 %middle_products.1 = (f32[576,256]{1,0:T(8,128)S(1)}, f32[576,256]{1,0:T(8,128)S(1)}) custom-call(s32[2]{0:T(128)S(1)} %pad_add_fusion.info, bf16[2,3,576,256]{3,2,1,0:T(8,128)(2,1)S(1)} %get-tuple-element.50.own_left, bf16[2,3,768,256]{3,2,1,0:T(8,128)(2,1)S(1)} %get-tuple-element.51.own_right, bf16[2,3,384,256]{3,2,1,0:T(8,128)(2,1)S(1)} %get-tuple-element.52.chip_left, ...), custom_call_target="tpu_custom_call" | custom-call | flops 4000000000 | bytes 20000000 | tf_op jit(solution)/shard_map/middle_products/pallas_call | solution.py:322
  30.4 0.0 collective-permute-done.7.near
  30.4 1.4 %mid_start.1 = (f32[576,256]{1,0:T(8,128)S(1)}, bf16[2,768,256]{2,1,0:T(8,128)(2,1)S(1)}) custom-call(s32[2]{0:T(128)S(1)} %pad_add_fusion.info, f32[864,128]{1,0:T(8,128)S(1)} %collective-permute-done.7.near, f32[576,256]{1,0:T(8,128)S(1)} %get-tuple-element.64.begun, bf16[2,3,576,256]{3,2,1,0:T(8,128)(2,1)S(1)} %get-tuple-element.50.own_left, ...), custom_call_target="tpu_custom_call" | custom-call | flops 4000000000 | bytes 20000000 | tf_op jit(solution)/shard_map/mid_start/pallas_call | solution.py:322
  31.8 0.0 collective-permute-done.4.link_b
  31.8 0.0 collective-permute-done.5.mid
  31.8 1.9 %square_far.1 = (f32[576,256]{1,0:T(8,128)S(1)}, f32[576,128]{1,0:T(8,128)S(1)}, f32[1152,128]{1,0:T(8,128)S(1)}, bf16[2,384,256]{2,1,0:T(8,128)(2,1)S(1)}, bf16[2,768,256]{2,1,0:T(8,128)(2,1)S(1)}) custom-call(s32[2]{0:T(128)S(1)} %pad_add_fusion.info, s32[9,9]{1,0:T(8,128)S(1)} %copy-done, f32[576,128]{1,0:T(8,128)S(1)} %collective-permute-done.4.link_b, ...), custom_call_target="tpu_custom_call" | custom-call | flops 4000000000 | bytes 20000000 | tf_op jit(solution)/shard_map/square_far/pallas_call | solution.py:322
  33.7 2.3 %collective-permute-start.12 = (f32[576,128]{1,0:T(8,128)S(1)}, f32[576,128]{1,0:T(8,128)S(1)}, u32[]{:S(2)}, u32[]{:S(2)}) collective-permute-start(f32[576,128]{1,0:T(8,128)S(1)} %get-tuple-element.78), channel_id=1, source_target_pairs={{0,7},{1,2},{2,1},{3,4},{4,3},{5,6},{6,5},{7,0},{8,15},{9,10},{10,... | collective-permute-start | bytes 884744 | tf_op jit(solution)/shard_map/ppermute | solution.py:350
  36.0 0.0 collective-permute-start.10
  36.0 0.0 collective-permute-done.3.link
  36.0 1.8 %cube_near.1.total = f32[3,576,256]{2,1,0:T(8,128)S(1)} custom-call(s32[2]{0:T(128)S(1)} %pad_add_fusion.info, f32[576,128]{1,0:T(8,128)S(1)} %collective-permute-done.3.link, f32[576,256]{1,0:T(8,128)S(1)} %get-tuple-element.56.s_near.near, f32[576,256]{1,0:T(8,128)S(1)} %get-tuple-element.67.far, bf16[2,768,256]{2,1,0:T(8,128)(2,1)S(1)} %get-tuple-element.54.right_near, ...), custom_call_target="tpu_custom_call" | custom-call | flops 4000000000 | bytes 20000000 | tf_op jit(solution)/shard_map/cube_near/pallas_call | solution.py:322
  37.8 0.0 collective-permute-done.8.far
  37.8 1.9 %square_mid.1 = (f32[576,256]{1,0:T(8,128)S(1)}, f32[576,128]{1,0:T(8,128)S(1)}, f32[576,128]{1,0:T(8,128)S(1)}, bf16[2,768,256]{2,1,0:T(8,128)(2,1)S(1)}) custom-call(s32[2]{0:T(128)S(1)} %pad_add_fusion.info, s32[9,9]{1,0:T(8,128)S(1)} %copy-done, f32[864,128]{1,0:T(8,128)S(1)} %collective-permute-done.8.far, ...), custom_call_target="tpu_custom_call" | custom-call | tf_op jit(solution)/shard_map/square_mid/pallas_call | solution.py:322
  39.7 1.8 %collective-permute-start.9 = (f32[576,128]{1,0:T(8,128)S(1)}, f32[576,128]{1,0:T(8,128)S(1)}, u32[]{:S(2)}, u32[]{:S(2)}) collective-permute-start(f32[576,128]{1,0:T(8,128)S(1)} %get-tuple-element.74), channel_id=1, source_target_pairs={{0,7},{1,2},{2,1},{3,4},{4,3},{5,6},{6,5},{7,0},{8,15},{9,10},{10,... | collective-permute-start | bytes 884744 | tf_op jit(solution)/shard_map/ppermute | solution.py:350
  41.4 0.0 collective-permute-start.11
  41.4 3.4 %collective-permute-done.12.link = f32[576,128]{1,0:T(8,128)S(1)} collective-permute-done((f32[576,128]{1,0:T(8,128)S(1)}, f32[576,128]{1,0:T(8,128)S(1)}, u32[]{:S(2)}, u32[]{:S(2)}) %collective-permute-start.12) | collective-permute-done | bytes 294944 | tf_op jit(solution)/shard_map/ppermute | solution.py:350
  44.8 0.0 copy-start.2
  44.8 2.2 %cube_own.1.base = f32[3,576,256]{2,1,0:T(8,128)S(1)} custom-call(s32[2]{0:T(128)S(1)} %pad_add_fusion.info, f32[576,128]{1,0:T(8,128)S(1)} %collective-permute-done.12.link, f32[3,576,256]{2,1,0:T(8,128)S(1)} %cube_near.1.total, f32[576,256]{1,0:T(8,128)S(1)} %get-tuple-element.56.s_near.near, f32[576,256]{1,0:T(8,128)S(1)} %get-tuple-element.80.mid, ...), custom_call_target="tpu_custom_call" | custom-call | flops 4000000000 | bytes 20000000 | tf_op jit(solution)/shard_map/cube_own/pallas_call | solution.py:322
  47.0 0.0 collective-permute-done.10.sides
  47.0 0.0 collective-permute-done.11.chip
  47.0 0.0 copy-done.2
  47.0 3.2 %cube_chip.1 = (f32[3,576,256]{2,1,0:T(8,128)S(1)}, f32[576,576]{1,0:T(8,128)}) custom-call(s32[2]{0:T(128)S(1)} %pad_add_fusion.info, s32[9,9]{1,0:T(8,128)S(1)} %copy-done.2, f32[1152,128]{1,0:T(8,128)S(1)} %collective-permute-done.10.sides, f32[576,128]{1,0:T(8,128)S(1)} %collective-permute-done.11.chip, ...), custom_call_target="tpu_custom_call" | custom-call | flops 4000000000 | bytes 20000000 | tf_op jit(solution)/shard_map/cube_chip/pallas_call | solution.py:322
  50.2 0.1 collective-permute-done.9.link
  50.3 2.2 %finish.1 = f32[576,576]{1,0:T(8,128)} custom-call(s32[2]{0:T(128)S(1)} %pad_add_fusion.info, s32[9,9]{1,0:T(8,128)S(1)} %copy-done.2, f32[576,128]{1,0:T(8,128)S(1)} %collective-permute-done.9.link, bf16[2,3,768,256]{3,2,1,0:T(8,128)(2,1)S(1)} %get-tuple-element.51.own_right, ...), custom_call_target="tpu_custom_call", output_to_operand_aliasing={{}: (5, {})} | custom-call | flops 4000000000 | bytes 20000000 | tf_op jit(solution)/shard_map/finish/pallas_call | solution.py:322
Async XLA Ops:
  0.1 8.9 %copy-start.1 = (f32[576,576]{1,0:T(8,128)S(1)}, f32[576,576]{1,0:T(8,128)}, u32[]{:S(2)}) copy-start(f32[576,576]{1,0:T(8,128)} %tile.2) | copy-start | bytes 3981316
  2.5 6.5 %collective-permute-start.2 = (f32[1728,128]{1,0:T(8,128)S(1)}, f32[1728,128]{1,0:T(8,128)S(1)}, u32[]{:S(2)}, u32[]{:S(2)}) collective-permute-start(f32[1728,128]{1,0:T(8,128)S(1)} %get-tuple-element.46), channel_id=1, source_target_pairs={{0,1},{1,0},{2,3},{3,2},{4,5},{5,4},{6,7},{7,6},{8,9},{9,8},{10,11... | collective-permute-start | bytes 2654216 | tf_op jit(solution)/shard_map/ppermute | solution.py:350
  3.0 13.6 %collective-permute-start.1 = (f32[864,128]{1,0:T(8,128)S(1)}, f32[864,128]{1,0:T(8,128)S(1)}, u32[]{:S(2)}, u32[]{:S(2)}) collective-permute-start(f32[864,128]{1,0:T(8,128)S(1)} %get-tuple-element.45), channel_id=1, source_target_pairs={{0,8},{8,0},{16,24},{24,16},{1,9},{9,1},{17,25},{25,17},{2,10},{10... | collective-permute-start | bytes 1327112 | tf_op jit(solution)/shard_map/ppermute | solution.py:350
  5.6 17.2 %collective-permute-start = (f32[1152,128]{1,0:T(8,128)S(1)}, f32[1152,128]{1,0:T(8,128)S(1)}, u32[]{:S(2)}, u32[]{:S(2)}) collective-permute-start(f32[1152,128]{1,0:T(8,128)S(1)} %get-tuple-element.44), channel_id=1, source_target_pairs={{0,7},{1,2},{2,1},{3,4},{4,3},{5,6},{6,5},{7,0},{8,15},{9,10},{10,... | collective-permute-start | bytes 1769480 | tf_op jit(solution)/shard_map/ppermute | solution.py:350
  9.8 22.0 %collective-permute-start.4 = (f32[576,128]{1,0:T(8,128)S(1)}, f32[576,128]{1,0:T(8,128)S(1)}, u32[]{:S(2)}, u32[]{:S(2)}) collective-permute-start(f32[576,128]{1,0:T(8,128)S(1)} %get-tuple-element.58), channel_id=1, source_target_pairs={{0,7},{1,2},{2,1},{3,4},{4,3},{5,6},{6,5},{7,0},{8,15},{9,10},{10,... | collective-permute-start | bytes 884744 | tf_op jit(solution)/shard_map/ppermute | solution.py:350
  10.6 17.3 %collective-permute-start.6 = (f32[864,128]{1,0:T(8,128)S(1)}, f32[864,128]{1,0:T(8,128)S(1)}, u32[]{:S(2)}, u32[]{:S(2)}) collective-permute-start(f32[864,128]{1,0:T(8,128)S(1)} %get-tuple-element.59), channel_id=1, source_target_pairs={{0,16},{8,24},{16,0},{24,8},{1,17},{9,25},{17,1},{25,9},{2,18},{10... | collective-permute-start | bytes 1327112 | tf_op jit(solution)/shard_map/ppermute | solution.py:350
  12.2 18.2 %collective-permute-start.7 = (f32[864,128]{1,0:T(8,128)S(1)}, f32[864,128]{1,0:T(8,128)S(1)}, u32[]{:S(2)}, u32[]{:S(2)}) collective-permute-start(f32[864,128]{1,0:T(8,128)S(1)} %get-tuple-element.63), channel_id=1, source_target_pairs={{0,8},{8,0},{16,24},{24,16},{1,9},{9,1},{17,25},{25,17},{2,10},{10... | collective-permute-start | bytes 1327112 | tf_op jit(solution)/shard_map/ppermute | solution.py:350
  16.6 15.2 %collective-permute-start.5 = (f32[864,128]{1,0:T(8,128)S(1)}, f32[864,128]{1,0:T(8,128)S(1)}, u32[]{:S(2)}, u32[]{:S(2)}) collective-permute-start(f32[864,128]{1,0:T(8,128)S(1)} %collective-permute-done.1.mid), channel_id=1, source_target_pairs={{0,16},{8,24},{16,0},{24,8},{1,17},{9,25},{17,1},{25,9},{2,18},{10... | collective-permute-start | bytes 1327112 | tf_op jit(solution)/shard_map/ppermute | solution.py:350
  18.6 4.2 %copy-start = (s32[9,9]{1,0:T(8,128)S(1)}, s32[9,9]{1,0:T(8,128)}, u32[]{:S(2)}) copy-start(s32[9,9]{1,0:T(8,128)} %kept.7) | copy-start | bytes 976
  24.2 11.8 %collective-permute-start.3 = (f32[576,128]{1,0:T(8,128)S(1)}, f32[576,128]{1,0:T(8,128)S(1)}, u32[]{:S(2)}, u32[]{:S(2)}) collective-permute-start(f32[576,128]{1,0:T(8,128)S(1)} %get-tuple-element.55), channel_id=1, source_target_pairs={{0,7},{1,2},{2,1},{3,4},{4,3},{5,6},{6,5},{7,0},{8,15},{9,10},{10,... | collective-permute-start | bytes 884744 | tf_op jit(solution)/shard_map/ppermute | solution.py:350
  27.9 9.9 %collective-permute-start.8 = (f32[864,128]{1,0:T(8,128)S(1)}, f32[864,128]{1,0:T(8,128)S(1)}, u32[]{:S(2)}, u32[]{:S(2)}) collective-permute-start(f32[864,128]{1,0:T(8,128)S(1)} %collective-permute-done.6), channel_id=1, source_target_pairs={{0,8},{8,0},{16,24},{24,16},{1,9},{9,1},{17,25},{25,17},{2,10},{10... | collective-permute-start | bytes 1327112 | tf_op jit(solution)/shard_map/ppermute | solution.py:350
  33.7 11.2 %collective-permute-start.12 = (f32[576,128]{1,0:T(8,128)S(1)}, f32[576,128]{1,0:T(8,128)S(1)}, u32[]{:S(2)}, u32[]{:S(2)}) collective-permute-start(f32[576,128]{1,0:T(8,128)S(1)} %get-tuple-element.78), channel_id=1, source_target_pairs={{0,7},{1,2},{2,1},{3,4},{4,3},{5,6},{6,5},{7,0},{8,15},{9,10},{10,... | collective-permute-start | bytes 884744 | tf_op jit(solution)/shard_map/ppermute | solution.py:350
  36.0 11.0 %collective-permute-start.10 = (f32[1152,128]{1,0:T(8,128)S(1)}, f32[1152,128]{1,0:T(8,128)S(1)}, u32[]{:S(2)}, u32[]{:S(2)}) collective-permute-start(f32[1152,128]{1,0:T(8,128)S(1)} %get-tuple-element.75), channel_id=1, source_target_pairs={{0,1},{1,0},{2,3},{3,2},{4,5},{5,4},{6,7},{7,6},{8,9},{9,8},{10,11... | collective-permute-start | bytes 1769480 | tf_op jit(solution)/shard_map/ppermute | solution.py:350
  39.7 10.6 %collective-permute-start.9 = (f32[576,128]{1,0:T(8,128)S(1)}, f32[576,128]{1,0:T(8,128)S(1)}, u32[]{:S(2)}, u32[]{:S(2)}) collective-permute-start(f32[576,128]{1,0:T(8,128)S(1)} %get-tuple-element.74), channel_id=1, source_target_pairs={{0,7},{1,2},{2,1},{3,4},{4,3},{5,6},{6,5},{7,0},{8,15},{9,10},{10,... | collective-permute-start | bytes 884744 | tf_op jit(solution)/shard_map/ppermute | solution.py:350
  41.4 5.6 %collective-permute-start.11 = (f32[576,128]{1,0:T(8,128)S(1)}, f32[576,128]{1,0:T(8,128)S(1)}, u32[]{:S(2)}, u32[]{:S(2)}) collective-permute-start(f32[576,128]{1,0:T(8,128)S(1)} %get-tuple-element.76), channel_id=1, source_target_pairs={{0,1},{1,0},{2,3},{3,2},{4,5},{5,4},{6,7},{7,6},{8,9},{9,8},{10,11... | collective-permute-start | bytes 884744 | tf_op jit(solution)/shard_map/ppermute | solution.py:350
  44.8 2.2 %copy-start.2 = (s32[9,9]{1,0:T(8,128)S(1)}, s32[9,9]{1,0:T(8,128)}, u32[]{:S(2)}) copy-start(s32[9,9]{1,0:T(8,128)} %kept.9) | copy-start | bytes 976

commit v13 on v12

--- a/solution.py
+++ b/solution.py
@@ -241,16 +241,12 @@
         out[part, shared_rows(info, LINK, group), :] += passes([other], [right(ref, info, LINK)])
 
 
-def cube_own_body(info, link, total, near, mid, far, own_right, right_far, mid_far, out):
-    group = near.shape[0] // 3
+def cube_own_body(info, total, near, mid, far, own_right, mid_far, out):
     own_mid, own_far = split(mid[...]), split(far[...])
-    link_far = split(unfold(link[...]))
     rights = [right(own_right, info, OWN, part) for part in range(3)]
     out[NEAR] = 3.0 * near[...] - 2.0 * (total[NEAR] + passes([own_mid], rights[NEAR:MID]))
     out[MID] = 3.0 * mid[...] - 2.0 * (total[MID] + passes([own_mid, own_far], [rights[MID], right(mid_far, info, OWN)]))
     out[FAR] = 3.0 * far[...] - 2.0 * (total[FAR] + passes([own_mid], rights[FAR:]))
-    for part, ref in ((MID, mid_far), (FAR, right_far)):
-        out[part, shared_rows(info, LINK, group), :] -= 2.0 * passes([link_far], [right(ref, info, LINK)])
 
 
 def send_rows(info, tile, out, sem, row, near, mid, far):
@@ -264,7 +260,7 @@
     return copy
 
 
-def cube_chip_body(info, kept, sides, chip, own_right, right_near, right_far, mid_near, mid_far, base, out, result, tile, sem):
+def cube_chip_body(info, kept, link, sides, chip, own_right, right_near, right_far, mid_near, mid_far, base, out, result, tile, sem):
     group = base.shape[1] // 3
     chip_start = place(info, CHIP, group)[0]
     rest = pl.multiple_of(2 * chip_start, 64)
@@ -276,6 +272,8 @@
         (chips, [right(mid_near, info, CHIP), own[MID], right(mid_far, info, CHIP)]),
         (chips[1:], [own[FAR], right(right_far, info, CHIP)]),
     )
+    for part in range(3):
+        out[part, pl.ds(link_only, group), :] = base[part, pl.ds(link_only, group), :]
     for part, factors in enumerate(products):
         out[part, shared_rows(info, CHIP, group), :] = base[part, shared_rows(info, CHIP, group), :] - 2.0 * passes(*factors)
 
@@ -284,8 +282,9 @@
         return [masked(out[part, at, :], kept, mask_at(info, part), row // 64) for part in range(3)]
 
     copy = send_rows(info, tile, result, sem, rest, *finished(rest))
-    for part in range(3):
-        out[part, pl.ds(link_only, group), :] = base[part, pl.ds(link_only, group), :]
+    link_far = split(unfold(link[...]))
+    for part, ref in ((MID, mid_far), (FAR, right_far)):
+        out[part, shared_rows(info, LINK, group), :] -= 2.0 * passes([link_far], [right(ref, info, LINK)])
     for row in (group, link_only):
         for part, value in enumerate(finished(row)):
             out[part, pl.ds(row, group), :] = value
@@ -296,14 +295,14 @@
     del begun
     group = tile.shape[1]
     start, first_row = place(info, LINK, group)[0], place(info, LINK, 3)[0]
-    link_mid = unfold(link[...])
+    factor = split(unfold(link[...]))
+    products = [-2.0 * passes([factor], [right(own_right, info, LINK, part)]) for part in range(3)]
     copies = []
     for half in range(2):
-        factor = split(link_mid[half * group : (half + 1) * group])
         row = pl.multiple_of(start + half * group, 64)
         values = []
         for part in range(3):
-            value = -2.0 * passes([factor], [right(own_right, info, LINK, part)])
+            value = products[part][half * group : (half + 1) * group]
             value = masked(value, kept, mask_at(info, part), first_row + 3 * half)
             values.append(base[part, pl.ds(row, group), :] + value)
         copies.append(send_rows(info, tile.at[half], result, sem.at[half], row, *values))
@@ -433,7 +432,7 @@
         cube_own_body,
         "cube_own",
         (info,),
-        (far_link, total, s_near, s_mid, s_far, own_right, right_far, mid_far),
+        (total, s_near, s_mid, s_far, own_right, mid_far),
         [three_wide],
     )
     result = ((side, side), F32)
@@ -441,7 +440,7 @@
         cube_chip_body,
         "cube_chip",
         (info, result_kept),
-        (sides_chip, mid_chip, own_right, right_near, right_far, mid_near, mid_far, base),
+        (far_link, sides_chip, mid_chip, own_right, right_near, right_far, mid_near, mid_far, base),
         [three_wide, result],
         result=True,
         scratch=[pltpu.VMEM((group, side), F32), pltpu.SemaphoreType.DMA(())],

time: 52.7 us -> 52.8 us (level)
  transfers between devices with their start and end apart: 13 -> 13, of which waited for: 4 -> 4; matrix products, arithmetic and copies ran while one was open for 0% -> 0% of each run, Pallas kernels for 36% -> 35%
where the time goes in v13:
time: 52.8 us; the launch traced here: 52.6 us
  Pallas kernels  23.4 us (44%)
  starting transfers between devices  20.7 us (39%)
  waiting for transfers between devices  8.32 us (16%)
    pallas_call x13, Pallas kernels, call(): pl.pallas_call(body, out_shape=[jax.ShapeDtypeStruct(shape, kind) for sha...  23.4 us
    ppermute x13, starting transfers between devices, exchange(): lax.ppermute(value, axis, [(i, (i + (even_step if i % 2 == 0 else -even_s...  20.7 us
    ppermute x13, waiting for transfers between devices, exchange(): lax.ppermute(value, axis, [(i, (i + (even_step if i % 2 == 0 else -even_s...  8.32 us
  transfers between devices with their start and end apart: 13, of which 4 were waited for; matrix products, arithmetic and copies ran while one was open for 0% of the time, Pallas kernels for 35%

profile of v13, /device:TPU:0, one launch (start us, length us, event | category | flops | bytes accessed | tf_op | source)
XLA Modules:
  0.0 52.6 jit_solution(13720849132529589530)
XLA Ops:
  0.0 0.1 pad_add_fusion.info
  0.1 0.0 copy-start.1
  0.1 2.4 %pack_first.1 = (f32[864,128]{1,0:T(8,128)S(1)}, f32[1152,128]{1,0:T(8,128)S(1)}, f32[1728,128]{1,0:T(8,128)S(1)}) custom-call(s32[2]{0:T(128)S(1)} %pad_add_fusion.info, f32[576,576]{1,0:T(8,128)} %tile.2), custom_call_target="tpu_custom_call" | custom-call | flops 4000000000 | bytes 20000000 | tf_op jit(solution)/shard_map/pack_first/pallas_call | solution.py:321
  2.5 0.5 %collective-permute-start.2 = (f32[1728,128]{1,0:T(8,128)S(1)}, f32[1728,128]{1,0:T(8,128)S(1)}, u32[]{:S(2)}, u32[]{:S(2)}) collective-permute-start(f32[1728,128]{1,0:T(8,128)S(1)} %get-tuple-element.46), channel_id=1, source_target_pairs={{0,1},{1,0},{2,3},{3,2},{4,5},{5,4},{6,7},{7,6},{8,9},{9,8},{10,11... | collective-permute-start | bytes 2654216 | tf_op jit(solution)/shard_map/ppermute | solution.py:349
  3.0 2.6 %collective-permute-start.1 = (f32[864,128]{1,0:T(8,128)S(1)}, f32[864,128]{1,0:T(8,128)S(1)}, u32[]{:S(2)}, u32[]{:S(2)}) collective-permute-start(f32[864,128]{1,0:T(8,128)S(1)} %get-tuple-element.45), channel_id=1, source_target_pairs={{0,8},{8,0},{16,24},{24,16},{1,9},{9,1},{17,25},{25,17},{2,10},{10... | collective-permute-start | bytes 1327112 | tf_op jit(solution)/shard_map/ppermute | solution.py:349
  5.6 3.4 %collective-permute-start = (f32[1152,128]{1,0:T(8,128)S(1)}, f32[1152,128]{1,0:T(8,128)S(1)}, u32[]{:S(2)}, u32[]{:S(2)}) collective-permute-start(f32[1152,128]{1,0:T(8,128)S(1)} %get-tuple-element.44), channel_id=1, source_target_pairs={{0,7},{1,2},{2,1},{3,4},{4,3},{5,6},{6,5},{7,0},{8,15},{9,10},{10,... | collective-permute-start | bytes 1769480 | tf_op jit(solution)/shard_map/ppermute | solution.py:349
  9.0 0.0 collective-permute-done.2.chip
  9.0 0.0 copy-done.1
  9.0 0.8 %pack_rest.1 = (f32[576,128]{1,0:T(8,128)S(1)}, f32[864,128]{1,0:T(8,128)S(1)}, f32[864,128]{1,0:T(8,128)S(1)}) custom-call(s32[2]{0:T(128)S(1)} %pad_add_fusion.info, f32[576,576]{1,0:T(8,128)S(1)} %copy-done.1), custom_call_target="tpu_custom_call" | custom-call | flops 4000000000 | bytes 20000000 | tf_op jit(solution)/shard_map/pack_rest/pallas_call | solution.py:321
  9.8 0.9 %collective-permute-start.4 = (f32[576,128]{1,0:T(8,128)S(1)}, f32[576,128]{1,0:T(8,128)S(1)}, u32[]{:S(2)}, u32[]{:S(2)}) collective-permute-start(f32[576,128]{1,0:T(8,128)S(1)} %get-tuple-element.58), channel_id=1, source_target_pairs={{0,7},{1,2},{2,1},{3,4},{4,3},{5,6},{6,5},{7,0},{8,15},{9,10},{10,... | collective-permute-start | bytes 884744 | tf_op jit(solution)/shard_map/ppermute | solution.py:349
  10.6 1.5 %collective-permute-start.6 = (f32[864,128]{1,0:T(8,128)S(1)}, f32[864,128]{1,0:T(8,128)S(1)}, u32[]{:S(2)}, u32[]{:S(2)}) collective-permute-start(f32[864,128]{1,0:T(8,128)S(1)} %get-tuple-element.59), channel_id=1, source_target_pairs={{0,16},{8,24},{16,0},{24,8},{1,17},{9,25},{17,1},{25,9},{2,18},{10... | collective-permute-start | bytes 1327112 | tf_op jit(solution)/shard_map/ppermute | solution.py:349
  12.2 1.5 %collective-permute-start.7 = (f32[864,128]{1,0:T(8,128)S(1)}, f32[864,128]{1,0:T(8,128)S(1)}, u32[]{:S(2)}, u32[]{:S(2)}) collective-permute-start(f32[864,128]{1,0:T(8,128)S(1)} %get-tuple-element.63), channel_id=1, source_target_pairs={{0,8},{8,0},{16,24},{24,16},{1,9},{9,1},{17,25},{25,17},{2,10},{10... | collective-permute-start | bytes 1327112 | tf_op jit(solution)/shard_map/ppermute | solution.py:349
  13.7 1.0 %prepare.1 = (bf16[2,3,576,256]{3,2,1,0:T(8,128)(2,1)S(1)}, bf16[2,3,768,256]{3,2,1,0:T(8,128)(2,1)S(1)}, bf16[2,3,384,256]{3,2,1,0:T(8,128)(2,1)S(1)}) custom-call(s32[2]{0:T(128)S(1)} %pad_add_fusion.info, f32[576,576]{1,0:T(8,128)S(1)} %copy-done.1, f32[1728,128]{1,0:T(8,128)S(1)} %collective-permute-done.2.chip), custom_call_target="tpu_custom_call" | custom-call | flops 4000000000 | bytes 20000000 | tf_op jit(solution)/shard_map/prepare/pallas_call | solution.py:321
  14.7 1.9 %collective-permute-done.1.mid = f32[864,128]{1,0:T(8,128)S(1)} collective-permute-done((f32[864,128]{1,0:T(8,128)S(1)}, f32[864,128]{1,0:T(8,128)S(1)}, u32[]{:S(2)}, u32[]{:S(2)}) %collective-permute-start.1) | collective-permute-done | bytes 442400 | tf_op jit(solution)/shard_map/ppermute | solution.py:349
  16.6 2.0 %collective-permute-start.5 = (f32[864,128]{1,0:T(8,128)S(1)}, f32[864,128]{1,0:T(8,128)S(1)}, u32[]{:S(2)}, u32[]{:S(2)}) collective-permute-start(f32[864,128]{1,0:T(8,128)S(1)} %collective-permute-done.1.mid), channel_id=1, source_target_pairs={{0,16},{8,24},{16,0},{24,8},{1,17},{9,25},{17,1},{25,9},{2,18},{10... | collective-permute-start | bytes 1327112 | tf_op jit(solution)/shard_map/ppermute | solution.py:349
  18.6 0.0 copy-start
  18.6 1.6 %near_start.1 = (f32[576,256]{1,0:T(8,128)S(1)}, bf16[2,768,256]{2,1,0:T(8,128)(2,1)S(1)}) custom-call(s32[2]{0:T(128)S(1)} %pad_add_fusion.info, f32[864,128]{1,0:T(8,128)S(1)} %collective-permute-done.1.mid, bf16[2,3,576,256]{3,2,1,0:T(8,128)(2,1)S(1)} %get-tuple-element.50.own_left, bf16[2,3,768,256]{3,2,1,0:T(8,128)(2,1)S(1)} %get-tuple-element.51.own_right, ...), custom_call_target="tpu_custom_call" | custom-call | flops 4000000000 | bytes 20000000 | tf_op jit(solution)/shard_map/near_start/pallas_call | solution.py:321
  20.2 2.6 %collective-permute-done.link_a = f32[1152,128]{1,0:T(8,128)S(1)} collective-permute-done((f32[1152,128]{1,0:T(8,128)S(1)}, f32[1152,128]{1,0:T(8,128)S(1)}, u32[]{:S(2)}, u32[]{:S(2)}) %collective-permute-start) | collective-permute-done | bytes 589856 | tf_op jit(solution)/shard_map/ppermute | solution.py:349
  22.8 0.0 copy-done
  22.8 1.4 %square_near.1 = (f32[576,256]{1,0:T(8,128)S(1)}, f32[576,128]{1,0:T(8,128)S(1)}, bf16[2,2,384,256]{3,2,1,0:T(8,128)(2,1)S(1)}) custom-call(s32[2]{0:T(128)S(1)} %pad_add_fusion.info, s32[9,9]{1,0:T(8,128)S(1)} %copy-done, f32[1152,128]{1,0:T(8,128)S(1)} %collective-permute-done.link_a, f32[576,256]{1,0:T(8,128)S(1)} %get-tuple-element.53.begun, ...), custom_call_target="tpu_custom_call" | custom-call | flops 4000000000 | bytes 20000000 | tf_op jit(solution)/shard_map/square_near/pallas_call | solution.py:321
  24.2 3.7 %collective-permute-start.3 = (f32[576,128]{1,0:T(8,128)S(1)}, f32[576,128]{1,0:T(8,128)S(1)}, u32[]{:S(2)}, u32[]{:S(2)}) collective-permute-start(f32[576,128]{1,0:T(8,128)S(1)} %get-tuple-element.55), channel_id=1, source_target_pairs={{0,7},{1,2},{2,1},{3,4},{4,3},{5,6},{6,5},{7,0},{8,15},{9,10},{10,... | collective-permute-start | bytes 884744 | tf_op jit(solution)/shard_map/ppermute | solution.py:349
  27.9 0.0 collective-permute-done.6
  27.9 0.5 %collective-permute-start.8 = (f32[864,128]{1,0:T(8,128)S(1)}, f32[864,128]{1,0:T(8,128)S(1)}, u32[]{:S(2)}, u32[]{:S(2)}) collective-permute-start(f32[864,128]{1,0:T(8,128)S(1)} %collective-permute-done.6), channel_id=1, source_target_pairs={{0,8},{8,0},{16,24},{24,16},{1,9},{9,1},{17,25},{25,17},{2,10},{10... | collective-permute-start | bytes 1327112 | tf_op jit(solution)/shard_map/ppermute | solution.py:349
  28.5 1.9 %middle_products.1 = (f32[576,256]{1,0:T(8,128)S(1)}, f32[576,256]{1,0:T(8,128)S(1)}) custom-call(s32[2]{0:T(128)S(1)} %pad_add_fusion.info, bf16[2,3,576,256]{3,2,1,0:T(8,128)(2,1)S(1)} %get-tuple-element.50.own_left, bf16[2,3,768,256]{3,2,1,0:T(8,128)(2,1)S(1)} %get-tuple-element.51.own_right, bf16[2,3,384,256]{3,2,1,0:T(8,128)(2,1)S(1)} %get-tuple-element.52.chip_left, ...), custom_call_target="tpu_custom_call" | custom-call | flops 4000000000 | bytes 20000000 | tf_op jit(solution)/shard_map/middle_products/pallas_call | solution.py:321
  30.4 0.0 collective-permute-done.7.near
  30.4 1.4 %mid_start.1 = (f32[576,256]{1,0:T(8,128)S(1)}, bf16[2,768,256]{2,1,0:T(8,128)(2,1)S(1)}) custom-call(s32[2]{0:T(128)S(1)} %pad_add_fusion.info, f32[864,128]{1,0:T(8,128)S(1)} %collective-permute-done.7.near, f32[576,256]{1,0:T(8,128)S(1)} %get-tuple-element.64.begun, bf16[2,3,576,256]{3,2,1,0:T(8,128)(2,1)S(1)} %get-tuple-element.50.own_left, ...), custom_call_target="tpu_custom_call" | custom-call | flops 4000000000 | bytes 20000000 | tf_op jit(solution)/shard_map/mid_start/pallas_call | solution.py:321
  31.8 0.0 collective-permute-done.4.link_b
  31.8 0.0 collective-permute-done.5.mid
  31.8 1.9 %square_far.1 = (f32[576,256]{1,0:T(8,128)S(1)}, f32[576,128]{1,0:T(8,128)S(1)}, f32[1152,128]{1,0:T(8,128)S(1)}, bf16[2,384,256]{2,1,0:T(8,128)(2,1)S(1)}, bf16[2,768,256]{2,1,0:T(8,128)(2,1)S(1)}) custom-call(s32[2]{0:T(128)S(1)} %pad_add_fusion.info, s32[9,9]{1,0:T(8,128)S(1)} %copy-done, f32[576,128]{1,0:T(8,128)S(1)} %collective-permute-done.4.link_b, ...), custom_call_target="tpu_custom_call" | custom-call | flops 4000000000 | bytes 20000000 | tf_op jit(solution)/shard_map/square_far/pallas_call | solution.py:321
  33.6 2.3 %collective-permute-start.10 = (f32[576,128]{1,0:T(8,128)S(1)}, f32[576,128]{1,0:T(8,128)S(1)}, u32[]{:S(2)}, u32[]{:S(2)}) collective-permute-start(f32[576,128]{1,0:T(8,128)S(1)} %get-tuple-element.75), channel_id=1, source_target_pairs={{0,7},{1,2},{2,1},{3,4},{4,3},{5,6},{6,5},{7,0},{8,15},{9,10},{10,... | collective-permute-start | bytes 884744 | tf_op jit(solution)/shard_map/ppermute | solution.py:349
  36.0 0.0 collective-permute-start.11
  36.0 0.0 collective-permute-done.3.link
  36.0 1.8 %cube_near.1.total = f32[3,576,256]{2,1,0:T(8,128)S(1)} custom-call(s32[2]{0:T(128)S(1)} %pad_add_fusion.info, f32[576,128]{1,0:T(8,128)S(1)} %collective-permute-done.3.link, f32[576,256]{1,0:T(8,128)S(1)} %get-tuple-element.56.s_near.near, f32[576,256]{1,0:T(8,128)S(1)} %get-tuple-element.67.far, bf16[2,768,256]{2,1,0:T(8,128)(2,1)S(1)} %get-tuple-element.54.right_near, ...), custom_call_target="tpu_custom_call" | custom-call | flops 4000000000 | bytes 20000000 | tf_op jit(solution)/shard_map/cube_near/pallas_call | solution.py:321
  37.8 0.0 collective-permute-done.8.far
  37.8 1.9 %square_mid.1 = (f32[576,256]{1,0:T(8,128)S(1)}, f32[576,128]{1,0:T(8,128)S(1)}, f32[576,128]{1,0:T(8,128)S(1)}, bf16[2,768,256]{2,1,0:T(8,128)(2,1)S(1)}) custom-call(s32[2]{0:T(128)S(1)} %pad_add_fusion.info, s32[9,9]{1,0:T(8,128)S(1)} %copy-done, f32[864,128]{1,0:T(8,128)S(1)} %collective-permute-done.8.far, ...), custom_call_target="tpu_custom_call" | custom-call | tf_op jit(solution)/shard_map/square_mid/pallas_call | solution.py:321
  39.7 1.8 %collective-permute-start.9 = (f32[576,128]{1,0:T(8,128)S(1)}, f32[576,128]{1,0:T(8,128)S(1)}, u32[]{:S(2)}, u32[]{:S(2)}) collective-permute-start(f32[576,128]{1,0:T(8,128)S(1)} %get-tuple-element.74), channel_id=1, source_target_pairs={{0,7},{1,2},{2,1},{3,4},{4,3},{5,6},{6,5},{7,0},{8,15},{9,10},{10,... | collective-permute-start | bytes 884744 | tf_op jit(solution)/shard_map/ppermute | solution.py:349
  41.4 0.0 collective-permute-start.12
  41.4 0.0 copy-start.2
  41.5 1.7 %cube_own.1.base = f32[3,576,256]{2,1,0:T(8,128)S(1)} custom-call(s32[2]{0:T(128)S(1)} %pad_add_fusion.info, f32[3,576,256]{2,1,0:T(8,128)S(1)} %cube_near.1.total, f32[576,256]{1,0:T(8,128)S(1)} %get-tuple-element.56.s_near.near, f32[576,256]{1,0:T(8,128)S(1)} %get-tuple-element.80.mid, f32[576,256]{1,0:T(8,128)S(1)} %get-tuple-element.67.far, ...), custom_call_target="tpu_custom_call" | custom-call | flops 4000000000 | bytes 20000000 | tf_op jit(solution)/shard_map/cube_own/pallas_call | solution.py:321
  43.2 1.6 %collective-permute-done.10.link = f32[576,128]{1,0:T(8,128)S(1)} collective-permute-done((f32[576,128]{1,0:T(8,128)S(1)}, f32[576,128]{1,0:T(8,128)S(1)}, u32[]{:S(2)}, u32[]{:S(2)}) %collective-permute-start.10) | collective-permute-done | bytes 294944 | tf_op jit(solution)/shard_map/ppermute | solution.py:349
  44.8 0.0 collective-permute-done.11.sides
  44.8 0.0 collective-permute-done.12.chip
  44.8 0.0 copy-done.2
  44.8 3.3 %cube_chip.1 = (f32[3,576,256]{2,1,0:T(8,128)S(1)}, f32[576,576]{1,0:T(8,128)}) custom-call(s32[2]{0:T(128)S(1)} %pad_add_fusion.info, s32[9,9]{1,0:T(8,128)S(1)} %copy-done.2, f32[576,128]{1,0:T(8,128)S(1)} %collective-permute-done.10.link, f32[1152,128]{1,0:T(8,128)S(1)} %collective-permute-done.11.sides, f32[576,128]{1,0:T(8,128)S(1)} %collective-permute-done.12.chip, ...), custom_call_target="tpu_custom_call" | custom-call | flops 4000000000 | bytes 20000000 | tf_op jit(solution)/shard_map/cube_chip/pallas_call | solution.py:321
  48.2 2.1 %collective-permute-done.9.link = f32[576,128]{1,0:T(8,128)S(1)} collective-permute-done((f32[576,128]{1,0:T(8,128)S(1)}, f32[576,128]{1,0:T(8,128)S(1)}, u32[]{:S(2)}, u32[]{:S(2)}) %collective-permute-start.9) | collective-permute-done | bytes 294944 | tf_op jit(solution)/shard_map/ppermute | solution.py:349
  50.3 2.3 %finish.1 = f32[576,576]{1,0:T(8,128)} custom-call(s32[2]{0:T(128)S(1)} %pad_add_fusion.info, s32[9,9]{1,0:T(8,128)S(1)} %copy-done.2, f32[576,128]{1,0:T(8,128)S(1)} %collective-permute-done.9.link, bf16[2,3,768,256]{3,2,1,0:T(8,128)(2,1)S(1)} %get-tuple-element.51.own_right, ...), custom_call_target="tpu_custom_call", output_to_operand_aliasing={{}: (5, {})} | custom-call | flops 4000000000 | bytes 20000000 | tf_op jit(solution)/shard_map/finish/pallas_call | solution.py:321
Async XLA Ops:
  0.1 8.9 %copy-start.1 = (f32[576,576]{1,0:T(8,128)S(1)}, f32[576,576]{1,0:T(8,128)}, u32[]{:S(2)}) copy-start(f32[576,576]{1,0:T(8,128)} %tile.2) | copy-start | bytes 3981316
  2.5 6.5 %collective-permute-start.2 = (f32[1728,128]{1,0:T(8,128)S(1)}, f32[1728,128]{1,0:T(8,128)S(1)}, u32[]{:S(2)}, u32[]{:S(2)}) collective-permute-start(f32[1728,128]{1,0:T(8,128)S(1)} %get-tuple-element.46), channel_id=1, source_target_pairs={{0,1},{1,0},{2,3},{3,2},{4,5},{5,4},{6,7},{7,6},{8,9},{9,8},{10,11... | collective-permute-start | bytes 2654216 | tf_op jit(solution)/shard_map/ppermute | solution.py:349
  3.0 13.6 %collective-permute-start.1 = (f32[864,128]{1,0:T(8,128)S(1)}, f32[864,128]{1,0:T(8,128)S(1)}, u32[]{:S(2)}, u32[]{:S(2)}) collective-permute-start(f32[864,128]{1,0:T(8,128)S(1)} %get-tuple-element.45), channel_id=1, source_target_pairs={{0,8},{8,0},{16,24},{24,16},{1,9},{9,1},{17,25},{25,17},{2,10},{10... | collective-permute-start | bytes 1327112 | tf_op jit(solution)/shard_map/ppermute | solution.py:349
  5.6 17.2 %collective-permute-start = (f32[1152,128]{1,0:T(8,128)S(1)}, f32[1152,128]{1,0:T(8,128)S(1)}, u32[]{:S(2)}, u32[]{:S(2)}) collective-permute-start(f32[1152,128]{1,0:T(8,128)S(1)} %get-tuple-element.44), channel_id=1, source_target_pairs={{0,7},{1,2},{2,1},{3,4},{4,3},{5,6},{6,5},{7,0},{8,15},{9,10},{10,... | collective-permute-start | bytes 1769480 | tf_op jit(solution)/shard_map/ppermute | solution.py:349
  9.8 22.0 %collective-permute-start.4 = (f32[576,128]{1,0:T(8,128)S(1)}, f32[576,128]{1,0:T(8,128)S(1)}, u32[]{:S(2)}, u32[]{:S(2)}) collective-permute-start(f32[576,128]{1,0:T(8,128)S(1)} %get-tuple-element.58), channel_id=1, source_target_pairs={{0,7},{1,2},{2,1},{3,4},{4,3},{5,6},{6,5},{7,0},{8,15},{9,10},{10,... | collective-permute-start | bytes 884744 | tf_op jit(solution)/shard_map/ppermute | solution.py:349
  10.6 17.3 %collective-permute-start.6 = (f32[864,128]{1,0:T(8,128)S(1)}, f32[864,128]{1,0:T(8,128)S(1)}, u32[]{:S(2)}, u32[]{:S(2)}) collective-permute-start(f32[864,128]{1,0:T(8,128)S(1)} %get-tuple-element.59), channel_id=1, source_target_pairs={{0,16},{8,24},{16,0},{24,8},{1,17},{9,25},{17,1},{25,9},{2,18},{10... | collective-permute-start | bytes 1327112 | tf_op jit(solution)/shard_map/ppermute | solution.py:349
  12.2 18.2 %collective-permute-start.7 = (f32[864,128]{1,0:T(8,128)S(1)}, f32[864,128]{1,0:T(8,128)S(1)}, u32[]{:S(2)}, u32[]{:S(2)}) collective-permute-start(f32[864,128]{1,0:T(8,128)S(1)} %get-tuple-element.63), channel_id=1, source_target_pairs={{0,8},{8,0},{16,24},{24,16},{1,9},{9,1},{17,25},{25,17},{2,10},{10... | collective-permute-start | bytes 1327112 | tf_op jit(solution)/shard_map/ppermute | solution.py:349
  16.6 15.2 %collective-permute-start.5 = (f32[864,128]{1,0:T(8,128)S(1)}, f32[864,128]{1,0:T(8,128)S(1)}, u32[]{:S(2)}, u32[]{:S(2)}) collective-permute-start(f32[864,128]{1,0:T(8,128)S(1)} %collective-permute-done.1.mid), channel_id=1, source_target_pairs={{0,16},{8,24},{16,0},{24,8},{1,17},{9,25},{17,1},{25,9},{2,18},{10... | collective-permute-start | bytes 1327112 | tf_op jit(solution)/shard_map/ppermute | solution.py:349
  18.6 4.2 %copy-start = (s32[9,9]{1,0:T(8,128)S(1)}, s32[9,9]{1,0:T(8,128)}, u32[]{:S(2)}) copy-start(s32[9,9]{1,0:T(8,128)} %kept.7) | copy-start | bytes 976
  24.2 11.8 %collective-permute-start.3 = (f32[576,128]{1,0:T(8,128)S(1)}, f32[576,128]{1,0:T(8,128)S(1)}, u32[]{:S(2)}, u32[]{:S(2)}) collective-permute-start(f32[576,128]{1,0:T(8,128)S(1)} %get-tuple-element.55), channel_id=1, source_target_pairs={{0,7},{1,2},{2,1},{3,4},{4,3},{5,6},{6,5},{7,0},{8,15},{9,10},{10,... | collective-permute-start | bytes 884744 | tf_op jit(solution)/shard_map/ppermute | solution.py:349
  27.9 9.8 %collective-permute-start.8 = (f32[864,128]{1,0:T(8,128)S(1)}, f32[864,128]{1,0:T(8,128)S(1)}, u32[]{:S(2)}, u32[]{:S(2)}) collective-permute-start(f32[864,128]{1,0:T(8,128)S(1)} %collective-permute-done.6), channel_id=1, source_target_pairs={{0,8},{8,0},{16,24},{24,16},{1,9},{9,1},{17,25},{25,17},{2,10},{10... | collective-permute-start | bytes 1327112 | tf_op jit(solution)/shard_map/ppermute | solution.py:349
  33.6 11.2 %collective-permute-start.10 = (f32[576,128]{1,0:T(8,128)S(1)}, f32[576,128]{1,0:T(8,128)S(1)}, u32[]{:S(2)}, u32[]{:S(2)}) collective-permute-start(f32[576,128]{1,0:T(8,128)S(1)} %get-tuple-element.75), channel_id=1, source_target_pairs={{0,7},{1,2},{2,1},{3,4},{4,3},{5,6},{6,5},{7,0},{8,15},{9,10},{10,... | collective-permute-start | bytes 884744 | tf_op jit(solution)/shard_map/ppermute | solution.py:349
  36.0 8.8 %collective-permute-start.11 = (f32[1152,128]{1,0:T(8,128)S(1)}, f32[1152,128]{1,0:T(8,128)S(1)}, u32[]{:S(2)}, u32[]{:S(2)}) collective-permute-start(f32[1152,128]{1,0:T(8,128)S(1)} %get-tuple-element.76), channel_id=1, source_target_pairs={{0,1},{1,0},{2,3},{3,2},{4,5},{5,4},{6,7},{7,6},{8,9},{9,8},{10,11... | collective-permute-start | bytes 1769480 | tf_op jit(solution)/shard_map/ppermute | solution.py:349
  39.7 10.6 %collective-permute-start.9 = (f32[576,128]{1,0:T(8,128)S(1)}, f32[576,128]{1,0:T(8,128)S(1)}, u32[]{:S(2)}, u32[]{:S(2)}) collective-permute-start(f32[576,128]{1,0:T(8,128)S(1)} %get-tuple-element.74), channel_id=1, source_target_pairs={{0,7},{1,2},{2,1},{3,4},{4,3},{5,6},{6,5},{7,0},{8,15},{9,10},{10,... | collective-permute-start | bytes 884744 | tf_op jit(solution)/shard_map/ppermute | solution.py:349
  41.4 3.4 %collective-permute-start.12 = (f32[576,128]{1,0:T(8,128)S(1)}, f32[576,128]{1,0:T(8,128)S(1)}, u32[]{:S(2)}, u32[]{:S(2)}) collective-permute-start(f32[576,128]{1,0:T(8,128)S(1)} %get-tuple-element.77), channel_id=1, source_target_pairs={{0,1},{1,0},{2,3},{3,2},{4,5},{5,4},{6,7},{7,6},{8,9},{9,8},{10,11... | collective-permute-start | bytes 884744 | tf_op jit(solution)/shard_map/ppermute | solution.py:349
  41.4 3.4 %copy-start.2 = (s32[9,9]{1,0:T(8,128)S(1)}, s32[9,9]{1,0:T(8,128)}, u32[]{:S(2)}) copy-start(s32[9,9]{1,0:T(8,128)} %kept.9) | copy-start | bytes 976

commit v14 on v13

--- a/solution.py
+++ b/solution.py
@@ -1,3 +1,5 @@
+import functools
+
 import jax
 import jax.numpy as jnp
 from jax import lax
@@ -221,14 +223,16 @@
         out[shared_rows(info, who, group), :] += passes([left(lefts, NEAR)], [right(rights, info, who)])
 
 
-def mid_body(info, kept, far, own_left, chip_left, link_left, begun, out, chip, link, rights):
+def mid_body(info, kept, far, own_left, chip_left, link_left, begun, out, chip, link_first, link_second, rights):
     group = out.shape[0] // 3
     store_right(rights, (), unfold(far[...]))
     out[...] = begun[...] + passes([left(own_left, FAR)], [right(rights, info, OWN)])
     for who, factor in ((CHIP, left(chip_left, FAR)), (LINK, left(link_left))):
         out[shared_rows(info, who, group), :] += passes([factor], [right(rights, info, who)])
     out[...] = masked(out[...], kept, 3)
-    store_fold(link, 0, out[shared_rows(info, LINK, group), :])
+    start = place(info, LINK, group)[0]
+    for k, link in enumerate((link_first, link_second)):
+        store_fold(link, 0, out[pl.ds(pl.multiple_of(start + k * group, 64), group), :])
     store_fold(chip, 0, out[shared_rows(info, CHIP, group), :])
 
 
@@ -291,23 +295,17 @@
     copy.wait()
 
 
-def finish_body(info, kept, link, own_right, base, begun, result, tile, sem):
+def finish_body(half, info, kept, link, own_right, base, begun, result, tile, sem):
     del begun
-    group = tile.shape[1]
-    start, first_row = place(info, LINK, group)[0], place(info, LINK, 3)[0]
+    group = tile.shape[0]
+    row = pl.multiple_of(place(info, LINK, group)[0] + half * group, 64)
+    first_row = place(info, LINK, 3)[0] + 3 * half
     factor = split(unfold(link[...]))
-    products = [-2.0 * passes([factor], [right(own_right, info, LINK, part)]) for part in range(3)]
-    copies = []
-    for half in range(2):
-        row = pl.multiple_of(start + half * group, 64)
-        values = []
-        for part in range(3):
-            value = products[part][half * group : (half + 1) * group]
-            value = masked(value, kept, mask_at(info, part), first_row + 3 * half)
-            values.append(base[part, pl.ds(row, group), :] + value)
-        copies.append(send_rows(info, tile.at[half], result, sem.at[half], row, *values))
-    for copy in copies:
-        copy.wait()
+    values = []
+    for part in range(3):
+        value = -2.0 * passes([factor], [right(own_right, info, LINK, part)])
+        values.append(base[part, pl.ds(row, group), :] + masked(value, kept, mask_at(info, part), first_row))
+    send_rows(info, tile, result, sem, row, *values).wait()
 
 
 VMEM = pl.BlockSpec(memory_space=pltpu.VMEM)
@@ -338,6 +336,7 @@
     info = jnp.stack([lax.axis_index("row") % 2, lax.axis_index("col") % 2]).astype(jnp.int32)
     strip = ((3 * side // 2, LANES), F32)
     slab = ((3 * group, LANES), F32)
+    half_slab = ((3 * group // 2, LANES), F32)
     two_slabs = ((6 * group, LANES), F32)
     three_slabs = ((9 * group, LANES), F32)
     wide = ((side, WIDE), F32)
@@ -418,15 +417,15 @@
         [three_wide],
     )
     total, other_far = lax.optimization_barrier((total, other_far))
-    s_mid, mid_chip, mid_link, mid_far = call(
+    s_mid, mid_chip, link_first, link_second, mid_far = call(
         mid_body,
         "square_mid",
         (info, square_kept),
         (other_far, own_left, chip_left, link_left_far, begun_mid),
-        [wide, slab, slab, rights],
+        [wide, slab, half_slab, half_slab, rights],
         work=0,
     )
-    mid_link = exchange(mid_link, "col", -1)
+    link_first = exchange(link_first, "col", -1)
     mid_chip = exchange(mid_chip, "col", 1)
     (base,) = call(
         cube_own_body,
@@ -435,6 +434,8 @@
         (total, s_near, s_mid, s_far, own_right, mid_far),
         [three_wide],
     )
+    link_second, sides_chip = lax.optimization_barrier((link_second, sides_chip))
+    link_second = exchange(link_second, "col", -1)
     result = ((side, side), F32)
     base, purified = call(
         cube_chip_body,
@@ -445,16 +446,17 @@
         result=True,
         scratch=[pltpu.VMEM((group, side), F32), pltpu.SemaphoreType.DMA(())],
     )
-    (purified,) = call(
-        finish_body,
-        "finish",
-        (info, result_kept),
-        (mid_link, own_right, base),
-        [result],
-        result=True,
-        begun=(purified,),
-        scratch=[pltpu.VMEM((2, group, side), F32), pltpu.SemaphoreType.DMA((2,))],
-    )
+    for half, link in enumerate((link_first, link_second)):
+        (purified,) = call(
+            functools.partial(finish_body, half),
+            ("finish_first", "finish_second")[half],
+            (info, result_kept),
+            (link, own_right, base),
+            [result],
+            result=True,
+            begun=(purified,),
+            scratch=[pltpu.VMEM((group, side), F32), pltpu.SemaphoreType.DMA(())],
+        )
     return purified
 
 

time: 52.8 us -> 52.4 us (level)
  waiting for transfers between devices: 8.32 us -> 4.56 us
  starting transfers between devices: 20.7 us -> 22.6 us
  Pallas kernels: 23.4 us -> 24.9 us
    ppermute x13 -> x14, waiting for transfers between devices: 8.32 us -> 4.56 us  [exchange(): lax.ppermute(value, axis, [(i, (i + (even_step if i % 2 == 0 else -even_s...]
    ppermute x13 -> x14, starting transfers between devices: 20.7 us -> 22.6 us  [exchange(): lax.ppermute(value, axis, [(i, (i + (even_step if i % 2 == 0 else -even_s...]
    pallas_call x13 -> x14, Pallas kernels: 23.4 us -> 24.9 us  [call(): pl.pallas_call(body, out_shape=[jax.ShapeDtypeStruct(shape, kind) for sha...]
  transfers between devices with their start and end apart: 13 -> 14, of which waited for: 4 -> 2; matrix products, arithmetic and copies ran while one was open for 0% -> 0% of each run, Pallas kernels for 35% -> 39%
where the time goes in v14:
time: 52.4 us; the launch traced here: 52.3 us
  Pallas kernels  24.9 us (48%)
  starting transfers between devices  22.6 us (43%)
  waiting for transfers between devices  4.56 us (9%)
    pallas_call x14, Pallas kernels, call(): pl.pallas_call(body, out_shape=[jax.ShapeDtypeStruct(shape, kind) for sha...  24.9 us
    ppermute x14, starting transfers between devices, exchange(): lax.ppermute(value, axis, [(i, (i + (even_step if i % 2 == 0 else -even_s...  22.6 us
    ppermute x14, waiting for transfers between devices, exchange(): lax.ppermute(value, axis, [(i, (i + (even_step if i % 2 == 0 else -even_s...  4.56 us
  transfers between devices with their start and end apart: 14, of which 2 were waited for; matrix products, arithmetic and copies ran while one was open for 0% of the time, Pallas kernels for 39%

profile of v14, /device:TPU:0, one launch (start us, length us, event | category | flops | bytes accessed | tf_op | source)
XLA Modules:
  0.0 52.3 jit_solution(8195388474979292994)
XLA Ops:
  0.0 0.1 pad_add_fusion.info
  0.1 2.4 %pack_first.1 = (f32[864,128]{1,0:T(8,128)S(1)}, f32[1152,128]{1,0:T(8,128)S(1)}, f32[1728,128]{1,0:T(8,128)S(1)}) custom-call(s32[2]{0:T(128)S(1)} %pad_add_fusion.info, f32[576,576]{1,0:T(8,128)} %tile.2), custom_call_target="tpu_custom_call" | custom-call | flops 4000000000 | bytes 20000000 | tf_op jit(solution)/shard_map/pack_first/pallas_call | solution.py:319
  2.5 0.5 %collective-permute-start.2 = (f32[1728,128]{1,0:T(8,128)S(1)}, f32[1728,128]{1,0:T(8,128)S(1)}, u32[]{:S(2)}, u32[]{:S(2)}) collective-permute-start(f32[1728,128]{1,0:T(8,128)S(1)} %get-tuple-element.49), channel_id=1, source_target_pairs={{0,1},{1,0},{2,3},{3,2},{4,5},{5,4},{6,7},{7,6},{8,9},{9,8},{10,11... | collective-permute-start | bytes 2654216 | tf_op jit(solution)/shard_map/ppermute | solution.py:348
  3.0 2.6 %collective-permute-start.1 = (f32[864,128]{1,0:T(8,128)S(1)}, f32[864,128]{1,0:T(8,128)S(1)}, u32[]{:S(2)}, u32[]{:S(2)}) collective-permute-start(f32[864,128]{1,0:T(8,128)S(1)} %get-tuple-element.48), channel_id=1, source_target_pairs={{0,8},{8,0},{16,24},{24,16},{1,9},{9,1},{17,25},{25,17},{2,10},{10... | collective-permute-start | bytes 1327112 | tf_op jit(solution)/shard_map/ppermute | solution.py:348
  5.6 3.4 %collective-permute-start = (f32[1152,128]{1,0:T(8,128)S(1)}, f32[1152,128]{1,0:T(8,128)S(1)}, u32[]{:S(2)}, u32[]{:S(2)}) collective-permute-start(f32[1152,128]{1,0:T(8,128)S(1)} %get-tuple-element.47), channel_id=1, source_target_pairs={{0,7},{1,2},{2,1},{3,4},{4,3},{5,6},{6,5},{7,0},{8,15},{9,10},{10,... | collective-permute-start | bytes 1769480 | tf_op jit(solution)/shard_map/ppermute | solution.py:348
  9.0 0.0 collective-permute-done.2.chip
  9.0 0.0 copy-done.1
  9.0 0.8 %pack_rest.1 = (f32[576,128]{1,0:T(8,128)S(1)}, f32[864,128]{1,0:T(8,128)S(1)}, f32[864,128]{1,0:T(8,128)S(1)}) custom-call(s32[2]{0:T(128)S(1)} %pad_add_fusion.info, f32[576,576]{1,0:T(8,128)S(1)} %copy-done.1), custom_call_target="tpu_custom_call" | custom-call | flops 4000000000 | bytes 20000000 | tf_op jit(solution)/shard_map/pack_rest/pallas_call | solution.py:319
  9.8 0.9 %collective-permute-start.4 = (f32[576,128]{1,0:T(8,128)S(1)}, f32[576,128]{1,0:T(8,128)S(1)}, u32[]{:S(2)}, u32[]{:S(2)}) collective-permute-start(f32[576,128]{1,0:T(8,128)S(1)} %get-tuple-element.61), channel_id=1, source_target_pairs={{0,7},{1,2},{2,1},{3,4},{4,3},{5,6},{6,5},{7,0},{8,15},{9,10},{10,... | collective-permute-start | bytes 884744 | tf_op jit(solution)/shard_map/ppermute | solution.py:348
  10.6 1.5 %collective-permute-start.6 = (f32[864,128]{1,0:T(8,128)S(1)}, f32[864,128]{1,0:T(8,128)S(1)}, u32[]{:S(2)}, u32[]{:S(2)}) collective-permute-start(f32[864,128]{1,0:T(8,128)S(1)} %get-tuple-element.62), channel_id=1, source_target_pairs={{0,16},{8,24},{16,0},{24,8},{1,17},{9,25},{17,1},{25,9},{2,18},{10... | collective-permute-start | bytes 1327112 | tf_op jit(solution)/shard_map/ppermute | solution.py:348
  12.2 1.5 %collective-permute-start.7 = (f32[864,128]{1,0:T(8,128)S(1)}, f32[864,128]{1,0:T(8,128)S(1)}, u32[]{:S(2)}, u32[]{:S(2)}) collective-permute-start(f32[864,128]{1,0:T(8,128)S(1)} %get-tuple-element.66), channel_id=1, source_target_pairs={{0,8},{8,0},{16,24},{24,16},{1,9},{9,1},{17,25},{25,17},{2,10},{10... | collective-permute-start | bytes 1327112 | tf_op jit(solution)/shard_map/ppermute | solution.py:348
  13.7 1.0 %prepare.1 = (bf16[2,3,576,256]{3,2,1,0:T(8,128)(2,1)S(1)}, bf16[2,3,768,256]{3,2,1,0:T(8,128)(2,1)S(1)}, bf16[2,3,384,256]{3,2,1,0:T(8,128)(2,1)S(1)}) custom-call(s32[2]{0:T(128)S(1)} %pad_add_fusion.info, f32[576,576]{1,0:T(8,128)S(1)} %copy-done.1, f32[1728,128]{1,0:T(8,128)S(1)} %collective-permute-done.2.chip), custom_call_target="tpu_custom_call" | custom-call | flops 4000000000 | bytes 20000000 | tf_op jit(solution)/shard_map/prepare/pallas_call | solution.py:319
  14.7 1.9 %collective-permute-done.1.mid = f32[864,128]{1,0:T(8,128)S(1)} collective-permute-done((f32[864,128]{1,0:T(8,128)S(1)}, f32[864,128]{1,0:T(8,128)S(1)}, u32[]{:S(2)}, u32[]{:S(2)}) %collective-permute-start.1) | collective-permute-done | bytes 442400 | tf_op jit(solution)/shard_map/ppermute | solution.py:348
  16.6 2.0 %collective-permute-start.5 = (f32[864,128]{1,0:T(8,128)S(1)}, f32[864,128]{1,0:T(8,128)S(1)}, u32[]{:S(2)}, u32[]{:S(2)}) collective-permute-start(f32[864,128]{1,0:T(8,128)S(1)} %collective-permute-done.1.mid), channel_id=1, source_target_pairs={{0,16},{8,24},{16,0},{24,8},{1,17},{9,25},{17,1},{25,9},{2,18},{10... | collective-permute-start | bytes 1327112 | tf_op jit(solution)/shard_map/ppermute | solution.py:348
  18.6 0.0 copy-start
  18.6 1.6 %near_start.1 = (f32[576,256]{1,0:T(8,128)S(1)}, bf16[2,768,256]{2,1,0:T(8,128)(2,1)S(1)}) custom-call(s32[2]{0:T(128)S(1)} %pad_add_fusion.info, f32[864,128]{1,0:T(8,128)S(1)} %collective-permute-done.1.mid, bf16[2,3,576,256]{3,2,1,0:T(8,128)(2,1)S(1)} %get-tuple-element.53.own_left, bf16[2,3,768,256]{3,2,1,0:T(8,128)(2,1)S(1)} %get-tuple-element.54.own_right, ...), custom_call_target="tpu_custom_call" | custom-call | flops 4000000000 | bytes 20000000 | tf_op jit(solution)/shard_map/near_start/pallas_call | solution.py:319
  20.2 2.6 %collective-permute-done.link_a = f32[1152,128]{1,0:T(8,128)S(1)} collective-permute-done((f32[1152,128]{1,0:T(8,128)S(1)}, f32[1152,128]{1,0:T(8,128)S(1)}, u32[]{:S(2)}, u32[]{:S(2)}) %collective-permute-start) | collective-permute-done | bytes 589856 | tf_op jit(solution)/shard_map/ppermute | solution.py:348
  22.8 0.0 copy-done
  22.8 1.4 %square_near.1 = (f32[576,256]{1,0:T(8,128)S(1)}, f32[576,128]{1,0:T(8,128)S(1)}, bf16[2,2,384,256]{3,2,1,0:T(8,128)(2,1)S(1)}) custom-call(s32[2]{0:T(128)S(1)} %pad_add_fusion.info, s32[9,9]{1,0:T(8,128)S(1)} %copy-done, f32[1152,128]{1,0:T(8,128)S(1)} %collective-permute-done.link_a, f32[576,256]{1,0:T(8,128)S(1)} %get-tuple-element.56.begun, ...), custom_call_target="tpu_custom_call" | custom-call | flops 4000000000 | bytes 20000000 | tf_op jit(solution)/shard_map/square_near/pallas_call | solution.py:319
  24.2 3.7 %collective-permute-start.3 = (f32[576,128]{1,0:T(8,128)S(1)}, f32[576,128]{1,0:T(8,128)S(1)}, u32[]{:S(2)}, u32[]{:S(2)}) collective-permute-start(f32[576,128]{1,0:T(8,128)S(1)} %get-tuple-element.58), channel_id=1, source_target_pairs={{0,7},{1,2},{2,1},{3,4},{4,3},{5,6},{6,5},{7,0},{8,15},{9,10},{10,... | collective-permute-start | bytes 884744 | tf_op jit(solution)/shard_map/ppermute | solution.py:348
  27.9 0.0 collective-permute-done.6
  27.9 0.5 %collective-permute-start.8 = (f32[864,128]{1,0:T(8,128)S(1)}, f32[864,128]{1,0:T(8,128)S(1)}, u32[]{:S(2)}, u32[]{:S(2)}) collective-permute-start(f32[864,128]{1,0:T(8,128)S(1)} %collective-permute-done.6), channel_id=1, source_target_pairs={{0,8},{8,0},{16,24},{24,16},{1,9},{9,1},{17,25},{25,17},{2,10},{10... | collective-permute-start | bytes 1327112 | tf_op jit(solution)/shard_map/ppermute | solution.py:348
  28.5 1.9 %middle_products.1 = (f32[576,256]{1,0:T(8,128)S(1)}, f32[576,256]{1,0:T(8,128)S(1)}) custom-call(s32[2]{0:T(128)S(1)} %pad_add_fusion.info, bf16[2,3,576,256]{3,2,1,0:T(8,128)(2,1)S(1)} %get-tuple-element.53.own_left, bf16[2,3,768,256]{3,2,1,0:T(8,128)(2,1)S(1)} %get-tuple-element.54.own_right, bf16[2,3,384,256]{3,2,1,0:T(8,128)(2,1)S(1)} %get-tuple-element.55.chip_left, ...), custom_call_target="tpu_custom_call" | custom-call | flops 4000000000 | bytes 20000000 | tf_op jit(solution)/shard_map/middle_products/pallas_call | solution.py:319
  30.4 0.0 collective-permute-done.7.near
  30.4 1.4 %mid_start.1 = (f32[576,256]{1,0:T(8,128)S(1)}, bf16[2,768,256]{2,1,0:T(8,128)(2,1)S(1)}) custom-call(s32[2]{0:T(128)S(1)} %pad_add_fusion.info, f32[864,128]{1,0:T(8,128)S(1)} %collective-permute-done.7.near, f32[576,256]{1,0:T(8,128)S(1)} %get-tuple-element.67.begun, bf16[2,3,576,256]{3,2,1,0:T(8,128)(2,1)S(1)} %get-tuple-element.53.own_left, ...), custom_call_target="tpu_custom_call" | custom-call | flops 4000000000 | bytes 20000000 | tf_op jit(solution)/shard_map/mid_start/pallas_call | solution.py:319
  31.8 0.0 collective-permute-done.4.link_b
  31.8 0.0 collective-permute-done.5.mid
  31.8 1.9 %square_far.1 = (f32[576,256]{1,0:T(8,128)S(1)}, f32[576,128]{1,0:T(8,128)S(1)}, f32[1152,128]{1,0:T(8,128)S(1)}, bf16[2,384,256]{2,1,0:T(8,128)(2,1)S(1)}, bf16[2,768,256]{2,1,0:T(8,128)(2,1)S(1)}) custom-call(s32[2]{0:T(128)S(1)} %pad_add_fusion.info, s32[9,9]{1,0:T(8,128)S(1)} %copy-done, f32[576,128]{1,0:T(8,128)S(1)} %collective-permute-done.4.link_b, ...), custom_call_target="tpu_custom_call" | custom-call | flops 4000000000 | bytes 20000000 | tf_op jit(solution)/shard_map/square_far/pallas_call | solution.py:319
  33.7 2.3 %collective-permute-start.11 = (f32[576,128]{1,0:T(8,128)S(1)}, f32[576,128]{1,0:T(8,128)S(1)}, u32[]{:S(2)}, u32[]{:S(2)}) collective-permute-start(f32[576,128]{1,0:T(8,128)S(1)} %get-tuple-element.80), channel_id=1, source_target_pairs={{0,7},{1,2},{2,1},{3,4},{4,3},{5,6},{6,5},{7,0},{8,15},{9,10},{10,... | collective-permute-start | bytes 884744 | tf_op jit(solution)/shard_map/ppermute | solution.py:348
  36.0 0.0 collective-permute-start.9
  36.0 0.0 collective-permute-done.3.link
  36.0 1.8 %cube_near.1.total = f32[3,576,256]{2,1,0:T(8,128)S(1)} custom-call(s32[2]{0:T(128)S(1)} %pad_add_fusion.info, f32[576,128]{1,0:T(8,128)S(1)} %collective-permute-done.3.link, f32[576,256]{1,0:T(8,128)S(1)} %get-tuple-element.59.s_near.near, f32[576,256]{1,0:T(8,128)S(1)} %get-tuple-element.70.far, bf16[2,768,256]{2,1,0:T(8,128)(2,1)S(1)} %get-tuple-element.57.right_near, ...), custom_call_target="tpu_custom_call" | custom-call | flops 4000000000 | bytes 20000000 | tf_op jit(solution)/shard_map/cube_near/pallas_call | solution.py:319
  37.8 0.0 collective-permute-done.8.far
  37.8 1.9 %square_mid.1 = (f32[576,256]{1,0:T(8,128)S(1)}, f32[576,128]{1,0:T(8,128)S(1)}, f32[288,128]{1,0:T(8,128)S(1)}, f32[288,128]{1,0:T(8,128)S(1)}, bf16[2,768,256]{2,1,0:T(8,128)(2,1)S(1)}) custom-call(s32[2]{0:T(128)S(1)} %pad_add_fusion.info, s32[9,9]{1,0:T(8,128)S(1)} %copy-done, f32[864,128]{1,0:T(8,128)S(1)} %collective-permute-done.8.far, ...), custom_call_target="tpu_custom_call" | custom-call | tf_op jit(solution)/shard_map/square_mid/pallas_call | solution.py:319
  39.7 1.8 %collective-permute-start.13 = (f32[288,128]{1,0:T(8,128)S(1)}, f32[288,128]{1,0:T(8,128)S(1)}, u32[]{:S(2)}, u32[]{:S(2)}) collective-permute-start(f32[288,128]{1,0:T(8,128)S(1)} %get-tuple-element.87), channel_id=1, source_target_pairs={{0,7},{1,2},{2,1},{3,4},{4,3},{5,6},{6,5},{7,0},{8,15},{9,10},{10,... | collective-permute-start | bytes 442376 | tf_op jit(solution)/shard_map/ppermute | solution.py:348
  41.4 0.0 collective-permute-start.12
  41.4 0.0 copy-start.2
  41.4 1.7 %cube_own.1.base = f32[3,576,256]{2,1,0:T(8,128)S(1)} custom-call(s32[2]{0:T(128)S(1)} %pad_add_fusion.info, f32[3,576,256]{2,1,0:T(8,128)S(1)} %cube_near.1.total, f32[576,256]{1,0:T(8,128)S(1)} %get-tuple-element.59.s_near.near, f32[576,256]{1,0:T(8,128)S(1)} %get-tuple-element.85.mid, f32[576,256]{1,0:T(8,128)S(1)} %get-tuple-element.70.far, ...), custom_call_target="tpu_custom_call" | custom-call | flops 4000000000 | bytes 20000000 | tf_op jit(solution)/shard_map/cube_own/pallas_call | solution.py:319
  43.1 0.0 collective-permute-done.9.sides
  43.2 1.9 %collective-permute-start.10 = (f32[288,128]{1,0:T(8,128)S(1)}, f32[288,128]{1,0:T(8,128)S(1)}, u32[]{:S(2)}, u32[]{:S(2)}) collective-permute-start(f32[288,128]{1,0:T(8,128)S(1)} %get-tuple-element.79), channel_id=1, source_target_pairs={{0,7},{1,2},{2,1},{3,4},{4,3},{5,6},{6,5},{7,0},{8,15},{9,10},{10,... | collective-permute-start | bytes 442376 | tf_op jit(solution)/shard_map/ppermute | solution.py:348
  45.1 0.0 collective-permute-done.11.link
  45.1 0.0 collective-permute-done.12.chip
  45.1 0.0 copy-done.2
  45.1 3.3 %cube_chip.1 = (f32[3,576,256]{2,1,0:T(8,128)S(1)}, f32[576,576]{1,0:T(8,128)}) custom-call(s32[2]{0:T(128)S(1)} %pad_add_fusion.info, s32[9,9]{1,0:T(8,128)S(1)} %copy-done.2, f32[576,128]{1,0:T(8,128)S(1)} %collective-permute-done.11.link, f32[1152,128]{1,0:T(8,128)S(1)} %collective-permute-done.9.sides, f32[576,128]{1,0:T(8,128)S(1)} %collective-permute-done.12.chip, ...), custom_call_target="tpu_custom_call" | custom-call | flops 4000000000 | bytes 20000000 | tf_op jit(solution)/shard_map/cube_chip/pallas_call | solution.py:319
  48.4 0.0 collective-permute-done.13.link
  48.4 1.9 %finish_first.1.begun = f32[576,576]{1,0:T(8,128)} custom-call(s32[2]{0:T(128)S(1)} %pad_add_fusion.info, s32[9,9]{1,0:T(8,128)S(1)} %copy-done.2, f32[288,128]{1,0:T(8,128)S(1)} %collective-permute-done.13.link, bf16[2,3,768,256]{3,2,1,0:T(8,128)(2,1)S(1)} %get-tuple-element.54.own_right, ...), custom_call_target="tpu_custom_call", output_to_operand_aliasing={{}: (5, {})} | custom-call | flops 4000000000 | bytes 20000000 | tf_op jit(solution)/shard_map/finish_first/pallas_call | solution.py:319
  50.4 0.0 collective-permute-done.10.link
  50.4 1.9 %finish_second.1 = f32[576,576]{1,0:T(8,128)} custom-call(s32[2]{0:T(128)S(1)} %pad_add_fusion.info, s32[9,9]{1,0:T(8,128)S(1)} %copy-done.2, f32[288,128]{1,0:T(8,128)S(1)} %collective-permute-done.10.link, bf16[2,3,768,256]{3,2,1,0:T(8,128)(2,1)S(1)} %get-tuple-element.54.own_right, ...), custom_call_target="tpu_custom_call", output_to_operand_aliasing={{}: (5, {})} | custom-call | flops 4000000000 | bytes 20000000 | tf_op jit(solution)/shard_map/finish_second/pallas_call | solution.py:319
  (1 shorter events, 0.0 us)
Async XLA Ops:
  0.1 8.9 %copy-start.1 = (f32[576,576]{1,0:T(8,128)S(1)}, f32[576,576]{1,0:T(8,128)}, u32[]{:S(2)}) copy-start(f32[576,576]{1,0:T(8,128)} %tile.2) | copy-start | bytes 3981316
  2.5 6.5 %collective-permute-start.2 = (f32[1728,128]{1,0:T(8,128)S(1)}, f32[1728,128]{1,0:T(8,128)S(1)}, u32[]{:S(2)}, u32[]{:S(2)}) collective-permute-start(f32[1728,128]{1,0:T(8,128)S(1)} %get-tuple-element.49), channel_id=1, source_target_pairs={{0,1},{1,0},{2,3},{3,2},{4,5},{5,4},{6,7},{7,6},{8,9},{9,8},{10,11... | collective-permute-start | bytes 2654216 | tf_op jit(solution)/shard_map/ppermute | solution.py:348
  3.0 13.6 %collective-permute-start.1 = (f32[864,128]{1,0:T(8,128)S(1)}, f32[864,128]{1,0:T(8,128)S(1)}, u32[]{:S(2)}, u32[]{:S(2)}) collective-permute-start(f32[864,128]{1,0:T(8,128)S(1)} %get-tuple-element.48), channel_id=1, source_target_pairs={{0,8},{8,0},{16,24},{24,16},{1,9},{9,1},{17,25},{25,17},{2,10},{10... | collective-permute-start | bytes 1327112 | tf_op jit(solution)/shard_map/ppermute | solution.py:348
  5.6 17.2 %collective-permute-start = (f32[1152,128]{1,0:T(8,128)S(1)}, f32[1152,128]{1,0:T(8,128)S(1)}, u32[]{:S(2)}, u32[]{:S(2)}) collective-permute-start(f32[1152,128]{1,0:T(8,128)S(1)} %get-tuple-element.47), channel_id=1, source_target_pairs={{0,7},{1,2},{2,1},{3,4},{4,3},{5,6},{6,5},{7,0},{8,15},{9,10},{10,... | collective-permute-start | bytes 1769480 | tf_op jit(solution)/shard_map/ppermute | solution.py:348
  9.8 22.0 %collective-permute-start.4 = (f32[576,128]{1,0:T(8,128)S(1)}, f32[576,128]{1,0:T(8,128)S(1)}, u32[]{:S(2)}, u32[]{:S(2)}) collective-permute-start(f32[576,128]{1,0:T(8,128)S(1)} %get-tuple-element.61), channel_id=1, source_target_pairs={{0,7},{1,2},{2,1},{3,4},{4,3},{5,6},{6,5},{7,0},{8,15},{9,10},{10,... | collective-permute-start | bytes 884744 | tf_op jit(solution)/shard_map/ppermute | solution.py:348
  10.6 17.3 %collective-permute-start.6 = (f32[864,128]{1,0:T(8,128)S(1)}, f32[864,128]{1,0:T(8,128)S(1)}, u32[]{:S(2)}, u32[]{:S(2)}) collective-permute-start(f32[864,128]{1,0:T(8,128)S(1)} %get-tuple-element.62), channel_id=1, source_target_pairs={{0,16},{8,24},{16,0},{24,8},{1,17},{9,25},{17,1},{25,9},{2,18},{10... | collective-permute-start | bytes 1327112 | tf_op jit(solution)/shard_map/ppermute | solution.py:348
  12.2 18.2 %collective-permute-start.7 = (f32[864,128]{1,0:T(8,128)S(1)}, f32[864,128]{1,0:T(8,128)S(1)}, u32[]{:S(2)}, u32[]{:S(2)}) collective-permute-start(f32[864,128]{1,0:T(8,128)S(1)} %get-tuple-element.66), channel_id=1, source_target_pairs={{0,8},{8,0},{16,24},{24,16},{1,9},{9,1},{17,25},{25,17},{2,10},{10... | collective-permute-start | bytes 1327112 | tf_op jit(solution)/shard_map/ppermute | solution.py:348
  16.6 15.2 %collective-permute-start.5 = (f32[864,128]{1,0:T(8,128)S(1)}, f32[864,128]{1,0:T(8,128)S(1)}, u32[]{:S(2)}, u32[]{:S(2)}) collective-permute-start(f32[864,128]{1,0:T(8,128)S(1)} %collective-permute-done.1.mid), channel_id=1, source_target_pairs={{0,16},{8,24},{16,0},{24,8},{1,17},{9,25},{17,1},{25,9},{2,18},{10... | collective-permute-start | bytes 1327112 | tf_op jit(solution)/shard_map/ppermute | solution.py:348
  18.6 4.2 %copy-start = (s32[9,9]{1,0:T(8,128)S(1)}, s32[9,9]{1,0:T(8,128)}, u32[]{:S(2)}) copy-start(s32[9,9]{1,0:T(8,128)} %kept.8) | copy-start | bytes 976
  24.2 11.8 %collective-permute-start.3 = (f32[576,128]{1,0:T(8,128)S(1)}, f32[576,128]{1,0:T(8,128)S(1)}, u32[]{:S(2)}, u32[]{:S(2)}) collective-permute-start(f32[576,128]{1,0:T(8,128)S(1)} %get-tuple-element.58), channel_id=1, source_target_pairs={{0,7},{1,2},{2,1},{3,4},{4,3},{5,6},{6,5},{7,0},{8,15},{9,10},{10,... | collective-permute-start | bytes 884744 | tf_op jit(solution)/shard_map/ppermute | solution.py:348
  27.9 9.9 %collective-permute-start.8 = (f32[864,128]{1,0:T(8,128)S(1)}, f32[864,128]{1,0:T(8,128)S(1)}, u32[]{:S(2)}, u32[]{:S(2)}) collective-permute-start(f32[864,128]{1,0:T(8,128)S(1)} %collective-permute-done.6), channel_id=1, source_target_pairs={{0,8},{8,0},{16,24},{24,16},{1,9},{9,1},{17,25},{25,17},{2,10},{10... | collective-permute-start | bytes 1327112 | tf_op jit(solution)/shard_map/ppermute | solution.py:348
  33.7 11.4 %collective-permute-start.11 = (f32[576,128]{1,0:T(8,128)S(1)}, f32[576,128]{1,0:T(8,128)S(1)}, u32[]{:S(2)}, u32[]{:S(2)}) collective-permute-start(f32[576,128]{1,0:T(8,128)S(1)} %get-tuple-element.80), channel_id=1, source_target_pairs={{0,7},{1,2},{2,1},{3,4},{4,3},{5,6},{6,5},{7,0},{8,15},{9,10},{10,... | collective-permute-start | bytes 884744 | tf_op jit(solution)/shard_map/ppermute | solution.py:348
  36.0 7.2 %collective-permute-start.9 = (f32[1152,128]{1,0:T(8,128)S(1)}, f32[1152,128]{1,0:T(8,128)S(1)}, u32[]{:S(2)}, u32[]{:S(2)}) collective-permute-start(f32[1152,128]{1,0:T(8,128)S(1)} %get-tuple-element.78), channel_id=1, source_target_pairs={{0,1},{1,0},{2,3},{3,2},{4,5},{5,4},{6,7},{7,6},{8,9},{9,8},{10,11... | collective-permute-start | bytes 1769480 | tf_op jit(solution)/shard_map/ppermute | solution.py:348
  39.7 8.8 %collective-permute-start.13 = (f32[288,128]{1,0:T(8,128)S(1)}, f32[288,128]{1,0:T(8,128)S(1)}, u32[]{:S(2)}, u32[]{:S(2)}) collective-permute-start(f32[288,128]{1,0:T(8,128)S(1)} %get-tuple-element.87), channel_id=1, source_target_pairs={{0,7},{1,2},{2,1},{3,4},{4,3},{5,6},{6,5},{7,0},{8,15},{9,10},{10,... | collective-permute-start | bytes 442376 | tf_op jit(solution)/shard_map/ppermute | solution.py:348
  41.4 3.6 %collective-permute-start.12 = (f32[576,128]{1,0:T(8,128)S(1)}, f32[576,128]{1,0:T(8,128)S(1)}, u32[]{:S(2)}, u32[]{:S(2)}) collective-permute-start(f32[576,128]{1,0:T(8,128)S(1)} %get-tuple-element.82), channel_id=1, source_target_pairs={{0,1},{1,0},{2,3},{3,2},{4,5},{5,4},{6,7},{7,6},{8,9},{9,8},{10,11... | collective-permute-start | bytes 884744 | tf_op jit(solution)/shard_map/ppermute | solution.py:348
  41.4 3.6 %copy-start.2 = (s32[9,9]{1,0:T(8,128)S(1)}, s32[9,9]{1,0:T(8,128)}, u32[]{:S(2)}) copy-start(s32[9,9]{1,0:T(8,128)} %kept.11) | copy-start | bytes 976
  43.2 7.2 %collective-permute-start.10 = (f32[288,128]{1,0:T(8,128)S(1)}, f32[288,128]{1,0:T(8,128)S(1)}, u32[]{:S(2)}, u32[]{:S(2)}) collective-permute-start(f32[288,128]{1,0:T(8,128)S(1)} %get-tuple-element.79), channel_id=1, source_target_pairs={{0,7},{1,2},{2,1},{3,4},{4,3},{5,6},{6,5},{7,0},{8,15},{9,10},{10,... | collective-permute-start | bytes 442376 | tf_op jit(solution)/shard_map/ppermute | solution.py:348

commit v15 on v14

--- a/solution.py
+++ b/solution.py
@@ -349,19 +349,19 @@
             value, axis, [(i, (i + (even_step if i % 2 == 0 else -even_step)) % size) for i in range(size)]
         )
 
-    mid, link_a, chip = call(
+    mid, link_a, chip, held = call(
         pack_first_body,
         "pack_first",
         (info,),
         (),
-        [strip, two_slabs, three_slabs],
+        [strip, two_slabs, three_slabs, ((side, side), F32)],
         unmoved=(pltpu.with_memory_space_constraint(p_tiles, pltpu.HBM),),
-        scratch=[pltpu.VMEM((side, side), F32), pltpu.SemaphoreType.DMA((3,))],
+        scratch=[pltpu.SemaphoreType.DMA((3,))],
     )
     link_a = exchange(link_a, "col", -1)
     partner_mid = exchange(mid, "row", 1)
     chip = exchange(chip, "col", 1)
-    chip, tile = lax.optimization_barrier((chip, p_tiles))
+    chip, tile = lax.optimization_barrier((chip, held))
     link_b, near, far = call(pack_rest_body, "pack_rest", (info,), (tile,), [slab, strip, strip])
     partner_near = exchange(near, "row", 1)
     link_b = exchange(link_b, "col", -1)
@@ -371,7 +371,7 @@
         prepare_body,
         "prepare",
         (info,),
-        (p_tiles, chip),
+        (held, chip),
         [((2, 3, side, WIDE), BF16), ((2, 3, 3 * WIDE, WIDE), BF16), ((2, 3, 2 * group, WIDE), BF16)],
     )
     partner_mid, own_left = lax.optimization_barrier((partner_mid, own_left))

time: 52.4 us -> 52.4 us (level)
  no operation moved by 1% of the time
where the time goes in v15:
time: 52.4 us; the launch traced here: 52.3 us
  Pallas kernels  24.9 us (48%)
  starting transfers between devices  22.6 us (43%)
  waiting for transfers between devices  4.58 us (9%)
    pallas_call x14, Pallas kernels, call(): pl.pallas_call(body, out_shape=[jax.ShapeDtypeStruct(shape, kind) for sha...  24.9 us
    ppermute x14, starting transfers between devices, exchange(): lax.ppermute(value, axis, [(i, (i + (even_step if i % 2 == 0 else -even_s...  22.6 us
    ppermute x14, waiting for transfers between devices, exchange(): lax.ppermute(value, axis, [(i, (i + (even_step if i % 2 == 0 else -even_s...  4.58 us
  transfers between devices with their start and end apart: 14, of which 2 were waited for; matrix products, arithmetic and copies ran while one was open for 0% of the time, Pallas kernels for 39%

profile of v15, /device:TPU:0, one launch (start us, length us, event | category | flops | bytes accessed | tf_op | source)
XLA Modules:
  0.0 52.3 jit_solution(7204342846754596190)
XLA Ops:
  0.0 0.1 pad_add_fusion.info
  0.1 2.4 %pack_first.1 = (f32[864,128]{1,0:T(8,128)S(1)}, f32[1152,128]{1,0:T(8,128)S(1)}, f32[1728,128]{1,0:T(8,128)S(1)}, f32[576,576]{1,0:T(8,128)S(1)}) custom-call(s32[2]{0:T(128)S(1)} %pad_add_fusion.info, f32[576,576]{1,0:T(8,128)} %source.1), custom_call_target="tpu_custom_call" | custom-call | flops 4000000000 | bytes 20000000 | tf_op jit(solution)/shard_map/pack_first/pallas_call | solution.py:319
  2.5 0.5 collective-permute-start.2
  3.0 2.6 %collective-permute-start.1 = (f32[864,128]{1,0:T(8,128)S(1)}, f32[864,128]{1,0:T(8,128)S(1)}, u32[]{:S(2)}, u32[]{:S(2)}) collective-permute-start(f32[864,128]{1,0:T(8,128)S(1)} %get-tuple-element.49), channel_id=1, source_target_pairs={{0,8},{8,0},{16,24},{24,16},{1,9},{9,1},{17,25},{25,17},{2,10},{10... | collective-permute-start | bytes 1327112 | tf_op jit(solution)/shard_map/ppermute | solution.py:348
  5.6 3.4 %collective-permute-start = (f32[1152,128]{1,0:T(8,128)S(1)}, f32[1152,128]{1,0:T(8,128)S(1)}, u32[]{:S(2)}, u32[]{:S(2)}) collective-permute-start(f32[1152,128]{1,0:T(8,128)S(1)} %get-tuple-element.48), channel_id=1, source_target_pairs={{0,7},{1,2},{2,1},{3,4},{4,3},{5,6},{6,5},{7,0},{8,15},{9,10},{10,... | collective-permute-start | bytes 1769480 | tf_op jit(solution)/shard_map/ppermute | solution.py:348
  9.0 0.0 collective-permute-done.2.chip
  9.0 0.8 %pack_rest.1 = (f32[576,128]{1,0:T(8,128)S(1)}, f32[864,128]{1,0:T(8,128)S(1)}, f32[864,128]{1,0:T(8,128)S(1)}) custom-call(s32[2]{0:T(128)S(1)} %pad_add_fusion.info, f32[576,576]{1,0:T(8,128)S(1)} %get-tuple-element.62.tile), custom_call_target="tpu_custom_call" | custom-call | flops 4000000000 | bytes 20000000 | tf_op jit(solution)/shard_map/pack_rest/pallas_call | solution.py:319
  9.8 0.9 %collective-permute-start.4 = (f32[576,128]{1,0:T(8,128)S(1)}, f32[576,128]{1,0:T(8,128)S(1)}, u32[]{:S(2)}, u32[]{:S(2)}) collective-permute-start(f32[576,128]{1,0:T(8,128)S(1)} %get-tuple-element.63), channel_id=1, source_target_pairs={{0,7},{1,2},{2,1},{3,4},{4,3},{5,6},{6,5},{7,0},{8,15},{9,10},{10,... | collective-permute-start | bytes 884744 | tf_op jit(solution)/shard_map/ppermute | solution.py:348
  10.6 1.5 %collective-permute-start.6 = (f32[864,128]{1,0:T(8,128)S(1)}, f32[864,128]{1,0:T(8,128)S(1)}, u32[]{:S(2)}, u32[]{:S(2)}) collective-permute-start(f32[864,128]{1,0:T(8,128)S(1)} %get-tuple-element.64), channel_id=1, source_target_pairs={{0,16},{8,24},{16,0},{24,8},{1,17},{9,25},{17,1},{25,9},{2,18},{10... | collective-permute-start | bytes 1327112 | tf_op jit(solution)/shard_map/ppermute | solution.py:348
  12.2 1.5 %collective-permute-start.7 = (f32[864,128]{1,0:T(8,128)S(1)}, f32[864,128]{1,0:T(8,128)S(1)}, u32[]{:S(2)}, u32[]{:S(2)}) collective-permute-start(f32[864,128]{1,0:T(8,128)S(1)} %get-tuple-element.68), channel_id=1, source_target_pairs={{0,8},{8,0},{16,24},{24,16},{1,9},{9,1},{17,25},{25,17},{2,10},{10... | collective-permute-start | bytes 1327112 | tf_op jit(solution)/shard_map/ppermute | solution.py:348
  13.7 1.0 %prepare.1 = (bf16[2,3,576,256]{3,2,1,0:T(8,128)(2,1)S(1)}, bf16[2,3,768,256]{3,2,1,0:T(8,128)(2,1)S(1)}, bf16[2,3,384,256]{3,2,1,0:T(8,128)(2,1)S(1)}) custom-call(s32[2]{0:T(128)S(1)} %pad_add_fusion.info, f32[576,576]{1,0:T(8,128)S(1)} %get-tuple-element.62.tile, f32[1728,128]{1,0:T(8,128)S(1)} %collective-permute-done.2.chip), custom_call_target="tpu_custom_call" | custom-call | flops 4000000000 | bytes 20000000 | tf_op jit(solution)/shard_map/prepare/pallas_call | solution.py:319
  14.7 1.9 %collective-permute-done.1.mid = f32[864,128]{1,0:T(8,128)S(1)} collective-permute-done((f32[864,128]{1,0:T(8,128)S(1)}, f32[864,128]{1,0:T(8,128)S(1)}, u32[]{:S(2)}, u32[]{:S(2)}) %collective-permute-start.1) | collective-permute-done | bytes 442400 | tf_op jit(solution)/shard_map/ppermute | solution.py:348
  16.6 2.0 %collective-permute-start.5 = (f32[864,128]{1,0:T(8,128)S(1)}, f32[864,128]{1,0:T(8,128)S(1)}, u32[]{:S(2)}, u32[]{:S(2)}) collective-permute-start(f32[864,128]{1,0:T(8,128)S(1)} %collective-permute-done.1.mid), channel_id=1, source_target_pairs={{0,16},{8,24},{16,0},{24,8},{1,17},{9,25},{17,1},{25,9},{2,18},{10... | collective-permute-start | bytes 1327112 | tf_op jit(solution)/shard_map/ppermute | solution.py:348
  18.6 0.0 copy-start
  18.6 1.6 %near_start.1 = (f32[576,256]{1,0:T(8,128)S(1)}, bf16[2,768,256]{2,1,0:T(8,128)(2,1)S(1)}) custom-call(s32[2]{0:T(128)S(1)} %pad_add_fusion.info, f32[864,128]{1,0:T(8,128)S(1)} %collective-permute-done.1.mid, bf16[2,3,576,256]{3,2,1,0:T(8,128)(2,1)S(1)} %get-tuple-element.55.own_left, bf16[2,3,768,256]{3,2,1,0:T(8,128)(2,1)S(1)} %get-tuple-element.56.own_right, ...), custom_call_target="tpu_custom_call" | custom-call | flops 4000000000 | bytes 20000000 | tf_op jit(solution)/shard_map/near_start/pallas_call | solution.py:319
  20.2 2.6 %collective-permute-done.link_a = f32[1152,128]{1,0:T(8,128)S(1)} collective-permute-done((f32[1152,128]{1,0:T(8,128)S(1)}, f32[1152,128]{1,0:T(8,128)S(1)}, u32[]{:S(2)}, u32[]{:S(2)}) %collective-permute-start) | collective-permute-done | bytes 589856 | tf_op jit(solution)/shard_map/ppermute | solution.py:348
  22.8 0.0 copy-done
  22.8 1.4 %square_near.1 = (f32[576,256]{1,0:T(8,128)S(1)}, f32[576,128]{1,0:T(8,128)S(1)}, bf16[2,2,384,256]{3,2,1,0:T(8,128)(2,1)S(1)}) custom-call(s32[2]{0:T(128)S(1)} %pad_add_fusion.info, s32[9,9]{1,0:T(8,128)S(1)} %copy-done, f32[1152,128]{1,0:T(8,128)S(1)} %collective-permute-done.link_a, f32[576,256]{1,0:T(8,128)S(1)} %get-tuple-element.58.begun, ...), custom_call_target="tpu_custom_call" | custom-call | flops 4000000000 | bytes 20000000 | tf_op jit(solution)/shard_map/square_near/pallas_call | solution.py:319
  24.2 3.7 %collective-permute-start.3 = (f32[576,128]{1,0:T(8,128)S(1)}, f32[576,128]{1,0:T(8,128)S(1)}, u32[]{:S(2)}, u32[]{:S(2)}) collective-permute-start(f32[576,128]{1,0:T(8,128)S(1)} %get-tuple-element.60), channel_id=1, source_target_pairs={{0,7},{1,2},{2,1},{3,4},{4,3},{5,6},{6,5},{7,0},{8,15},{9,10},{10,... | collective-permute-start | bytes 884744 | tf_op jit(solution)/shard_map/ppermute | solution.py:348
  27.9 0.0 collective-permute-done.6
  27.9 0.5 %collective-permute-start.8 = (f32[864,128]{1,0:T(8,128)S(1)}, f32[864,128]{1,0:T(8,128)S(1)}, u32[]{:S(2)}, u32[]{:S(2)}) collective-permute-start(f32[864,128]{1,0:T(8,128)S(1)} %collective-permute-done.6), channel_id=1, source_target_pairs={{0,8},{8,0},{16,24},{24,16},{1,9},{9,1},{17,25},{25,17},{2,10},{10... | collective-permute-start | bytes 1327112 | tf_op jit(solution)/shard_map/ppermute | solution.py:348
  28.5 1.9 %middle_products.1 = (f32[576,256]{1,0:T(8,128)S(1)}, f32[576,256]{1,0:T(8,128)S(1)}) custom-call(s32[2]{0:T(128)S(1)} %pad_add_fusion.info, bf16[2,3,576,256]{3,2,1,0:T(8,128)(2,1)S(1)} %get-tuple-element.55.own_left, bf16[2,3,768,256]{3,2,1,0:T(8,128)(2,1)S(1)} %get-tuple-element.56.own_right, bf16[2,3,384,256]{3,2,1,0:T(8,128)(2,1)S(1)} %get-tuple-element.57.chip_left, ...), custom_call_target="tpu_custom_call" | custom-call | flops 4000000000 | bytes 20000000 | tf_op jit(solution)/shard_map/middle_products/pallas_call | solution.py:319
  30.4 0.0 collective-permute-done.7.near
  30.4 1.4 %mid_start.1 = (f32[576,256]{1,0:T(8,128)S(1)}, bf16[2,768,256]{2,1,0:T(8,128)(2,1)S(1)}) custom-call(s32[2]{0:T(128)S(1)} %pad_add_fusion.info, f32[864,128]{1,0:T(8,128)S(1)} %collective-permute-done.7.near, f32[576,256]{1,0:T(8,128)S(1)} %get-tuple-element.69.begun, bf16[2,3,576,256]{3,2,1,0:T(8,128)(2,1)S(1)} %get-tuple-element.55.own_left, ...), custom_call_target="tpu_custom_call" | custom-call | flops 4000000000 | bytes 20000000 | tf_op jit(solution)/shard_map/mid_start/pallas_call | solution.py:319
  31.8 0.0 collective-permute-done.4.link_b
  31.8 0.0 collective-permute-done.5.mid
  31.8 1.9 %square_far.1 = (f32[576,256]{1,0:T(8,128)S(1)}, f32[576,128]{1,0:T(8,128)S(1)}, f32[1152,128]{1,0:T(8,128)S(1)}, bf16[2,384,256]{2,1,0:T(8,128)(2,1)S(1)}, bf16[2,768,256]{2,1,0:T(8,128)(2,1)S(1)}) custom-call(s32[2]{0:T(128)S(1)} %pad_add_fusion.info, s32[9,9]{1,0:T(8,128)S(1)} %copy-done, f32[576,128]{1,0:T(8,128)S(1)} %collective-permute-done.4.link_b, ...), custom_call_target="tpu_custom_call" | custom-call | flops 4000000000 | bytes 20000000 | tf_op jit(solution)/shard_map/square_far/pallas_call | solution.py:319
  33.7 2.3 %collective-permute-start.11 = (f32[576,128]{1,0:T(8,128)S(1)}, f32[576,128]{1,0:T(8,128)S(1)}, u32[]{:S(2)}, u32[]{:S(2)}) collective-permute-start(f32[576,128]{1,0:T(8,128)S(1)} %get-tuple-element.82), channel_id=1, source_target_pairs={{0,7},{1,2},{2,1},{3,4},{4,3},{5,6},{6,5},{7,0},{8,15},{9,10},{10,... | collective-permute-start | bytes 884744 | tf_op jit(solution)/shard_map/ppermute | solution.py:348
  36.0 0.0 collective-permute-start.9
  36.0 0.0 collective-permute-done.3.link
  36.0 1.8 %cube_near.1.total = f32[3,576,256]{2,1,0:T(8,128)S(1)} custom-call(s32[2]{0:T(128)S(1)} %pad_add_fusion.info, f32[576,128]{1,0:T(8,128)S(1)} %collective-permute-done.3.link, f32[576,256]{1,0:T(8,128)S(1)} %get-tuple-element.61.s_near.near, f32[576,256]{1,0:T(8,128)S(1)} %get-tuple-element.72.far, bf16[2,768,256]{2,1,0:T(8,128)(2,1)S(1)} %get-tuple-element.59.right_near, ...), custom_call_target="tpu_custom_call" | custom-call | flops 4000000000 | bytes 20000000 | tf_op jit(solution)/shard_map/cube_near/pallas_call | solution.py:319
  37.8 0.0 collective-permute-done.8.far
  37.8 1.9 %square_mid.1 = (f32[576,256]{1,0:T(8,128)S(1)}, f32[576,128]{1,0:T(8,128)S(1)}, f32[288,128]{1,0:T(8,128)S(1)}, f32[288,128]{1,0:T(8,128)S(1)}, bf16[2,768,256]{2,1,0:T(8,128)(2,1)S(1)}) custom-call(s32[2]{0:T(128)S(1)} %pad_add_fusion.info, s32[9,9]{1,0:T(8,128)S(1)} %copy-done, f32[864,128]{1,0:T(8,128)S(1)} %collective-permute-done.8.far, ...), custom_call_target="tpu_custom_call" | custom-call | tf_op jit(solution)/shard_map/square_mid/pallas_call | solution.py:319
  39.7 1.8 %collective-permute-start.13 = (f32[288,128]{1,0:T(8,128)S(1)}, f32[288,128]{1,0:T(8,128)S(1)}, u32[]{:S(2)}, u32[]{:S(2)}) collective-permute-start(f32[288,128]{1,0:T(8,128)S(1)} %get-tuple-element.89), channel_id=1, source_target_pairs={{0,7},{1,2},{2,1},{3,4},{4,3},{5,6},{6,5},{7,0},{8,15},{9,10},{10,... | collective-permute-start | bytes 442376 | tf_op jit(solution)/shard_map/ppermute | solution.py:348
  41.4 0.0 collective-permute-start.12
  41.4 0.0 copy-start.1
  41.4 1.7 %cube_own.1.base = f32[3,576,256]{2,1,0:T(8,128)S(1)} custom-call(s32[2]{0:T(128)S(1)} %pad_add_fusion.info, f32[3,576,256]{2,1,0:T(8,128)S(1)} %cube_near.1.total, f32[576,256]{1,0:T(8,128)S(1)} %get-tuple-element.61.s_near.near, f32[576,256]{1,0:T(8,128)S(1)} %get-tuple-element.87.mid, f32[576,256]{1,0:T(8,128)S(1)} %get-tuple-element.72.far, ...), custom_call_target="tpu_custom_call" | custom-call | flops 4000000000 | bytes 20000000 | tf_op jit(solution)/shard_map/cube_own/pallas_call | solution.py:319
  43.1 0.0 collective-permute-done.9.sides
  43.1 1.9 %collective-permute-start.10 = (f32[288,128]{1,0:T(8,128)S(1)}, f32[288,128]{1,0:T(8,128)S(1)}, u32[]{:S(2)}, u32[]{:S(2)}) collective-permute-start(f32[288,128]{1,0:T(8,128)S(1)} %get-tuple-element.81), channel_id=1, source_target_pairs={{0,7},{1,2},{2,1},{3,4},{4,3},{5,6},{6,5},{7,0},{8,15},{9,10},{10,... | collective-permute-start | bytes 442376 | tf_op jit(solution)/shard_map/ppermute | solution.py:348
  45.0 0.0 collective-permute-done.11.link
  45.0 0.0 collective-permute-done.12.chip
  45.0 0.0 copy-done.1
  45.0 3.3 %cube_chip.1 = (f32[3,576,256]{2,1,0:T(8,128)S(1)}, f32[576,576]{1,0:T(8,128)}) custom-call(s32[2]{0:T(128)S(1)} %pad_add_fusion.info, s32[9,9]{1,0:T(8,128)S(1)} %copy-done.1, f32[576,128]{1,0:T(8,128)S(1)} %collective-permute-done.11.link, f32[1152,128]{1,0:T(8,128)S(1)} %collective-permute-done.9.sides, f32[576,128]{1,0:T(8,128)S(1)} %collective-permute-done.12.chip, ...), custom_call_target="tpu_custom_call" | custom-call | flops 4000000000 | bytes 20000000 | tf_op jit(solution)/shard_map/cube_chip/pallas_call | solution.py:319
  48.4 0.0 collective-permute-done.13.link
  48.4 1.9 %finish_first.1.begun = f32[576,576]{1,0:T(8,128)} custom-call(s32[2]{0:T(128)S(1)} %pad_add_fusion.info, s32[9,9]{1,0:T(8,128)S(1)} %copy-done.1, f32[288,128]{1,0:T(8,128)S(1)} %collective-permute-done.13.link, bf16[2,3,768,256]{3,2,1,0:T(8,128)(2,1)S(1)} %get-tuple-element.56.own_right, ...), custom_call_target="tpu_custom_call", output_to_operand_aliasing={{}: (5, {})} | custom-call | flops 4000000000 | bytes 20000000 | tf_op jit(solution)/shard_map/finish_first/pallas_call | solution.py:319
  50.3 0.0 collective-permute-done.10.link
  50.3 1.9 %finish_second.1 = f32[576,576]{1,0:T(8,128)} custom-call(s32[2]{0:T(128)S(1)} %pad_add_fusion.info, s32[9,9]{1,0:T(8,128)S(1)} %copy-done.1, f32[288,128]{1,0:T(8,128)S(1)} %collective-permute-done.10.link, bf16[2,3,768,256]{3,2,1,0:T(8,128)(2,1)S(1)} %get-tuple-element.56.own_right, ...), custom_call_target="tpu_custom_call", output_to_operand_aliasing={{}: (5, {})} | custom-call | flops 4000000000 | bytes 20000000 | tf_op jit(solution)/shard_map/finish_second/pallas_call | solution.py:319
Async XLA Ops:
  2.5 6.5 %collective-permute-start.2 = (f32[1728,128]{1,0:T(8,128)S(1)}, f32[1728,128]{1,0:T(8,128)S(1)}, u32[]{:S(2)}, u32[]{:S(2)}) collective-permute-start(f32[1728,128]{1,0:T(8,128)S(1)} %get-tuple-element.51), channel_id=1, source_target_pairs={{0,1},{1,0},{2,3},{3,2},{4,5},{5,4},{6,7},{7,6},{8,9},{9,8},{10,11... | collective-permute-start | bytes 2654216 | tf_op jit(solution)/shard_map/ppermute | solution.py:348
  3.0 13.6 %collective-permute-start.1 = (f32[864,128]{1,0:T(8,128)S(1)}, f32[864,128]{1,0:T(8,128)S(1)}, u32[]{:S(2)}, u32[]{:S(2)}) collective-permute-start(f32[864,128]{1,0:T(8,128)S(1)} %get-tuple-element.49), channel_id=1, source_target_pairs={{0,8},{8,0},{16,24},{24,16},{1,9},{9,1},{17,25},{25,17},{2,10},{10... | collective-permute-start | bytes 1327112 | tf_op jit(solution)/shard_map/ppermute | solution.py:348
  5.6 17.2 %collective-permute-start = (f32[1152,128]{1,0:T(8,128)S(1)}, f32[1152,128]{1,0:T(8,128)S(1)}, u32[]{:S(2)}, u32[]{:S(2)}) collective-permute-start(f32[1152,128]{1,0:T(8,128)S(1)} %get-tuple-element.48), channel_id=1, source_target_pairs={{0,7},{1,2},{2,1},{3,4},{4,3},{5,6},{6,5},{7,0},{8,15},{9,10},{10,... | collective-permute-start | bytes 1769480 | tf_op jit(solution)/shard_map/ppermute | solution.py:348
  9.8 22.0 %collective-permute-start.4 = (f32[576,128]{1,0:T(8,128)S(1)}, f32[576,128]{1,0:T(8,128)S(1)}, u32[]{:S(2)}, u32[]{:S(2)}) collective-permute-start(f32[576,128]{1,0:T(8,128)S(1)} %get-tuple-element.63), channel_id=1, source_target_pairs={{0,7},{1,2},{2,1},{3,4},{4,3},{5,6},{6,5},{7,0},{8,15},{9,10},{10,... | collective-permute-start | bytes 884744 | tf_op jit(solution)/shard_map/ppermute | solution.py:348
  10.6 17.3 %collective-permute-start.6 = (f32[864,128]{1,0:T(8,128)S(1)}, f32[864,128]{1,0:T(8,128)S(1)}, u32[]{:S(2)}, u32[]{:S(2)}) collective-permute-start(f32[864,128]{1,0:T(8,128)S(1)} %get-tuple-element.64), channel_id=1, source_target_pairs={{0,16},{8,24},{16,0},{24,8},{1,17},{9,25},{17,1},{25,9},{2,18},{10... | collective-permute-start | bytes 1327112 | tf_op jit(solution)/shard_map/ppermute | solution.py:348
  12.2 18.2 %collective-permute-start.7 = (f32[864,128]{1,0:T(8,128)S(1)}, f32[864,128]{1,0:T(8,128)S(1)}, u32[]{:S(2)}, u32[]{:S(2)}) collective-permute-start(f32[864,128]{1,0:T(8,128)S(1)} %get-tuple-element.68), channel_id=1, source_target_pairs={{0,8},{8,0},{16,24},{24,16},{1,9},{9,1},{17,25},{25,17},{2,10},{10... | collective-permute-start | bytes 1327112 | tf_op jit(solution)/shard_map/ppermute | solution.py:348
  16.6 15.2 %collective-permute-start.5 = (f32[864,128]{1,0:T(8,128)S(1)}, f32[864,128]{1,0:T(8,128)S(1)}, u32[]{:S(2)}, u32[]{:S(2)}) collective-permute-start(f32[864,128]{1,0:T(8,128)S(1)} %collective-permute-done.1.mid), channel_id=1, source_target_pairs={{0,16},{8,24},{16,0},{24,8},{1,17},{9,25},{17,1},{25,9},{2,18},{10... | collective-permute-start | bytes 1327112 | tf_op jit(solution)/shard_map/ppermute | solution.py:348
  18.6 4.2 %copy-start = (s32[9,9]{1,0:T(8,128)S(1)}, s32[9,9]{1,0:T(8,128)}, u32[]{:S(2)}) copy-start(s32[9,9]{1,0:T(8,128)} %kept.8) | copy-start | bytes 976
  24.2 11.8 %collective-permute-start.3 = (f32[576,128]{1,0:T(8,128)S(1)}, f32[576,128]{1,0:T(8,128)S(1)}, u32[]{:S(2)}, u32[]{:S(2)}) collective-permute-start(f32[576,128]{1,0:T(8,128)S(1)} %get-tuple-element.60), channel_id=1, source_target_pairs={{0,7},{1,2},{2,1},{3,4},{4,3},{5,6},{6,5},{7,0},{8,15},{9,10},{10,... | collective-permute-start | bytes 884744 | tf_op jit(solution)/shard_map/ppermute | solution.py:348
  27.9 9.8 %collective-permute-start.8 = (f32[864,128]{1,0:T(8,128)S(1)}, f32[864,128]{1,0:T(8,128)S(1)}, u32[]{:S(2)}, u32[]{:S(2)}) collective-permute-start(f32[864,128]{1,0:T(8,128)S(1)} %collective-permute-done.6), channel_id=1, source_target_pairs={{0,8},{8,0},{16,24},{24,16},{1,9},{9,1},{17,25},{25,17},{2,10},{10... | collective-permute-start | bytes 1327112 | tf_op jit(solution)/shard_map/ppermute | solution.py:348
  33.7 11.4 %collective-permute-start.11 = (f32[576,128]{1,0:T(8,128)S(1)}, f32[576,128]{1,0:T(8,128)S(1)}, u32[]{:S(2)}, u32[]{:S(2)}) collective-permute-start(f32[576,128]{1,0:T(8,128)S(1)} %get-tuple-element.82), channel_id=1, source_target_pairs={{0,7},{1,2},{2,1},{3,4},{4,3},{5,6},{6,5},{7,0},{8,15},{9,10},{10,... | collective-permute-start | bytes 884744 | tf_op jit(solution)/shard_map/ppermute | solution.py:348
  36.0 7.2 %collective-permute-start.9 = (f32[1152,128]{1,0:T(8,128)S(1)}, f32[1152,128]{1,0:T(8,128)S(1)}, u32[]{:S(2)}, u32[]{:S(2)}) collective-permute-start(f32[1152,128]{1,0:T(8,128)S(1)} %get-tuple-element.80), channel_id=1, source_target_pairs={{0,1},{1,0},{2,3},{3,2},{4,5},{5,4},{6,7},{7,6},{8,9},{9,8},{10,11... | collective-permute-start | bytes 1769480 | tf_op jit(solution)/shard_map/ppermute | solution.py:348
  39.7 8.7 %collective-permute-start.13 = (f32[288,128]{1,0:T(8,128)S(1)}, f32[288,128]{1,0:T(8,128)S(1)}, u32[]{:S(2)}, u32[]{:S(2)}) collective-permute-start(f32[288,128]{1,0:T(8,128)S(1)} %get-tuple-element.89), channel_id=1, source_target_pairs={{0,7},{1,2},{2,1},{3,4},{4,3},{5,6},{6,5},{7,0},{8,15},{9,10},{10,... | collective-permute-start | bytes 442376 | tf_op jit(solution)/shard_map/ppermute | solution.py:348
  41.4 3.6 %collective-permute-start.12 = (f32[576,128]{1,0:T(8,128)S(1)}, f32[576,128]{1,0:T(8,128)S(1)}, u32[]{:S(2)}, u32[]{:S(2)}) collective-permute-start(f32[576,128]{1,0:T(8,128)S(1)} %get-tuple-element.84), channel_id=1, source_target_pairs={{0,1},{1,0},{2,3},{3,2},{4,5},{5,4},{6,7},{7,6},{8,9},{9,8},{10,11... | collective-permute-start | bytes 884744 | tf_op jit(solution)/shard_map/ppermute | solution.py:348
  41.4 3.6 %copy-start.1 = (s32[9,9]{1,0:T(8,128)S(1)}, s32[9,9]{1,0:T(8,128)}, u32[]{:S(2)}) copy-start(s32[9,9]{1,0:T(8,128)} %kept.11) | copy-start | bytes 976
  43.1 7.2 %collective-permute-start.10 = (f32[288,128]{1,0:T(8,128)S(1)}, f32[288,128]{1,0:T(8,128)S(1)}, u32[]{:S(2)}, u32[]{:S(2)}) collective-permute-start(f32[288,128]{1,0:T(8,128)S(1)} %get-tuple-element.81), channel_id=1, source_target_pairs={{0,7},{1,2},{2,1},{3,4},{4,3},{5,6},{6,5},{7,0},{8,15},{9,10},{10,... | collective-permute-start | bytes 442376 | tf_op jit(solution)/shard_map/ppermute | solution.py:348
